TPU v7x, 32 devices: a whole 2x2x4 slice. The times are simulated.
32 devices in a mesh: grp: 8 (over y, x, core), seq: 4 (over z).
Axes of the slice: x: 2, y: 2, z: 4, core: 2. Of those that a mesh axis runs over, the one named last changes fastest.
Arguments:
- tokens: bfloat16 [8192, 2048], P(('grp', 'seq')), may hold values from -6 to 6
- cotangent: bfloat16 [8192, 2048], P(('grp', 'seq')), may hold values from -6 to 6
- segment_ids: int32 [8192], P(('grp', 'seq')), may hold values from 0 to 31, never falling along the last dimension, each value on 1 to 768 neighbouring positions
- tile_owner_slots: int32 [166], replicated, may hold values from 0 to 167, as said below
- weights_low: bfloat16 [168, 2048, 128], P('grp', 'seq')
- master: float32 [168, 2048, 128], P('grp', 'seq')
- moment_one: float32 [168, 2048, 128], P('grp', 'seq')
- moment_two: float32 [168, 2048, 128], P('grp', 'seq'), as said below
- left_basis_set: float32 [168, 2048, 512], P('grp', 'seq'), as said below
- right_basis_set: float32 [168, 512, 128], P('grp', 'seq'), as said below
- gains: float32 [2, 2048], replicated, may hold values from 0.5 to 1.5
- gain_moment_one: float32 [2, 2048], replicated, may hold values from -28 to 28
- gain_moment_two: float32 [2, 2048], replicated, may hold values from 430.8992 to 1720.32
Outputs:
- block_out: bfloat16 [8192, 2048], P(('grp', 'seq'))
- input_grad: float32 [8192, 2048], P(('grp', 'seq'))
- new_master: float32 [168, 2048, 128], P('grp', 'seq')
- new_moment_one: float32 [168, 2048, 128], P('grp', 'seq')
- new_moment_two: float32 [168, 2048, 128], P('grp', 'seq')
- gain_grads: float32 [2, 2048], replicated
- new_gains: float32 [2, 2048], replicated
- new_gain_one: float32 [2, 2048], replicated
- new_gain_two: float32 [2, 2048], replicated
Inputs may be any that keep to these rules, and one draw needn't show every extreme that they name: `tile_owner_slots`: the entries are distinct; slot q belongs to data group q // 21. `segment_ids`: never falls along the tokens. `left_basis_set`: each 512 x 512 block is orthogonal. `right_basis_set`: each 128 x 128 block is orthogonal. `moment_two`: positive.
All inputs are finite; a program needn't handle non-finite values.
Results may differ from a plain program's by a relative error of at most 0.015.
Values may be sent and summed in bfloat16 or wider, within the bound.
A program may use at most 704 MiB of HBM per device.

v0:
```python
import jax
import jax.numpy as jnp
from jax import lax
from jax.sharding import PartitionSpec as P

MODEL_WIDTH = 2048
NH = 16
HD = 128
FF = 5632
SEQLEN = 1024


NORM_EPS = 1e-05
BETA_ONE = 0.95
BETA_TWO = 0.95
ADAM_EPS = 1e-08
WEIGHT_DECAY = 0.01
LEARN_RATE = 0.03
GAIN_RATE = 1.5
ROPE_BASE = 10000.0
MASKED = -1e30
PRECISE = lax.Precision.HIGHEST


def rotate(values, positions, direction):
    head_width = values.shape[-1]
    half_width = head_width // 2
    frequency = ROPE_BASE ** (-(jnp.arange(half_width, dtype=jnp.float32) * 2.0) / head_width)
    angles = positions.astype(jnp.float32)[:, None] * frequency[None, :]
    cosine = jnp.cos(angles)[:, None, :]
    sine_part = (jnp.sin(angles) * direction)[:, None, :]
    leading = values[..., :half_width]
    trailing = values[..., half_width:]
    return jnp.concatenate(
        [leading * cosine - trailing * sine_part, trailing * cosine + leading * sine_part], axis=-1
    )


def visible(query_index, key_index, query_seg, key_seg):
    causal = query_index[:, None] >= key_index[None, :]
    same_seq = query_index[:, None] // SEQLEN == key_index[None, :] // SEQLEN
    same_doc = query_seg[:, None] == key_seg[None, :]
    return causal & same_seq & same_doc


def contract(left_side, right_side):
    return lax.dot_general(
        left_side, right_side, (((0,), (0,)), ((), ())), preferred_element_type=jnp.float32
    )


def times_transpose(left_side, right_side):
    return lax.dot_general(
        left_side, right_side, (((1,), (1,)), ((), ())), preferred_element_type=jnp.float32
    )


def attend(queries, key_rows, value_rows, query_index, query_seg, key_index, key_seg):
    query_total, head_count, head_width = queries.shape
    block_rows = min(512, query_total)
    block_count = query_total // block_rows
    score_scale = head_width ** (-0.5)

    def one_block(inputs):
        block_queries, block_index, block_seg = inputs
        raw_scores = jnp.einsum(
            "qhd,kd->hqk", block_queries, key_rows, preferred_element_type=jnp.float32
        )
        allowed = visible(block_index, key_index, block_seg, key_seg)
        score_matrix = jnp.where(allowed[None], raw_scores * score_scale, MASKED)
        highest = jnp.max(score_matrix, axis=-1, keepdims=True)
        exponent = jnp.exp(score_matrix - highest)
        totals = jnp.sum(exponent, axis=-1, keepdims=True)
        probs_low = (exponent / totals).astype(jnp.bfloat16)
        context = jnp.einsum(
            "hqk,kd->qhd", probs_low, value_rows, preferred_element_type=jnp.float32
        )
        return (context, jnp.transpose((highest + jnp.log(totals))[..., 0]))

    context, log_totals = lax.map(
        one_block,
        (
            queries.reshape(block_count, block_rows, head_count, head_width),
            query_index.reshape(block_count, block_rows),
            query_seg.reshape(block_count, block_rows),
        ),
    )
    return (
        context.reshape(query_total, head_count, head_width),
        log_totals.reshape(query_total, head_count),
    )


def attend_back(
    queries, key_rows, value_rows, grads_low, log_totals, query_index, query_seg, key_index, key_seg
):
    query_total, head_count, head_width = queries.shape
    block_rows = min(512, query_total)
    block_count = query_total // block_rows
    score_scale = head_width ** (-0.5)

    def one_block(running, inputs):
        block_queries, block_grads, block_totals, block_index, block_seg = inputs
        raw_scores = jnp.einsum(
            "qhd,kd->hqk", block_queries, key_rows, preferred_element_type=jnp.float32
        )
        allowed = visible(block_index, key_index, block_seg, key_seg)
        shifted = raw_scores * score_scale - jnp.transpose(block_totals)[:, :, None]
        probs = jnp.where(allowed[None], jnp.exp(shifted), 0.0)
        prob_grad = jnp.einsum(
            "qhd,kd->hqk", block_grads, value_rows, preferred_element_type=jnp.float32
        )
        centre = jnp.sum(probs * prob_grad, axis=-1, keepdims=True)
        score_grad = (probs * (prob_grad - centre) * score_scale).astype(jnp.bfloat16)
        query_part = jnp.einsum(
            "hqk,kd->qhd", score_grad, key_rows, preferred_element_type=jnp.float32
        )
        key_part = running[0] + jnp.einsum(
            "hqk,qhd->kd", score_grad, block_queries, preferred_element_type=jnp.float32
        )
        value_part = running[1] + jnp.einsum(
            "hqk,qhd->kd",
            probs.astype(jnp.bfloat16),
            block_grads,
            preferred_element_type=jnp.float32,
        )
        return ((key_part, value_part), query_part)

    zeros_rows = jnp.zeros(key_rows.shape, jnp.float32)
    (key_grad, value_grad), query_grad = lax.scan(
        one_block,
        (zeros_rows, zeros_rows),
        (
            queries.reshape(block_count, block_rows, head_count, head_width),
            grads_low.reshape(block_count, block_rows, head_count, head_width),
            log_totals.reshape(block_count, block_rows, head_count),
            query_index.reshape(block_count, block_rows),
            query_seg.reshape(block_count, block_rows),
        ),
    )
    return (query_grad.reshape(query_total, head_count, head_width), key_grad, value_grad)


def local(
    tokens,
    cotangent,
    segment_ids,
    tile_owner_slots,
    weights_low,
    master,
    moment_one,
    moment_two,
    left_basis_set,
    right_basis_set,
    gains,
    gain_moment_one,
    gain_moment_two,
):
    grp_count = lax.axis_size("grp")
    seq_count = lax.axis_size("seq")
    rows_here = tokens.shape[0]
    slots_here, rows_block, tile_width = weights_low.shape
    tile_count = tile_owner_slots.shape[0]
    query_cols = NH * HD
    value_end = query_cols + 2 * HD
    output_end = value_end + MODEL_WIDTH
    gating_end = output_end + 2 * FF
    local_index = lax.axis_index("seq") * rows_here + jnp.arange(rows_here, dtype=jnp.int32)
    local_place = local_index % SEQLEN
    grid = lax.all_gather(weights_low[None], ("grp", "seq"), axis=0, tiled=True).reshape(
        grp_count, seq_count, slots_here, rows_block, tile_width
    )
    picked = grid[tile_owner_slots // slots_here, :, tile_owner_slots % slots_here]
    weight_cols = jnp.transpose(picked, (1, 2, 0, 3)).reshape(
        seq_count * rows_block, tile_count * tile_width
    )
    tok_float = tokens.astype(jnp.float32)
    inverse_one = lax.rsqrt(jnp.mean(tok_float * tok_float, axis=-1, keepdims=True) + NORM_EPS)
    normed = (tok_float * inverse_one * gains[0]).astype(jnp.bfloat16)
    projected = jnp.dot(normed, weight_cols[:, :value_end], preferred_element_type=jnp.float32)
    queries = rotate(projected[:, :query_cols].reshape(rows_here, NH, HD), local_place, 1.0).astype(
        jnp.bfloat16
    )
    key_rows = (
        rotate(
            projected[:, query_cols : query_cols + HD].reshape(rows_here, 1, HD), local_place, 1.0
        )
        .reshape(rows_here, HD)
        .astype(jnp.bfloat16)
    )
    value_rows = projected[:, query_cols + HD : value_end].astype(jnp.bfloat16)
    all_keys, all_values, all_segs = (
        lax.all_gather(key_rows, "seq", axis=0, tiled=True),
        lax.all_gather(value_rows, "seq", axis=0, tiled=True),
        lax.all_gather(segment_ids, "seq", axis=0, tiled=True),
    )
    group_index = jnp.arange(all_keys.shape[0], dtype=jnp.int32)
    group_place = group_index % SEQLEN
    heads_here = NH // seq_count
    head_queries = lax.all_to_all(
        queries.reshape(rows_here, query_cols), "seq", split_axis=1, concat_axis=0, tiled=True
    ).reshape(-1, heads_here, HD)
    head_context, log_totals = attend(
        head_queries, all_keys, all_values, group_index, all_segs, group_index, all_segs
    )
    context = lax.all_to_all(
        head_context.reshape(-1, heads_here * HD).astype(jnp.bfloat16),
        "seq",
        split_axis=0,
        concat_axis=1,
        tiled=True,
    )
    branch = jnp.dot(
        context, weight_cols[:, value_end:output_end], preferred_element_type=jnp.float32
    )
    hidden = tok_float + branch
    inverse_two = lax.rsqrt(jnp.mean(hidden * hidden, axis=-1, keepdims=True) + NORM_EPS)
    normed_two = (hidden * inverse_two * gains[1]).astype(jnp.bfloat16)
    gate_up = jnp.dot(
        normed_two, weight_cols[:, output_end:gating_end], preferred_element_type=jnp.float32
    )
    gate = gate_up[:, :FF]
    upper = gate_up[:, FF:]
    sigmoid_gate = jax.nn.sigmoid(gate)
    silu_gate = jax.nn.silu(gate)
    activated = (silu_gate * upper).astype(jnp.bfloat16)
    result = hidden + times_transpose(activated, weight_cols[:, gating_end:])
    block_out = result.astype(jnp.bfloat16)
    out_grad = cotangent.astype(jnp.float32)
    act_grad = jnp.dot(cotangent, weight_cols[:, gating_end:], preferred_element_type=jnp.float32)
    gate_grad = (act_grad * upper * sigmoid_gate * (1.0 + gate * (1.0 - sigmoid_gate))).astype(
        jnp.bfloat16
    )
    up_grad = (act_grad * silu_gate).astype(jnp.bfloat16)
    gating_grad = jnp.concatenate([gate_grad, up_grad], axis=1)
    norm_two_grad = times_transpose(gating_grad, weight_cols[:, output_end:gating_end])
    gain_two_term = jnp.sum(norm_two_grad * hidden * inverse_two, axis=0)
    hidden_grad = (
        out_grad
        + inverse_two * gains[1] * norm_two_grad
        - hidden
        * inverse_two**3
        * jnp.mean(hidden * gains[1] * norm_two_grad, axis=-1, keepdims=True)
    )
    branch_grad = hidden_grad.astype(jnp.bfloat16)
    context_grad = times_transpose(branch_grad, weight_cols[:, value_end:output_end]).astype(
        jnp.bfloat16
    )
    head_grads = lax.all_to_all(
        context_grad, "seq", split_axis=1, concat_axis=0, tiled=True
    ).reshape(-1, heads_here, HD)
    head_query_grad, key_part, value_part = attend_back(
        head_queries,
        all_keys,
        all_values,
        head_grads,
        log_totals,
        group_index,
        all_segs,
        group_index,
        all_segs,
    )
    turned_query = (
        rotate(head_query_grad, group_place, -1.0).reshape(-1, heads_here * HD).astype(jnp.bfloat16)
    )
    query_grad = lax.all_to_all(turned_query, "seq", split_axis=0, concat_axis=1, tiled=True)
    key_part = rotate(key_part[:, None, :], group_place, -1.0)[:, 0, :]
    key_grad, value_grad = (
        lax.psum_scatter(key_part, "seq", scatter_dimension=0, tiled=True),
        lax.psum_scatter(value_part, "seq", scatter_dimension=0, tiled=True),
    )
    projected_grad = jnp.concatenate(
        [query_grad, key_grad.astype(jnp.bfloat16), value_grad.astype(jnp.bfloat16)], axis=1
    )
    norm_one_grad = times_transpose(projected_grad, weight_cols[:, :value_end])
    gain_one_term = jnp.sum(norm_one_grad * tok_float * inverse_one, axis=0)
    input_grad = (
        hidden_grad
        + inverse_one * gains[0] * norm_one_grad
        - tok_float
        * inverse_one**3
        * jnp.mean(tok_float * gains[0] * norm_one_grad, axis=-1, keepdims=True)
    )
    grad_shard = lax.psum_scatter(
        jnp.concatenate(
            [
                contract(normed, projected_grad),
                contract(context, branch_grad),
                contract(normed_two, gating_grad),
                contract(cotangent, activated),
            ],
            axis=1,
        ).astype(jnp.bfloat16),
        "seq",
        scatter_dimension=0,
        tiled=True,
    ).astype(jnp.float32)
    grad_tiles = jnp.transpose(grad_shard.reshape(rows_block, tile_count, tile_width), (1, 0, 2))
    placed = (
        jnp.zeros((grp_count * slots_here, rows_block, tile_width), jnp.float32)
        .at[tile_owner_slots]
        .set(grad_tiles)
    )
    received = lax.all_to_all(
        placed.reshape(grp_count, slots_here, rows_block, tile_width).astype(jnp.bfloat16),
        "grp",
        split_axis=0,
        concat_axis=0,
        tiled=True,
    ).astype(jnp.float32)
    reduced_sum = jnp.sum(received, axis=0)
    gain_grads = lax.psum(jnp.stack([gain_one_term, gain_two_term]), ("grp", "seq"))
    turned = jnp.einsum("zji,zjc->zic", left_basis_set, reduced_sum, precision=PRECISE)
    turned = jnp.einsum("zic,zcd->zid", turned, right_basis_set, precision=PRECISE)
    new_one = BETA_ONE * moment_one + (1.0 - BETA_ONE) * turned
    new_two = BETA_TWO * moment_two + (1.0 - BETA_TWO) * turned * turned
    scaled = new_one / (jnp.sqrt(new_two) + ADAM_EPS)
    restored = jnp.einsum("zij,zjd->zid", left_basis_set, scaled, precision=PRECISE)
    restored = jnp.einsum("zid,zed->zie", restored, right_basis_set, precision=PRECISE)
    new_master = master * (1.0 - LEARN_RATE * WEIGHT_DECAY) - LEARN_RATE * restored
    gain_one = BETA_ONE * gain_moment_one + (1.0 - BETA_ONE) * gain_grads
    gain_two = BETA_TWO * gain_moment_two + (1.0 - BETA_TWO) * gain_grads * gain_grads
    new_gains = gains - GAIN_RATE * gain_one / (jnp.sqrt(gain_two) + ADAM_EPS)
    return (
        block_out,
        input_grad,
        new_master,
        new_one,
        new_two,
        gain_grads,
        new_gains,
        gain_one,
        gain_two,
    )


def solution(mesh):
    return jax.shard_map(
        local,
        mesh=mesh,
        in_specs=(
            P(("grp", "seq"), None),
            P(("grp", "seq"), None),
            P(("grp", "seq")),
            P(),
            P("grp", "seq", None),
            P("grp", "seq", None),
            P("grp", "seq", None),
            P("grp", "seq", None),
            P("grp", "seq", None),
            P("grp", "seq", None),
            P(),
            P(),
            P(),
        ),
        out_specs=(
            P(("grp", "seq"), None),
            P(("grp", "seq"), None),
            P("grp", "seq", None),
            P("grp", "seq", None),
            P("grp", "seq", None),
            P(),
            P(),
            P(),
            P(),
        ),
        check_vma=False,
    )
```

profile of v0, /device:TPU:0, one launch (start us, length us, event | category | flops | bytes accessed | tf_op | source)
XLA Modules:
  0.0 3165.8 jit_solution(15272076917358920668)
XLA Ops:
  13.7 456.7 %all-gather.5.cloned.1.call-done = bf16[672,512,128]{2,1,0:T(8,128)(2,1)} async-done(((bf16[21,512,128]{2,1,0:T(8,128)(2,1)}), bf16[672,512,128]{2,1,0:T(8,128)(2,1)}) %all-gather.5.cloned.1.call-update) | async-done | bytes 88080400 | tf_op jit(solution)/shard_map/all_gather | solution.py:170
  470.3 59.6 %gather_fusion = bf16[166,4,512,128]{3,2,1,0:T(8,128)(2,1)} fusion(bf16[8,4,21,512,128]{4,3,2,1,0:T(8,128)(2,1)} %bitcast.3, s32[166]{0:T(256)S(1)} %get-tuple-element.697), kind=kCustom, calls=%fused_computation | custom fusion | bytes 174064944 | tf_op jit(solution)/shard_map/gather | solution.py:173
  529.9 78.5 %copy.97 = bf16[4,512,166,128]{3,2,1,0:T(8,128)(2,1)} copy(bf16[4,512,166,128]{3,1,0,2:T(8,128)(2,1)} %bitcast.4) | data formatting | bytes 174063616 | tf_op jit(solution)/shard_map/transpose | solution.py:174
  608.4 58.0 %copy.151 = bf16[256,8,166,128]{3,1,2,0:T(8,128)(2,1)} copy(bf16[256,8,166,128]{3,2,1,0:T(8,128)(2,1)} %bitcast.63) | data formatting | bytes 174063616
  666.4 6.3 fusion.91
  683.5 23.6 all-gather.2
  709.5 18.3 all-gather.1
  728.0 14.5 all_gather.15
  747.3 18.7 while.36
  771.3 23.4 all_to_all.66
  797.0 7.7 multiply_reduce_fusion.2
  804.7 24.9 fusion.83
  829.6 17.0 multiply_convert_fusion.1
  846.6 22.7 multiply_reduce_fusion
  872.4 6.5 fusion.115
  887.6 19.4 all-to-all-done.2
  909.1 94.3 %while.37 = (s32[]{:T(128)}, f32[1024,128]{1,0:T(8,128)}, f32[1024,128]{1,0:T(8,128)}, f32[2,512,4,128]{3,1,0,2:T(8,128)}, s32[2,512]{1,0:T(2,128)S(1)}, /*index...) while((s32[]{:T(128)}, f32[1024,128]{1,0:T(8,128)}, ...), condition=%wide.region_9.10_spmd.clone.clone, body=%wide.region_7.9_spmd.clone.clone.sunk | while | flops 2742048256 | bytes 136143056 | solution.py:130
  915.8 4.5 fusion.204
  920.3 17.2 fusion.207
  937.5 18.0 fusion.209
  958.8 4.7 fusion.208
  963.5 4.5 fusion.204
  968.0 17.2 fusion.207
  985.2 18.0 fusion.209
  1006.7 21.6 convolution_convert_fusion
  1034.9 4.2 all-to-all-start.3
  1039.2 6.9 convolution_convert_fusion.2
  1046.1 12.4 copy.117
  1060.6 13.2 convert_bitcast_fusion.1
  1074.7 8.0 reduce-scatter.8.cloned.1.call-done
  1085.8 7.3 convolution_convert_fusion.1
  1093.1 56.7 %pad_maximum_fusion = bf16[2048,21248]{1,0:T(8,128)(2,1)} fusion(bf16[2048,5632]{1,0:T(8,128)(2,1)} %convert_bitcast_fusion.1, bf16[2048,11264]{1,0:T(8,128)(2,1)} %convolution_convert_fusion, bf16[2048,2048]{1,0:T(8,128)(2,1)} %copy.117, bf16[2048,2304]{1,0:T(8,128)(2,1)} %convolution_convert_fusion.1), kind=kLoop, calls=%fused_computation.104 | loop fusion | flops 348127232 | bytes 174063616 | tf_op jit(solution)/shard_map/concatenate | solution.py:285
  1149.9 1413.5 %reduce-scatter.10.cloned.1.call-done = bf16[512,21248]{1,0:T(8,128)(2,1)} async-done(((bf16[2048,21248]{1,0:T(8,128)(2,1)}), bf16[512,21248]{1,0:T(8,128)(2,1)}) %reduce-scatter.10.cloned.1.call-update) | async-done | bytes 21757968
  2563.4 28.6 copy.118
  2591.9 23.6 convert_bitcast_fusion
  2615.5 42.6 %copy.119 = f32[166,512,128]{2,1,0:T(8,128)} copy(f32[166,512,128]{1,2,0:T(8,128)} %convert_bitcast_fusion) | data formatting | bytes 87031808 | tf_op jit(solution)/shard_map/transpose | solution.py:298
  2658.2 14.5 broadcast_in_dim.129
  2672.6 78.0 %scatter_fusion = f32[168,512,128]{2,1,0:T(8,128)} fusion(f32[168,512,128]{2,1,0:T(8,128)} %broadcast_in_dim.129, s32[166]{0:T(256)S(1)} %copy-done.31, f32[166,512,128]{2,1,0:T(8,128)} %copy.119), kind=kCustom, calls=%fused_computation.1 | custom fusion | bytes 130548376 | tf_op jit(solution)/shard_map/scatter | solution.py:302
  2750.7 23.9 convert_element_type.140
  2774.6 6.5 all-to-all-start.4
  2781.1 12.4 fusion.112
  2793.5 9.1 fusion.126
  2802.6 251.9 %psum.7 = f32[2,2048]{1,0:T(2,128)S(1)} all-reduce(f32[2,2048]{1,0:T(2,128)S(1)} %pad_maximum_fusion.10), channel_id=1, replica_groups=mesh['grp'=8,'seq'=4] {'grp','seq'}, use_global_device_ids=true, to_apply=%region_18.19 | all-reduce | flops 4096 | bytes 32768 | tf_op jit(solution)/shard_map/psum | solution.py:312
  3060.5 13.7 convert_reduce_fusion
  3074.3 38.4 %fusion.164 = f32[21,128,512]{1,2,0:T(8,128)S(1)} fusion(f32[21,512,128]{2,1,0:T(8,128)S(1)} %convert_reduce_fusion, f32[21,512,512]{2,1,0:T(8,128)} %param.25), kind=kOutput, calls=%fused_computation.241 | convolution fusion | flops 8455716864 | bytes 33030144 | tf_op jit(solution)/shard_map/zji,zjc->zic/dot_general | solution.py:313
  3112.7 9.6 fusion.101
  3122.4 27.0 fusion.102
  3149.4 9.3 multiply_subtract_fusion
  (180 shorter events, 96.3 us)
Async XLA Ops:
  7.2 3105.5 %copy-start = (f32[21,128,128]{2,1,0:T(8,128)S(1)}, f32[21,128,128]{2,1,0:T(8,128)}, u32[]{:S(2)}) copy-start(f32[21,128,128]{2,1,0:T(8,128)} %param.26) | copy-start | bytes 4128772
  7.2 463.1 %all-gather.5.cloned.1.call-start = ((), (), s32[]{:S(2)}) async-start(), calls=%async_computation.10 | async-start | bytes 90832896 | tf_op jit(solution)/shard_map/all_gather | solution.py:170
  7.9 522.0 %copy-start.27 = (f32[64]{0:T(128)}, f32[64]{0:T(128)S(1)}, u32[]{:S(2)}) copy-start(f32[64]{0:T(128)S(1)} %multiply_power_fusion) | copy-start | bytes 772
  8.0 521.9 %copy-start.32 = (f32[256]{0:T(256)}, f32[256]{0:T(256)S(1)}, u32[]{:S(2)}) copy-start(f32[256]{0:T(256)S(1)} %fusion.152) | copy-start | bytes 3076
  10.0 656.4 %copy-start.24 = (f32[256]{0:T(256)}, f32[256]{0:T(256)S(1)}, u32[]{:S(2)}) copy-start(f32[256]{0:T(256)S(1)} %get-tuple-element.699) | copy-start | bytes 3076
  13.7 652.8 %copy-start.20 = (f32[1,2048]{1,0:T(1,128)}, f32[1,2048]{1,0:T(1,128)S(1)}, u32[]{:S(2)}) copy-start(f32[1,2048]{1,0:T(1,128)S(1)} %get-tuple-element.691) | copy-start | bytes 24580
  608.4 58.0 %copy-start.7 = (bf16[256,2048]{1,0:T(8,128)(2,1)S(1)}, bf16[256,2048]{1,0:T(8,128)(2,1)}, u32[]{:S(2)}) copy-start(bf16[256,2048]{1,0:T(8,128)(2,1)} %param.17) | copy-start | bytes 3145732
  672.8 1.4 copy-start.13
  674.2 3.6 copy-start.19
  675.8 7.7 copy-start.35
  675.8 33.3 %copy-start.28 = (f32[64]{0:T(128)S(1)}, f32[64]{0:T(128)}, u32[]{:S(2)}) copy-start(f32[64]{0:T(128)} %copy-done.27) | copy-start | bytes 772
  675.8 33.3 %copy-start.33 = (f32[256]{0:T(256)S(1)}, f32[256]{0:T(256)}, u32[]{:S(2)}) copy-start(f32[256]{0:T(256)} %copy-done.32) | copy-start | bytes 3076
  680.0 62.5 %all-to-all-start = ((bf16[256,4,512]{0,2,1:T(8,128)(2,1)}), bf16[256,4,512]{0,2,1:T(8,128)(2,1)S(1)}, u32[]{:S(2)}, u32[]{:S(2)}) async-start(bf16[256,4,512]{0,2,1:T(8,128)(2,1)} %bitcast.5), calls=%async_computation | async-start | bytes 2097152 | tf_op jit(solution)/shard_map/all_to_all | solution.py:200
  750.0 2.5 copy-start.14
  755.8 1.0 copy-start.15
  759.4 2.5 copy-start.14
  765.1 1.0 copy-start.15
  797.0 7.7 copy-start.16
  872.4 6.5 copy-start.4
  872.4 11.9 copy-start.29
  880.0 27.0 all-to-all-start.2
  884.2 189.6 %reduce-scatter.6.cloned.1.call-start = ((), (), s32[]{:S(2)}) async-start(), calls=%async_computation.8 | async-start | bytes 655360 | tf_op jit(solution)/shard_map/reduce_scatter | solution.py:269
  912.4 3.4 copy-start.1
  958.7 4.8 copy-start.1
  1006.7 21.7 copy-start.10
  1030.3 8.9 copy-start.5
  1034.9 49.3 %all-to-all-start.3 = ((bf16[4,256,512]{2,1,0:T(8,128)(2,1)}), bf16[4,256,512]{2,1,0:T(8,128)(2,1)}, u32[]{:S(2)}, u32[]{:S(2)}) async-start(bf16[4,256,512]{2,1,0:T(8,128)(2,1)} %convert_element_type.137), calls=%async_computation.3 | async-start | bytes 2097152 | tf_op jit(solution)/shard_map/all_to_all | solution.py:266
  1039.2 43.5 %reduce-scatter.8.cloned.1.call-start = ((), (), s32[]{:S(2)}) async-start(), calls=%async_computation.9 | async-start | bytes 655360 | tf_op jit(solution)/shard_map/reduce_scatter | solution.py:270
  1046.1 14.5 copy-start.12
  1060.5 1502.8 %reduce-scatter.10.cloned.1.call-start = ((), (), s32[]{:S(2)}) async-start(), calls=%async_computation.11 | async-start | bytes 108789760
  1060.6 25.1 copy-start.8
  1060.6 25.1 copy-start.21
  1060.6 25.1 copy-start.25
  1074.7 18.4 copy-start.17
  1085.7 7.4 copy-start.11
  2658.1 14.5 copy-start.31
  2774.6 6.5 copy-start.9
  2774.6 286.0 %all-to-all-start.4 = ((bf16[8,21,512,128]{3,2,1,0:T(8,128)(2,1)}), bf16[8,21,512,128]{3,2,1,0:T(8,128)(2,1)}, u32[]{:S(2)}, u32[]{:S(2)}) async-start(bf16[8,21,512,128]{3,2,1,0:T(8,128)(2,1)} %bitcast.279), calls=%async_computation.6 | async-start | bytes 44040192 | tf_op jit(solution)/shard_map/all_to_all | solution.py:304
  2781.1 12.4 copy-start.18
  2781.1 12.4 copy-start.22
  2781.1 12.4 copy-start.26
  2793.5 9.1 copy-start.30
  2793.5 263.2 %copy-start.6 = (f32[256,2048]{1,0:T(8,128)S(1)}, f32[256,2048]{1,0:T(8,128)}, u32[]{:S(2)}) copy-start(f32[256,2048]{1,0:T(8,128)} %copy-done.4) | copy-start | bytes 6291460
  2793.5 263.2 %copy-start.34 = (f32[256]{0:T(256)S(1)}, f32[256]{0:T(256)}, u32[]{:S(2)}) copy-start(f32[256]{0:T(256)} %get-tuple-element.698) | copy-start | bytes 3076
  3054.6 19.7 copy-start.23
  3122.4 27.0 copy-start.2
  3122.4 27.0 copy-start.3
Sparse Core Ops, SparseCore 0:
  10.8 459.4 all-gather.4
  1006.8 19.7 reduce-scatter.5
  1060.7 22.0 reduce-scatter.7
  1150.0 1413.3 reduce-scatter.9
where the time goes:
time: 3180 us; the launch traced here: 3170 us
  waiting for transfers between devices  1900 us (60%)
  local copies, waits for them, and re-layouts  409 us (13%)
  matrix products  340 us (11%)
  blocking collectives  332 us (10%)
  other arithmetic  152 us (5%)
    unnamed x5, waiting for transfers between devices  1410 us
    all_gather x1, waiting for transfers between devices, local(): lax.all_gather(weights_low[None], ('grp', 'seq'), axis=0, tiled=True)  457 us
    psum x1, blocking collectives, local(): lax.psum(jnp.stack([gain_one_term, gain_two_term]), ('grp', 'seq'))  252 us
    transpose x1, local copies, waits for them, and re-layouts, local(): jnp.transpose(picked, (1, 2, 0, 3))  78.5 us
    scatter x1, local copies, waits for them, and re-layouts, local(): placed = jnp.zeros((grp_count * slots_here, rows_block, tile_width), jnp....  78 us
  transfers between devices with their start and end apart: 8, of which 4 were waited for; matrix products, arithmetic and copies ran while one was open for 3% of the time, Pallas kernels for 0%

commit v1 on v0

--- a/solution.py
+++ b/solution.py
@@ -158,26 +158,48 @@
 ):
     grp_count = lax.axis_size("grp")
     seq_count = lax.axis_size("seq")
+    grp_here = lax.axis_index("grp")
     rows_here = tokens.shape[0]
     slots_here, rows_block, tile_width = weights_low.shape
-    tile_count = tile_owner_slots.shape[0]
     query_cols = NH * HD
     value_end = query_cols + 2 * HD
     output_end = value_end + MODEL_WIDTH
-    gating_end = output_end + 2 * FF
+    attn_tiles = output_end // tile_width
+    hidden_tiles = FF // tile_width
+    share = -(-hidden_tiles // grp_count)
+    share_cols = share * tile_width
+    sub_rows = rows_block // grp_count
     local_index = lax.axis_index("seq") * rows_here + jnp.arange(rows_here, dtype=jnp.int32)
     local_place = local_index % SEQLEN
-    grid = lax.all_gather(weights_low[None], ("grp", "seq"), axis=0, tiled=True).reshape(
-        grp_count, seq_count, slots_here, rows_block, tile_width
-    )
-    picked = grid[tile_owner_slots // slots_here, :, tile_owner_slots % slots_here]
-    weight_cols = jnp.transpose(picked, (1, 2, 0, 3)).reshape(
-        seq_count * rows_block, tile_count * tile_width
-    )
+
+    plane_tiles = lax.all_gather(weights_low, "grp", axis=0, tiled=True)
+    hidden_ids = grp_here * share + jnp.arange(share, dtype=jnp.int32)
+    real = hidden_ids < hidden_tiles
+    hidden_ids = jnp.minimum(hidden_ids, hidden_tiles - 1)
+    feed_ids = (
+        attn_tiles
+        + jnp.arange(3, dtype=jnp.int32)[:, None] * hidden_tiles
+        + hidden_ids[None, :]
+    ).reshape(-1)
+    attn_rows = lax.dynamic_slice_in_dim(plane_tiles, grp_here * sub_rows, sub_rows, axis=1)
+    attn_rows = jnp.transpose(attn_rows[tile_owner_slots[:attn_tiles]], (1, 0, 2)).reshape(
+        sub_rows, output_end
+    )
+    attn_weights = lax.all_gather(attn_rows, "seq", axis=0, tiled=False)
+    attn_weights = lax.all_gather(attn_weights, "grp", axis=1, tiled=True).reshape(
+        MODEL_WIDTH, output_end
+    )
+    feed_tiles = jnp.where(
+        jnp.tile(real, 3)[:, None, None], plane_tiles[tile_owner_slots[feed_ids]], 0
+    )
+    feed_rows = jnp.transpose(feed_tiles, (1, 0, 2)).reshape(rows_block, 3 * share_cols)
+    feed_weights = lax.all_gather(feed_rows, "seq", axis=0, tiled=True)
+    cot_plane = lax.all_gather(cotangent, "grp", axis=0, tiled=True)
+
     tok_float = tokens.astype(jnp.float32)
     inverse_one = lax.rsqrt(jnp.mean(tok_float * tok_float, axis=-1, keepdims=True) + NORM_EPS)
     normed = (tok_float * inverse_one * gains[0]).astype(jnp.bfloat16)
-    projected = jnp.dot(normed, weight_cols[:, :value_end], preferred_element_type=jnp.float32)
+    projected = jnp.dot(normed, attn_weights[:, :value_end], preferred_element_type=jnp.float32)
     queries = rotate(projected[:, :query_cols].reshape(rows_here, NH, HD), local_place, 1.0).astype(
         jnp.bfloat16
     )
@@ -189,11 +211,12 @@
         .astype(jnp.bfloat16)
     )
     value_rows = projected[:, query_cols + HD : value_end].astype(jnp.bfloat16)
-    all_keys, all_values, all_segs = (
-        lax.all_gather(key_rows, "seq", axis=0, tiled=True),
-        lax.all_gather(value_rows, "seq", axis=0, tiled=True),
-        lax.all_gather(segment_ids, "seq", axis=0, tiled=True),
-    )
+    all_pairs = lax.all_gather(
+        jnp.concatenate([key_rows, value_rows], axis=1), "seq", axis=0, tiled=True
+    )
+    all_keys = all_pairs[:, :HD]
+    all_values = all_pairs[:, HD:]
+    all_segs = lax.all_gather(segment_ids, "seq", axis=0, tiled=True)
     group_index = jnp.arange(all_keys.shape[0], dtype=jnp.int32)
     group_place = group_index % SEQLEN
     heads_here = NH // seq_count
@@ -211,29 +234,50 @@
         tiled=True,
     )
     branch = jnp.dot(
-        context, weight_cols[:, value_end:output_end], preferred_element_type=jnp.float32
+        context, attn_weights[:, value_end:], preferred_element_type=jnp.float32
     )
     hidden = tok_float + branch
     inverse_two = lax.rsqrt(jnp.mean(hidden * hidden, axis=-1, keepdims=True) + NORM_EPS)
     normed_two = (hidden * inverse_two * gains[1]).astype(jnp.bfloat16)
-    gate_up = jnp.dot(
-        normed_two, weight_cols[:, output_end:gating_end], preferred_element_type=jnp.float32
-    )
-    gate = gate_up[:, :FF]
-    upper = gate_up[:, FF:]
+
+    normed_plane = lax.all_gather(normed_two, "grp", axis=0, tiled=True)
+    gating_weights = feed_weights[:, : 2 * share_cols]
+    down_weights = feed_weights[:, 2 * share_cols :]
+    gate_up = jnp.dot(normed_plane, gating_weights, preferred_element_type=jnp.float32)
+    gate = gate_up[:, :share_cols]
+    upper = gate_up[:, share_cols:]
     sigmoid_gate = jax.nn.sigmoid(gate)
     silu_gate = jax.nn.silu(gate)
     activated = (silu_gate * upper).astype(jnp.bfloat16)
-    result = hidden + times_transpose(activated, weight_cols[:, gating_end:])
-    block_out = result.astype(jnp.bfloat16)
-    out_grad = cotangent.astype(jnp.float32)
-    act_grad = jnp.dot(cotangent, weight_cols[:, gating_end:], preferred_element_type=jnp.float32)
+    act_grad = jnp.dot(cot_plane, down_weights, preferred_element_type=jnp.float32)
     gate_grad = (act_grad * upper * sigmoid_gate * (1.0 + gate * (1.0 - sigmoid_gate))).astype(
         jnp.bfloat16
     )
     up_grad = (act_grad * silu_gate).astype(jnp.bfloat16)
     gating_grad = jnp.concatenate([gate_grad, up_grad], axis=1)
-    norm_two_grad = times_transpose(gating_grad, weight_cols[:, output_end:gating_end])
+    norm_two_grad = lax.psum_scatter(
+        times_transpose(gating_grad, gating_weights).astype(jnp.bfloat16),
+        "grp",
+        scatter_dimension=0,
+        tiled=True,
+    ).astype(jnp.float32)
+    feed_grads = jnp.concatenate(
+        [contract(normed_plane, gating_grad), contract(cot_plane, activated)], axis=1
+    ).astype(jnp.bfloat16)
+    feed_grads = lax.psum_scatter(feed_grads, "seq", scatter_dimension=0, tiled=True)
+    feed_grads = jnp.transpose(
+        feed_grads.reshape(rows_block, 3 * share, tile_width), (1, 0, 2)
+    )
+    feed_grads = lax.all_gather(feed_grads, "grp", axis=0, tiled=True)
+    feed_out = lax.psum_scatter(
+        times_transpose(activated, down_weights).astype(jnp.bfloat16),
+        "grp",
+        scatter_dimension=0,
+        tiled=True,
+    ).astype(jnp.float32)
+    block_out = (hidden + feed_out).astype(jnp.bfloat16)
+
+    out_grad = cotangent.astype(jnp.float32)
     gain_two_term = jnp.sum(norm_two_grad * hidden * inverse_two, axis=0)
     hidden_grad = (
         out_grad
@@ -243,12 +287,20 @@
         * jnp.mean(hidden * gains[1] * norm_two_grad, axis=-1, keepdims=True)
     )
     branch_grad = hidden_grad.astype(jnp.bfloat16)
-    context_grad = times_transpose(branch_grad, weight_cols[:, value_end:output_end]).astype(
-        jnp.bfloat16
-    )
+    context_grad = times_transpose(branch_grad, attn_weights[:, value_end:]).astype(jnp.bfloat16)
     head_grads = lax.all_to_all(
         context_grad, "seq", split_axis=1, concat_axis=0, tiled=True
     ).reshape(-1, heads_here, HD)
+
+    def reduce_rows(part):
+        cols = part.shape[1]
+        blocks = jnp.transpose(
+            part.astype(jnp.bfloat16).reshape(seq_count, grp_count, sub_rows, cols), (1, 0, 2, 3)
+        ).reshape(grp_count * seq_count * sub_rows, cols)
+        summed = lax.psum_scatter(blocks, ("grp", "seq"), scatter_dimension=0, tiled=True)
+        return lax.all_gather(summed, "grp", axis=0, tiled=True)
+
+    out_grads = reduce_rows(contract(context, branch_grad))
     head_query_grad, key_part, value_part = attend_back(
         head_queries,
         all_keys,
@@ -265,14 +317,12 @@
     )
     query_grad = lax.all_to_all(turned_query, "seq", split_axis=0, concat_axis=1, tiled=True)
     key_part = rotate(key_part[:, None, :], group_place, -1.0)[:, 0, :]
-    key_grad, value_grad = (
-        lax.psum_scatter(key_part, "seq", scatter_dimension=0, tiled=True),
-        lax.psum_scatter(value_part, "seq", scatter_dimension=0, tiled=True),
-    )
-    projected_grad = jnp.concatenate(
-        [query_grad, key_grad.astype(jnp.bfloat16), value_grad.astype(jnp.bfloat16)], axis=1
-    )
-    norm_one_grad = times_transpose(projected_grad, weight_cols[:, :value_end])
+    pair_grad = lax.psum_scatter(
+        jnp.concatenate([key_part, value_part], axis=1), "seq", scatter_dimension=0, tiled=True
+    )
+    projected_grad = jnp.concatenate([query_grad, pair_grad.astype(jnp.bfloat16)], axis=1)
+    in_grads = reduce_rows(contract(normed, projected_grad))
+    norm_one_grad = times_transpose(projected_grad, attn_weights[:, :value_end])
     gain_one_term = jnp.sum(norm_one_grad * tok_float * inverse_one, axis=0)
     input_grad = (
         hidden_grad
@@ -281,42 +331,35 @@
         * inverse_one**3
         * jnp.mean(tok_float * gains[0] * norm_one_grad, axis=-1, keepdims=True)
     )
-    grad_shard = lax.psum_scatter(
-        jnp.concatenate(
-            [
-                contract(normed, projected_grad),
-                contract(context, branch_grad),
-                contract(normed_two, gating_grad),
-                contract(cotangent, activated),
-            ],
-            axis=1,
-        ).astype(jnp.bfloat16),
-        "seq",
-        scatter_dimension=0,
-        tiled=True,
-    ).astype(jnp.float32)
-    grad_tiles = jnp.transpose(grad_shard.reshape(rows_block, tile_count, tile_width), (1, 0, 2))
-    placed = (
-        jnp.zeros((grp_count * slots_here, rows_block, tile_width), jnp.float32)
+    gain_grads = lax.psum(jnp.stack([gain_one_term, gain_two_term]), ("grp", "seq"))
+
+    tile_count = tile_owner_slots.shape[0]
+    tile_of_slot = (
+        jnp.full((grp_count * slots_here,), tile_count, jnp.int32)
         .at[tile_owner_slots]
-        .set(grad_tiles)
-    )
-    received = lax.all_to_all(
-        placed.reshape(grp_count, slots_here, rows_block, tile_width).astype(jnp.bfloat16),
-        "grp",
-        split_axis=0,
-        concat_axis=0,
-        tiled=True,
-    ).astype(jnp.float32)
-    reduced_sum = jnp.sum(received, axis=0)
-    gain_grads = lax.psum(jnp.stack([gain_one_term, gain_two_term]), ("grp", "seq"))
-    turned = jnp.einsum("zji,zjc->zic", left_basis_set, reduced_sum, precision=PRECISE)
-    turned = jnp.einsum("zic,zcd->zid", turned, right_basis_set, precision=PRECISE)
+        .set(jnp.arange(tile_count, dtype=jnp.int32))
+    )
+    tiles_here = lax.dynamic_slice_in_dim(tile_of_slot, grp_here * slots_here, slots_here)
+    attn_grads = jnp.transpose(
+        jnp.concatenate([in_grads, out_grads], axis=1).reshape(rows_block, attn_tiles, tile_width),
+        (1, 0, 2),
+    )
+    feed_at = jnp.clip(tiles_here - attn_tiles, 0, 3 * hidden_tiles - 1)
+    which, column = feed_at // hidden_tiles, feed_at % hidden_tiles
+    feed_at = (column // share) * (3 * share) + which * share + column % share
+    picked = jnp.where(
+        (tiles_here < attn_tiles)[:, None, None],
+        attn_grads[jnp.minimum(tiles_here, attn_tiles - 1)],
+        feed_grads[feed_at],
+    )
+    reduced_sum = jnp.where((tiles_here < tile_count)[:, None, None], picked, 0).astype(jnp.float32)
+    turned = jnp.einsum("zji,zjc->zic", left_basis_set, reduced_sum)
+    turned = jnp.einsum("zic,zcd->zid", turned, right_basis_set)
     new_one = BETA_ONE * moment_one + (1.0 - BETA_ONE) * turned
     new_two = BETA_TWO * moment_two + (1.0 - BETA_TWO) * turned * turned
     scaled = new_one / (jnp.sqrt(new_two) + ADAM_EPS)
-    restored = jnp.einsum("zij,zjd->zid", left_basis_set, scaled, precision=PRECISE)
-    restored = jnp.einsum("zid,zed->zie", restored, right_basis_set, precision=PRECISE)
+    restored = jnp.einsum("zij,zjd->zid", left_basis_set, scaled)
+    restored = jnp.einsum("zid,zed->zie", restored, right_basis_set)
     new_master = master * (1.0 - LEARN_RATE * WEIGHT_DECAY) - LEARN_RATE * restored
     gain_one = BETA_ONE * gain_moment_one + (1.0 - BETA_ONE) * gain_grads
     gain_two = BETA_TWO * gain_moment_two + (1.0 - BETA_TWO) * gain_grads * gain_grads

time: 3180 us -> 1740 us (0.55)
  waiting for transfers between devices: 1900 us -> 1020 us
  local copies, waits for them, and re-layouts: 409 us -> 111 us
  blocking collectives: 332 us -> 219 us
  other arithmetic: 152 us -> 59.8 us
  matrix products: 340 us -> 299 us
    unnamed x5 -> x15, waiting for transfers between devices: 1410 us -> 1.42 us
    reduce_scatter x2 -> x6, waiting for transfers between devices: 7.99 us -> 559 us  [the longest x2 266 us: reduce_rows(): lax.psum_scatter(blocks, ('grp', 'seq'), scatter_dimension=0, tiled=True)]
    psum x1, blocking collectives: 252 us -> 41.5 us  [local(): lax.psum(jnp.stack([gain_one_term, gain_two_term]), ('grp', 'seq'))]
    transpose x2 -> x1, local copies, waits for them, and re-layouts: 121 us -> 1.42 us  [local(): jnp.transpose(attn_rows[tile_owner_slots[:attn_tiles]], (1, 0, 2))]
    scatter x1, local copies, waits for them, and re-layouts: 78 us -> 1.11 us  [local(): tile_of_slot = jnp.full((grp_count * slots_here,), tile_count, jnp.int32)...]
    dot_general x8 -> x6, matrix products: 140 us -> 83 us  [the longest x1 19 us: local(): jnp.dot(normed_plane, gating_weights, preferred_element_type=jnp.float32)]
    unnamed x70 -> x61, local copies, waits for them, and re-layouts: 61.2 us -> 7.9 us
    all_to_all x0 -> x1, blocking collectives: none -> 41.2 us  [local(): lax.all_to_all(turned_query, 'seq', split_axis=0, concat_axis=1, tiled=True)]
  transfers between devices with their start and end apart: 8 -> 17, of which waited for: 4 -> 13; matrix products, arithmetic and copies ran while one was open for 3% -> 12% of each run, Pallas kernels for 0% -> 0%
where the time goes in v1:
time: 1740 us; the launch traced here: 1730 us
  waiting for transfers between devices  1020 us (59%)
  matrix products  299 us (17%)
  blocking collectives  219 us (13%)
  local copies, waits for them, and re-layouts  111 us (6%)
  other arithmetic  59.8 us (3%)
    reduce_scatter x2, waiting for transfers between devices, reduce_rows(): lax.psum_scatter(blocks, ('grp', 'seq'), scatter_dimension=0, tiled=True)  266 us
    reduce_scatter x1, waiting for transfers between devices, local(): lax.psum_scatter(feed_grads, 'seq', scatter_dimension=0, tiled=True)  161 us
    all_gather x1, waiting for transfers between devices, local(): plane_tiles = lax.all_gather(weights_low, 'grp', axis=0, tiled=True)  116 us
    all_gather x1, waiting for transfers between devices, local(): feed_grads = lax.all_gather(feed_grads, 'grp', axis=0, tiled=True)  76.1 us
    all_gather x1, waiting for transfers between devices, local(): lax.all_gather(attn_weights, 'grp', axis=1, tiled=True)  73.6 us
    reduce_scatter x1, waiting for transfers between devices, local(): lax.psum_scatter(times_transpose(activated, down_weights).astype(jnp.bflo...  72.2 us
    reduce_scatter x1, waiting for transfers between devices, local(): lax.psum_scatter(times_transpose(gating_grad, gating_weights).astype(jnp....  59.6 us
    all_to_all x1, blocking collectives, local(): lax.all_to_all(head_context.reshape(-1, heads_here * HD).astype(jnp.bfloa...  56.1 us
  transfers between devices with their start and end apart: 17, of which 13 were waited for; matrix products, arithmetic and copies ran while one was open for 12% of the time, Pallas kernels for 0%

profile of v1, /device:TPU:0, one launch (start us, length us, event | category | flops | bytes accessed | tf_op | source)
XLA Modules:
  0.0 1731.6 jit_solution(6610942294189539147)
XLA Ops:
  8.7 116.0 %all-gather.11.cloned.1.call-done = bf16[168,512,128]{2,1,0:T(8,128)(2,1)} async-done(((bf16[21,512,128]{2,1,0:T(8,128)(2,1)}), bf16[168,512,128]{2,1,0:T(8,128)(2,1)}) %all-gather.11.cloned.1.call-update) | async-done | bytes 22020112 | tf_op jit(solution)/shard_map/all_gather | solution.py:175
  134.4 48.4 %all-gather.13.cloned.1.call-done = bf16[4,64,4352]{2,1,0:T(8,128)(2,1)} async-done(((bf16[1,64,4352]{2,1,0:T(8,128)(2,1)}), bf16[4,64,4352]{2,1,0:T(8,128)(2,1)}) %all-gather.13.cloned.1.call-update) | async-done | bytes 2228240 | tf_op jit(solution)/shard_map/all_gather | solution.py:188
  184.3 10.7 gather_fusion.2
  204.3 73.6 %all-gather.15.cloned.1.call-done = bf16[4,512,4352]{2,1,0:T(8,128)(2,1)} async-done(((bf16[4,64,4352]{2,1,0:T(8,128)(2,1)}), bf16[4,512,4352]{2,1,0:T(8,128)(2,1)}) %all-gather.15.cloned.1.call-update) | async-done | bytes 17825808 | tf_op jit(solution)/shard_map/all_gather | solution.py:189
  277.9 6.3 fusion.83
  296.3 40.8 %all-gather = s32[4,1,256]{2,1,0:T(1,128)S(1)} all-gather(s32[1,1,256]{2,1,0:T(1,128)} %bitcast.336), channel_id=1, replica_groups=mesh['grp'=8,'seq'=4] {'seq'}, dimensions={0}, use_global_device_ids=true | all-gather | bytes 5120 | tf_op jit(solution)/shard_map/all_gather | solution.py:219
  339.6 38.9 %all_gather.37 = bf16[1024,256]{0,1:T(8,128)(2,1)S(1)} all-gather(bf16[256,256]{0,1:T(8,128)(2,1)S(1)} %pad_maximum_fusion.11), channel_id=1, replica_groups=mesh['grp'=8,'seq'=4] {'seq'}, dimensions={0}, use_global_device_ids=true | all-gather | bytes 655360 | tf_op jit(solution)/shard_map/all_gather | solution.py:214
  383.7 17.3 while.36
  406.2 56.1 %all_to_all.61 = bf16[4,256,512]{2,1,0:T(8,128)(2,1)} all-to-all(bf16[4,256,512]{2,1,0:T(8,128)(2,1)} %convert_element_type.137), channel_id=1, replica_groups=mesh['grp'=8,'seq'=4] {'seq'}, dimensions={0} | all-to-all | bytes 2097152 | tf_op jit(solution)/shard_map/all_to_all | solution.py:229
  464.6 6.4 multiply_reduce_fusion
  474.5 25.4 %all-gather.19.cloned.1.call-done = bf16[2048,2304]{0,1:T(8,128)(2,1)} async-done(((bf16[512,2304]{0,1:T(8,128)(2,1)}), bf16[2048,2304]{0,1:T(8,128)(2,1)}) %all-gather.19.cloned.1.call-update) | async-done | bytes 9437200 | tf_op jit(solution)/shard_map/all_gather | solution.py:196
  499.8 54.9 %all-gather.17.cloned.1.call-done = bf16[2048,2048]{1,0:T(8,128)(2,1)} async-done(((bf16[256,2048]{1,0:T(8,128)(2,1)}), bf16[2048,2048]{1,0:T(8,128)(2,1)}) %all-gather.17.cloned.1.call-update) | async-done | bytes 8388624 | tf_op jit(solution)/shard_map/all_gather | solution.py:243
  554.7 19.0 %fusion.95 = f32[2048,1536]{0,1:T(8,128)} fusion(bf16[2048,2048]{1,0:T(8,128)(2,1)} %all-gather.17.cloned.1.call-done, bf16[2048,2304]{0,1:T(8,128)(2,1)} %all-gather.19.cloned.1.call-done), kind=kOutput, calls=%fused_computation.134 | convolution fusion | flops 12884901888 | bytes 27262976 | tf_op jit(solution)/shard_map/dot_general | solution.py:246
  573.7 37.2 %all-gather.21.cloned.1.call-done = bf16[2048,2048]{1,0:T(8,128)(2,1)} async-done(((bf16[256,2048]{1,0:T(8,128)(2,1)}), bf16[2048,2048]{1,0:T(8,128)(2,1)}) %all-gather.21.cloned.1.call-update) | async-done | bytes 8388624 | tf_op jit(solution)/shard_map/all_gather | solution.py:197
  610.9 16.7 fusion.91
  629.2 19.0 %convolution_convert_fusion.3 = bf16[2048,2048]{1,0:T(8,128)(2,1)} fusion(bf16[2048,2304]{0,1:T(8,128)(2,1)} %all-gather.19.cloned.1.call-done, bf16[2048,768]{0,1:T(8,128)(2,1)} %get-tuple-element.680, bf16[2048,768]{0,1:T(8,128)(2,1)S(1)} %get-tuple-element.679), kind=kOutput, calls=%fused_computation.117 | convolution fusion | flops 12901679104 | bytes 20971520 | tf_op jit(solution)/shard_map/dot_general | solution.py:53
  648.3 11.8 convolution_convert_fusion.4
  660.1 59.6 %reduce-scatter.9.cloned.1.call-done = bf16[256,2048]{1,0:T(8,128)(2,1)} async-done(((bf16[2048,2048]{1,0:T(8,128)(2,1)}), bf16[256,2048]{1,0:T(8,128)(2,1)}) %reduce-scatter.9.cloned.1.call-update) | async-done | bytes 1048592 | tf_op jit(solution)/shard_map/reduce_scatter | solution.py:258
  722.7 72.2 %reduce-scatter.7.cloned.1.call-done = bf16[256,2048]{1,0:T(8,128)(2,1)} async-done(((bf16[2048,2048]{1,0:T(8,128)(2,1)}), bf16[256,2048]{1,0:T(8,128)(2,1)}) %reduce-scatter.7.cloned.1.call-update) | async-done | bytes 1048592 | tf_op jit(solution)/shard_map/reduce_scatter | solution.py:272
  799.1 6.5 fusion.114
  811.3 25.8 %all-to-all-done.2 = bf16[256,4,512]{2,0,1:T(8,128)(2,1)} async-done(((bf16[256,4,512]{2,0,1:T(8,128)(2,1)}), bf16[256,4,512]{2,0,1:T(8,128)(2,1)}, u32[]{:S(2)}, u32[]{:S(2)}) %all-to-all-start.2) | async-done | bytes 1048608 | tf_op jit(solution)/shard_map/all_to_all | solution.py:291
  839.5 123.5 %while.37 = (s32[]{:T(128)}, f32[1024,128]{1,0:T(8,128)}, f32[1024,128]{1,0:T(8,128)}, f32[2,512,4,128]{3,1,0,2:T(8,128)}, s32[2,512]{1,0:T(2,128)S(1)}, /*index...) while((s32[]{:T(128)}, f32[1024,128]{1,0:T(8,128)}, ...), condition=%wide.region_11.12_spmd.clone.clone, body=%wide.region_9.11_spmd.clone.clone.sunk | while | flops 2742048256 | bytes 106783928 | solution.py:130
  850.3 22.8 %fusion.228 = f32[2,512,4,128]{3,1,0,2:T(8,128)} fusion(f32[2,512,4,128]{3,1,0,2:T(8,128)} %get-tuple-element.900, s32[]{:T(128)} %get-tuple-element.897, f32[512,4,1024]{2,0,1:T(8,128)} %fusion.223, f32[512,4,1024]{2,0,1:T(8,128)} %fusion.224, f32[4,512]{1,0:T(4,128)S(1)} %dynamic-slice_bitcast_fusion.2, pred[512,1024]{1,0:T(8,128)(4,1)} %fusion.225, ...), kind=kOutput, calls=%fused_computation.67.clone.1 | convolution fusion | flops 559942656 | bytes 35930624 | tf_op jit(solution)/shard_map/while/body/eval_jaxpr/hqk,kd->qhd/dot_general | solution.py:115
  873.1 21.3 %fusion.226 = f32[1024,128]{1,0:T(8,128)} fusion(f32[512,4,1024]{2,0,1:T(8,128)} %fusion.223, f32[512,4,1024]{2,0,1:T(8,128)} %fusion.224, f32[4,512]{1,0:T(4,128)S(1)} %dynamic-slice_bitcast_fusion.2, pred[512,1024]{1,0:T(8,128)(4,1)} %fusion.225, f32[1024,128]{1,0:T(8,128)} %get-tuple-element.898, ...), kind=kOutput, calls=%fused_computation.70.clone.1 | convolution fusion | flops 560204800 | bytes 36192768 | tf_op jit(solution)/shard_map/while/body/eval_jaxpr/hqk,qhd->kd/dot_general | solution.py:118
  894.4 6.7 fusion.227
  911.9 22.8 %fusion.228 = f32[2,512,4,128]{3,1,0,2:T(8,128)} fusion(f32[2,512,4,128]{3,1,0,2:T(8,128)} %get-tuple-element.900, s32[]{:T(128)} %get-tuple-element.897, f32[512,4,1024]{2,0,1:T(8,128)} %fusion.223, f32[512,4,1024]{2,0,1:T(8,128)} %fusion.224, f32[4,512]{1,0:T(4,128)S(1)} %dynamic-slice_bitcast_fusion.2, pred[512,1024]{1,0:T(8,128)(4,1)} %fusion.225, ...), kind=kOutput, calls=%fused_computation.67.clone.1 | convolution fusion | flops 559942656 | bytes 35930624 | tf_op jit(solution)/shard_map/while/body/eval_jaxpr/hqk,kd->qhd/dot_general | solution.py:115
  934.7 21.3 %fusion.226 = f32[1024,128]{1,0:T(8,128)} fusion(f32[512,4,1024]{2,0,1:T(8,128)} %fusion.223, f32[512,4,1024]{2,0,1:T(8,128)} %fusion.224, f32[4,512]{1,0:T(4,128)S(1)} %dynamic-slice_bitcast_fusion.2, pred[512,1024]{1,0:T(8,128)(4,1)} %fusion.225, f32[1024,128]{1,0:T(8,128)} %get-tuple-element.898, ...), kind=kOutput, calls=%fused_computation.70.clone.1 | convolution fusion | flops 560204800 | bytes 36192768 | tf_op jit(solution)/shard_map/while/body/eval_jaxpr/hqk,qhd->kd/dot_general | solution.py:118
  956.1 6.9 fusion.227
  977.4 41.2 %all_to_all.62 = bf16[4,256,512]{2,1,0:T(8,128)(2,1)} all-to-all(bf16[4,256,512]{2,1,0:T(8,128)(2,1)} %convert_element_type.151), channel_id=1, replica_groups=mesh['grp'=8,'seq'=4] {'seq'}, dimensions={0} | all-to-all | bytes 2097152 | tf_op jit(solution)/shard_map/all_to_all | solution.py:318
  1021.3 5.3 convolution_convert_fusion
  1026.6 8.3 copy.118
  1036.4 6.9 convolution_convert_fusion.2
  1043.3 8.7 copy.119
  1052.2 10.7 fusion.102
  1062.9 15.8 convolution_convert_fusion.1
  1078.7 11.5 pad_maximum_fusion
  1090.3 79.4 %reduce-scatter.13.cloned.1.call-done = bf16[64,2304]{1,0:T(8,128)(2,1)} async-done(((bf16[2048,2304]{1,0:T(8,128)(2,1)}), bf16[64,2304]{1,0:T(8,128)(2,1)}) %reduce-scatter.13.cloned.1.call-update) | async-done | bytes 294928 | tf_op jit(solution)/shard_map/reduce_scatter | solution.py:300
  1169.8 187.0 %reduce-scatter.15.cloned.1.call-done = bf16[64,2048]{1,0:T(8,128)(2,1)} async-done(((bf16[2048,2048]{1,0:T(8,128)(2,1)}), bf16[64,2048]{1,0:T(8,128)(2,1)}) %reduce-scatter.15.cloned.1.call-update) | async-done | bytes 262160 | tf_op jit(solution)/shard_map/reduce_scatter | solution.py:300
  1356.9 161.1 %reduce-scatter.17.cloned.1.call-done = bf16[512,2304]{0,1:T(8,128)(2,1)} async-done(((bf16[2048,2304]{0,1:T(8,128)(2,1)}), bf16[512,2304]{0,1:T(8,128)(2,1)}) %reduce-scatter.17.cloned.1.call-update) | async-done | bytes 2359312 | tf_op jit(solution)/shard_map/reduce_scatter | solution.py:267
  1525.3 9.3 fusion.133
  1534.7 41.5 %psum.7 = f32[2,2048]{1,0:T(2,128)S(1)} all-reduce(f32[2,2048]{1,0:T(2,128)S(1)} %pad_maximum_fusion.12), channel_id=1, replica_groups=mesh['grp'=8,'seq'=4] {'grp','seq'}, use_global_device_ids=true, to_apply=%region_20.21 | all-reduce | flops 4096 | bytes 32768 | tf_op jit(solution)/shard_map/psum | solution.py:334
  1586.9 6.7 copy.120
  1593.5 6.7 copy.121
  1600.2 5.0 gather_fusion.3
  1605.2 76.1 %all-gather.27.cloned.1.call-done = bf16[144,512,128]{2,1,0:T(8,128)(2,1)} async-done(((bf16[18,512,128]{2,1,0:T(8,128)(2,1)}), bf16[144,512,128]{2,1,0:T(8,128)(2,1)}) %all-gather.27.cloned.1.call-update) | async-done | bytes 18874384 | tf_op jit(solution)/shard_map/all_gather | solution.py:271
  1681.3 8.9 gather_fusion.4
  1690.2 18.5 %fusion.97 = (f32[21,512,128]{2,1,0:T(8,128)}, f32[21,512,128]{2,1,0:T(8,128)}) fusion(f32[21,512,128]{2,1,0:T(8,128)} %param.24, f32[21,512,128]{2,1,0:T(8,128)} %param.23, f32[21,128,128]{2,1,0:T(8,128)S(1)} %copy-done, f32[21,512,512]{2,1,0:T(8,128)} %param.25, bf16[21,512,128]{2,1,0:T(8,128)(2,1)} %gather_fusion.3, ...), kind=kOutput, calls=%fused_computation.136 | convolution fusion | flops 1772617728 | bytes 50921512 | tf_op jit(solution)/shard_map/zic,zcd->zid/dot_general | solution.py:357
  1708.7 16.1 multiply_subtract_fusion
  (219 shorter events, 145.0 us)
Async XLA Ops:
  7.2 1683.1 %copy-start = (f32[21,128,128]{2,1,0:T(8,128)S(1)}, f32[21,128,128]{2,1,0:T(8,128)}, u32[]{:S(2)}) copy-start(f32[21,128,128]{2,1,0:T(8,128)} %param.26) | copy-start | bytes 4128772
  7.2 117.5 %all-gather.11.cloned.1.call-start = ((), (), s32[]{:S(2)}) async-start(), calls=%async_computation.10 | async-start | bytes 24772608 | tf_op jit(solution)/shard_map/all_gather | solution.py:175
  7.9 174.9 %all-gather.13.cloned.1.call-start = ((), (), s32[]{:S(2)}) async-start(), calls=%async_computation.11 | async-start | bytes 2785280 | tf_op jit(solution)/shard_map/all_gather | solution.py:188
  8.7 174.4 %copy-start.1 = (s32[166]{0:T(256)S(1)}, s32[166]{0:T(256)}, u32[]{:S(2)}) copy-start(s32[166]{0:T(256)} %param.20) | copy-start | bytes 1996
  8.7 175.3 %copy-start.7 = (bf16[256,2048]{1,0:T(8,128)(2,1)S(1)}, bf16[256,2048]{1,0:T(8,128)(2,1)}, u32[]{:S(2)}) copy-start(bf16[256,2048]{1,0:T(8,128)(2,1)} %param.17) | copy-start | bytes 3145732
  134.4 143.5 %all-gather.15.cloned.1.call-start = ((), (), s32[]{:S(2)}) async-start(), calls=%async_computation.12 | async-start | bytes 20054016 | tf_op jit(solution)/shard_map/all_gather | solution.py:189
  182.9 317.0 %all-gather.19.cloned.1.call-start = ((), (), s32[]{:S(2)}) async-start(), calls=%async_computation.14 | async-start | bytes 11796480 | tf_op jit(solution)/shard_map/all_gather | solution.py:196
  194.9 9.3 copy-start.15
  202.7 136.5 %copy-start.22 = (f32[64]{0:T(128)}, f32[64]{0:T(128)S(1)}, u32[]{:S(2)}) copy-start(f32[64]{0:T(128)S(1)} %multiply_power_fusion) | copy-start | bytes 772
  203.3 80.9 %copy-start.19 = (f32[256]{0:T(256)}, f32[256]{0:T(256)S(1)}, u32[]{:S(2)}) copy-start(f32[256]{0:T(256)S(1)} %get-tuple-element.703) | copy-start | bytes 3076
  204.3 80.0 %copy-start.13 = (f32[1,2048]{1,0:T(1,128)}, f32[1,2048]{1,0:T(1,128)S(1)}, u32[]{:S(2)}) copy-start(f32[1,2048]{1,0:T(1,128)S(1)} %get-tuple-element.697) | copy-start | bytes 24580
  284.3 1.4 copy-start.11
  291.7 87.1 %all-to-all-start = ((bf16[256,4,512]{0,2,1:T(8,128)(2,1)}), bf16[256,4,512]{0,2,1:T(8,128)(2,1)S(1)}, u32[]{:S(2)}, u32[]{:S(2)}) async-start(bf16[256,4,512]{0,2,1:T(8,128)(2,1)} %bitcast.5), calls=%async_computation | async-start | bytes 2097152 | tf_op jit(solution)/shard_map/all_to_all | solution.py:223
  296.3 258.4 %all-gather.17.cloned.1.call-start = ((), (), s32[]{:S(2)}) async-start(), calls=%async_computation.13 | async-start | bytes 9437184 | tf_op jit(solution)/shard_map/all_gather | solution.py:243
  471.0 1.3 copy-start.5
  473.6 137.3 %all-gather.21.cloned.1.call-start = ((), (), s32[]{:S(2)}) async-start(), calls=%async_computation.16 | async-start | bytes 9437184 | tf_op jit(solution)/shard_map/all_gather | solution.py:197
  474.2 245.5 %reduce-scatter.9.cloned.1.call-start = ((), (), s32[]{:S(2)}) async-start(), calls=%async_computation.17 | async-start | bytes 9437184 | tf_op jit(solution)/shard_map/reduce_scatter | solution.py:258
  627.6 1.7 copy-start.26
  648.3 146.6 %reduce-scatter.7.cloned.1.call-start = ((), (), s32[]{:S(2)}) async-start(), calls=%async_computation.15 | async-start | bytes 9437184 | tf_op jit(solution)/shard_map/reduce_scatter | solution.py:272
  799.1 6.5 copy-start.3
  806.7 30.4 %all-to-all-start.2 = ((bf16[256,4,512]{2,0,1:T(8,128)(2,1)}), bf16[256,4,512]{2,0,1:T(8,128)(2,1)}, u32[]{:S(2)}, u32[]{:S(2)}) async-start(bf16[256,4,512]{2,0,1:T(8,128)(2,1)} %bitcast.312), calls=%async_computation.4 | async-start | bytes 2097152 | tf_op jit(solution)/shard_map/all_to_all | solution.py:291
  811.3 208.7 %reduce-scatter.11.cloned.1.call-start = ((), (), s32[]{:S(2)}) async-start(), calls=%async_computation.18 | async-start | bytes 1310720 | tf_op jit(solution)/shard_map/reduce_scatter | solution.py:320
  839.5 127.7 %copy-start.23 = (f32[64]{0:T(128)S(1)}, f32[64]{0:T(128)}, u32[]{:S(2)}) copy-start(f32[64]{0:T(128)} %copy-done.22) | copy-start | bytes 772
  839.5 6.1 copy-start.6
  901.1 6.1 copy-start.6
  963.0 10.9 copy-start.9
  971.9 197.8 %reduce-scatter.13.cloned.1.call-start = ((), (), s32[]{:S(2)}) async-start(), calls=%async_computation.19 | async-start | bytes 9732096 | tf_op jit(solution)/shard_map/reduce_scatter | solution.py:300
  974.7 46.6 %copy-start.8 = (bf16[256,2048]{1,0:T(8,128)(2,1)S(1)}, bf16[256,2048]{1,0:T(8,128)(2,1)}, u32[]{:S(2)}) copy-start(bf16[256,2048]{1,0:T(8,128)(2,1)} %param.17) | copy-start | bytes 3145732
  974.7 46.6 %copy-start.14 = (f32[1,2048]{1,0:T(1,128)S(1)}, f32[1,2048]{1,0:T(1,128)}, u32[]{:S(2)}) copy-start(f32[1,2048]{1,0:T(1,128)} %copy-done.13) | copy-start | bytes 24580
  974.7 46.6 %copy-start.20 = (f32[256]{0:T(256)S(1)}, f32[256]{0:T(256)}, u32[]{:S(2)}) copy-start(f32[256]{0:T(256)} %copy-done.19) | copy-start | bytes 3076
  1020.0 6.6 copy-start.10
  1021.2 5.4 copy-start.12
  1034.9 1.6 copy-start.4
  1034.9 321.9 %reduce-scatter.15.cloned.1.call-start = ((), (), s32[]{:S(2)}) async-start(), calls=%async_computation.21 | async-start | bytes 8650752 | tf_op jit(solution)/shard_map/reduce_scatter | solution.py:300
  1052.1 465.9 %reduce-scatter.17.cloned.1.call-start = ((), (), s32[]{:S(2)}) async-start(), calls=%async_computation.23 | async-start | bytes 11796480 | tf_op jit(solution)/shard_map/reduce_scatter | solution.py:267
  1052.1 10.7 copy-start.27
  1052.1 10.7 copy-start.28
  1090.2 432.1 %copy-start.2 = (s32[166]{0:T(256)S(1)}, s32[166]{0:T(256)}, u32[]{:S(2)}) copy-start(s32[166]{0:T(256)} %param.20) | copy-start | bytes 1996
  1090.2 491.9 %all-gather.23.cloned.1.call-start = ((), (), s32[]{:S(2)}) async-start(), calls=%async_computation.20 | async-start | bytes 2654208 | tf_op jit(solution)/shard_map/all_gather | solution.py:301
  1169.7 412.4 %all-gather.25.cloned.1.call-start = ((), (), s32[]{:S(2)}) async-start(), calls=%async_computation.22 | async-start | bytes 2359296 | tf_op jit(solution)/shard_map/all_gather | solution.py:301
  1356.8 324.5 %all-gather.27.cloned.1.call-start = ((), (), s32[]{:S(2)}) async-start(), calls=%async_computation.24 | async-start | bytes 21233664 | tf_op jit(solution)/shard_map/all_gather | solution.py:271
  1525.3 9.3 copy-start.18
  1525.3 51.6 %copy-start.16 = (f32[2,2048]{1,0:T(2,128)S(1)}, f32[2,2048]{1,0:T(2,128)}, u32[]{:S(2)}) copy-start(f32[2,2048]{1,0:T(2,128)} %param.27) | copy-start | bytes 49156
  1525.3 51.6 %copy-start.21 = (f32[2,2048]{1,0:T(2,128)S(1)}, f32[2,2048]{1,0:T(2,128)}, u32[]{:S(2)}) copy-start(f32[2,2048]{1,0:T(2,128)} %param.28) | copy-start | bytes 49156
  1576.2 10.6 copy-start.17
  1600.2 90.0 %copy-start.24 = (pred[21]{0:T(512)(128)(4,1)S(1)}, pred[21]{0:T(512)(128)(4,1)}, u32[]{:S(2)}) copy-start(pred[21]{0:T(512)(128)(4,1)} %get-tuple-element.671) | copy-start | bytes 67
  1600.2 90.0 %copy-start.25 = (pred[21]{0:T(512)(128)(4,1)S(1)}, pred[21]{0:T(512)(128)(4,1)}, u32[]{:S(2)}) copy-start(pred[21]{0:T(512)(128)(4,1)} %broadcast_compare_fusion) | copy-start | bytes 67
Sparse Core Ops, SparseCore 0:
  9.9 114.7 all-gather.10
  134.5 48.3 all-gather.12
  184.8 93.1 all-gather.14
  279.9 219.8 all-gather.18
  502.1 52.5 all-gather.16
  556.5 54.3 all-gather.20
  648.4 71.2 reduce-scatter.8
  723.6 71.2 reduce-scatter.6
  972.1 35.7 reduce-scatter.10
  1035.0 134.6 reduce-scatter.12
  1172.0 184.7 reduce-scatter.14
  1359.0 158.9 reduce-scatter.16
  1519.9 30.3 all-gather.22
  1552.0 28.3 all-gather.24
  1582.7 98.5 all-gather.26

commit v2 on v1

v2 whole, which is shorter than its diff:
```python
import functools

import jax
import jax.numpy as jnp
from jax import lax
from jax.experimental import pallas as pl
from jax.experimental.pallas import tpu as pltpu
from jax.sharding import PartitionSpec as P

MODEL_WIDTH = 2048
NH = 16
HD = 128
FF = 5632
SEQLEN = 1024


NORM_EPS = 1e-05
BETA_ONE = 0.95
BETA_TWO = 0.95
ADAM_EPS = 1e-08
WEIGHT_DECAY = 0.01
LEARN_RATE = 0.03
GAIN_RATE = 1.5
ROPE_BASE = 10000.0
MASKED = -1e30
PRECISE = lax.Precision.HIGHEST


def rotate(values, positions, direction):
    head_width = values.shape[-1]
    half_width = head_width // 2
    frequency = ROPE_BASE ** (-(jnp.arange(half_width, dtype=jnp.float32) * 2.0) / head_width)
    angles = positions.astype(jnp.float32)[:, None] * frequency[None, :]
    cosine = jnp.cos(angles)[:, None, :]
    sine_part = (jnp.sin(angles) * direction)[:, None, :]
    leading = values[..., :half_width]
    trailing = values[..., half_width:]
    return jnp.concatenate(
        [leading * cosine - trailing * sine_part, trailing * cosine + leading * sine_part], axis=-1
    )


def contract(left_side, right_side):
    return lax.dot_general(
        left_side, right_side, (((0,), (0,)), ((), ())), preferred_element_type=jnp.float32
    )


def times_transpose(left_side, right_side):
    return lax.dot_general(
        left_side, right_side, (((1,), (1,)), ((), ())), preferred_element_type=jnp.float32
    )


def turn_tables(places):
    half_width = HD // 2
    frequency = ROPE_BASE ** (-(jnp.arange(half_width, dtype=jnp.float32) * 2.0) / HD)
    angles = places.astype(jnp.float32)[:, None] * frequency[None, :]
    cosine, sine = jnp.cos(angles), jnp.sin(angles)
    return (
        jnp.concatenate([cosine, cosine], axis=1),
        jnp.concatenate([-sine, sine], axis=1),
    )


ROWS = 256


def score_mask(key_seg_ref, query_seg_ref, block, rows):
    keys = (block + 1) * rows
    same = key_seg_ref[:keys, :] == query_seg_ref[:, block * rows : keys]
    key_at = lax.broadcasted_iota(jnp.int32, (keys, rows), 0)
    query_at = lax.broadcasted_iota(jnp.int32, (keys, rows), 1) + block * rows
    return same & (key_at <= query_at)


def dot_last(left_side, right_side):
    return lax.dot_general(
        left_side, right_side, (((1,), (1,)), ((), ())), preferred_element_type=jnp.float32
    )


def attend_kernel(q_ref, k_ref, v_ref, key_seg_ref, query_seg_ref, context_ref, total_ref):
    scale = HD ** (-0.5)
    values_t = jnp.transpose(v_ref[...].astype(jnp.float32)).astype(jnp.bfloat16)
    for block in range(SEQLEN // ROWS):
        here = slice(block * ROWS, (block + 1) * ROWS)
        keys = (block + 1) * ROWS
        scores = dot_last(k_ref[:keys, :], q_ref[here, :]) * scale
        allowed = score_mask(key_seg_ref, query_seg_ref, block, ROWS)
        scores = jnp.where(allowed, scores, MASKED)
        highest = jnp.max(scores, axis=0, keepdims=True)
        exponent = jnp.exp(scores - highest)
        totals = jnp.sum(exponent, axis=0, keepdims=True)
        probs_low = (exponent * (1.0 / totals)).astype(jnp.bfloat16)
        context_t = jnp.dot(values_t[:, :keys], probs_low, preferred_element_type=jnp.float32)
        context_ref[here, :] = jnp.transpose(context_t).astype(jnp.bfloat16)
        total_ref[0, 0, :, here] = highest + jnp.log(totals)


def attend_back_kernel(
    q_ref,
    k_ref,
    v_ref,
    grad_ref,
    total_ref,
    key_seg_ref,
    query_seg_ref,
    cosine_ref,
    sine_ref,
    query_grad_ref,
    pair_grad_ref,
    key_sum,
    value_sum,
):
    scale = HD ** (-0.5)
    head = pl.program_id(1)

    @pl.when(head == 0)
    def _():
        key_sum[...] = jnp.zeros_like(key_sum)
        value_sum[...] = jnp.zeros_like(value_sum)

    def turn_back(rows, here):
        return rows * cosine_ref[here, :] - pltpu.roll(rows, HD // 2, 1) * sine_ref[here, :]

    keys_t = jnp.transpose(k_ref[...].astype(jnp.float32)).astype(jnp.bfloat16)
    for block in range(SEQLEN // ROWS):
        here = slice(block * ROWS, (block + 1) * ROWS)
        keys = (block + 1) * ROWS
        queries, grads = q_ref[here, :], grad_ref[here, :]
        shifted = dot_last(k_ref[:keys, :], queries) * scale - total_ref[0, 0, :, here]
        allowed = score_mask(key_seg_ref, query_seg_ref, block, ROWS)
        probs = jnp.where(allowed, jnp.exp(shifted), 0.0)
        prob_grad = dot_last(v_ref[:keys, :], grads)
        centre = jnp.sum(probs * prob_grad, axis=0, keepdims=True)
        score_grad = (probs * (prob_grad - centre) * scale).astype(jnp.bfloat16)
        value_sum[:keys, :] += jnp.dot(
            probs.astype(jnp.bfloat16), grads, preferred_element_type=jnp.float32
        )
        key_sum[:keys, :] += jnp.dot(score_grad, queries, preferred_element_type=jnp.float32)
        query_grad = jnp.transpose(
            jnp.dot(keys_t[:, :keys], score_grad, preferred_element_type=jnp.float32)
        )
        query_grad_ref[here, :] = turn_back(query_grad, here).astype(jnp.bfloat16)

    @pl.when(head == pl.num_programs(1) - 1)
    def _():
        for block in range(SEQLEN // ROWS):
            here = slice(block * ROWS, (block + 1) * ROWS)
            pair_grad_ref[here, :HD] = turn_back(key_sum[here, :], here).astype(jnp.bfloat16)
            pair_grad_ref[here, HD:] = value_sum[here, :].astype(jnp.bfloat16)


def attention_specs(kinds):
    specs = {
        "head": pl.BlockSpec((SEQLEN, HD), lambda n, h: (n, h)),
        "keys": pl.BlockSpec((SEQLEN, HD), lambda n, h: (n, 0)),
        "values": pl.BlockSpec((SEQLEN, HD), lambda n, h: (n, 1)),
        "pair": pl.BlockSpec((SEQLEN, 2 * HD), lambda n, h: (n, 0)),
        "total": pl.BlockSpec((1, 1, 1, SEQLEN), lambda n, h: (n, h, 0, 0)),
        "key_seg": pl.BlockSpec((SEQLEN, 1), lambda n, h: (n, 0)),
        "query_seg": pl.BlockSpec((1, SEQLEN), lambda n, h: (0, n)),
        "table": pl.BlockSpec((SEQLEN, HD), lambda n, h: (0, 0)),
    }
    return [specs[kind] for kind in kinds]


def attend(queries, pairs, segments):
    tokens_all, columns = queries.shape
    grid = (tokens_all // SEQLEN, columns // HD)
    return pl.pallas_call(
        attend_kernel,
        grid=grid,
        in_specs=attention_specs(["head", "keys", "values", "key_seg", "query_seg"]),
        out_specs=attention_specs(["head", "total"]),
        out_shape=(
            jax.ShapeDtypeStruct((tokens_all, columns), jnp.bfloat16),
            jax.ShapeDtypeStruct((*grid, 1, SEQLEN), jnp.float32),
        ),
        compiler_params=pltpu.CompilerParams(vmem_limit_bytes=48 * 2**20),
        cost_estimate=pl.CostEstimate(
            flops=4 * tokens_all * SEQLEN * columns,
            bytes_accessed=6 * tokens_all * columns,
            transcendentals=tokens_all * SEQLEN * columns // HD,
        ),
        name="attend",
    )(queries, pairs, pairs, segments[:, None], segments[None, :])


def attend_back(queries, pairs, grads, totals, segments, tables):
    tokens_all, columns = queries.shape
    grid = (tokens_all // SEQLEN, columns // HD)
    return pl.pallas_call(
        attend_back_kernel,
        grid=grid,
        in_specs=attention_specs(
            ["head", "keys", "values", "head", "total", "key_seg", "query_seg", "table", "table"]
        ),
        out_specs=attention_specs(["head", "pair"]),
        out_shape=(
            jax.ShapeDtypeStruct((tokens_all, columns), jnp.bfloat16),
            jax.ShapeDtypeStruct((tokens_all, 2 * HD), jnp.bfloat16),
        ),
        scratch_shapes=[pltpu.VMEM((SEQLEN, HD), jnp.float32)] * 2,
        compiler_params=pltpu.CompilerParams(vmem_limit_bytes=48 * 2**20),
        cost_estimate=pl.CostEstimate(
            flops=10 * tokens_all * SEQLEN * columns,
            bytes_accessed=10 * tokens_all * columns,
            transcendentals=tokens_all * SEQLEN * columns // HD,
        ),
        name="attend_back",
    )(queries, pairs, pairs, grads, totals, segments[:, None], segments[None, :], *tables)


MESH = pl.DeviceIdType.MESH


def remote(source, target, sems, at, device):
    return pltpu.make_async_remote_copy(
        src_ref=source,
        dst_ref=target,
        send_sem=sems[0].at[at],
        recv_sem=sems[1].at[at],
        device_id=device,
        device_id_type=MESH,
    )


def columns_of(ref, index, width):
    return ref.at[:, pl.ds(pl.multiple_of(index * width, width), width)]


def rows_of(ref, index, height):
    return ref.at[pl.ds(pl.multiple_of(index * height, height), height), :]


class Exchange:
    def __init__(self, axis, out_shape, source_view, target_view):
        self.axis, self.out_shape = axis, out_shape
        self.source_view, self.target_view = source_view, target_view
        self.count = lax.axis_size(axis)
        self.sem_count = self.count

    def peers(self, grp, seq):
        me = grp if self.axis == "grp" else seq
        for step in range(1, self.count):
            there = (me + step) % self.count
            yield (there, seq) if self.axis == "grp" else (grp, there)

    def start(self, source, target, sems, grp, seq):
        me = grp if self.axis == "grp" else seq
        self.own = pltpu.make_async_copy(
            self.source_view(source, me), self.target_view(target, me), sems[0].at[0]
        )
        self.own.start()
        self.sent, self.due = [], []
        for step, device in enumerate(self.peers(grp, seq), 1):
            there = (me + step) % self.count
            back = (me + self.count - step) % self.count
            copy = remote(
                self.source_view(source, there), self.target_view(target, me), sems, step, device
            )
            copy.start()
            self.sent.append(copy)
            self.due.append(
                remote(
                    self.source_view(source, back), self.target_view(target, back), sems, step, device
                )
            )

    def forward(self):
        pass

    def finish(self):
        for copy in self.due:
            copy.wait_recv()
        for copy in self.sent:
            copy.wait_send()
        self.own.wait()


class PlaneGather:
    def __init__(self, shape):
        self.out_shape = (lax.axis_size("grp"), *shape)
        self.half = shape[0] // 2
        self.sem_count = 14

    def around(self, grp):
        core, across_x, across_y = grp % 2, (grp // 2) % 2, grp // 4
        return grp + 1 - 2 * core, grp + 2 - 4 * across_x, grp + 4 - 8 * across_y

    def peers(self, grp, seq):
        for other in self.around(grp):
            yield other, seq

    def start(self, source, target, sems, grp, seq):
        core, side_x, side_y = self.around(grp)
        half = self.half

        def part(block, piece):
            if piece == "all":
                return target.at[block]
            return target.at[block, pl.ds(0 if piece == "a" else half, half)]

        def own(piece):
            if piece == "all":
                return source
            return source.at[pl.ds(0 if piece == "a" else half, half)]

        def across(block):
            return self.around(self.around(block)[1])[2]

        def make(at, block, piece, via, first=False):
            view = own(piece) if first else part(block, piece)
            return remote(view, part(block, piece), sems, at, (via, seq))

        self.out = [
            make(1, grp, "a", side_x, True),
            make(2, grp, "b", side_x, True),
            make(3, side_y, "b", side_x),
            make(4, grp, "b", side_y, True),
            make(5, grp, "a", side_y, True),
            make(6, side_x, "a", side_y),
            make(7, grp, "all", core, True),
            make(8, side_x, "a", core),
            make(9, side_x, "b", core),
            make(10, side_y, "b", core),
            make(11, side_y, "a", core),
            make(12, across(grp), "a", core),
            make(13, across(grp), "b", core),
        ]
        self.due = [
            make(1, side_x, "a", side_x),
            make(2, side_x, "b", side_x),
            make(3, across(grp), "b", side_x),
            make(4, side_y, "b", side_y),
            make(5, side_y, "a", side_y),
            make(6, across(grp), "a", side_y),
            make(7, core, "all", core),
            make(8, self.around(core)[1], "a", core),
            make(9, self.around(core)[1], "b", core),
            make(10, self.around(core)[2], "b", core),
            make(11, self.around(core)[2], "a", core),
            make(12, across(core), "a", core),
            make(13, across(core), "b", core),
        ]
        self.kept = pltpu.make_async_copy(source, target.at[grp], sems[0].at[0])
        self.kept.start()
        for at in (1, 4, 2, 5, 7):
            self.out[at - 1].start()

    def forward(self):
        for came, then in ((1, (6, 8)), (4, (3, 10)), (2, (9,)), (5, (11,)), (6, (12,)), (3, (13,))):
            self.due[came - 1].wait_recv()
            for at in then:
                self.out[at - 1].start()

    def finish(self):
        for copy in self.due[6:]:
            copy.wait_recv()
        for copy in self.out:
            copy.wait_send()
        self.kept.wait()


def gather_plane(shape):
    if lax.axis_size("grp") == 8:
        return PlaneGather(shape)
    return Exchange(
        "grp",
        (lax.axis_size("grp"), *shape),
        lambda ref, index: ref,
        lambda ref, index: ref.at[index],
    )


def exchange_kernel(tasks, *refs):
    count = len(tasks)
    sources, targets, sems = refs[:count], refs[count : 2 * count], refs[2 * count :]
    grp, seq = lax.axis_index("grp"), lax.axis_index("seq")
    barrier = pltpu.get_barrier_semaphore()
    axes = {"grp": [], "seq": []}
    for task in tasks:
        axis = task.axis if isinstance(task, Exchange) else "grp"
        devices = list(task.peers(grp, seq))
        if len(devices) > len(axes[axis]):
            axes[axis] = devices
    devices = axes["grp"] + axes["seq"]
    for device in devices:
        pl.semaphore_signal(barrier, inc=1, device_id=device, device_id_type=MESH)
    pl.semaphore_wait(barrier, len(devices))
    for at, task in enumerate(tasks):
        task.start(sources[at], targets[at], sems[2 * at : 2 * at + 2], grp, seq)
    for task in tasks:
        task.forward()
    for task in tasks:
        task.finish()


def exchange(number, work):
    tasks = [task for task, _ in work]
    arrays = [array for _, array in work]
    scratch = []
    for task in tasks:
        scratch += [pltpu.SemaphoreType.DMA((task.sem_count,))] * 2
    return pl.pallas_call(
        functools.partial(exchange_kernel, tasks),
        in_specs=[pl.BlockSpec(memory_space=pl.ANY)] * len(work),
        out_specs=[pl.BlockSpec(memory_space=pl.ANY)] * len(work),
        out_shape=[
            jax.ShapeDtypeStruct(task.out_shape, array.dtype) for task, array in work
        ],
        scratch_shapes=scratch,
        compiler_params=pltpu.CompilerParams(collective_id=number, has_side_effects=True),
        name="exchange",
    )(*arrays)


def to_heads(array):
    count = lax.axis_size("seq")
    rows, columns = array.shape
    width = columns // count
    task = Exchange(
        "seq",
        (rows * count, width),
        lambda ref, index: columns_of(ref, index, width),
        lambda ref, index: rows_of(ref, index, rows),
    )
    return task, array


def to_tokens(array):
    count = lax.axis_size("seq")
    rows_all, width = array.shape
    rows = rows_all // count
    task = Exchange(
        "seq",
        (rows, width * count),
        lambda ref, index: rows_of(ref, index, rows),
        lambda ref, index: columns_of(ref, index, width),
    )
    return task, array


def gather_axis(axis, array):
    task = Exchange(
        axis,
        (lax.axis_size(axis), *array.shape),
        lambda ref, index: ref,
        lambda ref, index: ref.at[index],
    )
    return task, array


def split_rows(axis, array):
    count = lax.axis_size(axis)
    rows, columns = array.shape
    height = rows // count
    task = Exchange(
        axis,
        (count, height, columns),
        lambda ref, index: rows_of(ref, index, height),
        lambda ref, index: ref.at[index],
    )
    return task, array


def split_columns(axis, array):
    count = lax.axis_size(axis)
    rows, columns = array.shape
    width = columns // count
    task = Exchange(
        axis,
        (count, rows, width),
        lambda ref, index: columns_of(ref, index, width),
        lambda ref, index: ref.at[index],
    )
    return task, array


def add_rows(total, first, second):
    step = 32

    def some(at, _):
        rows = pl.ds(pl.multiple_of(at * step, step), step)
        total[rows, :] = (
            first[rows, :].astype(jnp.float32) + second[rows, :].astype(jnp.float32)
        ).astype(total.dtype)
        return 0

    lax.fori_loop(0, total.shape[0] // step, some, 0)


def plane_sum_kernel(
    part_ref, total_ref, core_in, chip, half_x, half_y, whole_x, whole_y, send_sems, recv_sems
):
    grp, seq = lax.axis_index("grp"), lax.axis_index("seq")

    def around(device):
        core, across_x, across_y = device % 2, (device // 2) % 2, device // 4
        return device + 1 - 2 * core, device + 2 - 4 * across_x, device + 4 - 8 * across_y

    def order(device):
        _, side_x, side_y = around(device)
        return around(side_x)[2], side_x, side_y, device

    core, side_x, side_y = around(grp)
    half = total_ref.shape[0] // 2
    low, high = pl.ds(0, half), pl.ds(half, half)
    barrier = pltpu.get_barrier_semaphore()
    for device in (core, side_x, side_y):
        pl.semaphore_signal(barrier, inc=1, device_id=(device, seq), device_id_type=MESH)
    pl.semaphore_wait(barrier, 3)

    sems = (send_sems, recv_sems)
    copies = [
        remote(part_ref.at[block], core_in.at[at], sems, at, (core, seq))
        for at, block in enumerate(order(core))
    ]
    copies += [
        remote(chip.at[0, low], half_x, sems, 4, (side_x, seq)),
        remote(chip.at[0, high], half_y, sems, 5, (side_y, seq)),
        remote(chip.at[1, low], whole_x.at[low], sems, 6, (side_x, seq)),
        remote(chip.at[2, high], whole_y.at[high], sems, 7, (side_y, seq)),
        remote(chip.at[1, high], whole_x.at[high], sems, 8, (side_x, seq)),
        remote(chip.at[2, low], whole_y.at[low], sems, 9, (side_y, seq)),
    ]
    for copy in copies[:4]:
        copy.start()
    blocks = order(grp)
    for at, then in ((0, (4, 5)), (1, (6,)), (2, (7,))):
        copies[at].wait_recv()
        add_rows(chip.at[at], part_ref.at[blocks[at]], core_in.at[at])
        for start in then:
            copies[start].start()
    copies[5].wait_recv()
    add_rows(chip.at[1, high], chip.at[1, high], half_y)
    copies[8].start()
    copies[4].wait_recv()
    add_rows(chip.at[2, low], chip.at[2, low], half_x)
    copies[9].start()
    copies[3].wait_recv()
    add_rows(total_ref, part_ref.at[blocks[3]], core_in.at[3])
    for at, came in ((6, whole_x.at[low]), (7, whole_y.at[high]), (8, whole_x.at[high]), (9, whole_y.at[low])):
        copies[at].wait_recv()
        rows = low if at in (6, 9) else high
        add_rows(total_ref.at[rows], total_ref.at[rows], came)
    for copy in copies:
        copy.wait_send()


def plane_sum(number, part):
    count = lax.axis_size("grp")
    rows_all, columns = part.shape
    rows = rows_all // count
    if count != 8:
        return lax.psum_scatter(part, "grp", scatter_dimension=0, tiled=True).astype(jnp.float32)
    low = jnp.bfloat16
    return pl.pallas_call(
        plane_sum_kernel,
        in_specs=[pl.BlockSpec(memory_space=pltpu.VMEM)],
        out_specs=pl.BlockSpec(memory_space=pltpu.VMEM),
        out_shape=jax.ShapeDtypeStruct((rows, columns), jnp.float32),
        scratch_shapes=[
            pltpu.VMEM((4, rows, columns), low),
            pltpu.VMEM((3, rows, columns), low),
            pltpu.VMEM((rows // 2, columns), low),
            pltpu.VMEM((rows // 2, columns), low),
            pltpu.VMEM((rows, columns), low),
            pltpu.VMEM((rows, columns), low),
            pltpu.SemaphoreType.DMA((10,)),
            pltpu.SemaphoreType.DMA((10,)),
        ],
        compiler_params=pltpu.CompilerParams(
            collective_id=number, has_side_effects=True, vmem_limit_bytes=40 * 2**20
        ),
        name="plane_sum",
    )(part.reshape(count, rows, columns))


def local(
    tokens,
    cotangent,
    segment_ids,
    tile_owner_slots,
    weights_low,
    master,
    moment_one,
    moment_two,
    left_basis_set,
    right_basis_set,
    gains,
    gain_moment_one,
    gain_moment_two,
):
    grp_count = lax.axis_size("grp")
    seq_count = lax.axis_size("seq")
    grp_here = lax.axis_index("grp")
    rows_here = tokens.shape[0]
    slots_here, rows_block, tile_width = weights_low.shape
    query_cols = NH * HD
    value_end = query_cols + 2 * HD
    output_end = value_end + MODEL_WIDTH
    attn_tiles = output_end // tile_width
    hidden_tiles = FF // tile_width
    share = -(-hidden_tiles // grp_count)
    share_cols = share * tile_width
    sub_rows = rows_block // grp_count
    local_index = lax.axis_index("seq") * rows_here + jnp.arange(rows_here, dtype=jnp.int32)
    local_place = local_index % SEQLEN

    plane_tiles = lax.all_gather(weights_low, "grp", axis=0, tiled=True)
    hidden_ids = grp_here * share + jnp.arange(share, dtype=jnp.int32)
    real = hidden_ids < hidden_tiles
    hidden_ids = jnp.minimum(hidden_ids, hidden_tiles - 1)
    feed_ids = (
        attn_tiles
        + jnp.arange(3, dtype=jnp.int32)[:, None] * hidden_tiles
        + hidden_ids[None, :]
    ).reshape(-1)
    attn_rows = lax.dynamic_slice_in_dim(plane_tiles, grp_here * sub_rows, sub_rows, axis=1)
    attn_rows = jnp.transpose(attn_rows[tile_owner_slots[:attn_tiles]], (1, 0, 2)).reshape(
        sub_rows, output_end
    )
    attn_weights = lax.all_gather(attn_rows, "seq", axis=0, tiled=False)
    attn_weights = lax.all_gather(attn_weights, "grp", axis=1, tiled=True).reshape(
        MODEL_WIDTH, output_end
    )
    feed_tiles = jnp.where(
        jnp.tile(real, 3)[:, None, None], plane_tiles[tile_owner_slots[feed_ids]], 0
    )
    feed_rows = jnp.transpose(feed_tiles, (1, 0, 2)).reshape(rows_block, 3 * share_cols)
    feed_weights = lax.all_gather(feed_rows, "seq", axis=0, tiled=True)

    tok_float = tokens.astype(jnp.float32)
    inverse_one = lax.rsqrt(jnp.mean(tok_float * tok_float, axis=-1, keepdims=True) + NORM_EPS)
    normed = (tok_float * inverse_one * gains[0]).astype(jnp.bfloat16)
    projected = jnp.dot(normed, attn_weights[:, :value_end], preferred_element_type=jnp.float32)
    queries = rotate(projected[:, :query_cols].reshape(rows_here, NH, HD), local_place, 1.0).astype(
        jnp.bfloat16
    )
    key_rows = (
        rotate(
            projected[:, query_cols : query_cols + HD].reshape(rows_here, 1, HD), local_place, 1.0
        )
        .reshape(rows_here, HD)
        .astype(jnp.bfloat16)
    )
    value_rows = projected[:, query_cols + HD : value_end].astype(jnp.bfloat16)
    queries, pairs, segments, normed_plane = exchange(
        0,
        [
            to_heads(queries.reshape(rows_here, query_cols)),
            gather_axis("seq", jnp.concatenate([key_rows, value_rows], axis=1)),
            gather_axis("seq", segment_ids.reshape(-1, tile_width)),
            (gather_plane(normed.shape), normed),
        ],
    )
    pairs = pairs.reshape(-1, 2 * HD)
    segments = segments.reshape(-1).astype(jnp.float32)
    head_context, log_totals = attend(queries, pairs, segments)
    context, cot_plane = exchange(
        1, [to_tokens(head_context), (gather_plane(cotangent.shape), cotangent)]
    )
    normed_plane = normed_plane.reshape(-1, MODEL_WIDTH)
    cot_plane = cot_plane.reshape(-1, MODEL_WIDTH)
    branch = jnp.dot(
        context, attn_weights[:, value_end:], preferred_element_type=jnp.float32
    )
    hidden = tok_float + branch
    inverse_two = lax.rsqrt(jnp.mean(hidden * hidden, axis=-1, keepdims=True) + NORM_EPS)
    normed_two = (hidden * inverse_two * gains[1]).astype(jnp.bfloat16)

    (second_plane,) = exchange(2, [(gather_plane(normed_two.shape), normed_two)])
    second_plane = second_plane.reshape(-1, MODEL_WIDTH)
    gating_weights = feed_weights[:, : 2 * share_cols]
    down_weights = feed_weights[:, 2 * share_cols :]
    gate_up = jnp.dot(second_plane, gating_weights, preferred_element_type=jnp.float32)
    gate = gate_up[:, :share_cols]
    upper = gate_up[:, share_cols:]
    sigmoid_gate = jax.nn.sigmoid(gate)
    silu_gate = jax.nn.silu(gate)
    activated = (silu_gate * upper).astype(jnp.bfloat16)
    feed_part = times_transpose(activated, down_weights).astype(jnp.bfloat16)
    feed_part, cot_plane = lax.optimization_barrier((feed_part, cot_plane))
    feed_out = lax.psum_scatter(feed_part, "grp", scatter_dimension=0, tiled=True)
    act_grad = jnp.dot(cot_plane, down_weights, preferred_element_type=jnp.float32)
    gate_grad = (act_grad * upper * sigmoid_gate * (1.0 + gate * (1.0 - sigmoid_gate))).astype(
        jnp.bfloat16
    )
    up_grad = (act_grad * silu_gate).astype(jnp.bfloat16)
    gating_grad = jnp.concatenate([gate_grad, up_grad], axis=1)
    two_part = times_transpose(gating_grad, gating_weights).astype(jnp.bfloat16)
    feed_grads = jnp.concatenate(
        [contract(second_plane, gating_grad), contract(cot_plane, activated)], axis=1
    ).astype(jnp.bfloat16)
    two_part, feed_grads = lax.optimization_barrier((two_part, feed_grads))
    feed_grads = lax.psum_scatter(feed_grads, "seq", scatter_dimension=0, tiled=True)
    norm_two_grad = plane_sum(3, two_part)

    out_grad = cotangent.astype(jnp.float32)
    gain_two_term = jnp.sum(norm_two_grad * hidden * inverse_two, axis=0)
    hidden_grad = (
        out_grad
        + inverse_two * gains[1] * norm_two_grad
        - hidden
        * inverse_two**3
        * jnp.mean(hidden * gains[1] * norm_two_grad, axis=-1, keepdims=True)
    )
    branch_grad = hidden_grad.astype(jnp.bfloat16)
    context_grad = times_transpose(branch_grad, attn_weights[:, value_end:]).astype(jnp.bfloat16)
    head_grads, context_plane = exchange(
        4, [to_heads(context_grad), (gather_plane(context.shape), context)]
    )
    head_query_grad, pair_part = attend_back(
        queries,
        pairs,
        head_grads,
        log_totals,
        segments,
        turn_tables(jnp.arange(SEQLEN, dtype=jnp.int32)),
    )
    query_grad, pair_parts, branch_share = exchange(
        5,
        [
            to_tokens(head_query_grad),
            split_rows("seq", pair_part),
            split_columns("grp", branch_grad),
        ],
    )
    query_grad, feed_grads, feed_out = lax.optimization_barrier((query_grad, feed_grads, feed_out))
    block_out = (hidden + feed_out.astype(jnp.float32)).astype(jnp.bfloat16)
    feed_grads = jnp.transpose(
        feed_grads.reshape(rows_block, 3 * share, tile_width), (1, 0, 2)
    )
    feed_grads = lax.all_gather(feed_grads, "grp", axis=0, tiled=True)
    pair_grad = jnp.sum(pair_parts.astype(jnp.float32), axis=0).astype(jnp.bfloat16)
    projected_grad = jnp.concatenate([query_grad, pair_grad], axis=1)
    norm_one_grad = times_transpose(projected_grad, attn_weights[:, :value_end])
    gain_one_term = jnp.sum(norm_one_grad * tok_float * inverse_one, axis=0)
    input_grad = (
        hidden_grad
        + inverse_one * gains[0] * norm_one_grad
        - tok_float
        * inverse_one**3
        * jnp.mean(tok_float * gains[0] * norm_one_grad, axis=-1, keepdims=True)
    )
    query_share, pair_plane, gain_parts = exchange(
        6,
        [
            split_columns("grp", query_grad),
            gather_axis("grp", pair_grad),
            gather_axis("grp", jnp.stack([gain_one_term, gain_two_term])),
        ],
    )
    gain_plane = jnp.sum(gain_parts, axis=0)
    share_width = MODEL_WIDTH // grp_count
    normed_rows = lax.dynamic_slice_in_dim(
        normed_plane.reshape(-1, seq_count, grp_count, sub_rows), grp_here, 1, axis=2
    ).reshape(-1, seq_count * sub_rows)
    query_weight_grad = contract(normed_plane, query_share.reshape(-1, share_width))
    out_weight_grad = contract(
        context_plane.reshape(-1, MODEL_WIDTH), branch_share.reshape(-1, share_width)
    )
    pair_weight_grad = contract(normed_rows, pair_plane.reshape(-1, 2 * HD))
    shares = jnp.concatenate([query_weight_grad, out_weight_grad], axis=1).astype(jnp.bfloat16)
    share_parts, pair_parts, gain_parts = exchange(
        7,
        [
            split_rows("seq", shares),
            split_rows("seq", pair_weight_grad.astype(jnp.bfloat16)),
            gather_axis("seq", gain_plane),
        ],
    )
    gain_grads = jnp.sum(gain_parts, axis=0)
    shares = jnp.sum(share_parts.astype(jnp.float32), axis=0).astype(jnp.bfloat16)
    pair_rows = jnp.sum(pair_parts.astype(jnp.float32), axis=0).astype(jnp.bfloat16)
    share_plane, pair_weight = exchange(
        8,
        [(gather_plane(shares.shape), shares), (gather_plane(pair_rows.shape), pair_rows)],
    )
    query_tiles, out_tiles = [
        jnp.transpose(
            half.reshape(grp_count, rows_block, share_width // tile_width, tile_width),
            (0, 2, 1, 3),
        ).reshape(-1, rows_block, tile_width)
        for half in (share_plane[:, :, :share_width], share_plane[:, :, share_width:])
    ]
    pair_tiles = jnp.transpose(pair_weight.reshape(rows_block, 2, tile_width), (1, 0, 2))
    attn_grads = jnp.concatenate([query_tiles, pair_tiles, out_tiles], axis=0)

    tile_count = tile_owner_slots.shape[0]
    tile_of_slot = (
        jnp.full((grp_count * slots_here,), tile_count, jnp.int32)
        .at[tile_owner_slots]
        .set(jnp.arange(tile_count, dtype=jnp.int32))
    )
    tiles_here = lax.dynamic_slice_in_dim(tile_of_slot, grp_here * slots_here, slots_here)
    feed_at = jnp.clip(tiles_here - attn_tiles, 0, 3 * hidden_tiles - 1)
    which, column = feed_at // hidden_tiles, feed_at % hidden_tiles
    feed_at = (column // share) * (3 * share) + which * share + column % share
    picked = jnp.where(
        (tiles_here < attn_tiles)[:, None, None],
        attn_grads[jnp.minimum(tiles_here, attn_tiles - 1)],
        feed_grads[feed_at],
    )
    reduced_sum = jnp.where((tiles_here < tile_count)[:, None, None], picked, 0).astype(jnp.float32)
    turned = jnp.einsum("zji,zjc->zic", left_basis_set, reduced_sum)
    turned = jnp.einsum("zic,zcd->zid", turned, right_basis_set)
    new_one = BETA_ONE * moment_one + (1.0 - BETA_ONE) * turned
    new_two = BETA_TWO * moment_two + (1.0 - BETA_TWO) * turned * turned
    scaled = new_one / (jnp.sqrt(new_two) + ADAM_EPS)
    restored = jnp.einsum("zij,zjd->zid", left_basis_set, scaled)
    restored = jnp.einsum("zid,zed->zie", restored, right_basis_set)
    new_master = master * (1.0 - LEARN_RATE * WEIGHT_DECAY) - LEARN_RATE * restored
    gain_one = BETA_ONE * gain_moment_one + (1.0 - BETA_ONE) * gain_grads
    gain_two = BETA_TWO * gain_moment_two + (1.0 - BETA_TWO) * gain_grads * gain_grads
    new_gains = gains - GAIN_RATE * gain_one / (jnp.sqrt(gain_two) + ADAM_EPS)
    return (
        block_out,
        input_grad,
        new_master,
        new_one,
        new_two,
        gain_grads,
        new_gains,
        gain_one,
        gain_two,
    )


def solution(mesh):
    return jax.shard_map(
        local,
        mesh=mesh,
        in_specs=(
            P(("grp", "seq"), None),
            P(("grp", "seq"), None),
            P(("grp", "seq")),
            P(),
            P("grp", "seq", None),
            P("grp", "seq", None),
            P("grp", "seq", None),
            P("grp", "seq", None),
            P("grp", "seq", None),
            P("grp", "seq", None),
            P(),
            P(),
            P(),
        ),
        out_specs=(
            P(("grp", "seq"), None),
            P(("grp", "seq"), None),
            P("grp", "seq", None),
            P("grp", "seq", None),
            P("grp", "seq", None),
            P(),
            P(),
            P(),
            P(),
        ),
        check_vma=False,
    )
```

time: 1740 us -> 1110 us (0.64)
  waiting for transfers between devices: 1020 us -> 265 us
  Pallas kernels: 0 us -> 498 us
  blocking collectives: 219 us -> 0 us
  matrix products: 299 us -> 171 us
    pallas_call x0 -> x11, Pallas kernels: none -> 498 us  [the longest x8 438 us: exchange(): pl.pallas_call(functools.partial(exchange_kernel, tasks), in_specs=[pl.Bl...]
    reduce_scatter x5 -> x1, waiting for transfers between devices: 398 us -> 0.02 us  [local(): lax.psum_scatter(feed_part, 'grp', scatter_dimension=0, tiled=True)]
    reduce_scatter x1, waiting for transfers between devices: 161 us -> 4.52 us  [local(): lax.psum_scatter(feed_grads, 'seq', scatter_dimension=0, tiled=True)]
    dot_general x15 -> x1, matrix products: 150 us -> 17.7 us  [local(): jnp.dot(second_plane, gating_weights, preferred_element_type=jnp.float32)]
    all_to_all x2 -> x0, blocking collectives: 97.3 us -> none  [the longest x1 56.1 us: local(): lax.all_to_all(head_context.reshape(-1, heads_here * HD).astype(jnp.bfloa...]
    all_gather x4 -> x0, waiting for transfers between devices: 92.1 us -> none  [the longest x1 54.9 us: local(): normed_plane = lax.all_gather(normed_two, 'grp', axis=0, tiled=True)]
    all_gather x2 -> x0, blocking collectives: 79.7 us -> none  [the longest x1 40.8 us: local(): all_segs = lax.all_gather(segment_ids, 'seq', axis=0, tiled=True)]
    all_gather x1, waiting for transfers between devices: 76.1 us -> 0.01 us  [local(): feed_grads = lax.all_gather(feed_grads, 'grp', axis=0, tiled=True)]
  transfers between devices with their start and end apart: 17 -> 7, of which waited for: 13 -> 5; matrix products, arithmetic and copies ran while one was open for 12% -> 19% of each run, Pallas kernels for 0% -> 45%
where the time goes in v2:
time: 1110 us; the launch traced here: 1100 us
  Pallas kernels  498 us (45%)
  waiting for transfers between devices  265 us (24%)
  matrix products  171 us (15%)
  local copies, waits for them, and re-layouts  96.1 us (9%)
  other arithmetic  51.8 us (5%)
  between operations  15.2 us (1%)
    pallas_call x8, Pallas kernels, exchange(): pl.pallas_call(functools.partial(exchange_kernel, tasks), in_specs=[pl.Bl...  438 us
    all_gather x1, waiting for transfers between devices, local(): plane_tiles = lax.all_gather(weights_low, 'grp', axis=0, tiled=True)  116 us
    all_gather x1, waiting for transfers between devices, local(): lax.all_gather(attn_weights, 'grp', axis=1, tiled=True)  72.6 us
    all_gather x1, waiting for transfers between devices, local(): attn_weights = lax.all_gather(attn_rows, 'seq', axis=0, tiled=False)  48.4 us
    dot_general x4, matrix products, times_transpose(): lax.dot_general(left_side, right_side, (((1,), (1,)), ((), ())), preferre...  45.8 us
    dot_general x5, matrix products, contract(): lax.dot_general(left_side, right_side, (((0,), (0,)), ((), ())), preferre...  45.6 us
    pallas_call x1, Pallas kernels, plane_sum(): pl.pallas_call(plane_sum_kernel, in_specs=[pl.BlockSpec(memory_space=pltp...  39.9 us
    all_gather x1, waiting for transfers between devices, local(): feed_weights = lax.all_gather(feed_rows, 'seq', axis=0, tiled=True)  22.4 us
  transfers between devices with their start and end apart: 7, of which 5 were waited for; matrix products, arithmetic and copies ran while one was open for 19% of the time, Pallas kernels for 45%

profile of v2, /device:TPU:0, one launch (start us, length us, event | category | flops | bytes accessed | tf_op | source)
XLA Modules:
  0.0 1097.8 jit_solution(9611058865041031424)
XLA Ops:
  8.7 116.0 %all-gather.6.cloned.1.call-done = bf16[168,512,128]{2,1,0:T(8,128)(2,1)} async-done(((bf16[21,512,128]{2,1,0:T(8,128)(2,1)}), bf16[168,512,128]{2,1,0:T(8,128)(2,1)}) %all-gather.6.cloned.1.call-update) | async-done | bytes 22020112 | tf_op jit(solution)/shard_map/all_gather | solution.py:613
  124.7 3.9 constant_dynamic-slice_fusion.1
  128.6 2.4 gather_fusion
  132.6 48.4 %all-gather.8.cloned.1.call-done = bf16[4,64,4352]{2,1,0:T(8,128)(2,1)} async-done(((bf16[1,64,4352]{2,1,0:T(8,128)(2,1)}), bf16[4,64,4352]{2,1,0:T(8,128)(2,1)}) %all-gather.8.cloned.1.call-update) | async-done | bytes 2228240 | tf_op jit(solution)/shard_map/all_gather | solution.py:626
  182.1 10.4 gather_fusion.2
  192.5 3.7 select_bitcast_fusion
  196.2 4.4 copy.70
  203.5 72.6 %all-gather.10.cloned.1.call-done = bf16[4,512,4352]{2,1,0:T(8,128)(2,1)} async-done(((bf16[4,64,4352]{2,1,0:T(8,128)(2,1)}), bf16[4,512,4352]{2,1,0:T(8,128)(2,1)}) %all-gather.10.cloned.1.call-update) | async-done | bytes 17825808 | tf_op jit(solution)/shard_map/all_gather | solution.py:627
  276.1 6.6 fusion.2
  287.4 81.5 %exchange.8 = (bf16[1024,512]{1,0:T(8,128)(2,1)}, bf16[4,256,256]{2,1,0:T(8,128)(2,1)}, s32[4,2,128]{2,1,0:T(2,128)}, bf16[8,256,2048]{2,1,0:T(8,128)(2,1)}) custom-call(bf16[256,2048]{1,0:T(8,128)(2,1)} %bitcast.86, bf16[256,256]{1,0:T(8,128)(2,1)} %pad_maximum_fusion.11.refs_1_, s32[2,128]{1,0:T(2,128)} %bitcast.99, bf16[256,2048]{1,0:T(8,128)(2,1)} %fusion.38.refs_3_), custom_call_target="tpu_custom_call" | custom-call | tf_op jit(solution)/shard_map/exchange/pallas_call | solution.py:407
  372.2 9.5 attend.1
  382.7 47.8 %exchange.9 = (bf16[256,2048]{1,0:T(8,128)(2,1)}, bf16[8,256,2048]{2,1,0:T(8,128)(2,1)}) custom-call(bf16[1024,512]{1,0:T(8,128)(2,1)} %copy-done.3, bf16[256,2048]{1,0:T(8,128)(2,1)} %refs_1_.1), custom_call_target="tpu_custom_call" | custom-call | tf_op jit(solution)/shard_map/exchange/pallas_call | solution.py:407
  430.5 6.2 multiply_reduce_fusion.2
  439.2 39.0 %exchange.10 = bf16[8,256,2048]{2,1,0:T(8,128)(2,1)} custom-call(bf16[256,2048]{1,0:T(8,128)(2,1)} %multiply_convert_fusion.3.refs_0_), custom_call_target="tpu_custom_call" | custom-call | tf_op jit(solution)/shard_map/exchange/pallas_call | solution.py:407
  478.3 22.4 %all-gather.12.cloned.1.call-done = bf16[2048,2304]{0,1:T(8,128)(2,1)} async-done(((bf16[512,2304]{0,1:T(8,128)(2,1)}), bf16[2048,2304]{0,1:T(8,128)(2,1)}) %all-gather.12.cloned.1.call-update) | async-done | bytes 9437200 | tf_op jit(solution)/shard_map/all_gather | solution.py:634
  500.7 17.7 %fusion.10 = f32[2048,1536]{0,1:T(8,128)S(1)} fusion(bf16[2048,2048]{1,0:T(8,128)(2,1)} %bitcast.82, bf16[2048,2304]{0,1:T(8,128)(2,1)} %all-gather.12.cloned.1.call-done), kind=kOutput, calls=%fused_computation.27 | convolution fusion | flops 12884901888 | bytes 27262976 | tf_op jit(solution)/shard_map/dot_general | solution.py:679
  520.4 2.6 copy-done.19
  524.6 10.9 convolution_convert_fusion.2
  535.6 12.7 %convolution_convert_fusion.3 = bf16[2048,768]{0,1:T(8,128)(2,1)} fusion(bf16[2048,768]{0,1:T(8,128)(2,1)} %copy-done.28, bf16[2048,2048]{1,0:T(8,128)(2,1)} %bitcast.104), kind=kOutput, calls=%fused_computation.42 | convolution fusion | flops 6444023808 | bytes 14680064 | tf_op jit(solution)/shard_map/dot_general | solution.py:44
  548.3 14.7 %multiply_convert_fusion.1 = (bf16[2048,768]{0,1:T(8,128)(2,1)}, bf16[2048,768]{0,1:T(8,128)(2,1)}) fusion(f32[2048,1536]{0,1:T(8,128)S(1)} %copy-done.20, bf16[2048,2048]{1,0:T(8,128)(2,1)} %bitcast.105, bf16[2048,2304]{0,1:T(8,128)(2,1)} %all-gather.12.cloned.1.call-done), kind=kOutput, calls=%fused_computation.22 | convolution fusion | flops 6462898176 | bytes 30408704 | tf_op jit(solution)/shard_map/dot_general | solution.py:688
  563.0 18.1 %convolution_convert_fusion = bf16[2048,1536]{0,1:T(8,128)(2,1)S(1)} fusion(bf16[2048,2048]{1,0:T(8,128)(2,1)} %bitcast.83, bf16[2048,768]{0,1:T(8,128)(2,1)} %get-tuple-element.81, bf16[2048,768]{0,1:T(8,128)(2,1)} %get-tuple-element.80), kind=kOutput, calls=%fused_computation.13 | convolution fusion | flops 12900630528 | bytes 20971520 | tf_op jit(solution)/shard_map/dot_general | solution.py:44
  581.1 11.6 %pad_maximum_fusion = bf16[2048,2304]{0,1:T(8,128)(2,1)} fusion(bf16[2048,768]{0,1:T(8,128)(2,1)S(1)} %copy-done.27, bf16[2048,1536]{0,1:T(8,128)(2,1)S(1)} %convolution_convert_fusion), kind=kLoop, calls=%fused_computation.6 | loop fusion | flops 18874368 | bytes 18874368 | tf_op jit(solution)/shard_map/concatenate | solution.py:695
  592.7 19.8 %convolution_convert_fusion.1 = bf16[2048,2048]{1,0:T(8,128)(2,1)} fusion(bf16[2048,2304]{0,1:T(8,128)(2,1)} %all-gather.12.cloned.1.call-done, bf16[2048,768]{0,1:T(8,128)(2,1)} %get-tuple-element.81, bf16[2048,768]{0,1:T(8,128)(2,1)} %get-tuple-element.80), kind=kOutput, calls=%fused_computation.14 | convolution fusion | flops 12901679104 | bytes 20971520 | tf_op jit(solution)/shard_map/dot_general | solution.py:50
  615.4 4.3 copy-done.1
  619.7 39.9 %plane_sum.1 = f32[256,2048]{1,0:T(8,128)S(1)} custom-call(bf16[8,256,2048]{2,1,0:T(8,128)(2,1)S(1)} %bitcast.69), custom_call_target="tpu_custom_call" | custom-call | tf_op jit(solution)/shard_map/plane_sum/pallas_call | solution.py:560
  663.8 6.8 fusion.30.refs_0_
  670.6 42.6 %exchange.11 = (bf16[1024,512]{1,0:T(8,128)(2,1)}, bf16[8,256,2048]{2,1,0:T(8,128)(2,1)}) custom-call(bf16[256,2048]{1,0:T(8,128)(2,1)} %fusion.30.refs_0_, bf16[256,2048]{1,0:T(8,128)(2,1)} %get-tuple-element.43.refs_1_), custom_call_target="tpu_custom_call" | custom-call | tf_op jit(solution)/shard_map/exchange/pallas_call | solution.py:407
  715.9 11.4 %attend_back.1 = (bf16[1024,512]{1,0:T(8,128)(2,1)S(1)}, bf16[1024,256]{1,0:T(8,128)(2,1)S(1)}) custom-call(bf16[1024,512]{1,0:T(8,128)(2,1)S(1)} %copy-done.10, bf16[1024,256]{1,0:T(8,128)(2,1)S(1)} %bitcast.75, bf16[1024,256]{1,0:T(8,128)(2,1)S(1)} %bitcast.76, bf16[1024,512]{1,0:T(8,128)(2,1)S(1)} %copy-done.11, ...), custom_call_target="tpu_custom_call" | custom-call | flops 5368709120 | bytes 5242880 | tf_op jit(solution)/shard_map/attend_back/pallas_call | solution.py:194
  729.0 84.7 %exchange.12 = (bf16[256,2048]{1,0:T(8,128)(2,1)}, bf16[4,256,256]{2,1,0:T(8,128)(2,1)}, bf16[8,256,256]{2,1,0:T(8,128)(2,1)}) custom-call(bf16[1024,512]{1,0:T(8,128)(2,1)} %copy-done.2, bf16[1024,256]{1,0:T(8,128)(2,1)} %copy-done.4, bf16[256,2048]{1,0:T(8,128)(2,1)} %copy-done.26), custom_call_target="tpu_custom_call" | custom-call | tf_op jit(solution)/shard_map/exchange/pallas_call | solution.py:407
  813.8 4.5 reduce-scatter.3.cloned.1.call-done
  818.3 4.3 copy.78
  825.5 12.8 %copy.76 = bf16[8,256,2048]{1,0,2:T(8,128)(2,1)} copy(bf16[8,256,2048]{2,1,0:T(8,128)(2,1)} %get-tuple-element.57) | data formatting | bytes 16777216 | tf_op jit(solution)/shard_map/exchange/pallas_call | solution.py:407
  838.2 13.9 %reshape_reshape.3 = bf16[2048,4,8,64]{0,3,2,1:T(8,128)(2,1)} reshape(bf16[8,256,2048]{1,0,2:T(8,128)(2,1)} %copy.76) | data formatting | bytes 16777216 | tf_op jit(solution)/shard_map/reshape;reshape | solution.py:760
  854.3 7.2 fusion.29
  861.5 8.3 fusion.44
  870.5 51.1 %exchange.13 = (bf16[8,256,256]{2,1,0:T(8,128)(2,1)}, bf16[8,256,256]{2,1,0:T(8,128)(2,1)}, f32[8,2,2048]{2,1,0:T(2,128)}) custom-call(bf16[256,2048]{1,0:T(8,128)(2,1)} %get-tuple-element.55.refs_0_, bf16[256,256]{1,0:T(8,128)(2,1)} %reduce_sum.111.refs_1_, f32[2,2048]{1,0:T(2,128)} %pad_maximum_fusion.12.refs_2_), custom_call_target="tpu_custom_call" | custom-call | tf_op jit(solution)/shard_map/exchange/pallas_call | solution.py:407
  923.2 6.5 fusion.28
  932.4 65.3 %exchange.14 = (bf16[4,512,512]{2,1,0:T(8,128)(2,1)}, bf16[4,64,256]{2,1,0:T(8,128)(2,1)}, f32[4,2,2048]{2,1,0:T(2,128)}) custom-call(bf16[2048,512]{1,0:T(8,128)(2,1)} %pad_maximum_fusion.5.refs_0_, bf16[256,256]{1,0:T(8,128)(2,1)} %convolution_convert_fusion.4.refs_1_, f32[2,2048]{1,0:T(2,128)} %reduce_sum.115.refs_2_), custom_call_target="tpu_custom_call" | custom-call | tf_op jit(solution)/shard_map/exchange/pallas_call | solution.py:407
  997.7 2.9 reduce_sum.116.refs_0_
  1002.1 25.6 %exchange.15 = (bf16[8,512,512]{2,1,0:T(8,128)(2,1)}, bf16[8,64,256]{2,1,0:T(8,128)(2,1)}) custom-call(bf16[512,512]{1,0:T(8,128)(2,1)} %reduce_sum.116.refs_0_, bf16[64,256]{1,0:T(8,128)(2,1)} %reduce_sum.117.refs_1_), custom_call_target="tpu_custom_call" | custom-call | tf_op jit(solution)/shard_map/exchange/pallas_call | solution.py:407
  1028.8 2.7 fusion.80
  1031.8 2.6 pad_maximum_fusion.2
  1034.4 5.2 gather_fusion.3
  1041.1 2.5 add_convert_fusion
  1043.6 3.6 fusion.40
  1047.2 8.9 gather_fusion.4
  1056.1 18.5 %fusion.12 = (f32[21,512,128]{2,1,0:T(8,128)}, f32[21,512,128]{2,1,0:T(8,128)}) fusion(f32[21,512,128]{2,1,0:T(8,128)} %param.20, f32[21,512,128]{2,1,0:T(8,128)} %param.19, f32[21,128,128]{2,1,0:T(8,128)S(1)} %copy-done, f32[21,512,512]{2,1,0:T(8,128)} %param.21, bf16[21,512,128]{2,1,0:T(8,128)(2,1)} %gather_fusion.3, ...), kind=kOutput, calls=%fused_computation.29 | convolution fusion | flops 1772617728 | bytes 50921512 | tf_op jit(solution)/shard_map/zic,zcd->zid/dot_general | solution.py:810
  1074.6 16.1 %multiply_subtract_fusion = f32[21,512,128]{2,1,0:T(8,128)} fusion(f32[21,512,128]{2,1,0:T(8,128)} %param.18, f32[21,128,128]{2,1,0:T(8,128)S(1)} %copy-done, f32[21,512,512]{2,1,0:T(8,128)} %param.21, f32[21,512,128]{2,1,0:T(8,128)} %get-tuple-element.83, f32[21,512,128]{2,1,0:T(8,128)} %get-tuple-element.82), kind=kOutput, calls=%fused_computation.30 | convolution fusion | flops 1768488960 | bytes 45416448 | tf_op jit(solution)/shard_map/zid,zed->zie/dot_general | solution.py:815
  (179 shorter events, 47.6 us)
Async XLA Ops:
  7.2 1048.9 %copy-start = (f32[21,128,128]{2,1,0:T(8,128)S(1)}, f32[21,128,128]{2,1,0:T(8,128)}, u32[]{:S(2)}) copy-start(f32[21,128,128]{2,1,0:T(8,128)} %param.22) | copy-start | bytes 4128772
  7.2 117.5 %all-gather.6.cloned.1.call-start = ((), (), s32[]{:S(2)}) async-start(), calls=%async_computation.2 | async-start | bytes 24772608 | tf_op jit(solution)/shard_map/all_gather | solution.py:613
  7.9 173.1 %all-gather.8.cloned.1.call-start = ((), (), s32[]{:S(2)}) async-start(), calls=%async_computation.3 | async-start | bytes 2785280 | tf_op jit(solution)/shard_map/all_gather | solution.py:626
  128.6 52.7 %copy-start.14 = (s32[166]{0:T(256)S(1)}, s32[166]{0:T(256)}, u32[]{:S(2)}) copy-start(s32[166]{0:T(256)} %param.16) | copy-start | bytes 1996
  132.5 143.6 %all-gather.10.cloned.1.call-start = ((), (), s32[]{:S(2)}) async-start(), calls=%async_computation.4 | async-start | bytes 20054016 | tf_op jit(solution)/shard_map/all_gather | solution.py:627
  181.0 319.6 %all-gather.12.cloned.1.call-start = ((), (), s32[]{:S(2)}) async-start(), calls=%async_computation.5 | async-start | bytes 11796480 | tf_op jit(solution)/shard_map/all_gather | solution.py:634
  196.2 4.5 copy-start.21
  196.2 5.9 copy-start.38
  200.6 613.1 %reduce-scatter.5.cloned.1.call-start = ((), (), s32[]{:S(2)}) async-start(), calls=%async_computation.7 | async-start | bytes 9437184 | tf_op jit(solution)/shard_map/reduce_scatter | solution.py:687
  200.7 85.3 %copy-start.44 = (f32[64]{0:T(128)}, f32[64]{0:T(128)S(1)}, u32[]{:S(2)}) copy-start(f32[64]{0:T(128)S(1)} %multiply_power_fusion) | copy-start | bytes 772
  201.6 74.5 %copy-start.42 = (f32[256]{0:T(256)}, f32[256]{0:T(256)S(1)}, u32[]{:S(2)}) copy-start(f32[256]{0:T(256)S(1)} %get-tuple-element.100) | copy-start | bytes 3076
  202.2 73.9 %copy-start.34 = (f32[1,2048]{1,0:T(1,128)}, f32[1,2048]{1,0:T(1,128)S(1)}, u32[]{:S(2)}) copy-start(f32[1,2048]{1,0:T(1,128)S(1)} %get-tuple-element.93) | copy-start | bytes 24580
  369.6 12.2 %copy-start.7 = (f32[4,2,128]{2,1,0:T(2,128)}, f32[4,2,128]{2,1,0:T(2,128)S(1)}, u32[]{:S(2)}) copy-start(f32[4,2,128]{2,1,0:T(2,128)S(1)} %convert_element_type.114) | copy-start | bytes 12292
  369.8 11.9 %copy-start.5 = (f32[1024,1]{1,0:T(8,128)}, f32[1024,1]{1,0:T(8,128)S(1)}, u32[]{:S(2)}) copy-start(f32[1024,1]{1,0:T(8,128)S(1)} %copy.69.key_seg_ref) | copy-start | bytes 12292
  369.8 1.4 copy-start.9
  436.7 1.3 copy-start.16
  518.4 4.6 copy-start.19
  523.0 1.7 copy-start.28
  535.6 282.7 %reduce-scatter.3.cloned.1.call-start = ((), (), s32[]{:S(2)}) async-start(), calls=%async_computation.6 | async-start | bytes 11796480 | tf_op jit(solution)/shard_map/reduce_scatter | solution.py:699
  535.6 12.7 %copy-start.20 = (f32[2048,1536]{0,1:T(8,128)S(1)}, f32[2048,1536]{0,1:T(8,128)}, u32[]{:S(2)}) copy-start(f32[2048,1536]{0,1:T(8,128)} %copy-done.19) | copy-start | bytes 37748740
  563.0 18.1 %copy-start.27 = (bf16[2048,768]{0,1:T(8,128)(2,1)S(1)}, bf16[2048,768]{0,1:T(8,128)(2,1)}, u32[]{:S(2)}) copy-start(bf16[2048,768]{0,1:T(8,128)(2,1)} %convolution_convert_fusion.3) | copy-start | bytes 9437188
  612.5 434.6 %all-gather.14.cloned.1.call-start = ((), (), s32[]{:S(2)}) async-start(), calls=%async_computation.8 | async-start | bytes 21233664 | tf_op jit(solution)/shard_map/all_gather | solution.py:737
  615.4 4.3 copy-start.1
  619.7 39.9 %copy-start.17 = (f32[256,2048]{1,0:T(8,128)S(1)}, f32[256,2048]{1,0:T(8,128)}, u32[]{:S(2)}) copy-start(f32[256,2048]{1,0:T(8,128)} %copy-done.16) | copy-start | bytes 6291460
  663.8 49.5 %copy-start.6 = (f32[1024,1]{1,0:T(8,128)S(1)}, f32[1024,1]{1,0:T(8,128)}, u32[]{:S(2)}) copy-start(f32[1024,1]{1,0:T(8,128)} %copy-done.5) | copy-start | bytes 12292
  663.8 49.5 %copy-start.8 = (f32[4,2,128]{2,1,0:T(2,128)S(1)}, f32[4,2,128]{2,1,0:T(2,128)}, u32[]{:S(2)}) copy-start(f32[4,2,128]{2,1,0:T(2,128)} %copy-done.7) | copy-start | bytes 12292
  663.8 49.5 %copy-start.13 = (bf16[4,256,256]{2,1,0:T(8,128)(2,1)S(1)}, bf16[4,256,256]{2,1,0:T(8,128)(2,1)}, u32[]{:S(2)}) copy-start(bf16[4,256,256]{2,1,0:T(8,128)(2,1)} %get-tuple-element.40) | copy-start | bytes 1572868
  713.2 1.4 copy-start.10
  818.3 4.3 copy-start.15
  838.2 13.9 %copy-start.32 = (bf16[4,256,256]{2,1,0:T(8,128)(2,1)S(1)}, bf16[4,256,256]{2,1,0:T(8,128)(2,1)}, u32[]{:S(2)}) copy-start(bf16[4,256,256]{2,1,0:T(8,128)(2,1)} %get-tuple-element.56) | copy-start | bytes 1572868
  854.2 7.3 copy-start.22
  854.2 7.3 copy-start.29
  854.2 7.3 copy-start.33
  854.3 7.3 copy-start.35
  854.3 7.3 copy-start.43
  923.2 6.5 copy-start.31
  929.7 1.5 copy-start.30
  997.7 31.1 %copy-start.37 = (f32[4,2,2048]{2,1,0:T(2,128)S(1)}, f32[4,2,2048]{2,1,0:T(2,128)}, u32[]{:S(2)}) copy-start(f32[4,2,2048]{2,1,0:T(2,128)} %get-tuple-element.68) | copy-start | bytes 196612
  1028.8 11.6 %copy-start.36 = (f32[2,2048]{1,0:T(2,128)}, f32[2,2048]{1,0:T(2,128)S(1)}, u32[]{:S(2)}) copy-start(f32[2,2048]{1,0:T(2,128)S(1)} %reduce_sum.118) | copy-start | bytes 49156
  1034.4 6.1 copy-start.39
  1034.4 6.0 copy-start.40
  1034.4 6.0 copy-start.41
  1034.4 6.7 copy-start.18
  1039.6 4.0 copy-start.23
  1039.6 4.0 copy-start.24
  1039.6 4.0 copy-start.46
  1047.2 9.0 copy-start.48
  1047.2 9.0 copy-start.49
  (9 other events, 9.1 us)
Sparse Core Ops, SparseCore 0:
  9.9 114.7 all-gather.5
  132.6 48.3 all-gather.7
  182.9 93.1 all-gather.9
  278.1 222.5 all-gather.11
  535.7 69.5 reduce-scatter.4
  612.6 205.5 reduce-scatter.2
  822.7 129.4 all-gather.13

commit v3 on v2

v3 whole, which is shorter than its diff:
```python
import functools

import jax
import jax.numpy as jnp
from jax import lax
from jax.experimental import pallas as pl
from jax.experimental.pallas import tpu as pltpu
from jax.sharding import PartitionSpec as P

MODEL_WIDTH = 2048
NH = 16
HD = 128
FF = 5632
SEQLEN = 1024


NORM_EPS = 1e-05
BETA_ONE = 0.95
BETA_TWO = 0.95
ADAM_EPS = 1e-08
WEIGHT_DECAY = 0.01
LEARN_RATE = 0.03
GAIN_RATE = 1.5
ROPE_BASE = 10000.0
MASKED = -1e30
PRECISE = lax.Precision.HIGHEST


def contract(left_side, right_side):
    return lax.dot_general(
        left_side, right_side, (((0,), (0,)), ((), ())), preferred_element_type=jnp.float32
    )


def times_transpose(left_side, right_side):
    return lax.dot_general(
        left_side, right_side, (((1,), (1,)), ((), ())), preferred_element_type=jnp.float32
    )


def turn_tables(places):
    half_width = HD // 2
    frequency = ROPE_BASE ** (-(jnp.arange(half_width, dtype=jnp.float32) * 2.0) / HD)
    angles = places.astype(jnp.float32)[:, None] * frequency[None, :]
    cosine, sine = jnp.cos(angles), jnp.sin(angles)
    return (
        jnp.concatenate([cosine, cosine], axis=1),
        jnp.concatenate([-sine, sine], axis=1),
    )


def turn(rows, cosine, sine):
    return rows * cosine + pltpu.roll(rows, HD // 2, 1) * sine


def turn_back(rows, cosine, sine):
    return rows * cosine - pltpu.roll(rows, HD // 2, 1) * sine


def dot_last(left_side, right_side):
    return lax.dot_general(
        left_side, right_side, (((1,), (1,)), ((), ())), preferred_element_type=jnp.float32
    )


def dot_first(left_side, right_side):
    return lax.dot_general(
        left_side, right_side, (((0,), (0,)), ((), ())), preferred_element_type=jnp.float32
    )


def project_kernel(x_ref, w_ref, cosine_ref, sine_ref, out_ref):
    made = jnp.dot(x_ref[...], w_ref[...], preferred_element_type=jnp.float32)
    cosine, sine = cosine_ref[...], sine_ref[...]
    first, second = made[:, :HD], made[:, HD:]
    last = pl.program_id(0) == pl.num_programs(0) - 1
    out_ref[:, :HD] = turn(first, cosine, sine).astype(out_ref.dtype)
    out_ref[:, HD:] = jnp.where(last, second, turn(second, cosine, sine)).astype(out_ref.dtype)


def project(normed, weights, tables):
    rows, width = normed.shape
    steps = NH // 2 + 1
    return pl.pallas_call(
        project_kernel,
        grid=(steps,),
        in_specs=[
            pl.BlockSpec((rows, width), lambda j: (0, 0)),
            pl.BlockSpec((width, 2 * HD), lambda j: (0, j)),
            pl.BlockSpec((rows, HD), lambda j: (0, 0)),
            pl.BlockSpec((rows, HD), lambda j: (0, 0)),
        ],
        out_specs=pl.BlockSpec((rows, 2 * HD), lambda j: (0, j)),
        out_shape=jax.ShapeDtypeStruct((rows, steps * 2 * HD), jnp.bfloat16),
        compiler_params=pltpu.CompilerParams(vmem_limit_bytes=32 * 2**20),
        cost_estimate=pl.CostEstimate(
            flops=4 * rows * width * steps * HD,
            bytes_accessed=4 * width * steps * HD,
            transcendentals=0,
        ),
        name="project",
    )(normed, weights, *tables)


def score_mask(key_seg_ref, query_seg_ref, block, rows):
    keys = (block + 1) * rows
    same = key_seg_ref[:keys, :] == query_seg_ref[...]
    key_at = lax.broadcasted_iota(jnp.int32, (keys, rows), 0)
    query_at = lax.broadcasted_iota(jnp.int32, (keys, rows), 1) + block * rows
    return same & (key_at <= query_at)


def attend_kernel(at_ref, q_ref, k_ref, v_ref, key_seg_ref, query_seg_ref, context_ref, total_ref):
    scale = HD ** (-0.5)
    rows = q_ref.shape[0]
    for block in range(SEQLEN // rows):

        @pl.when(at_ref[0] == block)
        def _():
            keys = (block + 1) * rows
            scores = dot_last(k_ref[:keys, :], q_ref[...]) * scale
            scores = jnp.where(
                score_mask(key_seg_ref, query_seg_ref, block, rows), scores, MASKED
            )
            highest = jnp.max(scores, axis=0, keepdims=True)
            exponent = jnp.exp(scores - highest)
            totals = jnp.sum(exponent, axis=0, keepdims=True)
            probs_low = (exponent * (1.0 / totals)).astype(jnp.bfloat16)
            context = dot_first(probs_low, v_ref[:keys, :])
            context_ref[...] = context.astype(jnp.bfloat16)
            total_ref[0] = highest + jnp.log(totals)


def attend_back_kernel(
    at_ref,
    q_ref,
    k_ref,
    v_ref,
    grad_ref,
    total_ref,
    key_seg_ref,
    query_seg_ref,
    key_cosine_ref,
    key_sine_ref,
    cosine_ref,
    sine_ref,
    query_grad_ref,
    pair_grad_ref,
    key_sum,
    value_sum,
):
    scale = HD ** (-0.5)
    rows = q_ref.shape[0]
    head = pl.program_id(0)

    @pl.when(head == 0)
    def _():
        key_sum[...] = jnp.zeros_like(key_sum)
        value_sum[...] = jnp.zeros_like(value_sum)

    for block in range(SEQLEN // rows):

        @pl.when(at_ref[0] == block)
        def _():
            keys = (block + 1) * rows
            queries, grads = q_ref[...], grad_ref[...]
            shifted = dot_last(k_ref[:keys, :], queries) * scale - total_ref[0]
            allowed = score_mask(key_seg_ref, query_seg_ref, block, rows)
            probs = jnp.where(allowed, jnp.exp(shifted), 0.0)
            prob_grad = dot_last(v_ref[:keys, :], grads)
            centre = jnp.sum(probs * prob_grad, axis=0, keepdims=True)
            score_grad = (probs * (prob_grad - centre) * scale).astype(jnp.bfloat16)
            value_sum[:keys, :] += jnp.dot(
                probs.astype(jnp.bfloat16), grads, preferred_element_type=jnp.float32
            )
            key_sum[:keys, :] += jnp.dot(score_grad, queries, preferred_element_type=jnp.float32)
            query_grad = dot_first(score_grad, k_ref[:keys, :])
            query_grad_ref[...] = turn_back(query_grad, cosine_ref[...], sine_ref[...]).astype(
                jnp.bfloat16
            )

    @pl.when(head == pl.num_programs(0) - 1)
    def _():
        pair_grad_ref[:, :HD] = turn_back(
            key_sum[...], key_cosine_ref[...], key_sine_ref[...]
        ).astype(jnp.bfloat16)
        pair_grad_ref[:, HD:] = value_sum[...].astype(jnp.bfloat16)


def attention_specs(kinds, rows):
    specs = {
        "at": pl.BlockSpec(memory_space=pltpu.SMEM),
        "head": pl.BlockSpec((rows, HD), lambda h: (0, h)),
        "keys": pl.BlockSpec((SEQLEN, HD), lambda h: (0, 0)),
        "values": pl.BlockSpec((SEQLEN, HD), lambda h: (0, 1)),
        "pair": pl.BlockSpec((SEQLEN, 2 * HD), lambda h: (0, 0)),
        "total": pl.BlockSpec((1, 1, rows), lambda h: (h, 0, 0)),
        "key_seg": pl.BlockSpec((SEQLEN, 1), lambda h: (0, 0)),
        "query_seg": pl.BlockSpec((1, rows), lambda h: (0, 0)),
        "key_table": pl.BlockSpec((SEQLEN, HD), lambda h: (0, 0)),
        "table": pl.BlockSpec((rows, HD), lambda h: (0, 0)),
    }
    return [specs[kind] for kind in kinds]


def attend(at, projected, pairs, key_segs, query_segs):
    rows = projected.shape[0]
    columns = NH * HD
    return pl.pallas_call(
        attend_kernel,
        grid=(NH,),
        in_specs=attention_specs(["at", "head", "keys", "values", "key_seg", "query_seg"], rows),
        out_specs=attention_specs(["head", "total"], rows),
        out_shape=(
            jax.ShapeDtypeStruct((rows, columns), jnp.bfloat16),
            jax.ShapeDtypeStruct((NH, 1, rows), jnp.float32),
        ),
        compiler_params=pltpu.CompilerParams(vmem_limit_bytes=32 * 2**20),
        cost_estimate=pl.CostEstimate(
            flops=4 * rows * SEQLEN * columns,
            bytes_accessed=6 * rows * columns,
            transcendentals=rows * SEQLEN * NH,
        ),
        name="attend",
    )(at, projected, pairs, pairs, key_segs[:, None], query_segs[None, :])


def attend_back(at, projected, pairs, grads, totals, key_segs, query_segs, key_tables, tables):
    rows = projected.shape[0]
    columns = NH * HD
    return pl.pallas_call(
        attend_back_kernel,
        grid=(NH,),
        in_specs=attention_specs(
            ["at", "head", "keys", "values", "head", "total", "key_seg", "query_seg"]
            + ["key_table", "key_table", "table", "table"],
            rows,
        ),
        out_specs=attention_specs(["head", "pair"], rows),
        out_shape=(
            jax.ShapeDtypeStruct((rows, columns), jnp.bfloat16),
            jax.ShapeDtypeStruct((SEQLEN, 2 * HD), jnp.bfloat16),
        ),
        scratch_shapes=[pltpu.VMEM((SEQLEN, HD), jnp.float32)] * 2,
        compiler_params=pltpu.CompilerParams(vmem_limit_bytes=32 * 2**20),
        cost_estimate=pl.CostEstimate(
            flops=10 * rows * SEQLEN * columns,
            bytes_accessed=10 * rows * columns,
            transcendentals=rows * SEQLEN * NH,
        ),
        name="attend_back",
    )(
        at, projected, pairs, pairs, grads, totals, key_segs[:, None], query_segs[None, :],
        *key_tables, *tables,
    )


def pick_kernel(rows, feed_ref, attn_ref, tiles_ref, feed_out, attn_out, sems):
    grp = lax.axis_index("grp")
    width = tiles_ref.shape[2]
    copies = []
    for at in range(feed_ref.shape[0]):
        copies.append(
            (tiles_ref.at[feed_ref[at]], feed_out.at[:, at * width : (at + 1) * width])
        )
    share = pl.ds(pl.multiple_of(grp * rows, rows), rows)
    for at in range(attn_ref.shape[0]):
        copies.append(
            (tiles_ref.at[attn_ref[at], share], attn_out.at[:, at * width : (at + 1) * width])
        )
    copies = [
        pltpu.make_async_copy(source, target, sems.at[at])
        for at, (source, target) in enumerate(copies)
    ]
    for copy in copies:
        copy.start()
    for copy in copies:
        copy.wait()


def pick(tiles, feed_slots, attn_slots):
    _, rows, width = tiles.shape
    share = rows // lax.axis_size("grp")
    feed, attn = feed_slots.shape[0], attn_slots.shape[0]
    return pl.pallas_call(
        functools.partial(pick_kernel, share),
        in_specs=[pl.BlockSpec(memory_space=pltpu.SMEM)] * 2 + [pl.BlockSpec(memory_space=pl.ANY)],
        out_specs=[pl.BlockSpec(memory_space=pl.ANY)] * 2,
        out_shape=[
            jax.ShapeDtypeStruct((rows, feed * width), tiles.dtype),
            jax.ShapeDtypeStruct((share, attn * width), tiles.dtype),
        ],
        scratch_shapes=[pltpu.SemaphoreType.DMA((feed + attn,))],
        cost_estimate=pl.CostEstimate(
            flops=0, bytes_accessed=4 * (rows * feed + share * attn) * width, transcendentals=0
        ),
        name="pick",
    )(feed_slots, attn_slots, tiles)


def adam_kernel(
    at_ref, gate_ref, up_ref, down_ref, share_ref, pair_ref, left_ref, right_ref, master_ref,
    one_ref, two_ref, new_master_ref, new_one_ref, new_two_ref, grad,
):
    kind = at_ref[0, pl.program_id(0)]
    for number, ref in enumerate((gate_ref, up_ref, down_ref, share_ref, pair_ref)):

        @pl.when(kind == number)
        def _():
            grad[...] = ref[...].reshape(grad.shape)

    @pl.when(kind == 5)
    def _():
        grad[...] = jnp.zeros_like(grad)

    low = jnp.bfloat16
    left, right = left_ref[0].astype(low), right_ref[0].astype(low)
    turned = dot_first(grad[...], left)
    turned = dot_first(turned.astype(low), right)
    new_one = BETA_ONE * one_ref[0] + (1.0 - BETA_ONE) * turned
    new_two = BETA_TWO * two_ref[0] + (1.0 - BETA_TWO) * turned * turned
    new_one_ref[0], new_two_ref[0] = new_one, new_two
    scaled = new_one / (jnp.sqrt(new_two) + ADAM_EPS)
    restored = dot_last(scaled.astype(low), right)
    restored = jnp.dot(left, restored.astype(low), preferred_element_type=jnp.float32)
    new_master_ref[0] = master_ref[0] * (1.0 - LEARN_RATE * WEIGHT_DECAY) - LEARN_RATE * restored


def adam(at, gate, up, down, shares, pairs, left, right, master, one, two):
    slots, rows, width = master.shape
    tile = pl.BlockSpec((1, rows, width), lambda i, at: (i, 0, 0))
    shape = jax.ShapeDtypeStruct(master.shape, jnp.float32)
    feed = pl.BlockSpec((1, rows, width), lambda i, at: (at[1, i], 0, at[2, i]))
    return pl.pallas_call(
        adam_kernel,
        grid_spec=pltpu.PrefetchScalarGridSpec(
            num_scalar_prefetch=1,
            grid=(slots,),
            in_specs=[
                feed,
                feed,
                feed,
                pl.BlockSpec((1, rows, width), lambda i, at: (at[3, i], 0, at[4, i])),
                pl.BlockSpec((*pairs.shape[:2], width), lambda i, at: (0, 0, at[5, i])),
                pl.BlockSpec((1, rows, rows), lambda i, at: (i, 0, 0)),
                pl.BlockSpec((1, width, width), lambda i, at: (i, 0, 0)),
                tile,
                tile,
                tile,
            ],
            out_specs=[tile] * 3,
            scratch_shapes=[pltpu.VMEM((rows, width), jnp.bfloat16)],
        ),
        out_shape=[shape] * 3,
        compiler_params=pltpu.CompilerParams(vmem_limit_bytes=32 * 2**20),
        cost_estimate=pl.CostEstimate(
            flops=4 * slots * rows * width * (rows + width),
            bytes_accessed=4 * slots * rows * (rows + 6 * width),
            transcendentals=slots * rows * width,
        ),
        name="adam",
    )(at, gate, up, down, shares, pairs, left, right, master, one, two)


MESH = pl.DeviceIdType.MESH


def remote(source, target, sems, at, device):
    return pltpu.make_async_remote_copy(
        src_ref=source,
        dst_ref=target,
        send_sem=sems[0].at[at],
        recv_sem=sems[1].at[at],
        device_id=device,
        device_id_type=MESH,
    )


def columns_of(ref, index, width):
    return ref.at[:, pl.ds(pl.multiple_of(index * width, width), width)]


def rows_of(ref, index, height):
    return ref.at[pl.ds(pl.multiple_of(index * height, height), height), :]


class Exchange:
    def __init__(self, axis, out_shape, source_view, target_view):
        self.axis, self.out_shape = axis, out_shape
        self.source_view, self.target_view = source_view, target_view
        self.count = lax.axis_size(axis)
        self.sem_count = self.count

    def peers(self, grp, seq):
        me = grp if self.axis == "grp" else seq
        for step in range(1, self.count):
            there = (me + step) % self.count
            yield (there, seq) if self.axis == "grp" else (grp, there)

    def start(self, source, target, sems, grp, seq):
        me = grp if self.axis == "grp" else seq
        self.own = pltpu.make_async_copy(
            self.source_view(source, me), self.target_view(target, me), sems[0].at[0]
        )
        self.own.start()
        self.sent, self.due = [], []
        for step, device in enumerate(self.peers(grp, seq), 1):
            there = (me + step) % self.count
            back = (me + self.count - step) % self.count
            copy = remote(
                self.source_view(source, there), self.target_view(target, me), sems, step, device
            )
            copy.start()
            self.sent.append(copy)
            self.due.append(
                remote(
                    self.source_view(source, back), self.target_view(target, back), sems, step, device
                )
            )

    def forward(self):
        pass

    def finish(self):
        for copy in self.due:
            copy.wait_recv()
        for copy in self.sent:
            copy.wait_send()
        self.own.wait()


class PlaneGather:
    axis = "grp"
    sem_count = 14

    def __init__(self, out_shape, source_view, target_view, half_of):
        self.out_shape = out_shape
        self.source_view, self.target_view, self.half_of = source_view, target_view, half_of

    def around(self, grp):
        core, across_x, across_y = grp % 2, (grp // 2) % 2, grp // 4
        return grp + 1 - 2 * core, grp + 2 - 4 * across_x, grp + 4 - 8 * across_y

    def peers(self, grp, seq):
        for other in self.around(grp):
            yield other, seq

    def start(self, source, target, sems, grp, seq):
        core, side_x, side_y = self.around(grp)

        def part(block, piece):
            view = self.target_view(target, block)
            return view if piece == "all" else self.half_of(view, piece == "b")

        def own(piece):
            view = self.source_view(source, grp)
            return view if piece == "all" else self.half_of(view, piece == "b")

        def across(block):
            return self.around(self.around(block)[1])[2]

        def make(at, block, piece, via, first=False):
            view = own(piece) if first else part(block, piece)
            return remote(view, part(block, piece), sems, at, (via, seq))

        self.out = [
            make(1, grp, "a", side_x, True),
            make(2, grp, "b", side_x, True),
            make(3, side_y, "b", side_x),
            make(4, grp, "b", side_y, True),
            make(5, grp, "a", side_y, True),
            make(6, side_x, "a", side_y),
            make(7, grp, "all", core, True),
            make(8, side_x, "a", core),
            make(9, side_x, "b", core),
            make(10, side_y, "b", core),
            make(11, side_y, "a", core),
            make(12, across(grp), "a", core),
            make(13, across(grp), "b", core),
        ]
        self.due = [
            make(1, side_x, "a", side_x),
            make(2, side_x, "b", side_x),
            make(3, across(grp), "b", side_x),
            make(4, side_y, "b", side_y),
            make(5, side_y, "a", side_y),
            make(6, across(grp), "a", side_y),
            make(7, core, "all", core),
            make(8, self.around(core)[1], "a", core),
            make(9, self.around(core)[1], "b", core),
            make(10, self.around(core)[2], "b", core),
            make(11, self.around(core)[2], "a", core),
            make(12, across(core), "a", core),
            make(13, across(core), "b", core),
        ]
        self.kept = pltpu.make_async_copy(own("all"), part(grp, "all"), sems[0].at[0])
        self.kept.start()
        for at in (1, 4, 2, 5, 7):
            self.out[at - 1].start()

    def forward(self):
        for came, then in ((1, (6, 8)), (4, (3, 10)), (2, (9,)), (5, (11,)), (6, (12,)), (3, (13,))):
            self.due[came - 1].wait_recv()
            for at in then:
                self.out[at - 1].start()

    def finish(self):
        for copy in self.due[6:]:
            copy.wait_recv()
        for copy in self.out:
            copy.wait_send()
        self.kept.wait()


def half_rows(axis, height):
    def half_of(view, second):
        index = (slice(None),) * axis + (pl.ds(height if second else 0, height),)
        return view.at[index]

    return half_of


def whole(ref, index):
    return ref


def block_of(ref, index):
    return ref.at[index]


def gather_plane(shape, split=0, source_view=whole, target_view=block_of, out_shape=None):
    out_shape = out_shape or (lax.axis_size("grp"), *shape)
    if lax.axis_size("grp") == 8:
        return PlaneGather(out_shape, source_view, target_view, half_rows(split, shape[split] // 2))
    return Exchange("grp", out_shape, source_view, target_view)


def exchange_kernel(tasks, wires, arrays, outputs, *refs):
    sources, targets = refs[:arrays], refs[arrays : arrays + outputs]
    sems = refs[arrays + outputs :]
    grp, seq = lax.axis_index("grp"), lax.axis_index("seq")
    barrier = pltpu.get_barrier_semaphore()
    axes = {"grp": [], "seq": []}
    for task in tasks:
        devices = list(task.peers(grp, seq))
        if len(devices) > len(axes[task.axis]):
            axes[task.axis] = devices
    devices = axes["grp"] + axes["seq"]
    for device in devices:
        pl.semaphore_signal(barrier, inc=1, device_id=device, device_id_type=MESH)
    pl.semaphore_wait(barrier, len(devices))

    def start(at):
        after, source, target = wires[at]
        source = targets[source] if after is not None else sources[source]
        tasks[at].start(source, targets[target], sems[2 * at : 2 * at + 2], grp, seq)

    open_tasks = list(range(len(tasks)))
    first = [at for at in open_tasks if wires[at][0] is None]
    for at in first:
        start(at)
    for at in first:
        tasks[at].forward()
    for at in open_tasks[:]:
        after = wires[at][0]
        if after is not None:
            tasks[after].finish()
            open_tasks.remove(after)
            start(at)
            tasks[at].forward()
    for at in open_tasks:
        tasks[at].finish()


def exchange(number, work):
    tasks = [piece[0] for piece in work]
    arrays, shapes, wires = [], [], []
    for piece in work:
        if isinstance(piece[1], int):
            after, source = piece[1], wires[piece[1]][2]
            kind = shapes[source].dtype
        else:
            after, source = None, len(arrays)
            arrays.append(piece[1])
            kind = piece[1].dtype
        if len(piece) == 3:
            target = wires[piece[2]][2]
        else:
            target = len(shapes)
            shapes.append(jax.ShapeDtypeStruct(piece[0].out_shape, kind))
        wires.append((after, source, target))
    scratch = []
    for task in tasks:
        scratch += [pltpu.SemaphoreType.DMA((task.sem_count,))] * 2
    return pl.pallas_call(
        functools.partial(exchange_kernel, tasks, wires, len(arrays), len(shapes)),
        in_specs=[pl.BlockSpec(memory_space=pl.ANY)] * len(arrays),
        out_specs=[pl.BlockSpec(memory_space=pl.ANY)] * len(shapes),
        out_shape=shapes,
        scratch_shapes=scratch,
        compiler_params=pltpu.CompilerParams(collective_id=number, has_side_effects=True),
        name="exchange",
    )(*arrays)


def gather_axis(axis, array):
    task = Exchange(axis, (lax.axis_size(axis), *array.shape), whole, block_of)
    return task, array


def split_rows(axis, array):
    count = lax.axis_size(axis)
    rows, columns = array.shape
    height = rows // count
    task = Exchange(
        axis,
        (count, height, columns),
        lambda ref, index: rows_of(ref, index, height),
        block_of,
    )
    return task, array


def split_columns(axis, array):
    count = lax.axis_size(axis)
    rows, columns = array.shape
    width = columns // count
    task = Exchange(
        axis,
        (count, rows, width),
        lambda ref, index: columns_of(ref, index, width),
        block_of,
    )
    return task, array


def add_rows(total, first, second):
    step = 32

    def some(at, _):
        rows = pl.ds(pl.multiple_of(at * step, step), step)
        total[rows, :] = (
            first[rows, :].astype(jnp.float32) + second[rows, :].astype(jnp.float32)
        ).astype(total.dtype)
        return 0

    lax.fori_loop(0, total.shape[0] // step, some, 0)


def plane_sum_kernel(
    part_ref, total_ref, core_in, chip, half_x, half_y, whole_x, whole_y, send_sems, recv_sems
):
    grp, seq = lax.axis_index("grp"), lax.axis_index("seq")

    def around(device):
        core, across_x, across_y = device % 2, (device // 2) % 2, device // 4
        return device + 1 - 2 * core, device + 2 - 4 * across_x, device + 4 - 8 * across_y

    def order(device):
        _, side_x, side_y = around(device)
        return around(side_x)[2], side_x, side_y, device

    core, side_x, side_y = around(grp)
    half = total_ref.shape[0] // 2
    low, high = pl.ds(0, half), pl.ds(half, half)
    barrier = pltpu.get_barrier_semaphore()
    for device in (core, side_x, side_y):
        pl.semaphore_signal(barrier, inc=1, device_id=(device, seq), device_id_type=MESH)
    pl.semaphore_wait(barrier, 3)

    sems = (send_sems, recv_sems)
    copies = [
        remote(part_ref.at[block], core_in.at[at], sems, at, (core, seq))
        for at, block in enumerate(order(core))
    ]
    copies += [
        remote(chip.at[0, low], half_x, sems, 4, (side_x, seq)),
        remote(chip.at[0, high], half_y, sems, 5, (side_y, seq)),
        remote(chip.at[1, low], whole_x.at[low], sems, 6, (side_x, seq)),
        remote(chip.at[2, high], whole_y.at[high], sems, 7, (side_y, seq)),
        remote(chip.at[1, high], whole_x.at[high], sems, 8, (side_x, seq)),
        remote(chip.at[2, low], whole_y.at[low], sems, 9, (side_y, seq)),
    ]
    for copy in copies[:4]:
        copy.start()
    blocks = order(grp)
    for at, then in ((0, (4, 5)), (1, (6,)), (2, (7,))):
        copies[at].wait_recv()
        add_rows(chip.at[at], part_ref.at[blocks[at]], core_in.at[at])
        for start in then:
            copies[start].start()
    copies[5].wait_recv()
    add_rows(chip.at[1, high], chip.at[1, high], half_y)
    copies[8].start()
    copies[4].wait_recv()
    add_rows(chip.at[2, low], chip.at[2, low], half_x)
    copies[9].start()
    copies[3].wait_recv()
    add_rows(total_ref, part_ref.at[blocks[3]], core_in.at[3])
    for at, came in ((6, whole_x.at[low]), (7, whole_y.at[high]), (8, whole_x.at[high]), (9, whole_y.at[low])):
        copies[at].wait_recv()
        rows = low if at in (6, 9) else high
        add_rows(total_ref.at[rows], total_ref.at[rows], came)
    for copy in copies:
        copy.wait_send()


def plane_sum(number, part):
    count = lax.axis_size("grp")
    rows_all, columns = part.shape
    rows = rows_all // count
    if count != 8:
        return lax.psum_scatter(part, "grp", scatter_dimension=0, tiled=True).astype(jnp.float32)
    low = jnp.bfloat16
    return pl.pallas_call(
        plane_sum_kernel,
        in_specs=[pl.BlockSpec(memory_space=pltpu.VMEM)],
        out_specs=pl.BlockSpec(memory_space=pltpu.VMEM),
        out_shape=jax.ShapeDtypeStruct((rows, columns), jnp.float32),
        scratch_shapes=[
            pltpu.VMEM((4, rows, columns), low),
            pltpu.VMEM((3, rows, columns), low),
            pltpu.VMEM((rows // 2, columns), low),
            pltpu.VMEM((rows // 2, columns), low),
            pltpu.VMEM((rows, columns), low),
            pltpu.VMEM((rows, columns), low),
            pltpu.SemaphoreType.DMA((10,)),
            pltpu.SemaphoreType.DMA((10,)),
        ],
        compiler_params=pltpu.CompilerParams(
            collective_id=number, has_side_effects=True, vmem_limit_bytes=40 * 2**20
        ),
        name="plane_sum",
    )(part.reshape(count, rows, columns))


def behind_gather(array):
    if lax.axis_size("grp") != 8:
        return lax.all_gather(array, "grp", axis=0, tiled=True)
    half = array.shape[0] // 2

    def via(values, bit):
        return lax.ppermute(values, "grp", [(at, at ^ bit) for at in range(8)])

    from_x, from_y = via(array, 2), via(array, 4)
    across = jnp.concatenate([via(from_x[:half], 4), via(from_y[half:], 2)], axis=0)
    chip = jnp.concatenate([array, from_x, from_y, across], axis=0)
    return jnp.concatenate([chip, via(chip, 1)], axis=0)


def behind_order():
    grp = lax.axis_index("grp")
    if lax.axis_size("grp") != 8:
        return jnp.arange(lax.axis_size("grp"), dtype=jnp.int32)
    return jnp.bitwise_xor(grp, jnp.array([0, 2, 4, 6, 1, 3, 5, 7], jnp.int32))


def local(
    tokens,
    cotangent,
    segment_ids,
    tile_owner_slots,
    weights_low,
    master,
    moment_one,
    moment_two,
    left_basis_set,
    right_basis_set,
    gains,
    gain_moment_one,
    gain_moment_two,
):
    grp_count = lax.axis_size("grp")
    seq_count = lax.axis_size("seq")
    grp_here, seq_here = lax.axis_index("grp"), lax.axis_index("seq")
    rows_here = tokens.shape[0]
    slots_here, rows_block, tile_width = weights_low.shape
    tile_count = tile_owner_slots.shape[0]
    query_cols = NH * HD
    value_end = query_cols + 2 * HD
    output_end = value_end + MODEL_WIDTH
    attn_tiles = output_end // tile_width
    query_tiles = query_cols // tile_width
    hidden_tiles = FF // tile_width
    share = -(-hidden_tiles // grp_count)
    share_cols = share * tile_width
    share_width = MODEL_WIDTH // grp_count
    sub_rows = rows_block // grp_count
    halves = 2 if sub_rows >= 32 else 1
    half_block, half_sub = rows_block // halves, sub_rows // halves
    first_place = (seq_here * rows_here) % SEQLEN
    key_tables = turn_tables(jnp.arange(SEQLEN, dtype=jnp.int32))
    tables = [lax.dynamic_slice_in_dim(table, first_place, rows_here) for table in key_tables]

    hidden_ids = grp_here * share + jnp.arange(share, dtype=jnp.int32)
    real = jnp.repeat(hidden_ids < hidden_tiles, tile_width)[None, :]
    hidden_ids = jnp.minimum(hidden_ids, hidden_tiles - 1)
    feed_ids = (
        attn_tiles
        + jnp.arange(3, dtype=jnp.int32)[:, None] * hidden_tiles
        + hidden_ids[None, :]
    ).reshape(-1)
    feed_slots, attn_slots = tile_owner_slots[feed_ids], tile_owner_slots[:attn_tiles]

    def weight_half(at):
        return gather_plane(
            (slots_here, half_block, tile_width),
            split=1,
            source_view=lambda ref, index: ref.at[:, pl.ds(at * half_block, half_block)],
        )

    def attn_half(at):
        return gather_plane(
            (seq_count, half_sub, output_end),
            target_view=lambda ref, index: ref.at[:, at, index],
            out_shape=(seq_count, halves, grp_count, half_sub, output_end),
        )

    flat = (grp_count * slots_here, half_block, tile_width)
    (tiles,) = exchange(0, [(weight_half(0), weights_low)])
    feed_rows, attn_rows = pick(tiles.reshape(flat), feed_slots, attn_slots)
    feed_parts = [lax.all_gather(feed_rows, "seq", axis=0, tiled=False)]
    if halves == 2:
        tiles, attn_first = exchange(
            1, [(weight_half(1), weights_low), gather_axis("seq", attn_rows)]
        )
        feed_rows, attn_rows = pick(tiles.reshape(flat), feed_slots, attn_slots)
        feed_parts.append(lax.all_gather(feed_rows, "seq", axis=0, tiled=False))
        attn_weights, _ = exchange(
            2,
            [(attn_half(0), attn_first), gather_axis("seq", attn_rows), (attn_half(1), 1, 0)],
        )
        feed_weights = jnp.zeros((seq_count, 2, half_block, 3 * share_cols), jnp.bfloat16)
        for at in range(2):
            feed_weights = lax.dynamic_update_slice(
                feed_weights, feed_parts[at][:, None], (0, at, 0, 0)
            )
    else:
        _, attn_weights = exchange(2, [gather_axis("seq", attn_rows), (attn_half(0), 0)])
        feed_weights = feed_parts[0]
    attn_weights = attn_weights.reshape(MODEL_WIDTH, output_end)
    feed_weights = feed_weights.reshape(MODEL_WIDTH, 3 * share_cols)

    tok_float = tokens.astype(jnp.float32)
    inverse_one = lax.rsqrt(jnp.mean(tok_float * tok_float, axis=-1, keepdims=True) + NORM_EPS)
    normed = (tok_float * inverse_one * gains[0]).astype(jnp.bfloat16)
    projected = project(normed, attn_weights, tables)
    pairs, segments = exchange(
        3,
        [
            gather_axis("seq", projected[:, query_cols:]),
            gather_axis("seq", segment_ids.reshape(-1, tile_width)),
        ],
    )
    first_key = seq_here * rows_here - first_place
    pairs = lax.dynamic_slice_in_dim(pairs.reshape(-1, 2 * HD), first_key, SEQLEN)
    key_segs = lax.dynamic_slice_in_dim(segments.reshape(-1), first_key, SEQLEN)
    at = (first_place // rows_here).reshape(1)
    context, log_totals = attend(at, projected, pairs, key_segs, segment_ids)
    branch = jnp.dot(
        context, attn_weights[:, value_end:], preferred_element_type=jnp.float32
    )
    hidden = tok_float + branch
    inverse_two = lax.rsqrt(jnp.mean(hidden * hidden, axis=-1, keepdims=True) + NORM_EPS)
    normed_two = (hidden * inverse_two * gains[1]).astype(jnp.bfloat16)

    second_plane, cot_plane = exchange(
        4,
        [
            (gather_plane(normed_two.shape), normed_two),
            (gather_plane(cotangent.shape), cotangent),
        ],
    )
    second_plane = second_plane.reshape(-1, MODEL_WIDTH)
    cot_plane = cot_plane.reshape(-1, MODEL_WIDTH)
    second_plane, normed, context_late = lax.optimization_barrier((second_plane, normed, context))
    normed_plane = behind_gather(normed)
    context_plane = behind_gather(context_late)
    gating_weights = feed_weights[:, : 2 * share_cols]
    down_weights = feed_weights[:, 2 * share_cols :]
    gate_up = jnp.dot(second_plane, gating_weights, preferred_element_type=jnp.float32)
    gate = gate_up[:, :share_cols]
    upper = gate_up[:, share_cols:]
    sigmoid_gate = jax.nn.sigmoid(gate)
    silu_gate = gate * sigmoid_gate
    activated = jnp.where(real, silu_gate * upper, 0.0).astype(jnp.bfloat16)
    down_grad = contract(cot_plane, activated).astype(jnp.bfloat16)
    down_grad, cot_plane = lax.optimization_barrier((down_grad, cot_plane))
    down_grad = lax.psum_scatter(down_grad, "seq", scatter_dimension=0, tiled=True)
    act_grad = jnp.dot(cot_plane, down_weights, preferred_element_type=jnp.float32)
    act_grad = jnp.where(real, act_grad, 0.0)
    gate_grad = (act_grad * upper * sigmoid_gate * (1.0 + gate * (1.0 - sigmoid_gate))).astype(
        jnp.bfloat16
    )
    up_grad = (act_grad * silu_gate).astype(jnp.bfloat16)
    gate_weight_grad = contract(second_plane, gate_grad).astype(jnp.bfloat16)
    up_weight_grad = contract(second_plane, up_grad).astype(jnp.bfloat16)
    gating_grad = jnp.concatenate([gate_grad, up_grad], axis=1)
    two_part = times_transpose(gating_grad, gating_weights).astype(jnp.bfloat16)
    feed_part = times_transpose(activated, down_weights).astype(jnp.bfloat16)
    two_part, feed_part, gate_weight_grad, up_weight_grad = lax.optimization_barrier(
        (two_part, feed_part, gate_weight_grad, up_weight_grad)
    )
    gate_weight_grad = lax.psum_scatter(gate_weight_grad, "seq", scatter_dimension=0, tiled=True)
    up_weight_grad = lax.psum_scatter(up_weight_grad, "seq", scatter_dimension=0, tiled=True)
    norm_two_grad = plane_sum(5, two_part)

    out_grad = cotangent.astype(jnp.float32)
    gain_two_term = jnp.sum(norm_two_grad * hidden * inverse_two, axis=0)
    hidden_grad = (
        out_grad
        + inverse_two * gains[1] * norm_two_grad
        - hidden
        * inverse_two**3
        * jnp.mean(hidden * gains[1] * norm_two_grad, axis=-1, keepdims=True)
    )
    branch_grad = hidden_grad.astype(jnp.bfloat16)
    context_grad = times_transpose(branch_grad, attn_weights[:, value_end:]).astype(jnp.bfloat16)
    query_grad, pair_part = attend_back(
        at,
        projected,
        pairs,
        context_grad,
        log_totals,
        key_segs,
        segment_ids,
        key_tables,
        tables,
    )
    if seq_count * rows_here > SEQLEN:
        pair_part = lax.dynamic_update_slice_in_dim(
            jnp.zeros((seq_count * rows_here, 2 * HD), pair_part.dtype), pair_part, first_key, 0
        )
    pair_parts, query_share, branch_share = exchange(
        6,
        [
            split_rows("seq", pair_part),
            split_columns("grp", query_grad),
            split_columns("grp", branch_grad),
        ],
    )
    pair_grad = jnp.sum(pair_parts.astype(jnp.float32), axis=0).astype(jnp.bfloat16)
    projected_grad = jnp.concatenate([query_grad, pair_grad], axis=1)
    norm_one_grad = times_transpose(projected_grad, attn_weights[:, :value_end])
    gain_one_term = jnp.sum(norm_one_grad * tok_float * inverse_one, axis=0)
    input_grad = (
        hidden_grad
        + inverse_one * gains[0] * norm_one_grad
        - tok_float
        * inverse_one**3
        * jnp.mean(tok_float * gains[0] * norm_one_grad, axis=-1, keepdims=True)
    )
    pair_plane, gain_parts = exchange(
        7,
        [
            gather_axis("grp", pair_grad),
            gather_axis("grp", jnp.stack([gain_one_term, gain_two_term])),
        ],
    )
    gain_plane = jnp.sum(gain_parts, axis=0)
    order = behind_order()
    normed_rows = lax.dynamic_slice_in_dim(
        normed_plane.reshape(-1, seq_count, grp_count, sub_rows), grp_here, 1, axis=2
    ).reshape(-1, seq_count * sub_rows)
    query_weight_grad = contract(normed_plane, query_share[order].reshape(-1, share_width))
    out_weight_grad = contract(context_plane, branch_share[order].reshape(-1, share_width))
    pair_weight_grad = contract(normed_rows, pair_plane[order].reshape(-1, 2 * HD))
    shares = jnp.concatenate([query_weight_grad, out_weight_grad], axis=1).astype(jnp.bfloat16)
    shares, down_grad, gate_weight_grad = lax.optimization_barrier(
        (shares, down_grad, gate_weight_grad)
    )
    feed_shape = (rows_block, share_cols)
    share_parts, pair_parts, gain_parts, down_plane, gate_plane = exchange(
        8,
        [
            split_rows("seq", shares),
            split_rows("seq", pair_weight_grad.astype(jnp.bfloat16)),
            gather_axis("seq", gain_plane),
            (gather_plane(feed_shape), down_grad),
            (gather_plane(feed_shape), gate_weight_grad),
        ],
    )
    gain_grads = jnp.sum(gain_parts, axis=0)
    shares = jnp.sum(share_parts.astype(jnp.float32), axis=0).astype(jnp.bfloat16)
    pair_rows = jnp.sum(pair_parts.astype(jnp.float32), axis=0).astype(jnp.bfloat16)
    shares, up_weight_grad, feed_part = lax.optimization_barrier((shares, up_weight_grad, feed_part))
    feed_out = lax.psum_scatter(feed_part, "grp", scatter_dimension=0, tiled=True)
    block_out = (hidden + feed_out.astype(jnp.float32)).astype(jnp.bfloat16)
    up_plane, share_plane, pair_plane = exchange(
        9,
        [
            (gather_plane(feed_shape), up_weight_grad),
            (gather_plane(shares.shape), shares),
            (gather_plane(pair_rows.shape), pair_rows),
        ],
    )

    tile_of_slot = (
        jnp.full((grp_count * slots_here,), tile_count, jnp.int32)
        .at[tile_owner_slots]
        .set(jnp.arange(tile_count, dtype=jnp.int32))
    )
    tiles_here = lax.dynamic_slice_in_dim(tile_of_slot, grp_here * slots_here, slots_here)
    feed_at = jnp.clip(tiles_here - attn_tiles, 0, 3 * hidden_tiles - 1)
    which, column = feed_at // hidden_tiles, feed_at % hidden_tiles
    is_query = tiles_here < query_tiles
    is_pair = (tiles_here >= query_tiles) & (tiles_here < query_tiles + 2)
    is_feed = tiles_here >= attn_tiles
    kind = jnp.where(is_feed, jnp.minimum(which, 2), 3)
    kind = jnp.where(is_pair, 4, jnp.where(is_feed, kind, 3))
    kind = jnp.where(tiles_here == tile_count, 5, kind)
    out_at = jnp.clip(tiles_here - query_tiles - 2, 0, query_tiles - 1)
    per_share = share_width // tile_width
    share_at = jnp.where(is_query, jnp.minimum(tiles_here, query_tiles - 1), out_at)
    at = jnp.stack(
        [
            kind,
            column // share,
            column % share,
            share_at // per_share,
            share_at % per_share + jnp.where(is_query, 0, per_share),
            jnp.where(is_pair, tiles_here - query_tiles, 0),
        ]
    )
    new_master, new_one, new_two = adam(
        at,
        gate_plane,
        up_plane,
        down_plane,
        share_plane,
        pair_plane,
        left_basis_set,
        right_basis_set,
        master,
        moment_one,
        moment_two,
    )
    gain_one = BETA_ONE * gain_moment_one + (1.0 - BETA_ONE) * gain_grads
    gain_two = BETA_TWO * gain_moment_two + (1.0 - BETA_TWO) * gain_grads * gain_grads
    new_gains = gains - GAIN_RATE * gain_one / (jnp.sqrt(gain_two) + ADAM_EPS)
    return (
        block_out,
        input_grad,
        new_master,
        new_one,
        new_two,
        gain_grads,
        new_gains,
        gain_one,
        gain_two,
    )


def solution(mesh):
    return jax.shard_map(
        local,
        mesh=mesh,
        in_specs=(
            P(("grp", "seq"), None),
            P(("grp", "seq"), None),
            P(("grp", "seq")),
            P(),
            P("grp", "seq", None),
            P("grp", "seq", None),
            P("grp", "seq", None),
            P("grp", "seq", None),
            P("grp", "seq", None),
            P("grp", "seq", None),
            P(),
            P(),
            P(),
        ),
        out_specs=(
            P(("grp", "seq"), None),
            P(("grp", "seq"), None),
            P("grp", "seq", None),
            P("grp", "seq", None),
            P("grp", "seq", None),
            P(),
            P(),
            P(),
            P(),
        ),
        check_vma=False,
    )
```

time: 1110 us -> 1030 us (0.928)
  waiting for transfers between devices: 265 us -> 43.8 us
  Pallas kernels: 498 us -> 694 us
  matrix products: 171 us -> 132 us
  other arithmetic: 51.8 us -> 35.4 us
    all_gather x5 -> x2, waiting for transfers between devices: 259 us -> 0.01 us  [the longest x1 0.01 us: local(): feed_parts.append(lax.all_gather(feed_rows, 'seq', axis=0, tiled=False))]
    pallas_call x10 -> x15, Pallas kernels: 459 us -> 654 us  [the longest x9 506 us: exchange(): pl.pallas_call(functools.partial(exchange_kernel, tasks, wires, len(array...]
    ppermute x0 -> x10, waiting for transfers between devices: none -> 43 us  [via(): return lax.ppermute(values, 'grp', [(at, at ^ bit) for at in range(8)])]
    dot_general x3 -> x0, matrix products: 41.2 us -> none  [the longest x1 18.5 us: local(): turned = jnp.einsum('zic,zcd->zid', turned, right_basis_set)]
    unnamed x103 -> x130, local copies, waits for them, and re-layouts: 21.2 us -> 51.2 us
    concatenate x0 -> x5, local copies, waits for them, and re-layouts: none -> 23.3 us  [the longest x3 21.3 us: behind_gather(): return jnp.concatenate([chip, via(chip, 1)], axis=0)]
    gather x4 -> x3, local copies, waits for them, and re-layouts: 26.9 us -> 7.85 us  [the longest x1 2.93 us: local(): query_share[order].reshape(-1, share_width)]
    concatenate x5 -> x1, other arithmetic: 15.5 us -> 0.14 us  [turn_tables(): jnp.concatenate([-sine, sine], axis=1)]
  transfers between devices with their start and end apart: 7 -> 16, of which waited for: 5 -> 4; matrix products, arithmetic and copies ran while one was open for 19% -> 11% of each run, Pallas kernels for 45% -> 48%
where the time goes in v3:
time: 1030 us; the launch traced here: 1020 us
  Pallas kernels  694 us (67%)
  matrix products  132 us (13%)
  local copies, waits for them, and re-layouts  95.2 us (9%)
  waiting for transfers between devices  43.8 us (4%)
  other arithmetic  35.4 us (3%)
  between operations  15.5 us (2%)
    pallas_call x9, Pallas kernels, exchange(): pl.pallas_call(functools.partial(exchange_kernel, tasks, wires, len(array...  506 us
    pallas_call x2, Pallas kernels, pick(): pl.pallas_call(functools.partial(pick_kernel, share), in_specs=[pl.BlockS...  92.9 us
    unnamed x130, local copies, waits for them, and re-layouts  51.2 us
    dot_general x6, matrix products, contract(): lax.dot_general(left_side, right_side, (((0,), (0,)), ((), ())), preferre...  44.9 us
    dot_general x4, matrix products, times_transpose(): lax.dot_general(left_side, right_side, (((1,), (1,)), ((), ())), preferre...  44.9 us
    ppermute x10, waiting for transfers between devices, via(): return lax.ppermute(values, 'grp', [(at, at ^ bit) for at in range(8)])  43 us
    pallas_call x1, Pallas kernels, plane_sum(): pl.pallas_call(plane_sum_kernel, in_specs=[pl.BlockSpec(memory_space=pltp...  40 us
    pallas_call x1, Pallas kernels, adam(): pl.pallas_call(adam_kernel, grid_spec=pltpu.PrefetchScalarGridSpec(num_sc...  28.4 us
  transfers between devices with their start and end apart: 16, of which 4 were waited for; matrix products, arithmetic and copies ran while one was open for 11% of the time, Pallas kernels for 48%

profile of v3, /device:TPU:0, one launch (start us, length us, event | category | flops | bytes accessed | tf_op | source)
XLA Modules:
  0.0 1024.9 jit_solution(288141975641895155)
XLA Ops:
  11.8 52.8 %exchange.9 = bf16[8,21,256,128]{3,2,1,0:T(8,128)(2,1)} custom-call(bf16[21,512,128]{2,1,0:T(8,128)(2,1)} %refs_0_.3), custom_call_target="tpu_custom_call" | custom-call | tf_op jit(solution)/shard_map/exchange/pallas_call | solution.py:595
  64.5 46.5 %pick.2 = (bf16[256,2304]{1,0:T(8,128)(2,1)}, bf16[32,4352]{1,0:T(8,128)(2,1)}) custom-call(s32[18]{0:T(128)} %gather_fusion, s32[34]{0:T(128)} %slice.48.attn_ref, bf16[168,256,128]{2,1,0:T(8,128)(2,1)} %bitcast.72), custom_call_target="tpu_custom_call" | custom-call | bytes 2916352 | tf_op jit(solution)/shard_map/pick/pallas_call | solution.py:285
  111.0 55.3 %exchange.10 = (bf16[8,21,256,128]{3,2,1,0:T(8,128)(2,1)}, bf16[4,32,4352]{2,1,0:T(8,128)(2,1)}) custom-call(bf16[21,512,128]{2,1,0:T(8,128)(2,1)} %refs_0_.3, bf16[32,4352]{1,0:T(8,128)(2,1)} %get-tuple-element.55.refs_1_), custom_call_target="tpu_custom_call" | custom-call | tf_op jit(solution)/shard_map/exchange/pallas_call | solution.py:595
  166.3 46.5 %pick.3 = (bf16[256,2304]{1,0:T(8,128)(2,1)}, bf16[32,4352]{1,0:T(8,128)(2,1)}) custom-call(s32[18]{0:T(128)} %gather_fusion, s32[34]{0:T(128)} %slice.48.attn_ref, bf16[168,256,128]{2,1,0:T(8,128)(2,1)} %bitcast.73), custom_call_target="tpu_custom_call" | custom-call | bytes 2916352 | tf_op jit(solution)/shard_map/pick/pallas_call | solution.py:285
  213.6 85.5 %exchange.11 = (bf16[4,2,8,32,4352]{4,3,2,1,0:T(8,128)(2,1)}, bf16[4,32,4352]{2,1,0:T(8,128)(2,1)}) custom-call(bf16[4,32,4352]{2,1,0:T(8,128)(2,1)} %get-tuple-element.56.refs_0_, bf16[32,4352]{1,0:T(8,128)(2,1)} %get-tuple-element.58.refs_1_), custom_call_target="tpu_custom_call" | custom-call | tf_op jit(solution)/shard_map/exchange/pallas_call | solution.py:595
  303.5 6.2 copy-done
  309.7 5.7 project.1.q_ref
  316.2 38.2 %exchange.12 = (bf16[4,256,256]{2,1,0:T(8,128)(2,1)}, s32[4,2,128]{2,1,0:T(2,128)}) custom-call(bf16[256,256]{1,0:T(8,128)(2,1)} %slice.69.refs_0_, s32[2,128]{1,0:T(2,128)} %bitcast.65), custom_call_target="tpu_custom_call" | custom-call | tf_op jit(solution)/shard_map/exchange/pallas_call | solution.py:595
  356.4 9.1 attend.1
  365.5 6.2 multiply_reduce_fusion.2
  374.3 74.4 %exchange.13 = (bf16[8,256,2048]{2,1,0:T(8,128)(2,1)}, bf16[8,256,2048]{2,1,0:T(8,128)(2,1)}) custom-call(bf16[256,2048]{1,0:T(8,128)(2,1)} %multiply_convert_fusion.2.refs_0_, bf16[256,2048]{1,0:T(8,128)(2,1)} %refs_1_.1), custom_call_target="tpu_custom_call" | custom-call | tf_op jit(solution)/shard_map/exchange/pallas_call | solution.py:595
  448.8 8.2 pad_maximum_fusion
  456.9 17.7 %fusion.11 = f32[2048,1536]{0,1:T(8,128)S(1)} fusion(bf16[2048,2048]{1,0:T(8,128)(2,1)} %bitcast.94, bf16[2048,2304]{1,0:T(8,128)(2,1)} %bitcast.75), kind=kOutput, calls=%fused_computation.23 | convolution fusion | flops 12884901888 | bytes 27262976 | tf_op jit(solution)/shard_map/dot_general | solution.py:881
  474.7 2.9 select_convert_fusion
  477.6 3.5 copy-done.25
  483.7 8.5 convolution_convert_fusion.4
  492.2 17.9 %multiply_convert_fusion.1 = (bf16[2048,768]{0,1:T(8,128)(2,1)}, bf16[2048,768]{0,1:T(8,128)(2,1)}) fusion(f32[2048,1536]{0,1:T(8,128)} %copy-done.25, pred[768]{0:T(1024)(128)(4,1)S(1)} %broadcast_bitcast_fusion, bf16[2048,2048]{1,0:T(8,128)(2,1)} %bitcast.97, bf16[2048,2304]{1,0:T(8,128)(2,1)} %bitcast.76), kind=kOutput, calls=%fused_computation.18 | convolution fusion | flops 6464471040 | bytes 30409472 | tf_op jit(solution)/shard_map/dot_general | solution.py:890
  510.2 11.8 %convolution_convert_fusion.2 = bf16[2048,768]{1,0:T(8,128)(2,1)} fusion(bf16[2048,2048]{1,0:T(8,128)(2,1)} %bitcast.95, bf16[2048,768]{0,1:T(8,128)(2,1)} %get-tuple-element.117), kind=kOutput, calls=%fused_computation.31 | convolution fusion | flops 6444023808 | bytes 14680064 | tf_op jit(solution)/shard_map/dot_general | solution.py:30
  522.0 11.4 %convolution_convert_fusion.3 = bf16[2048,768]{1,0:T(8,128)(2,1)} fusion(bf16[2048,2048]{1,0:T(8,128)(2,1)} %bitcast.96, bf16[2048,768]{0,1:T(8,128)(2,1)} %get-tuple-element.116), kind=kOutput, calls=%fused_computation.32 | convolution fusion | flops 6444023808 | bytes 14680064 | tf_op jit(solution)/shard_map/dot_general | solution.py:30
  533.4 19.5 %convolution_convert_fusion.1 = bf16[2048,2048]{1,0:T(8,128)(2,1)} fusion(bf16[2048,768]{0,1:T(8,128)(2,1)} %get-tuple-element.117, bf16[2048,768]{0,1:T(8,128)(2,1)} %get-tuple-element.116, bf16[2048,2304]{1,0:T(8,128)(2,1)} %bitcast.77), kind=kOutput, calls=%fused_computation.9 | convolution fusion | flops 12901679104 | bytes 20971520 | tf_op jit(solution)/shard_map/dot_general | solution.py:36
  552.9 11.0 %convolution_convert_fusion = bf16[2048,2048]{1,0:T(8,128)(2,1)} fusion(bf16[2048,768]{0,1:T(8,128)(2,1)S(1)} %copy-done.38, bf16[2048,2304]{1,0:T(8,128)(2,1)} %bitcast.78), kind=kOutput, calls=%fused_computation.8 | convolution fusion | flops 6446645248 | bytes 14680064 | tf_op jit(solution)/shard_map/dot_general | solution.py:36
  571.2 19.0 %collective-permute-done = bf16[256,2048]{1,0:T(8,128)(2,1)} collective-permute-done((bf16[256,2048]{1,0:T(8,128)(2,1)S(1)}, bf16[256,2048]{1,0:T(8,128)(2,1)}, u32[]{:S(2)}, u32[]{:S(2)}) %collective-permute-start) | collective-permute-done | bytes 1048608 | tf_op jit(solution)/shard_map/ppermute | solution.py:743
  594.5 18.1 %collective-permute-done.5 = bf16[256,2048]{1,0:T(8,128)(2,1)} collective-permute-done((bf16[256,2048]{1,0:T(8,128)(2,1)S(1)}, bf16[256,2048]{1,0:T(8,128)(2,1)}, u32[]{:S(2)}, u32[]{:S(2)}) %collective-permute-start.5) | collective-permute-done | bytes 1048608 | tf_op jit(solution)/shard_map/ppermute | solution.py:743
  617.0 2.8 constant_dynamic-update-slice_fusion.3
  619.8 2.8 constant_dynamic-update-slice_fusion.2
  629.6 5.8 collective-permute-done.7
  637.2 3.3 copy-done.41
  640.8 4.8 constant_dynamic-update-slice_fusion.5
  645.6 11.8 %copy.31 = bf16[2048,2048]{0,1:T(8,128)(2,1)} copy(bf16[2048,2048]{1,0:T(8,128)(2,1)} %constant_dynamic-update-slice_fusion.5) | data formatting | bytes 16777216 | tf_op jit(solution)/shard_map/concatenate | solution.py:748
  659.7 4.8 constant_dynamic-update-slice_fusion.16
  664.5 3.5 copy-done.3
  668.0 40.0 %plane_sum.1 = f32[256,2048]{1,0:T(8,128)S(1)} custom-call(bf16[8,256,2048]{2,1,0:T(8,128)(2,1)S(1)} %bitcast.64), custom_call_target="tpu_custom_call" | custom-call | tf_op jit(solution)/shard_map/plane_sum/pallas_call | solution.py:715
  711.2 6.2 fusion.18.grad_ref
  717.5 12.1 %attend_back.1 = (bf16[256,2048]{1,0:T(8,128)(2,1)S(1)}, bf16[1024,256]{1,0:T(8,128)(2,1)S(1)}) custom-call(s32[1]{0:T(128)} %bitcast.at_ref, bf16[256,2304]{1,0:T(8,128)(2,1)S(1)} %copy-done.9, bf16[1024,256]{1,0:T(8,128)(2,1)S(1)} %bitcast.70, bf16[1024,256]{1,0:T(8,128)(2,1)S(1)} %bitcast.71, bf16[256,2048]{1,0:T(8,128)(2,1)S(1)} %fusion.18.grad_ref, ...), custom_call_target="tpu_custom_call" | custom-call | flops 5368709120 | bytes 5242880 | tf_op jit(solution)/shard_map/attend_back/pallas_call | solution.py:231
  731.4 39.8 %exchange.14 = (bf16[4,256,256]{2,1,0:T(8,128)(2,1)}, bf16[8,256,256]{2,1,0:T(8,128)(2,1)}, bf16[8,256,256]{2,1,0:T(8,128)(2,1)}) custom-call(bf16[1024,256]{1,0:T(8,128)(2,1)} %copy-done.16, bf16[256,2048]{1,0:T(8,128)(2,1)} %copy-done.11, bf16[256,2048]{1,0:T(8,128)(2,1)} %copy-done.36), custom_call_target="tpu_custom_call" | custom-call | tf_op jit(solution)/shard_map/exchange/pallas_call | solution.py:595
  772.4 8.2 fusion.29
  781.1 17.5 %exchange.15 = (bf16[8,256,256]{2,1,0:T(8,128)(2,1)}, f32[8,2,2048]{2,1,0:T(2,128)}) custom-call(bf16[256,256]{1,0:T(8,128)(2,1)} %copy-done.40, f32[2,2048]{1,0:T(2,128)} %pad_maximum_fusion.4.refs_1_), custom_call_target="tpu_custom_call" | custom-call | tf_op jit(solution)/shard_map/exchange/pallas_call | solution.py:595
  800.7 2.9 gather_fusion.1
  803.6 2.9 gather_fusion.2
  807.2 6.2 convolution_convert_fusion.6
  813.4 5.9 convolution_convert_fusion.5
  822.0 68.8 %exchange.16 = (bf16[4,512,512]{2,1,0:T(8,128)(2,1)}, bf16[4,64,256]{2,1,0:T(8,128)(2,1)}, f32[4,2,2048]{2,1,0:T(2,128)}, bf16[8,512,768]{2,1,0:T(8,128)(2,1)}, bf16[8,512,768]{2,1,0:T(8,128)(2,1)}) custom-call(bf16[2048,512]{1,0:T(8,128)(2,1)} %pad_maximum_fusion.1.refs_0_, bf16[256,256]{1,0:T(8,128)(2,1)} %convolution_convert_fusion.7.refs_1_, ...), custom_call_target="tpu_custom_call" | custom-call | tf_op jit(solution)/shard_map/exchange/pallas_call | solution.py:595
  890.8 2.9 reduce_sum.115.refs_1_
  896.0 4.3 fusion.27
  901.0 73.9 %exchange.17 = (bf16[8,512,768]{2,1,0:T(8,128)(2,1)}, bf16[8,512,512]{2,1,0:T(8,128)(2,1)}, bf16[8,64,256]{2,1,0:T(8,128)(2,1)}) custom-call(bf16[512,768]{1,0:T(8,128)(2,1)} %reduce-scatter.9.cloned.1.call-done.refs_0_, bf16[512,512]{1,0:T(8,128)(2,1)} %reduce_sum.115.refs_1_, bf16[64,256]{1,0:T(8,128)(2,1)} %reduce_sum.117.refs_2_), custom_call_target="tpu_custom_call" | custom-call | tf_op jit(solution)/shard_map/exchange/pallas_call | solution.py:595
  977.4 2.6 copy-done.5
  980.0 2.6 copy-done.6
  985.9 28.4 %adam.1 = (f32[21,512,128]{2,1,0:T(8,128)}, f32[21,512,128]{2,1,0:T(8,128)}, f32[21,512,128]{2,1,0:T(8,128)}) custom-call(s32[6,21]{1,0:T(8,128)S(1)} %stack.39.at_ref, bf16[8,512,768]{2,1,0:T(8,128)(2,1)} %get-tuple-element.89.gate_ref, bf16[8,512,768]{2,1,0:T(8,128)(2,1)} %get-tuple-element.93.up_ref, bf16[8,512,768]{2,1,0:T(8,128)(2,1)} %get-tuple-element.94.down_ref, ...), custom_call_target="tpu_custom_call" | custom-call | flops 3523215360 | bytes 55050240 | tf_op jit(solution)/shard_map/adam/pallas_call | solution.py:334
  (210 shorter events, 68.9 us)
Async XLA Ops:
  7.2 441.6 %all-gather.7.cloned.1.call-start = ((), (), s32[]{:S(2)}) async-start(), calls=%async_computation.9 | async-start | bytes 5898240 | tf_op jit(solution)/shard_map/all_gather | solution.py:828
  212.7 89.3 %copy-start.26 = (bf16[256,2048]{1,0:T(8,128)(2,1)S(1)}, bf16[256,2048]{1,0:T(8,128)(2,1)}, u32[]{:S(2)}) copy-start(bf16[256,2048]{1,0:T(8,128)(2,1)} %param.14) | copy-start | bytes 3145732
  212.7 90.1 %copy-start.50 = (f32[2,2048]{1,0:T(2,128)S(1)}, f32[2,2048]{1,0:T(2,128)}, u32[]{:S(2)}) copy-start(f32[2,2048]{1,0:T(2,128)} %param.24) | copy-start | bytes 49156
  212.8 236.0 %all-gather.5.cloned.1.call-start = ((), (), s32[]{:S(2)}) async-start(), calls=%async_computation.8 | async-start | bytes 5898240 | tf_op jit(solution)/shard_map/all_gather | solution.py:822
  213.5 608.5 %reduce-scatter.7.cloned.1.call-start = ((), (), s32[]{:S(2)}) async-start(), calls=%async_computation.5 | async-start | bytes 3932160 | tf_op jit(solution)/shard_map/reduce_scatter | solution.py:904
  302.0 13.5 %copy-start.12 = (f32[256,128]{1,0:T(8,128)}, f32[256,128]{1,0:T(8,128)S(1)}, u32[]{:S(2)}) copy-start(f32[256,128]{1,0:T(8,128)S(1)} %get-tuple-element.154.sine_ref) | copy-start | bytes 393220
  302.0 13.5 %copy-start.14 = (f32[256,128]{1,0:T(8,128)}, f32[256,128]{1,0:T(8,128)S(1)}, u32[]{:S(2)}) copy-start(f32[256,128]{1,0:T(8,128)S(1)} %get-tuple-element.155.cosine_ref) | copy-start | bytes 393220
  302.9 69.4 %copy-start.44 = (f32[1,2048]{1,0:T(1,128)}, f32[1,2048]{1,0:T(1,128)S(1)}, u32[]{:S(2)}) copy-start(f32[1,2048]{1,0:T(1,128)S(1)} %get-tuple-element.138) | copy-start | bytes 24580
  303.2 12.2 %copy-start.1 = (bf16[256,2048]{1,0:T(8,128)(2,1)}, bf16[256,2048]{1,0:T(8,128)(2,1)S(1)}, u32[]{:S(2)}) copy-start(bf16[256,2048]{1,0:T(8,128)(2,1)S(1)} %fusion.23.x_ref) | copy-start | bytes 3145732
  309.7 45.7 %copy-start.18 = (s32[256]{0:T(256)S(1)}, s32[256]{0:T(256)}, u32[]{:S(2)}) copy-start(s32[256]{0:T(256)} %param.16) | copy-start | bytes 3076
  315.5 50.0 %copy-start.8 = (bf16[256,2304]{1,0:T(8,128)(2,1)}, bf16[256,2304]{1,0:T(8,128)(2,1)S(1)}, u32[]{:S(2)}) copy-start(bf16[256,2304]{1,0:T(8,128)(2,1)S(1)} %project.1.q_ref) | copy-start | bytes 3538948
  372.3 84.6 %copy-start.54 = (f32[256]{0:T(256)}, f32[256]{0:T(256)S(1)}, u32[]{:S(2)}) copy-start(f32[256]{0:T(256)S(1)} %get-tuple-element.146) | copy-start | bytes 3076
  474.7 6.4 copy-start.25
  474.7 9.1 copy-start.60
  533.4 19.5 %copy-start.38 = (bf16[2048,768]{0,1:T(8,128)(2,1)S(1)}, bf16[2048,768]{0,1:T(8,128)(2,1)}, u32[]{:S(2)}) copy-start(bf16[2048,768]{0,1:T(8,128)(2,1)} %copy-done.37) | copy-start | bytes 9437188
  552.9 11.1 %copy-start.2 = (bf16[256,2048]{1,0:T(8,128)(2,1)S(1)}, bf16[256,2048]{1,0:T(8,128)(2,1)}, u32[]{:S(2)}) copy-start(bf16[256,2048]{1,0:T(8,128)(2,1)} %copy-done.1) | copy-start | bytes 3145732
  564.0 258.0 %reduce-scatter.5.cloned.1.call-start = ((), (), s32[]{:S(2)}) async-start(), calls=%async_computation.4 | async-start | bytes 3932160 | tf_op jit(solution)/shard_map/reduce_scatter | solution.py:889
  564.0 26.2 %collective-permute-start = (bf16[256,2048]{1,0:T(8,128)(2,1)S(1)}, bf16[256,2048]{1,0:T(8,128)(2,1)}, u32[]{:S(2)}, u32[]{:S(2)}) collective-permute-start(bf16[256,2048]{1,0:T(8,128)(2,1)S(1)} %copy-done.2), channel_id=1, source_target_pairs={{0,8},{4,12},{8,0},{12,4},{16,24},{20,28},{24,16},{28,20},{1,9},{5... | collective-permute-start | bytes 3145736 | tf_op jit(solution)/shard_map/ppermute | solution.py:743
  565.3 27.2 %collective-permute-start.1 = (bf16[256,2048]{1,0:T(8,128)(2,1)S(1)}, bf16[256,2048]{1,0:T(8,128)(2,1)}, u32[]{:S(2)}, u32[]{:S(2)}) collective-permute-start(bf16[256,2048]{1,0:T(8,128)(2,1)S(1)} %copy-done.2), channel_id=1, source_target_pairs={{0,16},{4,20},{8,24},{12,28},{16,0},{20,4},{24,8},{28,12},{1,17},{... | collective-permute-start | bytes 3145736 | tf_op jit(solution)/shard_map/ppermute | solution.py:743
  566.2 46.5 %collective-permute-start.5 = (bf16[256,2048]{1,0:T(8,128)(2,1)S(1)}, bf16[256,2048]{1,0:T(8,128)(2,1)}, u32[]{:S(2)}, u32[]{:S(2)}) collective-permute-start(bf16[256,2048]{1,0:T(8,128)(2,1)S(1)} %get-tuple-element.75), channel_id=1, source_target_pairs={{0,8},{4,12},{8,0},{12,4},{16,24},{20,28},{24,16},{28,20},{1,9},{5... | collective-permute-start | bytes 3145736 | tf_op jit(solution)/shard_map/ppermute | solution.py:743
  567.4 47.7 %collective-permute-start.6 = (bf16[256,2048]{1,0:T(8,128)(2,1)S(1)}, bf16[256,2048]{1,0:T(8,128)(2,1)}, u32[]{:S(2)}, u32[]{:S(2)}) collective-permute-start(bf16[256,2048]{1,0:T(8,128)(2,1)S(1)} %get-tuple-element.75), channel_id=1, source_target_pairs={{0,16},{4,20},{8,24},{12,28},{16,0},{20,4},{24,8},{28,12},{1,17},{... | collective-permute-start | bytes 3145736 | tf_op jit(solution)/shard_map/ppermute | solution.py:743
  569.8 323.9 %reduce-scatter.9.cloned.1.call-start = ((), (), s32[]{:S(2)}) async-start(), calls=%async_computation.6 | async-start | bytes 3932160 | tf_op jit(solution)/shard_map/reduce_scatter | solution.py:905
  591.3 33.8 %collective-permute-start.2 = (bf16[128,2048]{1,0:T(8,128)(2,1)S(1)}, bf16[128,2048]{1,0:T(8,128)(2,1)S(1)}, u32[]{:S(2)}, u32[]{:S(2)}) collective-permute-start(bf16[128,2048]{1,0:T(8,128)(2,1)S(1)} %slice.71), channel_id=1, source_target_pairs={{0,16},{4,20},{8,24},{12,28},{16,0},{20,4},{24,8},{28,12},{1,17},{... | collective-permute-start | bytes 1572872 | tf_op jit(solution)/shard_map/ppermute | solution.py:743
  593.7 32.5 %collective-permute-start.3 = (bf16[128,2048]{1,0:T(8,128)(2,1)S(1)}, bf16[128,2048]{1,0:T(8,128)(2,1)S(1)}, u32[]{:S(2)}, u32[]{:S(2)}) collective-permute-start(bf16[128,2048]{1,0:T(8,128)(2,1)S(1)} %slice.72), channel_id=1, source_target_pairs={{0,8},{4,12},{8,0},{12,4},{16,24},{20,28},{24,16},{28,20},{1,9},{5... | collective-permute-start | bytes 1572872 | tf_op jit(solution)/shard_map/ppermute | solution.py:743
  613.8 21.7 %collective-permute-start.7 = (bf16[128,2048]{1,0:T(8,128)(2,1)S(1)}, bf16[128,2048]{1,0:T(8,128)(2,1)S(1)}, u32[]{:S(2)}, u32[]{:S(2)}) collective-permute-start(bf16[128,2048]{1,0:T(8,128)(2,1)S(1)} %slice.77), channel_id=1, source_target_pairs={{0,16},{4,20},{8,24},{12,28},{16,0},{20,4},{24,8},{28,12},{1,17},{... | collective-permute-start | bytes 1572872 | tf_op jit(solution)/shard_map/ppermute | solution.py:743
  616.1 20.2 %collective-permute-start.8 = (bf16[128,2048]{1,0:T(8,128)(2,1)S(1)}, bf16[128,2048]{1,0:T(8,128)(2,1)S(1)}, u32[]{:S(2)}, u32[]{:S(2)}) collective-permute-start(bf16[128,2048]{1,0:T(8,128)(2,1)S(1)} %slice.78), channel_id=1, source_target_pairs={{0,8},{4,12},{8,0},{12,4},{16,24},{20,28},{24,16},{28,20},{1,9},{5... | collective-permute-start | bytes 1572872 | tf_op jit(solution)/shard_map/ppermute | solution.py:743
  626.2 14.3 %copy-start.29 = (f32[1024,64]{1,0:T(8,128)S(1)}, f32[1024,64]{1,0:T(8,128)}, u32[]{:S(2)}) copy-start(f32[1024,64]{1,0:T(8,128)} %copy-done.28) | copy-start | bytes 786436
  626.2 14.3 %copy-start.31 = (f32[1024,64]{1,0:T(8,128)S(1)}, f32[1024,64]{1,0:T(8,128)}, u32[]{:S(2)}) copy-start(f32[1024,64]{1,0:T(8,128)} %copy-done.30) | copy-start | bytes 786436
  626.2 14.3 %copy-start.33 = (f32[1024,64]{1,0:T(8,128)S(1)}, f32[1024,64]{1,0:T(8,128)}, u32[]{:S(2)}) copy-start(f32[1024,64]{1,0:T(8,128)} %copy-done.32) | copy-start | bytes 786436
  627.3 13.6 %collective-permute-start.4 = (bf16[1024,2048]{1,0:T(8,128)(2,1)}, bf16[1024,2048]{1,0:T(8,128)(2,1)}, u32[]{:S(2)}, u32[]{:S(2)}) collective-permute-start(bf16[1024,2048]{1,0:T(8,128)(2,1)} %get-tuple-element.130), channel_id=1, source_target_pairs={{0,4},{4,0},{8,12},{12,8},{16,20},{20,16},{24,28},{28,24},{1,5},{5... | collective-permute-start | bytes 12582920 | tf_op jit(solution)/shard_map/ppermute | solution.py:743
  640.5 19.3 %collective-permute-start.9 = (bf16[1024,2048]{1,0:T(8,128)(2,1)}, bf16[1024,2048]{1,0:T(8,128)(2,1)}, u32[]{:S(2)}, u32[]{:S(2)}) collective-permute-start(bf16[1024,2048]{1,0:T(8,128)(2,1)} %get-tuple-element.134), channel_id=1, source_target_pairs={{0,4},{4,0},{8,12},{12,8},{16,20},{20,16},{24,28},{28,24},{1,5},{5... | collective-permute-start | bytes 12582920 | tf_op jit(solution)/shard_map/ppermute | solution.py:743
  657.4 357.6 %reduce-scatter.11.cloned.1.call-start = ((), (), s32[]{:S(2)}) async-start(), calls=%async_computation.7 | async-start | bytes 9437184 | tf_op jit(solution)/shard_map/reduce_scatter | solution.py:987
  668.0 40.0 %copy-start.23 = (f32[256,2048]{1,0:T(8,128)S(1)}, f32[256,2048]{1,0:T(8,128)}, u32[]{:S(2)}) copy-start(f32[256,2048]{1,0:T(8,128)} %copy-done.22) | copy-start | bytes 6291460
  668.0 40.0 %copy-start.45 = (f32[1,2048]{1,0:T(1,128)S(1)}, f32[1,2048]{1,0:T(1,128)}, u32[]{:S(2)}) copy-start(f32[1,2048]{1,0:T(1,128)} %copy-done.44) | copy-start | bytes 24580
  668.0 40.0 %copy-start.55 = (f32[256]{0:T(256)S(1)}, f32[256]{0:T(256)}, u32[]{:S(2)}) copy-start(f32[256]{0:T(256)} %copy-done.54) | copy-start | bytes 3076
  717.5 54.9 %copy-start.27 = (bf16[256,2048]{1,0:T(8,128)(2,1)S(1)}, bf16[256,2048]{1,0:T(8,128)(2,1)}, u32[]{:S(2)}) copy-start(bf16[256,2048]{1,0:T(8,128)(2,1)} %param.14) | copy-start | bytes 3145732
  717.5 54.9 %copy-start.47 = (f32[1,2048]{1,0:T(1,128)S(1)}, f32[1,2048]{1,0:T(1,128)}, u32[]{:S(2)}) copy-start(f32[1,2048]{1,0:T(1,128)} %copy-done.46) | copy-start | bytes 24580
  717.5 54.9 %copy-start.57 = (f32[256]{0:T(256)S(1)}, f32[256]{0:T(256)}, u32[]{:S(2)}) copy-start(f32[256]{0:T(256)} %copy-done.56) | copy-start | bytes 3076
  772.4 8.2 copy-start.40
  798.7 7.9 copy-start.43
  893.7 6.6 copy-start.42
  893.7 7.2 copy-start.49
  896.0 78.8 %copy-start.10 = (f32[21,128,128]{2,1,0:T(8,128)S(1)}, f32[21,128,128]{2,1,0:T(8,128)}, u32[]{:S(2)}) copy-start(f32[21,128,128]{2,1,0:T(8,128)} %right_ref.1) | copy-start | bytes 4128772
  901.0 113.4 %copy-start.48 = (f32[2,2048]{1,0:T(2,128)}, f32[2,2048]{1,0:T(2,128)S(1)}, u32[]{:S(2)}) copy-start(f32[2,2048]{1,0:T(2,128)S(1)} %reduce_sum.118) | copy-start | bytes 49156
  985.9 28.5 %copy-start.51 = (f32[2,2048]{1,0:T(2,128)S(1)}, f32[2,2048]{1,0:T(2,128)}, u32[]{:S(2)}) copy-start(f32[2,2048]{1,0:T(2,128)} %param.24) | copy-start | bytes 49156
  985.9 28.5 %copy-start.52 = (f32[2,2048]{1,0:T(2,128)S(1)}, f32[2,2048]{1,0:T(2,128)}, u32[]{:S(2)}) copy-start(f32[2,2048]{1,0:T(2,128)} %param.25) | copy-start | bytes 49156
  985.9 28.5 %copy-start.53 = (f32[2,2048]{1,0:T(2,128)S(1)}, f32[2,2048]{1,0:T(2,128)}, u32[]{:S(2)}) copy-start(f32[2,2048]{1,0:T(2,128)} %param.26) | copy-start | bytes 49156
  985.9 29.1 %copy-start.24 = (f32[256,2048]{1,0:T(8,128)S(1)}, f32[256,2048]{1,0:T(8,128)}, u32[]{:S(2)}) copy-start(f32[256,2048]{1,0:T(8,128)} %copy-done.22) | copy-start | bytes 6291460
  (29 other events, 80.2 us)
Sparse Core Ops, SparseCore 0:
  212.9 104.8 all-gather.6
  319.9 95.8 all-gather.4
  564.1 62.5 reduce-scatter.6
  628.9 60.2 reduce-scatter.4
  691.3 60.2 reduce-scatter.8
  893.8 92.2 reduce-scatter.10

commit v4 on v3

--- a/solution.py
+++ b/solution.py
@@ -67,6 +67,9 @@
     return lax.dot_general(
         left_side, right_side, (((0,), (0,)), ((), ())), preferred_element_type=jnp.float32
     )
+
+
+SMALL_COST = pl.CostEstimate(flops=1, bytes_accessed=1, transcendentals=0)
 
 
 def project_kernel(x_ref, w_ref, cosine_ref, sine_ref, out_ref):
@@ -92,12 +95,8 @@
         ],
         out_specs=pl.BlockSpec((rows, 2 * HD), lambda j: (0, j)),
         out_shape=jax.ShapeDtypeStruct((rows, steps * 2 * HD), jnp.bfloat16),
-        compiler_params=pltpu.CompilerParams(vmem_limit_bytes=32 * 2**20),
-        cost_estimate=pl.CostEstimate(
-            flops=4 * rows * width * steps * HD,
-            bytes_accessed=4 * width * steps * HD,
-            transcendentals=0,
-        ),
+        compiler_params=pltpu.CompilerParams(vmem_limit_bytes=56 * 2**20),
+        cost_estimate=SMALL_COST,
         name="project",
     )(normed, weights, *tables)
 
@@ -216,11 +215,7 @@
             jax.ShapeDtypeStruct((NH, 1, rows), jnp.float32),
         ),
         compiler_params=pltpu.CompilerParams(vmem_limit_bytes=32 * 2**20),
-        cost_estimate=pl.CostEstimate(
-            flops=4 * rows * SEQLEN * columns,
-            bytes_accessed=6 * rows * columns,
-            transcendentals=rows * SEQLEN * NH,
-        ),
+        cost_estimate=SMALL_COST,
         name="attend",
     )(at, projected, pairs, pairs, key_segs[:, None], query_segs[None, :])
 
@@ -243,16 +238,81 @@
         ),
         scratch_shapes=[pltpu.VMEM((SEQLEN, HD), jnp.float32)] * 2,
         compiler_params=pltpu.CompilerParams(vmem_limit_bytes=32 * 2**20),
-        cost_estimate=pl.CostEstimate(
-            flops=10 * rows * SEQLEN * columns,
-            bytes_accessed=10 * rows * columns,
-            transcendentals=rows * SEQLEN * NH,
-        ),
+        cost_estimate=SMALL_COST,
         name="attend_back",
     )(
         at, projected, pairs, pairs, grads, totals, key_segs[:, None], query_segs[None, :],
         *key_tables, *tables,
     )
+
+
+def feed_kernel(
+    real_ref, x_ref, cot_ref, *refs
+):
+    parts, refs = refs[:-7], refs[-7:]
+    act_ref, gate_grad_ref, up_grad_ref, two_ref, out_ref, weights, sems = refs
+    cols = act_ref.shape[1]
+    count, rows, _ = parts[0].shape
+    halves = len(parts)
+
+    @pl.when(pl.program_id(0) == 0)
+    def _():
+        copies = [
+            pltpu.make_async_copy(
+                parts[half].at[block],
+                weights.at[pl.ds((block * halves + half) * rows, rows)],
+                sems.at[block * halves + half],
+            )
+            for half in range(halves)
+            for block in range(count)
+        ]
+        for copy in copies:
+            copy.start()
+        for copy in copies:
+            copy.wait()
+
+    low = jnp.bfloat16
+    wide = jnp.float32
+    gate = jnp.dot(x_ref[...], weights[:, :cols], preferred_element_type=wide)
+    upper = jnp.dot(x_ref[...], weights[:, cols : 2 * cols], preferred_element_type=wide)
+    act_grad = jnp.dot(cot_ref[...], weights[:, 2 * cols :], preferred_element_type=wide)
+    real = lax.broadcasted_iota(jnp.int32, gate.shape, 1) < real_ref[0]
+    sigmoid = 1.0 / (1.0 + jnp.exp(-gate))
+    silu = gate * sigmoid
+    activated = jnp.where(real, silu * upper, 0.0).astype(low)
+    act_grad = jnp.where(real, act_grad, 0.0)
+    gate_grad = (act_grad * upper * sigmoid * (1.0 + gate * (1.0 - sigmoid))).astype(low)
+    up_grad = (act_grad * silu).astype(low)
+    act_ref[...], gate_grad_ref[...], up_grad_ref[...] = activated, gate_grad, up_grad
+    two = dot_last(gate_grad, weights[:, :cols]) + dot_last(up_grad, weights[:, cols : 2 * cols])
+    two_ref[...] = two.astype(low)
+    out_ref[...] = dot_last(activated, weights[:, 2 * cols :]).astype(low)
+
+
+def feed_forward(real_cols, x, cot, parts, seq_count):
+    tokens_all, width = x.shape
+    _, rows, cols = parts[0].shape
+    cols = cols // 3
+    step = 256
+    low = jnp.bfloat16
+    block = pl.BlockSpec((step, width), lambda i: (i, 0))
+    narrow = pl.BlockSpec((step, cols), lambda i: (i, 0))
+    return pl.pallas_call(
+        feed_kernel,
+        grid=(tokens_all // step,),
+        in_specs=[pl.BlockSpec(memory_space=pltpu.SMEM), block, block]
+        + [pl.BlockSpec(memory_space=pl.ANY)] * len(parts),
+        out_specs=[narrow, narrow, narrow, block, block],
+        out_shape=[jax.ShapeDtypeStruct((tokens_all, cols), low)] * 3
+        + [jax.ShapeDtypeStruct((tokens_all, width), low)] * 2,
+        scratch_shapes=[
+            pltpu.VMEM((width, 3 * cols), low),
+            pltpu.SemaphoreType.DMA((len(parts) * seq_count,)),
+        ],
+        compiler_params=pltpu.CompilerParams(vmem_limit_bytes=52 * 2**20),
+        cost_estimate=SMALL_COST,
+        name="feed_forward",
+    )(real_cols, x, cot, *parts)
 
 
 def pick_kernel(rows, feed_ref, attn_ref, tiles_ref, feed_out, attn_out, sems):
@@ -285,15 +345,13 @@
     return pl.pallas_call(
         functools.partial(pick_kernel, share),
         in_specs=[pl.BlockSpec(memory_space=pltpu.SMEM)] * 2 + [pl.BlockSpec(memory_space=pl.ANY)],
-        out_specs=[pl.BlockSpec(memory_space=pl.ANY)] * 2,
+        out_specs=[pl.BlockSpec(memory_space=pltpu.VMEM)] * 2,
         out_shape=[
             jax.ShapeDtypeStruct((rows, feed * width), tiles.dtype),
             jax.ShapeDtypeStruct((share, attn * width), tiles.dtype),
         ],
         scratch_shapes=[pltpu.SemaphoreType.DMA((feed + attn,))],
-        cost_estimate=pl.CostEstimate(
-            flops=0, bytes_accessed=4 * (rows * feed + share * attn) * width, transcendentals=0
-        ),
+        cost_estimate=SMALL_COST,
         name="pick",
     )(feed_slots, attn_slots, tiles)
 
@@ -352,12 +410,8 @@
             scratch_shapes=[pltpu.VMEM((rows, width), jnp.bfloat16)],
         ),
         out_shape=[shape] * 3,
-        compiler_params=pltpu.CompilerParams(vmem_limit_bytes=32 * 2**20),
-        cost_estimate=pl.CostEstimate(
-            flops=4 * slots * rows * width * (rows + width),
-            bytes_accessed=4 * slots * rows * (rows + 6 * width),
-            transcendentals=slots * rows * width,
-        ),
+        compiler_params=pltpu.CompilerParams(vmem_limit_bytes=60 * 2**20),
+        cost_estimate=SMALL_COST,
         name="adam",
     )(at, gate, up, down, shares, pairs, left, right, master, one, two)
 
@@ -599,6 +653,7 @@
         out_shape=shapes,
         scratch_shapes=scratch,
         compiler_params=pltpu.CompilerParams(collective_id=number, has_side_effects=True),
+        cost_estimate=SMALL_COST,
         name="exchange",
     )(*arrays)
 
@@ -730,29 +785,9 @@
         compiler_params=pltpu.CompilerParams(
             collective_id=number, has_side_effects=True, vmem_limit_bytes=40 * 2**20
         ),
+        cost_estimate=SMALL_COST,
         name="plane_sum",
     )(part.reshape(count, rows, columns))
-
-
-def behind_gather(array):
-    if lax.axis_size("grp") != 8:
-        return lax.all_gather(array, "grp", axis=0, tiled=True)
-    half = array.shape[0] // 2
-
-    def via(values, bit):
-        return lax.ppermute(values, "grp", [(at, at ^ bit) for at in range(8)])
-
-    from_x, from_y = via(array, 2), via(array, 4)
-    across = jnp.concatenate([via(from_x[:half], 4), via(from_y[half:], 2)], axis=0)
-    chip = jnp.concatenate([array, from_x, from_y, across], axis=0)
-    return jnp.concatenate([chip, via(chip, 1)], axis=0)
-
-
-def behind_order():
-    grp = lax.axis_index("grp")
-    if lax.axis_size("grp") != 8:
-        return jnp.arange(lax.axis_size("grp"), dtype=jnp.int32)
-    return jnp.bitwise_xor(grp, jnp.array([0, 2, 4, 6, 1, 3, 5, 7], jnp.int32))
 
 
 def local(
@@ -793,7 +828,6 @@
     tables = [lax.dynamic_slice_in_dim(table, first_place, rows_here) for table in key_tables]
 
     hidden_ids = grp_here * share + jnp.arange(share, dtype=jnp.int32)
-    real = jnp.repeat(hidden_ids < hidden_tiles, tile_width)[None, :]
     hidden_ids = jnp.minimum(hidden_ids, hidden_tiles - 1)
     feed_ids = (
         attn_tiles
@@ -801,6 +835,10 @@
         + hidden_ids[None, :]
     ).reshape(-1)
     feed_slots, attn_slots = tile_owner_slots[feed_ids], tile_owner_slots[:attn_tiles]
+
+    tok_float = tokens.astype(jnp.float32)
+    inverse_one = lax.rsqrt(jnp.mean(tok_float * tok_float, axis=-1, keepdims=True) + NORM_EPS)
+    normed = (tok_float * inverse_one * gains[0]).astype(jnp.bfloat16)
 
     def weight_half(at):
         return gather_plane(
@@ -826,30 +864,34 @@
         )
         feed_rows, attn_rows = pick(tiles.reshape(flat), feed_slots, attn_slots)
         feed_parts.append(lax.all_gather(feed_rows, "seq", axis=0, tiled=False))
-        attn_weights, _ = exchange(
+        attn_weights, _, normed_plane = exchange(
             2,
-            [(attn_half(0), attn_first), gather_axis("seq", attn_rows), (attn_half(1), 1, 0)],
+            [
+                (attn_half(0), attn_first),
+                gather_axis("seq", attn_rows),
+                (attn_half(1), 1, 0),
+                (gather_plane(normed.shape), normed),
+            ],
         )
-        feed_weights = jnp.zeros((seq_count, 2, half_block, 3 * share_cols), jnp.bfloat16)
-        for at in range(2):
-            feed_weights = lax.dynamic_update_slice(
-                feed_weights, feed_parts[at][:, None], (0, at, 0, 0)
-            )
     else:
-        _, attn_weights = exchange(2, [gather_axis("seq", attn_rows), (attn_half(0), 0)])
-        feed_weights = feed_parts[0]
+        _, attn_weights, normed_plane = exchange(
+            2,
+            [
+                gather_axis("seq", attn_rows),
+                (attn_half(0), 0),
+                (gather_plane(normed.shape), normed),
+            ],
+        )
+    attn_weights, feed_parts[0] = lax.optimization_barrier((attn_weights, feed_parts[0]))
     attn_weights = attn_weights.reshape(MODEL_WIDTH, output_end)
-    feed_weights = feed_weights.reshape(MODEL_WIDTH, 3 * share_cols)
-
-    tok_float = tokens.astype(jnp.float32)
-    inverse_one = lax.rsqrt(jnp.mean(tok_float * tok_float, axis=-1, keepdims=True) + NORM_EPS)
-    normed = (tok_float * inverse_one * gains[0]).astype(jnp.bfloat16)
+
     projected = project(normed, attn_weights, tables)
-    pairs, segments = exchange(
+    pairs, segments, cot_plane = exchange(
         3,
         [
             gather_axis("seq", projected[:, query_cols:]),
             gather_axis("seq", segment_ids.reshape(-1, tile_width)),
+            (gather_plane(cotangent.shape), cotangent),
         ],
     )
     first_key = seq_here * rows_here - first_place
@@ -864,40 +906,18 @@
     inverse_two = lax.rsqrt(jnp.mean(hidden * hidden, axis=-1, keepdims=True) + NORM_EPS)
     normed_two = (hidden * inverse_two * gains[1]).astype(jnp.bfloat16)
 
-    second_plane, cot_plane = exchange(
-        4,
-        [
-            (gather_plane(normed_two.shape), normed_two),
-            (gather_plane(cotangent.shape), cotangent),
-        ],
-    )
+    (second_plane,) = exchange(4, [(gather_plane(normed_two.shape), normed_two)])
     second_plane = second_plane.reshape(-1, MODEL_WIDTH)
     cot_plane = cot_plane.reshape(-1, MODEL_WIDTH)
-    second_plane, normed, context_late = lax.optimization_barrier((second_plane, normed, context))
-    normed_plane = behind_gather(normed)
-    context_plane = behind_gather(context_late)
-    gating_weights = feed_weights[:, : 2 * share_cols]
-    down_weights = feed_weights[:, 2 * share_cols :]
-    gate_up = jnp.dot(second_plane, gating_weights, preferred_element_type=jnp.float32)
-    gate = gate_up[:, :share_cols]
-    upper = gate_up[:, share_cols:]
-    sigmoid_gate = jax.nn.sigmoid(gate)
-    silu_gate = gate * sigmoid_gate
-    activated = jnp.where(real, silu_gate * upper, 0.0).astype(jnp.bfloat16)
+    real_cols = jnp.clip((hidden_tiles - grp_here * share) * tile_width, 0, share_cols)
+    activated, gate_grad, up_grad, two_part, feed_part = feed_forward(
+        real_cols.reshape(1), second_plane, cot_plane, feed_parts, seq_count
+    )
     down_grad = contract(cot_plane, activated).astype(jnp.bfloat16)
-    down_grad, cot_plane = lax.optimization_barrier((down_grad, cot_plane))
+    down_grad, gate_grad, up_grad = lax.optimization_barrier((down_grad, gate_grad, up_grad))
     down_grad = lax.psum_scatter(down_grad, "seq", scatter_dimension=0, tiled=True)
-    act_grad = jnp.dot(cot_plane, down_weights, preferred_element_type=jnp.float32)
-    act_grad = jnp.where(real, act_grad, 0.0)
-    gate_grad = (act_grad * upper * sigmoid_gate * (1.0 + gate * (1.0 - sigmoid_gate))).astype(
-        jnp.bfloat16
-    )
-    up_grad = (act_grad * silu_gate).astype(jnp.bfloat16)
     gate_weight_grad = contract(second_plane, gate_grad).astype(jnp.bfloat16)
     up_weight_grad = contract(second_plane, up_grad).astype(jnp.bfloat16)
-    gating_grad = jnp.concatenate([gate_grad, up_grad], axis=1)
-    two_part = times_transpose(gating_grad, gating_weights).astype(jnp.bfloat16)
-    feed_part = times_transpose(activated, down_weights).astype(jnp.bfloat16)
     two_part, feed_part, gate_weight_grad, up_weight_grad = lax.optimization_barrier(
         (two_part, feed_part, gate_weight_grad, up_weight_grad)
     )
@@ -916,6 +936,7 @@
     )
     branch_grad = hidden_grad.astype(jnp.bfloat16)
     context_grad = times_transpose(branch_grad, attn_weights[:, value_end:]).astype(jnp.bfloat16)
+    context_grad, down_grad = lax.optimization_barrier((context_grad, down_grad))
     query_grad, pair_part = attend_back(
         at,
         projected,
@@ -931,15 +952,17 @@
         pair_part = lax.dynamic_update_slice_in_dim(
             jnp.zeros((seq_count * rows_here, 2 * HD), pair_part.dtype), pair_part, first_key, 0
         )
-    pair_parts, query_share, branch_share = exchange(
+    pair_parts, query_share, branch_share, context_plane = exchange(
         6,
         [
             split_rows("seq", pair_part),
             split_columns("grp", query_grad),
             split_columns("grp", branch_grad),
+            (gather_plane(context.shape), context),
         ],
     )
     pair_grad = jnp.sum(pair_parts.astype(jnp.float32), axis=0).astype(jnp.bfloat16)
+    pair_grad, gate_weight_grad = lax.optimization_barrier((pair_grad, gate_weight_grad))
     projected_grad = jnp.concatenate([query_grad, pair_grad], axis=1)
     norm_one_grad = times_transpose(projected_grad, attn_weights[:, :value_end])
     gain_one_term = jnp.sum(norm_one_grad * tok_float * inverse_one, axis=0)
@@ -950,50 +973,51 @@
         * inverse_one**3
         * jnp.mean(tok_float * gains[0] * norm_one_grad, axis=-1, keepdims=True)
     )
-    pair_plane, gain_parts = exchange(
-        7,
-        [
-            gather_axis("grp", pair_grad),
-            gather_axis("grp", jnp.stack([gain_one_term, gain_two_term])),
-        ],
-    )
-    gain_plane = jnp.sum(gain_parts, axis=0)
-    order = behind_order()
-    normed_rows = lax.dynamic_slice_in_dim(
-        normed_plane.reshape(-1, seq_count, grp_count, sub_rows), grp_here, 1, axis=2
-    ).reshape(-1, seq_count * sub_rows)
-    query_weight_grad = contract(normed_plane, query_share[order].reshape(-1, share_width))
-    out_weight_grad = contract(context_plane, branch_share[order].reshape(-1, share_width))
-    pair_weight_grad = contract(normed_rows, pair_plane[order].reshape(-1, 2 * HD))
+    normed_plane = normed_plane.reshape(-1, MODEL_WIDTH)
+    context_plane = context_plane.reshape(-1, MODEL_WIDTH)
+    query_weight_grad = contract(normed_plane, query_share.reshape(-1, share_width))
+    out_weight_grad = contract(context_plane, branch_share.reshape(-1, share_width))
+    pair_weight_grad = contract(normed, pair_grad).astype(jnp.bfloat16)
     shares = jnp.concatenate([query_weight_grad, out_weight_grad], axis=1).astype(jnp.bfloat16)
     shares, down_grad, gate_weight_grad = lax.optimization_barrier(
         (shares, down_grad, gate_weight_grad)
     )
     feed_shape = (rows_block, share_cols)
+    pair_task = Exchange(
+        "grp",
+        (grp_count, seq_count, sub_rows, 2 * HD),
+        lambda ref, index: ref.at[:, index],
+        block_of,
+    )
     share_parts, pair_parts, gain_parts, down_plane, gate_plane = exchange(
-        8,
+        7,
         [
             split_rows("seq", shares),
-            split_rows("seq", pair_weight_grad.astype(jnp.bfloat16)),
-            gather_axis("seq", gain_plane),
+            (pair_task, pair_weight_grad.reshape(seq_count, grp_count, sub_rows, 2 * HD)),
+            gather_axis("seq", jnp.stack([gain_one_term, gain_two_term])),
             (gather_plane(feed_shape), down_grad),
             (gather_plane(feed_shape), gate_weight_grad),
         ],
     )
-    gain_grads = jnp.sum(gain_parts, axis=0)
+    gain_seq = jnp.sum(gain_parts, axis=0)
     shares = jnp.sum(share_parts.astype(jnp.float32), axis=0).astype(jnp.bfloat16)
-    pair_rows = jnp.sum(pair_parts.astype(jnp.float32), axis=0).astype(jnp.bfloat16)
+    pair_parts = jnp.sum(pair_parts.astype(jnp.float32), axis=0).astype(jnp.bfloat16)
+    pair_task = Exchange("seq", pair_parts.shape, block_of, block_of)
     shares, up_weight_grad, feed_part = lax.optimization_barrier((shares, up_weight_grad, feed_part))
     feed_out = lax.psum_scatter(feed_part, "grp", scatter_dimension=0, tiled=True)
     block_out = (hidden + feed_out.astype(jnp.float32)).astype(jnp.bfloat16)
-    up_plane, share_plane, pair_plane = exchange(
-        9,
+    _, pair_plane, up_plane, share_plane, gain_parts = exchange(
+        8,
         [
+            (pair_task, pair_parts),
+            (gather_plane(pair_parts.shape), 0),
             (gather_plane(feed_shape), up_weight_grad),
             (gather_plane(shares.shape), shares),
-            (gather_plane(pair_rows.shape), pair_rows),
+            gather_axis("grp", gain_seq),
         ],
     )
+    pair_plane = jnp.sum(pair_plane.astype(jnp.float32), axis=1).astype(jnp.bfloat16)
+    gain_grads = jnp.sum(gain_parts, axis=0)
 
     tile_of_slot = (
         jnp.full((grp_count * slots_here,), tile_count, jnp.int32)

time: 1030 us -> 844 us (0.82)
  local copies, waits for them, and re-layouts: 95.2 us -> 22.5 us
  matrix products: 132 us -> 63.9 us
  waiting for transfers between devices: 43.8 us -> 0.65 us
  Pallas kernels: 694 us -> 706 us
    pallas_call x2, Pallas kernels: 92.9 us -> 7.26 us  [pick(): pl.pallas_call(functools.partial(pick_kernel, share), in_specs=[pl.BlockS...]
    pallas_call x0 -> x1, Pallas kernels: none -> 50.2 us  [feed_forward(): pl.pallas_call(feed_kernel, grid=(tokens_all // step,), in_specs=[pl.Bloc...]
    ppermute x10 -> x0, waiting for transfers between devices: 43 us -> none  [via(): return lax.ppermute(values, 'grp', [(at, at ^ bit) for at in range(8)])]
    pallas_call x9 -> x8, Pallas kernels: 506 us -> 545 us  [exchange(): pl.pallas_call(functools.partial(exchange_kernel, tasks, wires, len(array...]
    unnamed x130 -> x90, local copies, waits for them, and re-layouts: 51.2 us -> 14.8 us
    dot_general x2 -> x0, matrix products: 35.6 us -> none  [the longest x1 17.9 us: local(): jnp.dot(cot_plane, down_weights, preferred_element_type=jnp.float32)]
    dot_general x4 -> x2, matrix products: 44.9 us -> 11.9 us  [times_transpose(): lax.dot_general(left_side, right_side, (((1,), (1,)), ((), ())), preferre...]
    concatenate x5 -> x0, local copies, waits for them, and re-layouts: 23.3 us -> none  [the longest x3 21.3 us: behind_gather(): return jnp.concatenate([chip, via(chip, 1)], axis=0)]
  transfers between devices with their start and end apart: 16 -> 6, of which waited for: 4 -> 0; matrix products, arithmetic and copies ran while one was open for 11% -> 10% of each run, Pallas kernels for 48% -> 72%
where the time goes in v4:
time: 844 us; the launch traced here: 837 us
  Pallas kernels  706 us (84%)
  matrix products  63.9 us (8%)
  other arithmetic  29.1 us (3%)
  local copies, waits for them, and re-layouts  22.5 us (3%)
  between operations  14.9 us (2%)
    pallas_call x8, Pallas kernels, exchange(): pl.pallas_call(functools.partial(exchange_kernel, tasks, wires, len(array...  545 us
    pallas_call x1, Pallas kernels, feed_forward(): pl.pallas_call(feed_kernel, grid=(tokens_all // step,), in_specs=[pl.Bloc...  50.2 us
    dot_general x6, matrix products, contract(): lax.dot_general(left_side, right_side, (((0,), (0,)), ((), ())), preferre...  45.7 us
    pallas_call x1, Pallas kernels, plane_sum(): pl.pallas_call(plane_sum_kernel, in_specs=[pl.BlockSpec(memory_space=pltp...  40.4 us
    pallas_call x1, Pallas kernels, adam(): pl.pallas_call(adam_kernel, grid_spec=pltpu.PrefetchScalarGridSpec(num_sc...  31.7 us
  transfers between devices with their start and end apart: 6, of which 0 were waited for; matrix products, arithmetic and copies ran while one was open for 10% of the time, Pallas kernels for 72%

profile of v4, /device:TPU:0, one launch (start us, length us, event | category | flops | bytes accessed | tf_op | source)
XLA Modules:
  0.0 837.0 jit_solution(8049414833458240750)
XLA Ops:
  7.3 1.2 slice.24.attn_ref
  8.6 1.9 gather_fusion
  10.5 52.8 %exchange.8 = bf16[8,21,256,128]{3,2,1,0:T(8,128)(2,1)} custom-call(bf16[21,512,128]{2,1,0:T(8,128)(2,1)} %refs_0_.3), custom_call_target="tpu_custom_call" | custom-call | flops 1 | bytes 1 | tf_op jit(solution)/shard_map/exchange/pallas_call | solution.py:649
  63.3 3.6 pick.2
  66.9 55.3 %exchange.9 = (bf16[8,21,256,128]{3,2,1,0:T(8,128)(2,1)}, bf16[4,32,4352]{2,1,0:T(8,128)(2,1)}) custom-call(bf16[21,512,128]{2,1,0:T(8,128)(2,1)} %refs_0_.3, bf16[32,4352]{1,0:T(8,128)(2,1)} %get-tuple-element.64.refs_1_), custom_call_target="tpu_custom_call" | custom-call | flops 1 | bytes 1 | tf_op jit(solution)/shard_map/exchange/pallas_call | solution.py:649
  122.2 3.7 pick.3
  126.9 1.3 fusion.15.refs_2_.x_ref
  128.1 117.6 %exchange.10 = (bf16[4,2,8,32,4352]{4,3,2,1,0:T(8,128)(2,1)}, bf16[4,32,4352]{2,1,0:T(8,128)(2,1)}, bf16[8,256,2048]{2,1,0:T(8,128)(2,1)}) custom-call(bf16[4,32,4352]{2,1,0:T(8,128)(2,1)} %get-tuple-element.65.refs_0_, bf16[32,4352]{1,0:T(8,128)(2,1)} %get-tuple-element.67.refs_1_, bf16[256,2048]{1,0:T(8,128)(2,1)} %fusion.15.refs_2_.x_ref), custom_call_target="tpu_custom_call" | custom-call | flops 1 | bytes 1 | tf_op jit(solution)/shard_map/exchange/pallas_call | solution.py:649
  245.8 1.9 multiply_sine_fusion
  249.6 10.4 %project.1.q_ref = bf16[256,2304]{1,0:T(8,128)(2,1)} custom-call(bf16[256,2048]{1,0:T(8,128)(2,1)} %fusion.15.refs_2_.x_ref, bf16[2048,4352]{1,0:T(8,128)(2,1)} %bitcast.68, f32[256,128]{1,0:T(8,128)} %get-tuple-element.149.cosine_ref, f32[256,128]{1,0:T(8,128)} %get-tuple-element.148.sine_ref), custom_call_target="tpu_custom_call" | custom-call | flops 1 | bytes 1 | tf_op jit(solution)/shard_map/project/pallas_call | solution.py:87
  260.0 1.7 slice.31.refs_0_
  261.6 41.8 %exchange.11 = (bf16[4,256,256]{2,1,0:T(8,128)(2,1)}, s32[4,2,128]{2,1,0:T(2,128)}, bf16[8,256,2048]{2,1,0:T(8,128)(2,1)}) custom-call(bf16[256,256]{1,0:T(8,128)(2,1)} %slice.31.refs_0_, s32[2,128]{1,0:T(2,128)} %bitcast.61, bf16[256,2048]{1,0:T(8,128)(2,1)} %refs_2_.1), custom_call_target="tpu_custom_call" | custom-call | flops 1 | bytes 1 | tf_op jit(solution)/shard_map/exchange/pallas_call | solution.py:649
  304.4 1.0 copy-done.2
  305.4 9.0 %attend.1 = (bf16[256,2048]{1,0:T(8,128)(2,1)S(1)}, f32[16,1,256]{2,1,0:T(1,128)S(1)}) custom-call(s32[1]{0:T(128)} %bitcast.at_ref, bf16[256,2304]{1,0:T(8,128)(2,1)S(1)} %copy-done, bf16[1024,256]{1,0:T(8,128)(2,1)S(1)} %bitcast.57, bf16[1024,256]{1,0:T(8,128)(2,1)S(1)} %bitcast.58, s32[1024,1]{1,0:T(8,128)S(1)} %copy.26.key_seg_ref, s32[1,256]{1,0:T(1,128)S(1)} %bitcast.62), custom_call_target="tpu_custom_call" | custom-call | flops 1 | bytes 1 | tf_op jit(solution)/shard_map/attend/pallas_call | solution.py:208
  314.4 6.3 multiply_reduce_fusion.2
  320.7 1.3 copy-done.14
  322.1 1.2 multiply_convert_fusion.refs_0_
  323.3 39.9 %exchange.12 = bf16[8,256,2048]{2,1,0:T(8,128)(2,1)} custom-call(bf16[256,2048]{1,0:T(8,128)(2,1)} %multiply_convert_fusion.refs_0_), custom_call_target="tpu_custom_call" | custom-call | flops 1 | bytes 1 | tf_op jit(solution)/shard_map/exchange/pallas_call | solution.py:649
  363.2 50.2 %feed_forward.1 = (bf16[2048,768]{1,0:T(8,128)(2,1)}, bf16[2048,768]{1,0:T(8,128)(2,1)}, bf16[2048,768]{1,0:T(8,128)(2,1)}, bf16[2048,2048]{1,0:T(8,128)(2,1)}, bf16[2048,2048]{1,0:T(8,128)(2,1)}) custom-call(s32[1]{0:T(128)} %bitcast.12.real_ref, bf16[2048,2048]{1,0:T(8,128)(2,1)} %bitcast.65, bf16[2048,2048]{1,0:T(8,128)(2,1)} %bitcast.75, ...), custom_call_target="tpu_custom_call" | custom-call | flops 1 | bytes 1 | tf_op jit(solution)/shard_map/feed_forward/pallas_call | solution.py:300
  413.4 11.6 %convolution_convert_fusion.2 = bf16[2048,768]{1,0:T(8,128)(2,1)} fusion(bf16[2048,2048]{1,0:T(8,128)(2,1)} %bitcast.76, bf16[2048,768]{1,0:T(8,128)(2,1)} %get-tuple-element.80), kind=kOutput, calls=%fused_computation.16 | convolution fusion | flops 6444023808 | bytes 14680064 | tf_op jit(solution)/shard_map/dot_general | solution.py:30
  425.2 11.4 %convolution_convert_fusion.1 = bf16[2048,768]{1,0:T(8,128)(2,1)} fusion(bf16[2048,2048]{1,0:T(8,128)(2,1)} %bitcast.66, bf16[2048,768]{1,0:T(8,128)(2,1)} %get-tuple-element.83), kind=kOutput, calls=%fused_computation.15 | convolution fusion | flops 6444023808 | bytes 14680064 | tf_op jit(solution)/shard_map/dot_general | solution.py:30
  436.5 11.4 %convolution_convert_fusion = bf16[2048,768]{1,0:T(8,128)(2,1)} fusion(bf16[2048,2048]{1,0:T(8,128)(2,1)} %bitcast.67, bf16[2048,768]{1,0:T(8,128)(2,1)} %get-tuple-element.84), kind=kOutput, calls=%fused_computation.14 | convolution fusion | flops 6444023808 | bytes 14680064 | tf_op jit(solution)/shard_map/dot_general | solution.py:30
  448.6 1.7 pad_maximum_fusion.1
  450.3 3.4 copy-done.1
  453.8 40.4 %plane_sum.1 = f32[256,2048]{1,0:T(8,128)S(1)} custom-call(bf16[8,256,2048]{2,1,0:T(8,128)(2,1)S(1)} %bitcast.56), custom_call_target="tpu_custom_call" | custom-call | flops 1 | bytes 1 | tf_op jit(solution)/shard_map/plane_sum/pallas_call | solution.py:770
  494.2 1.2 multiply_reduce_fusion
  495.4 2.0 fusion.42
  497.4 1.0 copy-done.22
  498.4 6.8 fusion.10.grad_ref
  505.2 1.2 copy-done.9
  507.1 11.9 %attend_back.1 = (bf16[256,2048]{1,0:T(8,128)(2,1)S(1)}, bf16[1024,256]{1,0:T(8,128)(2,1)S(1)}) custom-call(s32[1]{0:T(128)} %bitcast.at_ref, bf16[256,2304]{1,0:T(8,128)(2,1)S(1)} %copy-done, bf16[1024,256]{1,0:T(8,128)(2,1)S(1)} %bitcast.59, bf16[1024,256]{1,0:T(8,128)(2,1)S(1)} %bitcast.60, bf16[256,2048]{1,0:T(8,128)(2,1)S(1)} %copy-done.9, ...), custom_call_target="tpu_custom_call" | custom-call | flops 1 | bytes 1 | tf_op jit(solution)/shard_map/attend_back/pallas_call | solution.py:226
  519.0 1.0 copy-done.7
  520.8 83.6 %exchange.13 = (bf16[4,256,256]{2,1,0:T(8,128)(2,1)}, bf16[8,256,256]{2,1,0:T(8,128)(2,1)}, bf16[8,256,256]{2,1,0:T(8,128)(2,1)}, bf16[8,256,2048]{2,1,0:T(8,128)(2,1)}) custom-call(bf16[1024,256]{1,0:T(8,128)(2,1)} %copy-done.10, bf16[256,2048]{1,0:T(8,128)(2,1)} %copy-done.7, bf16[256,2048]{1,0:T(8,128)(2,1)} %copy-done.22, bf16[256,2048]{1,0:T(8,128)(2,1)} %copy-done.6), custom_call_target="tpu_custom_call" | custom-call | flops 1 | bytes 1 | tf_op jit(solution)/shard_map/exchange/pallas_call | solution.py:649
  604.4 1.8 reduce_sum.123
  606.2 6.3 fusion.8
  612.5 2.7 fusion.9
  615.3 1.5 pad_maximum_fusion.refs_0_
  616.7 1.7 slice-done.3
  619.2 5.1 fusion.21
  625.0 2.4 convolution_convert_fusion.3
  627.4 72.5 %exchange.14 = (bf16[4,512,512]{2,1,0:T(8,128)(2,1)}, bf16[8,4,64,256]{3,2,1,0:T(8,128)(2,1)}, f32[4,2,2048]{2,1,0:T(2,128)}, bf16[8,512,768]{2,1,0:T(8,128)(2,1)}, bf16[8,512,768]{2,1,0:T(8,128)(2,1)}) custom-call(bf16[2048,512]{1,0:T(8,128)(2,1)} %pad_maximum_fusion.refs_0_, bf16[4,8,64,256]{3,2,1,0:T(8,128)(2,1)} %bitcast.79, ...), custom_call_target="tpu_custom_call" | custom-call | flops 1 | bytes 1 | tf_op jit(solution)/shard_map/exchange/pallas_call | solution.py:649
  699.9 2.9 reduce_sum.126.refs_2_
  703.4 1.3 scatter_custom_fusion
  707.0 81.5 %exchange.15 = (bf16[4,64,256]{2,1,0:T(8,128)(2,1)}, bf16[8,4,64,256]{3,2,1,0:T(8,128)(2,1)}, bf16[8,512,768]{2,1,0:T(8,128)(2,1)}, bf16[8,512,512]{2,1,0:T(8,128)(2,1)}, f32[8,2,2048]{2,1,0:T(2,128)}) custom-call(bf16[4,64,256]{2,1,0:T(8,128)(2,1)} %reduce_sum.128.refs_0_, bf16[512,768]{1,0:T(8,128)(2,1)} %reduce-scatter.9.cloned.1.call-done.refs_1_, ...), custom_call_target="tpu_custom_call" | custom-call | flops 1 | bytes 1 | tf_op jit(solution)/shard_map/exchange/pallas_call | solution.py:649
  788.5 2.2 reduce_sum.130.pair_ref
  790.6 31.7 %adam.1 = (f32[21,512,128]{2,1,0:T(8,128)}, f32[21,512,128]{2,1,0:T(8,128)}, f32[21,512,128]{2,1,0:T(8,128)}) custom-call(s32[6,21]{1,0:T(8,128)} %stack.39.at_ref, bf16[8,512,768]{2,1,0:T(8,128)(2,1)} %get-tuple-element.106.gate_ref, bf16[8,512,768]{2,1,0:T(8,128)(2,1)} %get-tuple-element.111.up_ref, bf16[8,512,768]{2,1,0:T(8,128)(2,1)} %get-tuple-element.112.down_ref, ...), custom_call_target="tpu_custom_call" | custom-call | flops 1 | bytes 1 | tf_op jit(solution)/shard_map/adam/pallas_call | solution.py:392
  823.1 4.3 fusion.19
  827.5 2.5 add_convert_fusion
  (130 shorter events, 11.4 us)
Async XLA Ops:
  7.2 242.4 %all-gather.5.cloned.1.call-start = ((), (), s32[]{:S(2)}) async-start(), calls=%async_computation.8 | async-start | bytes 5898240 | tf_op jit(solution)/shard_map/all_gather | solution.py:860
  66.9 296.3 %all-gather.7.cloned.1.call-start = ((), (), s32[]{:S(2)}) async-start(), calls=%async_computation.9 | async-start | bytes 5898240 | tf_op jit(solution)/shard_map/all_gather | solution.py:866
  122.2 3.8 copy-start.18
  125.9 0.9 copy-start.30
  126.0 379.2 %reduce-scatter.5.cloned.1.call-start = ((), (), s32[]{:S(2)}) async-start(), calls=%async_computation.4 | async-start | bytes 3932160 | tf_op jit(solution)/shard_map/reduce_scatter | solution.py:918
  126.8 118.9 %copy-start.35 = (f32[256]{0:T(256)}, f32[256]{0:T(256)S(1)}, u32[]{:S(2)}) copy-start(f32[256]{0:T(256)S(1)} %get-tuple-element.140) | copy-start | bytes 3076
  126.9 118.9 %copy-start.26 = (f32[1,2048]{1,0:T(1,128)}, f32[1,2048]{1,0:T(1,128)S(1)}, u32[]{:S(2)}) copy-start(f32[1,2048]{1,0:T(1,128)S(1)} %get-tuple-element.135) | copy-start | bytes 24580
  247.7 1.0 copy-start.21
  249.6 54.8 %copy-start.11 = (s32[256]{0:T(256)S(1)}, s32[256]{0:T(256)}, u32[]{:S(2)}) copy-start(s32[256]{0:T(256)} %param.15) | copy-start | bytes 3076
  259.9 44.4 %copy-start = (bf16[256,2304]{1,0:T(8,128)(2,1)S(1)}, bf16[256,2304]{1,0:T(8,128)(2,1)}, u32[]{:S(2)}) copy-start(bf16[256,2304]{1,0:T(8,128)(2,1)} %project.1.q_ref) | copy-start | bytes 3538948
  304.4 1.0 copy-start.2
  314.4 6.3 copy-start.6
  320.7 1.4 copy-start.14
  425.1 181.1 %reduce-scatter.7.cloned.1.call-start = ((), (), s32[]{:S(2)}) async-start(), calls=%async_computation.5 | async-start | bytes 3932160 | tf_op jit(solution)/shard_map/reduce_scatter | solution.py:924
  448.0 254.8 %reduce-scatter.9.cloned.1.call-start = ((), (), s32[]{:S(2)}) async-start(), calls=%async_computation.6 | async-start | bytes 3932160 | tf_op jit(solution)/shard_map/reduce_scatter | solution.py:925
  448.6 378.9 %reduce-scatter.11.cloned.1.call-start = ((), (), s32[]{:S(2)}) async-start(), calls=%async_computation.7 | async-start | bytes 9437184 | tf_op jit(solution)/shard_map/reduce_scatter | solution.py:1007
  450.3 3.5 copy-start.1
  453.8 40.4 %copy-start.15 = (f32[256,2048]{1,0:T(8,128)S(1)}, f32[256,2048]{1,0:T(8,128)}, u32[]{:S(2)}) copy-start(f32[256,2048]{1,0:T(8,128)} %copy-done.14) | copy-start | bytes 6291460
  494.2 1.2 copy-start.23
  497.4 1.0 copy-start.22
  498.4 6.8 copy-start.3
  498.4 6.8 copy-start.4
  498.4 6.8 copy-start.5
  505.2 1.2 copy-start.9
  519.0 1.0 copy-start.7
  519.9 0.8 copy-start.10
  606.2 6.3 copy-start.38
  606.2 6.4 copy-start.39
  606.2 10.6 %slice-start = ((s8[17825792]{0:T(1024)(128)(4,1)}), s8[4194304]{0:T(1024)(128)(4,1)S(1)}, s32[]{:S(2)}) async-start(s8[17825792]{0:T(1024)(128)(4,1)} %bitcast.71), calls=%async_computation.10 | async-start | bytes 8388608
  606.2 10.6 %slice-start.1 = ((s8[17825792]{0:T(1024)(128)(4,1)}), s8[4194304]{0:T(1024)(128)(4,1)S(1)}, s32[]{:S(2)}) async-start(s8[17825792]{0:T(1024)(128)(4,1)} %bitcast.71), calls=%async_computation.11 | async-start | bytes 8388608
  606.2 10.6 %slice-start.2 = ((s8[17825792]{0:T(1024)(128)(4,1)}), s8[4194304]{0:T(1024)(128)(4,1)S(1)}, s32[]{:S(2)}) async-start(s8[17825792]{0:T(1024)(128)(4,1)} %bitcast.71), calls=%async_computation.12 | async-start | bytes 8388608
  612.5 5.9 slice-start.3
  612.5 6.1 slice-start.4
  615.2 3.7 copy-start.8
  615.2 4.0 copy-start.19
  615.2 4.0 copy-start.27
  615.2 4.0 copy-start.36
  619.2 5.2 copy-start.32
  619.2 5.8 copy-start.17
  702.8 2.8 copy-start.24
  702.8 3.6 copy-start.29
  790.6 31.7 %copy-start.25 = (f32[8,2,2048]{2,1,0:T(2,128)S(1)}, f32[8,2,2048]{2,1,0:T(2,128)}, u32[]{:S(2)}) copy-start(f32[8,2,2048]{2,1,0:T(2,128)} %get-tuple-element.118) | copy-start | bytes 393220
  790.6 31.8 %copy-start.31 = (f32[2,2048]{1,0:T(2,128)S(1)}, f32[2,2048]{1,0:T(2,128)}, u32[]{:S(2)}) copy-start(f32[2,2048]{1,0:T(2,128)} %param.23) | copy-start | bytes 49156
  790.6 31.8 %copy-start.33 = (f32[2,2048]{1,0:T(2,128)S(1)}, f32[2,2048]{1,0:T(2,128)}, u32[]{:S(2)}) copy-start(f32[2,2048]{1,0:T(2,128)} %param.24) | copy-start | bytes 49156
  790.6 31.8 %copy-start.34 = (f32[2,2048]{1,0:T(2,128)S(1)}, f32[2,2048]{1,0:T(2,128)}, u32[]{:S(2)}) copy-start(f32[2,2048]{1,0:T(2,128)} %param.25) | copy-start | bytes 49156
  790.6 32.5 %copy-start.37 = (f32[256]{0:T(256)S(1)}, f32[256]{0:T(256)}, u32[]{:S(2)}) copy-start(f32[256]{0:T(256)} %get-tuple-element.139) | copy-start | bytes 3076
  822.4 5.0 copy-start.28
  823.1 4.3 copy-start.16
  (3 other events, 2.2 us)
Sparse Core Ops, SparseCore 0:
  67.0 129.4 all-gather.4
  198.6 99.9 all-gather.6
  425.2 68.6 reduce-scatter.4
  496.7 68.6 reduce-scatter.6
  568.1 61.5 reduce-scatter.8
  702.9 92.7 reduce-scatter.10

commit v5 on v4

--- a/solution.py
+++ b/solution.py
@@ -246,47 +246,55 @@
     )
 
 
-def feed_kernel(
-    real_ref, x_ref, cot_ref, *refs
-):
-    parts, refs = refs[:-7], refs[-7:]
-    act_ref, gate_grad_ref, up_grad_ref, two_ref, out_ref, weights, sems = refs
-    cols = act_ref.shape[1]
+def load_weights(parts, weights, sems):
     count, rows, _ = parts[0].shape
     halves = len(parts)
-
-    @pl.when(pl.program_id(0) == 0)
-    def _():
-        copies = [
-            pltpu.make_async_copy(
-                parts[half].at[block],
-                weights.at[pl.ds((block * halves + half) * rows, rows)],
-                sems.at[block * halves + half],
-            )
-            for half in range(halves)
-            for block in range(count)
-        ]
-        for copy in copies:
-            copy.start()
-        for copy in copies:
-            copy.wait()
-
+    return [
+        pltpu.make_async_copy(
+            parts[half].at[block],
+            weights.at[pl.ds((block * halves + half) * rows, rows)],
+            sems.at[block * halves + half],
+        )
+        for half in range(halves)
+        for block in range(count)
+    ]
+
+
+def feed_block(real, x, cot, weights, act_ref, gate_grad_ref, up_grad_ref, two_ref, out_ref):
     low = jnp.bfloat16
     wide = jnp.float32
-    gate = jnp.dot(x_ref[...], weights[:, :cols], preferred_element_type=wide)
-    upper = jnp.dot(x_ref[...], weights[:, cols : 2 * cols], preferred_element_type=wide)
-    act_grad = jnp.dot(cot_ref[...], weights[:, 2 * cols :], preferred_element_type=wide)
-    real = lax.broadcasted_iota(jnp.int32, gate.shape, 1) < real_ref[0]
+    cols = act_ref.shape[0]
+    gate = jnp.dot(x, weights[:, :cols], preferred_element_type=wide)
+    upper = jnp.dot(x, weights[:, cols : 2 * cols], preferred_element_type=wide)
+    act_grad = jnp.dot(cot, weights[:, 2 * cols :], preferred_element_type=wide)
+    real = lax.broadcasted_iota(jnp.int32, gate.shape, 1) < real
     sigmoid = 1.0 / (1.0 + jnp.exp(-gate))
     silu = gate * sigmoid
     activated = jnp.where(real, silu * upper, 0.0).astype(low)
     act_grad = jnp.where(real, act_grad, 0.0)
     gate_grad = (act_grad * upper * sigmoid * (1.0 + gate * (1.0 - sigmoid))).astype(low)
     up_grad = (act_grad * silu).astype(low)
-    act_ref[...], gate_grad_ref[...], up_grad_ref[...] = activated, gate_grad, up_grad
+    act_ref[...] = jnp.transpose(activated)
+    gate_grad_ref[...] = jnp.transpose(gate_grad)
+    up_grad_ref[...] = jnp.transpose(up_grad)
     two = dot_last(gate_grad, weights[:, :cols]) + dot_last(up_grad, weights[:, cols : 2 * cols])
     two_ref[...] = two.astype(low)
     out_ref[...] = dot_last(activated, weights[:, 2 * cols :]).astype(low)
+
+
+def feed_kernel(real_ref, x_ref, cot_ref, *refs):
+    parts, refs = refs[:-7], refs[-7:]
+    weights, sems = refs[5:]
+
+    @pl.when(pl.program_id(0) == 0)
+    def _():
+        copies = load_weights(parts, weights, sems)
+        for copy in copies:
+            copy.start()
+        for copy in copies:
+            copy.wait()
+
+    feed_block(real_ref[0], x_ref[...], cot_ref[...], weights, *refs[:5])
 
 
 def feed_forward(real_cols, x, cot, parts, seq_count):
@@ -296,14 +304,14 @@
     step = 256
     low = jnp.bfloat16
     block = pl.BlockSpec((step, width), lambda i: (i, 0))
-    narrow = pl.BlockSpec((step, cols), lambda i: (i, 0))
+    narrow = pl.BlockSpec((cols, step), lambda i: (0, i))
     return pl.pallas_call(
         feed_kernel,
         grid=(tokens_all // step,),
         in_specs=[pl.BlockSpec(memory_space=pltpu.SMEM), block, block]
         + [pl.BlockSpec(memory_space=pl.ANY)] * len(parts),
         out_specs=[narrow, narrow, narrow, block, block],
-        out_shape=[jax.ShapeDtypeStruct((tokens_all, cols), low)] * 3
+        out_shape=[jax.ShapeDtypeStruct((cols, tokens_all), low)] * 3
         + [jax.ShapeDtypeStruct((tokens_all, width), low)] * 2,
         scratch_shapes=[
             pltpu.VMEM((width, 3 * cols), low),
@@ -315,45 +323,229 @@
     )(real_cols, x, cot, *parts)
 
 
-def pick_kernel(rows, feed_ref, attn_ref, tiles_ref, feed_out, attn_out, sems):
-    grp = lax.axis_index("grp")
-    width = tiles_ref.shape[2]
+def feed_gather_kernel(
+    first, second, real_ref, own_ref, context_ref, cot_ref, cot_all_ref, part_ref, gate_grad_ref,
+    up_grad_ref, two_ref, out_ref, second_ref, context_plane_ref, down_out, blocks, weights,
+    act_block, act, x_block, stage, load_sems, keep_sems, x_sems, out_sems, first_send,
+    first_recv, second_send, second_recv,
+):
+    step = pl.program_id(0)
+    grp, seq = lax.axis_index("grp"), lax.axis_index("seq")
+    first.start(own_ref, blocks, (first_send, first_recv), grp, seq, begin=False)
+    second.start(context_ref, context_plane_ref, (second_send, second_recv), grp, seq, begin=False)
+    loads = load_weights([part_ref], weights, load_sems)
+    cols = act.shape[0]
+    step_rows = act_block.shape[1]
+    rows = x_block.shape[2]
+    count = cot_all_ref.shape[1] // rows
+
+    @pl.when(step == 0)
+    def _():
+        for copy in loads:
+            copy.start()
+        barrier = pltpu.get_barrier_semaphore()
+        for device in first.peers(grp, seq):
+            pl.semaphore_signal(barrier, inc=1, device_id=device, device_id_type=MESH)
+        pl.semaphore_wait(barrier, 3)
+        first.begin()
+        first.kept.wait()
+        for copy in loads:
+            copy.wait()
+
+    @pl.when(step == 1)
+    def _():
+        first.due[7].wait_recv()
+
+    @pl.when(step == 2)
+    def _():
+        for came in (1, 4, 2):
+            first.pass_on(came)
+
+    @pl.when(step == 3)
+    def _():
+        first.pass_on(5)
+
+    @pl.when(step == 4)
+    def _():
+        first.due[8].wait_recv()
+        first.due[9].wait_recv()
+        first.pass_on(6)
+        first.pass_on(3)
+        second.begin()
+
+    @pl.when(step == 5)
+    def _():
+        first.due[10].wait_recv()
+        first.due[11].wait_recv()
+
+    @pl.when(step == 7)
+    def _():
+        first.due[12].wait_recv()
+        first.due[13].wait_recv()
+        second.pass_on(1)
+        second.pass_on(4)
+
+    keep = pltpu.make_async_copy(blocks.at[step], second_ref.at[step], keep_sems.at[step])
+    keep.start()
+    feed_block(
+        real_ref[0], blocks[step], cot_ref[...], weights, act_block, gate_grad_ref, up_grad_ref,
+        two_ref, out_ref,
+    )
+    act[:, pl.ds(pl.multiple_of(step * step_rows, step_rows), step_rows)] = act_block[...]
+
+    def x_copy(at):
+        view = cot_all_ref.at[:, pl.ds(pl.multiple_of(at * rows, rows), rows)]
+        return pltpu.make_async_copy(view, x_block.at[at % 2], x_sems.at[at % 2])
+
+    def out_copy(at):
+        place = pl.ds(pl.multiple_of(at * cols, cols), cols)
+        return pltpu.make_async_copy(stage.at[at % 2], down_out.at[place], out_sems.at[at % 2])
+
+    @pl.when(step == 7)
+    def _():
+        x_copy(0).start()
+        second.pass_on(2)
+        second.pass_on(5)
+
+        def one(at, _):
+            @pl.when(at == 2)
+            def _():
+                second.pass_on(6)
+                second.pass_on(3)
+
+            x_copy(at).wait()
+
+            @pl.when(at + 1 < count)
+            def _():
+                x_copy(at + 1).start()
+
+            @pl.when(at >= 2)
+            def _():
+                out_copy(at - 2).wait()
+
+            stage[at % 2] = jnp.dot(
+                act[...], x_block[at % 2], preferred_element_type=jnp.float32
+            ).astype(stage.dtype)
+            out_copy(at).start()
+            return 0
+
+        lax.fori_loop(0, count, one, 0)
+        out_copy(count - 2).wait()
+        out_copy(count - 1).wait()
+        second.finish()
+        for copy in first.out[1:]:
+            copy.wait_send()
+        for at in range(8):
+            pltpu.make_async_copy(blocks.at[at], second_ref.at[at], keep_sems.at[at]).wait()
+
+
+def feed_gather(number, real_cols, normed, context, cot, part, seq_count):
+    rows, width = normed.shape
+    cols = part.shape[2] // 3
+    low = jnp.bfloat16
+    block = pl.BlockSpec((rows, width), lambda i: (i, 0))
+    narrow = pl.BlockSpec((cols, rows), lambda i: (0, i))
+    first = gather_plane(normed.shape, placed=True)
+    second = gather_plane(context.shape, placed=True)
+    hbm = pl.BlockSpec(memory_space=pl.ANY)
+    plane = jax.ShapeDtypeStruct((8, rows, width), low)
+    model_rows = width // seq_count
+    return pl.pallas_call(
+        functools.partial(feed_gather_kernel, first, second),
+        grid=(8,),
+        in_specs=[pl.BlockSpec(memory_space=pltpu.SMEM), hbm, hbm, block, hbm, hbm],
+        out_specs=[narrow, narrow, block, block, hbm, hbm, hbm],
+        out_shape=[jax.ShapeDtypeStruct((cols, 8 * rows), low)] * 2
+        + [jax.ShapeDtypeStruct((8 * rows, width), low)] * 2
+        + [plane, plane, jax.ShapeDtypeStruct((seq_count * cols, model_rows), low)],
+        scratch_shapes=[
+            pltpu.VMEM((8, rows, width), low),
+            pltpu.VMEM((width, 3 * cols), low),
+            pltpu.VMEM((cols, rows), low),
+            pltpu.VMEM((cols, 8 * rows), low),
+            pltpu.VMEM((2, 8 * rows, model_rows), low),
+            pltpu.VMEM((2, cols, model_rows), low),
+            pltpu.SemaphoreType.DMA((seq_count,)),
+            pltpu.SemaphoreType.DMA((8,)),
+            pltpu.SemaphoreType.DMA((2,)),
+            pltpu.SemaphoreType.DMA((2,)),
+        ]
+        + [pltpu.SemaphoreType.DMA((14,))] * 4,
+        compiler_params=pltpu.CompilerParams(
+            collective_id=number, has_side_effects=True, vmem_limit_bytes=60 * 2**20
+        ),
+        cost_estimate=SMALL_COST,
+        name="feed_gather",
+    )(real_cols, normed, context, cot, cot, part)
+
+
+def weight_grad_kernel(left_ref, x_ref, out_ref):
+    out_ref[...] = jnp.dot(
+        left_ref[...], x_ref[...], preferred_element_type=jnp.float32
+    ).astype(out_ref.dtype)
+
+
+def weight_grad(left, x, seq_count):
+    cols, tokens_all = left.shape
+    rows = x.shape[1] // seq_count
+    return pl.pallas_call(
+        weight_grad_kernel,
+        grid=(seq_count,),
+        in_specs=[
+            pl.BlockSpec((cols, tokens_all), lambda i: (0, 0)),
+            pl.BlockSpec((tokens_all, rows), lambda i: (0, i)),
+        ],
+        out_specs=pl.BlockSpec((cols, rows), lambda i: (i, 0)),
+        out_shape=jax.ShapeDtypeStruct((seq_count * cols, rows), jnp.bfloat16),
+        compiler_params=pltpu.CompilerParams(vmem_limit_bytes=40 * 2**20),
+        cost_estimate=SMALL_COST,
+        name="weight_grad",
+    )(left, x)
+
+
+def pick_kernel(share, slots_ref, *refs):
+    count = len(refs) - 2
+    sources, out_ref, sems = refs[:count], refs[count], refs[count + 1]
+    width = sources[0].shape[2]
+    start = 0
     copies = []
-    for at in range(feed_ref.shape[0]):
-        copies.append(
-            (tiles_ref.at[feed_ref[at]], feed_out.at[:, at * width : (at + 1) * width])
-        )
-    share = pl.ds(pl.multiple_of(grp * rows, rows), rows)
-    for at in range(attn_ref.shape[0]):
-        copies.append(
-            (tiles_ref.at[attn_ref[at], share], attn_out.at[:, at * width : (at + 1) * width])
-        )
-    copies = [
-        pltpu.make_async_copy(source, target, sems.at[at])
-        for at, (source, target) in enumerate(copies)
-    ]
+    for at, source in enumerate(sources):
+        rows = source.shape[1]
+        if at == 0 and share is not None:
+            rows = share
+            part = pl.ds(pl.multiple_of(lax.axis_index("grp") * rows, rows), rows)
+        else:
+            part = pl.ds(0, rows)
+        for tile in range(slots_ref.shape[0]):
+            copies.append(
+                pltpu.make_async_copy(
+                    source.at[slots_ref[tile], part],
+                    out_ref.at[pl.ds(start, rows), tile * width : (tile + 1) * width],
+                    sems.at[len(copies)],
+                )
+            )
+        start += rows
     for copy in copies:
         copy.start()
     for copy in copies:
         copy.wait()
 
 
-def pick(tiles, feed_slots, attn_slots):
-    _, rows, width = tiles.shape
-    share = rows // lax.axis_size("grp")
-    feed, attn = feed_slots.shape[0], attn_slots.shape[0]
+def pick(slots, sources, share=None):
+    count, width = slots.shape[0], sources[0].shape[2]
+    rows = sum(source.shape[1] for source in sources)
+    if share is not None:
+        rows += share - sources[0].shape[1]
     return pl.pallas_call(
         functools.partial(pick_kernel, share),
-        in_specs=[pl.BlockSpec(memory_space=pltpu.SMEM)] * 2 + [pl.BlockSpec(memory_space=pl.ANY)],
-        out_specs=[pl.BlockSpec(memory_space=pltpu.VMEM)] * 2,
-        out_shape=[
-            jax.ShapeDtypeStruct((rows, feed * width), tiles.dtype),
-            jax.ShapeDtypeStruct((share, attn * width), tiles.dtype),
-        ],
-        scratch_shapes=[pltpu.SemaphoreType.DMA((feed + attn,))],
+        in_specs=[pl.BlockSpec(memory_space=pltpu.SMEM)]
+        + [pl.BlockSpec(memory_space=pl.ANY)] * len(sources),
+        out_specs=pl.BlockSpec(memory_space=pltpu.VMEM),
+        out_shape=jax.ShapeDtypeStruct((rows, count * width), sources[0].dtype),
+        scratch_shapes=[pltpu.SemaphoreType.DMA((count * len(sources),))],
         cost_estimate=SMALL_COST,
         name="pick",
-    )(feed_slots, attn_slots, tiles)
+    )(slots, *sources)
 
 
 def adam_kernel(
@@ -361,11 +553,16 @@
     one_ref, two_ref, new_master_ref, new_one_ref, new_two_ref, grad,
 ):
     kind = at_ref[0, pl.program_id(0)]
-    for number, ref in enumerate((gate_ref, up_ref, down_ref, share_ref, pair_ref)):
+    for number, ref in enumerate((gate_ref, up_ref, down_ref, share_ref)):
 
         @pl.when(kind == number)
         def _():
-            grad[...] = ref[...].reshape(grad.shape)
+            grad[...] = ref[0]
+
+    @pl.when(kind == 4)
+    def _():
+        pair = pair_ref[...].reshape(grad.shape[1], grad.shape[0])
+        grad[...] = jnp.transpose(pair.astype(jnp.float32)).astype(grad.dtype)
 
     @pl.when(kind == 5)
     def _():
@@ -373,7 +570,7 @@
 
     low = jnp.bfloat16
     left, right = left_ref[0].astype(low), right_ref[0].astype(low)
-    turned = dot_first(grad[...], left)
+    turned = jnp.dot(grad[...], left, preferred_element_type=jnp.float32)
     turned = dot_first(turned.astype(low), right)
     new_one = BETA_ONE * one_ref[0] + (1.0 - BETA_ONE) * turned
     new_two = BETA_TWO * two_ref[0] + (1.0 - BETA_TWO) * turned * turned
@@ -388,7 +585,7 @@
     slots, rows, width = master.shape
     tile = pl.BlockSpec((1, rows, width), lambda i, at: (i, 0, 0))
     shape = jax.ShapeDtypeStruct(master.shape, jnp.float32)
-    feed = pl.BlockSpec((1, rows, width), lambda i, at: (at[1, i], 0, at[2, i]))
+    feed = pl.BlockSpec((1, width, rows), lambda i, at: (at[1, i], at[2, i], 0))
     return pl.pallas_call(
         adam_kernel,
         grid_spec=pltpu.PrefetchScalarGridSpec(
@@ -398,7 +595,7 @@
                 feed,
                 feed,
                 feed,
-                pl.BlockSpec((1, rows, width), lambda i, at: (at[3, i], 0, at[4, i])),
+                pl.BlockSpec((1, width, rows), lambda i, at: (at[3, i], at[4, i], 0)),
                 pl.BlockSpec((*pairs.shape[:2], width), lambda i, at: (0, 0, at[5, i])),
                 pl.BlockSpec((1, rows, rows), lambda i, at: (i, 0, 0)),
                 pl.BlockSpec((1, width, width), lambda i, at: (i, 0, 0)),
@@ -407,7 +604,7 @@
                 tile,
             ],
             out_specs=[tile] * 3,
-            scratch_shapes=[pltpu.VMEM((rows, width), jnp.bfloat16)],
+            scratch_shapes=[pltpu.VMEM((width, rows), jnp.bfloat16)],
         ),
         out_shape=[shape] * 3,
         compiler_params=pltpu.CompilerParams(vmem_limit_bytes=60 * 2**20),
@@ -436,6 +633,51 @@
 
 def rows_of(ref, index, height):
     return ref.at[pl.ds(pl.multiple_of(index * height, height), height), :]
+
+
+PLACES = {0: 0, 1: 1, 2: 2, 4: 3, 3: 4, 5: 5, 6: 6, 7: 7}
+
+
+def flip(device, bits):
+    core, side_x, side_y = device % 2, (device // 2) % 2, device // 4
+    for bit, there in ((1, 1 - 2 * core), (2, 2 - 4 * side_x), (4, 4 - 8 * side_y)):
+        if bits & bit:
+            device = device + there
+    return device
+
+
+class PlacedExchange:
+    axis = "grp"
+    sem_count = 8
+
+    def __init__(self, out_shape, source_view):
+        self.out_shape, self.source_view = out_shape, source_view
+
+    def peers(self, grp, seq):
+        for bits in range(1, 8):
+            yield flip(grp, bits), seq
+
+    def start(self, source, target, sems, grp, seq):
+        self.own = pltpu.make_async_copy(
+            self.source_view(source, grp), target.at[0], sems[0].at[0]
+        )
+        self.own.start()
+        self.copies = []
+        for bits in range(1, 8):
+            there = flip(grp, bits)
+            copy = remote(
+                self.source_view(source, there), target.at[PLACES[bits]], sems, bits, (there, seq)
+            )
+            copy.start()
+            self.copies.append(copy)
+
+    def forward(self):
+        return iter(())
+
+    def finish(self):
+        for copy in self.copies:
+            copy.wait()
+        self.own.wait()
 
 
 class Exchange:
@@ -473,7 +715,7 @@
             )
 
     def forward(self):
-        pass
+        return iter(())
 
     def finish(self):
         for copy in self.due:
@@ -487,83 +729,225 @@
     axis = "grp"
     sem_count = 14
 
-    def __init__(self, out_shape, source_view, target_view, half_of):
-        self.out_shape = out_shape
+    def __init__(self, out_shape, source_view, target_view, half_of, placed):
+        self.out_shape, self.placed = out_shape, placed
         self.source_view, self.target_view, self.half_of = source_view, target_view, half_of
 
-    def around(self, grp):
-        core, across_x, across_y = grp % 2, (grp // 2) % 2, grp // 4
-        return grp + 1 - 2 * core, grp + 2 - 4 * across_x, grp + 4 - 8 * across_y
-
     def peers(self, grp, seq):
-        for other in self.around(grp):
-            yield other, seq
-
-    def start(self, source, target, sems, grp, seq):
-        core, side_x, side_y = self.around(grp)
-
-        def part(block, piece):
-            view = self.target_view(target, block)
+        for bits in (1, 2, 4):
+            yield flip(grp, bits), seq
+
+    def start(self, source, target, sems, grp, seq, begin=True):
+        def part(device, bits, piece):
+            view = self.target_view(target, PLACES[bits] if self.placed else flip(device, bits))
             return view if piece == "all" else self.half_of(view, piece == "b")
 
         def own(piece):
             view = self.source_view(source, grp)
             return view if piece == "all" else self.half_of(view, piece == "b")
 
-        def across(block):
-            return self.around(self.around(block)[1])[2]
-
-        def make(at, block, piece, via, first=False):
-            view = own(piece) if first else part(block, piece)
-            return remote(view, part(block, piece), sems, at, (via, seq))
-
-        self.out = [
-            make(1, grp, "a", side_x, True),
-            make(2, grp, "b", side_x, True),
-            make(3, side_y, "b", side_x),
-            make(4, grp, "b", side_y, True),
-            make(5, grp, "a", side_y, True),
-            make(6, side_x, "a", side_y),
-            make(7, grp, "all", core, True),
-            make(8, side_x, "a", core),
-            make(9, side_x, "b", core),
-            make(10, side_y, "b", core),
-            make(11, side_y, "a", core),
-            make(12, across(grp), "a", core),
-            make(13, across(grp), "b", core),
-        ]
-        self.due = [
-            make(1, side_x, "a", side_x),
-            make(2, side_x, "b", side_x),
-            make(3, across(grp), "b", side_x),
-            make(4, side_y, "b", side_y),
-            make(5, side_y, "a", side_y),
-            make(6, across(grp), "a", side_y),
-            make(7, core, "all", core),
-            make(8, self.around(core)[1], "a", core),
-            make(9, self.around(core)[1], "b", core),
-            make(10, self.around(core)[2], "b", core),
-            make(11, self.around(core)[2], "a", core),
-            make(12, across(core), "a", core),
-            make(13, across(core), "b", core),
-        ]
-        self.kept = pltpu.make_async_copy(own("all"), part(grp, "all"), sems[0].at[0])
+        self.out, self.due = [None], [None]
+        for via, here, there, piece in (
+            (2, 0, 2, "a"),
+            (2, 0, 2, "b"),
+            (2, 4, 6, "b"),
+            (4, 0, 4, "b"),
+            (4, 0, 4, "a"),
+            (4, 2, 6, "a"),
+            (1, 0, 1, "all"),
+            (1, 2, 3, "a"),
+            (1, 2, 3, "b"),
+            (1, 4, 5, "b"),
+            (1, 4, 5, "a"),
+            (1, 6, 7, "a"),
+            (1, 6, 7, "b"),
+        ):
+            device = flip(grp, via)
+            view = own(piece) if here == 0 else part(grp, here, piece)
+            at = len(self.out)
+            self.out.append(remote(view, part(device, there, piece), sems, at, (device, seq)))
+            self.due.append(remote(view, part(grp, there, piece), sems, at, (device, seq)))
+        self.kept = pltpu.make_async_copy(own("all"), part(grp, 0, "all"), sems[0].at[0])
+        if begin:
+            self.begin()
+
+    def begin(self):
         self.kept.start()
         for at in (1, 4, 2, 5, 7):
-            self.out[at - 1].start()
+            self.out[at].start()
+
+    def pass_on(self, came):
+        self.due[came].wait_recv()
+        for at in {1: (6, 8), 4: (3, 10), 2: (9,), 5: (11,), 6: (12,), 3: (13,)}[came]:
+            self.out[at].start()
 
     def forward(self):
-        for came, then in ((1, (6, 8)), (4, (3, 10)), (2, (9,)), (5, (11,)), (6, (12,)), (3, (13,))):
-            self.due[came - 1].wait_recv()
-            for at in then:
-                self.out[at - 1].start()
+        for pair in ((1, 4), (2, 5), (6, 3)):
+            for came in pair:
+                self.pass_on(came)
+            yield
 
     def finish(self):
-        for copy in self.due[6:]:
+        for copy in self.due[7:]:
             copy.wait_recv()
-        for copy in self.out:
+        for copy in self.out[1:]:
             copy.wait_send()
         self.kept.wait()
+
+
+def add_rows(total, first, second):
+    step = 32
+
+    def some(at, _):
+        rows = pl.ds(pl.multiple_of(at * step, step), step)
+        total[rows, :] = (
+            first[rows, :].astype(jnp.float32) + second[rows, :].astype(jnp.float32)
+        ).astype(total.dtype)
+        return 0
+
+    lax.fori_loop(0, total.shape[0] // step, some, 0)
+
+
+class PlaneSum:
+    axis = "grp"
+    sem_count = 15
+
+    def __init__(self, rows, columns):
+        self.rows, self.columns = rows, columns
+        self.out_shape = (rows, columns)
+
+    def scratch(self):
+        low = jnp.bfloat16
+        shape = (self.rows, self.columns)
+        half = (self.rows // 2, self.columns)
+        return [
+            pltpu.VMEM((4, *shape), low),
+            pltpu.VMEM((4, *shape), low),
+            pltpu.VMEM((2, *half), low),
+            pltpu.VMEM((2, *shape), low),
+        ]
+
+    def peers(self, grp, seq):
+        for bits in (1, 2, 4):
+            yield flip(grp, bits), seq
+
+    def start(self, source, target, sems, grp, seq, scratch):
+        self.target = target
+        self.mine, self.core_in, self.halves, self.wholes = scratch
+        core, side_x, side_y = [(flip(grp, bits), seq) for bits in (1, 2, 4)]
+        half = self.rows // 2
+        self.low, self.high = low, high = pl.ds(0, half), pl.ds(half, half)
+        mine, halves, wholes = self.mine, self.halves, self.wholes
+        self.copies = [
+            remote(source.at[PLACES[bits]], self.core_in.at[at], sems, at, core)
+            for at, bits in enumerate((7, 3, 5, 1))
+        ] + [
+            remote(mine.at[0, low], halves.at[0], sems, 4, side_x),
+            remote(mine.at[0, high], halves.at[1], sems, 5, side_y),
+            remote(mine.at[1, low], wholes.at[0, low], sems, 6, side_x),
+            remote(mine.at[2, high], wholes.at[1, high], sems, 7, side_y),
+            remote(mine.at[1, high], wholes.at[0, high], sems, 8, side_x),
+            remote(mine.at[2, low], wholes.at[1, low], sems, 9, side_y),
+        ]
+        self.loads = [
+            pltpu.make_async_copy(source.at[PLACES[bits]], mine.at[at], sems[0].at[10 + at])
+            for at, bits in enumerate((6, 2, 4, 0))
+        ]
+        self.store = pltpu.make_async_copy(mine.at[3], target, sems[0].at[14])
+        for copy in self.copies[:4] + self.loads:
+            copy.start()
+
+    def first_sums(self):
+        for came, then in ((0, (4, 5)), (1, (6,)), (2, (7,)), (3, ())):
+            self.copies[came].wait_recv()
+            self.loads[came].wait()
+            add_rows(self.mine.at[came], self.mine.at[came], self.core_in.at[came])
+            for at in then:
+                self.copies[at].start()
+
+    def forward(self):
+        mine, low, high = self.mine, self.low, self.high
+        yield
+        self.copies[5].wait_recv()
+        add_rows(mine.at[1, high], mine.at[1, high], self.halves.at[1])
+        self.copies[8].start()
+        self.copies[4].wait_recv()
+        add_rows(mine.at[2, low], mine.at[2, low], self.halves.at[0])
+        self.copies[9].start()
+
+    def finish(self):
+        mine = self.mine
+        for at, side, rows in ((6, 0, self.low), (7, 1, self.high), (8, 0, self.high), (9, 1, self.low)):
+            self.copies[at].wait_recv()
+            add_rows(mine.at[3, rows], mine.at[3, rows], self.wholes.at[side, rows])
+        self.store.start()
+        for copy in self.copies:
+            copy.wait_send()
+        self.store.wait()
+
+
+class LineGather:
+    axis = "seq"
+
+    def __init__(self, shape):
+        self.count = lax.axis_size("seq")
+        self.out_shape = (self.count, *shape)
+        self.sem_count = 2 * self.count
+
+    def peers(self, grp, seq):
+        for step in range(1, self.count):
+            yield grp, (seq + step) % self.count
+
+    def start(self, source, target, sems, grp, seq):
+        self.seq, self.sems = seq, sems
+        self.own = pltpu.make_async_copy(source, target.at[seq], sems[0].at[0])
+        self.own.start()
+
+        def make(away, up):
+            there = (seq + (1 if up else self.count - 1)) % self.count
+            block = (seq + (self.count - away if up else away)) % self.count
+            view = source if away == 0 else target.at[block]
+            at = 1 + away if up else self.count + away
+            return remote(view, target.at[block], sems, at, (grp, there))
+
+        def came(away, up):
+            block = (seq + (self.count - away if up else away)) % self.count
+            at = away if up else self.count + away - 1
+            side = (seq + (self.count - 1 if up else 1)) % self.count
+            return remote(target.at[block], target.at[block], sems, at, (grp, side))
+
+        self.make, self.came = make, came
+        self.has = lambda away, up: (seq - away >= 0) if up else (seq + away < self.count)
+        self.last = lambda up: (seq + 1 < self.count) if up else (seq >= 1)
+        for up in (True, False):
+
+            @pl.when(self.last(up))
+            def _():
+                make(0, up).start()
+
+    def forward(self):
+        for away in range(1, self.count):
+            for up in (True, False):
+
+                @pl.when(self.has(away, up))
+                def _():
+                    self.came(away, up).wait_recv()
+                    if away < self.count - 1:
+
+                        @pl.when(self.last(up))
+                        def _():
+                            self.make(away, up).start()
+
+            yield
+
+    def finish(self):
+        for away in range(self.count - 1):
+            for up in (True, False):
+
+                @pl.when(self.has(away, up) & self.last(up))
+                def _():
+                    self.make(away, up).wait_send()
+        self.own.wait()
 
 
 def half_rows(axis, height):
@@ -582,16 +966,30 @@
     return ref.at[index]
 
 
-def gather_plane(shape, split=0, source_view=whole, target_view=block_of, out_shape=None):
+def gather_plane(
+    shape, split=0, source_view=whole, target_view=block_of, out_shape=None, placed=False
+):
     out_shape = out_shape or (lax.axis_size("grp"), *shape)
     if lax.axis_size("grp") == 8:
-        return PlaneGather(out_shape, source_view, target_view, half_rows(split, shape[split] // 2))
+        halves = half_rows(split, shape[split] // 2)
+        return PlaneGather(out_shape, source_view, target_view, halves, placed)
     return Exchange("grp", out_shape, source_view, target_view)
+
+
+def hand_on(tasks):
+    going = [task.forward() for task in tasks]
+    while going:
+        going = [steps for steps in going if next(steps, going) is not going]
 
 
 def exchange_kernel(tasks, wires, arrays, outputs, *refs):
     sources, targets = refs[:arrays], refs[arrays : arrays + outputs]
-    sems = refs[arrays + outputs :]
+    refs = list(refs[arrays + outputs :])
+    sems, scratch = [], []
+    for task in tasks:
+        sems.append((refs.pop(0), refs.pop(0)))
+        held = len(task.scratch()) if isinstance(task, PlaneSum) else 0
+        scratch.append([refs.pop(0) for _ in range(held)])
     grp, seq = lax.axis_index("grp"), lax.axis_index("seq")
     barrier = pltpu.get_barrier_semaphore()
     axes = {"grp": [], "seq": []}
@@ -607,21 +1005,24 @@
     def start(at):
         after, source, target = wires[at]
         source = targets[source] if after is not None else sources[source]
-        tasks[at].start(source, targets[target], sems[2 * at : 2 * at + 2], grp, seq)
+        more = (scratch[at],) if scratch[at] else ()
+        tasks[at].start(source, targets[target], sems[at], grp, seq, *more)
 
     open_tasks = list(range(len(tasks)))
     first = [at for at in open_tasks if wires[at][0] is None]
     for at in first:
         start(at)
     for at in first:
-        tasks[at].forward()
+        if isinstance(tasks[at], PlaneSum):
+            tasks[at].first_sums()
+    hand_on([tasks[at] for at in first])
     for at in open_tasks[:]:
         after = wires[at][0]
         if after is not None:
             tasks[after].finish()
             open_tasks.remove(after)
             start(at)
-            tasks[at].forward()
+            hand_on([tasks[at]])
     for at in open_tasks:
         tasks[at].finish()
 
@@ -646,6 +1047,8 @@
     scratch = []
     for task in tasks:
         scratch += [pltpu.SemaphoreType.DMA((task.sem_count,))] * 2
+        if isinstance(task, PlaneSum):
+            scratch += task.scratch()
     return pl.pallas_call(
         functools.partial(exchange_kernel, tasks, wires, len(arrays), len(shapes)),
         in_specs=[pl.BlockSpec(memory_space=pl.ANY)] * len(arrays),
@@ -676,10 +1079,15 @@
     return task, array
 
 
-def split_columns(axis, array):
+def split_columns(axis, array, placed=False):
     count = lax.axis_size(axis)
     rows, columns = array.shape
     width = columns // count
+    if placed and count == 8:
+        task = PlacedExchange(
+            (count, rows, width), lambda ref, index: columns_of(ref, index, width)
+        )
+        return task, array
     task = Exchange(
         axis,
         (count, rows, width),
@@ -689,35 +1097,34 @@
     return task, array
 
 
-def add_rows(total, first, second):
-    step = 32
-
-    def some(at, _):
-        rows = pl.ds(pl.multiple_of(at * step, step), step)
-        total[rows, :] = (
-            first[rows, :].astype(jnp.float32) + second[rows, :].astype(jnp.float32)
-        ).astype(total.dtype)
-        return 0
-
-    lax.fori_loop(0, total.shape[0] // step, some, 0)
-
-
 def plane_sum_kernel(
-    part_ref, total_ref, core_in, chip, half_x, half_y, whole_x, whole_y, send_sems, recv_sems
+    part_ref, gate_ref, up_ref, x_ref, total_ref, gate_out, up_out, core_in, chip, half_x, half_y,
+    whole_x, whole_y, x_block, stage, send_sems, recv_sems, x_sems, out_sems,
 ):
     grp, seq = lax.axis_index("grp"), lax.axis_index("seq")
-
-    def around(device):
-        core, across_x, across_y = device % 2, (device // 2) % 2, device // 4
-        return device + 1 - 2 * core, device + 2 - 4 * across_x, device + 4 - 8 * across_y
-
-    def order(device):
-        _, side_x, side_y = around(device)
-        return around(side_x)[2], side_x, side_y, device
-
-    core, side_x, side_y = around(grp)
+    core, side_x, side_y = [flip(grp, bits) for bits in (1, 2, 4)]
+    blocks = [PLACES[bits] for bits in (6, 2, 4, 0)]
+    core_blocks = [PLACES[bits] for bits in (7, 3, 5, 1)]
     half = total_ref.shape[0] // 2
     low, high = pl.ds(0, half), pl.ds(half, half)
+    cols = gate_ref.shape[0]
+    rows = x_block.shape[2]
+    count = x_ref.shape[1] // rows
+
+    def x_copy(at):
+        view = x_ref.at[:, pl.ds(pl.multiple_of(at * rows, rows), rows)]
+        return pltpu.make_async_copy(view, x_block.at[at % 2], x_sems.at[at % 2])
+
+    def out_copies(at):
+        place = pl.ds(pl.multiple_of(at * cols, cols), cols)
+        return [
+            pltpu.make_async_copy(
+                stage.at[which, at % 2], out.at[place], out_sems.at[which, at % 2]
+            )
+            for which, out in enumerate((gate_out, up_out))
+        ]
+
+    x_copy(0).start()
     barrier = pltpu.get_barrier_semaphore()
     for device in (core, side_x, side_y):
         pl.semaphore_signal(barrier, inc=1, device_id=(device, seq), device_id_type=MESH)
@@ -726,7 +1133,7 @@
     sems = (send_sems, recv_sems)
     copies = [
         remote(part_ref.at[block], core_in.at[at], sems, at, (core, seq))
-        for at, block in enumerate(order(core))
+        for at, block in enumerate(core_blocks)
     ]
     copies += [
         remote(chip.at[0, low], half_x, sems, 4, (side_x, seq)),
@@ -738,40 +1145,84 @@
     ]
     for copy in copies[:4]:
         copy.start()
-    blocks = order(grp)
-    for at, then in ((0, (4, 5)), (1, (6,)), (2, (7,))):
-        copies[at].wait_recv()
-        add_rows(chip.at[at], part_ref.at[blocks[at]], core_in.at[at])
-        for start in then:
-            copies[start].start()
-    copies[5].wait_recv()
-    add_rows(chip.at[1, high], chip.at[1, high], half_y)
-    copies[8].start()
-    copies[4].wait_recv()
-    add_rows(chip.at[2, low], chip.at[2, low], half_x)
-    copies[9].start()
+
+    def step(at, _):
+        @pl.when(at == 1)
+        def _():
+            for came, then in ((0, (4, 5)), (1, (6,)), (2, (7,))):
+                copies[came].wait_recv()
+                add_rows(chip.at[came], part_ref.at[blocks[came]], core_in.at[came])
+                for start in then:
+                    copies[start].start()
+
+        @pl.when(at == count - 1)
+        def _():
+            copies[5].wait_recv()
+            add_rows(chip.at[1, high], chip.at[1, high], half_y)
+            copies[8].start()
+            copies[4].wait_recv()
+            add_rows(chip.at[2, low], chip.at[2, low], half_x)
+            copies[9].start()
+
+        x_copy(at).wait()
+
+        @pl.when(at + 1 < count)
+        def _():
+            x_copy(at + 1).start()
+
+        @pl.when(at >= 2)
+        def _():
+            for copy in out_copies(at - 2):
+                copy.wait()
+
+        for which, ref in enumerate((gate_ref, up_ref)):
+            stage[which, at % 2] = jnp.dot(
+                ref[...], x_block[at % 2], preferred_element_type=jnp.float32
+            ).astype(stage.dtype)
+        for copy in out_copies(at):
+            copy.start()
+        return 0
+
+    lax.fori_loop(0, count, step, 0)
     copies[3].wait_recv()
     add_rows(total_ref, part_ref.at[blocks[3]], core_in.at[3])
-    for at, came in ((6, whole_x.at[low]), (7, whole_y.at[high]), (8, whole_x.at[high]), (9, whole_y.at[low])):
+    for at, came, rows_at in (
+        (6, whole_x, low),
+        (7, whole_y, high),
+        (8, whole_x, high),
+        (9, whole_y, low),
+    ):
         copies[at].wait_recv()
-        rows = low if at in (6, 9) else high
-        add_rows(total_ref.at[rows], total_ref.at[rows], came)
+        add_rows(total_ref.at[rows_at], total_ref.at[rows_at], came.at[rows_at])
     for copy in copies:
         copy.wait_send()
-
-
-def plane_sum(number, part):
+    for at in (count - 2, count - 1):
+        for copy in out_copies(at):
+            copy.wait()
+
+
+def plane_sum(number, part, gate_grad, up_grad, x, seq_count):
     count = lax.axis_size("grp")
     rows_all, columns = part.shape
     rows = rows_all // count
     if count != 8:
-        return lax.psum_scatter(part, "grp", scatter_dimension=0, tiled=True).astype(jnp.float32)
+        total = lax.psum_scatter(part, "grp", scatter_dimension=0, tiled=True)
+        return (
+            total.astype(jnp.float32),
+            weight_grad(gate_grad, x, seq_count),
+            weight_grad(up_grad, x, seq_count),
+        )
     low = jnp.bfloat16
+    cols, tokens_all = gate_grad.shape
+    width = x.shape[1] // seq_count
+    vmem = pl.BlockSpec(memory_space=pltpu.VMEM)
+    hbm = pl.BlockSpec(memory_space=pl.ANY)
+    grads = jax.ShapeDtypeStruct((seq_count * cols, width), low)
     return pl.pallas_call(
         plane_sum_kernel,
-        in_specs=[pl.BlockSpec(memory_space=pltpu.VMEM)],
-        out_specs=pl.BlockSpec(memory_space=pltpu.VMEM),
-        out_shape=jax.ShapeDtypeStruct((rows, columns), jnp.float32),
+        in_specs=[vmem, vmem, vmem, hbm],
+        out_specs=[vmem, hbm, hbm],
+        out_shape=[jax.ShapeDtypeStruct((rows, columns), jnp.float32), grads, grads],
         scratch_shapes=[
             pltpu.VMEM((4, rows, columns), low),
             pltpu.VMEM((3, rows, columns), low),
@@ -779,15 +1230,19 @@
             pltpu.VMEM((rows // 2, columns), low),
             pltpu.VMEM((rows, columns), low),
             pltpu.VMEM((rows, columns), low),
+            pltpu.VMEM((2, tokens_all, width), low),
+            pltpu.VMEM((2, 2, cols, width), low),
             pltpu.SemaphoreType.DMA((10,)),
             pltpu.SemaphoreType.DMA((10,)),
+            pltpu.SemaphoreType.DMA((2,)),
+            pltpu.SemaphoreType.DMA((2, 2)),
         ],
         compiler_params=pltpu.CompilerParams(
-            collective_id=number, has_side_effects=True, vmem_limit_bytes=40 * 2**20
+            collective_id=number, has_side_effects=True, vmem_limit_bytes=56 * 2**20
         ),
         cost_estimate=SMALL_COST,
         name="plane_sum",
-    )(part.reshape(count, rows, columns))
+    )(part.reshape(count, rows, columns), gate_grad, up_grad, x)
 
 
 def local(
@@ -847,51 +1302,44 @@
             source_view=lambda ref, index: ref.at[:, pl.ds(at * half_block, half_block)],
         )
 
-    def attn_half(at):
-        return gather_plane(
-            (seq_count, half_sub, output_end),
-            target_view=lambda ref, index: ref.at[:, at, index],
-            out_shape=(seq_count, halves, grp_count, half_sub, output_end),
+    flat = (grp_count * slots_here, -1, tile_width)
+    work = [(weight_half(0), weights_low)]
+    if halves == 2:
+        late_rows = Exchange(
+            "grp",
+            (grp_count, slots_here, half_sub, tile_width),
+            lambda ref, index: ref.at[:, pl.ds(half_block + index * half_sub, half_sub)],
+            block_of,
         )
-
-    flat = (grp_count * slots_here, half_block, tile_width)
-    (tiles,) = exchange(0, [(weight_half(0), weights_low)])
-    feed_rows, attn_rows = pick(tiles.reshape(flat), feed_slots, attn_slots)
+        work.append((late_rows, weights_low))
+    tiles = [part.reshape(flat) for part in exchange(0, work)]
+    attn_rows = pick(attn_slots, tiles, half_sub).reshape(halves, half_sub, output_end)
+    if grp_count == 8 and seq_count == 4:
+        work = [(LineGather(attn_rows.shape), attn_rows)]
+    else:
+        work = [gather_axis("seq", attn_rows)]
+    if halves == 2:
+        work.append((weight_half(1), weights_low))
+    attn_seq, *more = exchange(1, work)
+    tiles = tiles[:1] + [part.reshape(flat) for part in more]
+    feed_rows = pick(feed_slots, tiles)
     feed_parts = [lax.all_gather(feed_rows, "seq", axis=0, tiled=False)]
-    if halves == 2:
-        tiles, attn_first = exchange(
-            1, [(weight_half(1), weights_low), gather_axis("seq", attn_rows)]
-        )
-        feed_rows, attn_rows = pick(tiles.reshape(flat), feed_slots, attn_slots)
-        feed_parts.append(lax.all_gather(feed_rows, "seq", axis=0, tiled=False))
-        attn_weights, _, normed_plane = exchange(
-            2,
-            [
-                (attn_half(0), attn_first),
-                gather_axis("seq", attn_rows),
-                (attn_half(1), 1, 0),
-                (gather_plane(normed.shape), normed),
-            ],
-        )
-    else:
-        _, attn_weights, normed_plane = exchange(
-            2,
-            [
-                gather_axis("seq", attn_rows),
-                (attn_half(0), 0),
-                (gather_plane(normed.shape), normed),
-            ],
-        )
-    attn_weights, feed_parts[0] = lax.optimization_barrier((attn_weights, feed_parts[0]))
+    attn_plane = gather_plane(
+        attn_seq.shape,
+        target_view=lambda ref, index: ref.at[:, :, index],
+        out_shape=(seq_count, halves, grp_count, half_sub, output_end),
+    )
+    (attn_weights,) = exchange(2, [(attn_plane, attn_seq)])
     attn_weights = attn_weights.reshape(MODEL_WIDTH, output_end)
 
     projected = project(normed, attn_weights, tables)
-    pairs, segments, cot_plane = exchange(
+    pairs, segments, cot_plane, normed_plane = exchange(
         3,
         [
             gather_axis("seq", projected[:, query_cols:]),
             gather_axis("seq", segment_ids.reshape(-1, tile_width)),
-            (gather_plane(cotangent.shape), cotangent),
+            (gather_plane(cotangent.shape, placed=True), cotangent),
+            (gather_plane(normed.shape, placed=True), normed),
         ],
     )
     first_key = seq_here * rows_here - first_place
@@ -906,24 +1354,37 @@
     inverse_two = lax.rsqrt(jnp.mean(hidden * hidden, axis=-1, keepdims=True) + NORM_EPS)
     normed_two = (hidden * inverse_two * gains[1]).astype(jnp.bfloat16)
 
-    (second_plane,) = exchange(4, [(gather_plane(normed_two.shape), normed_two)])
-    second_plane = second_plane.reshape(-1, MODEL_WIDTH)
     cot_plane = cot_plane.reshape(-1, MODEL_WIDTH)
-    real_cols = jnp.clip((hidden_tiles - grp_here * share) * tile_width, 0, share_cols)
-    activated, gate_grad, up_grad, two_part, feed_part = feed_forward(
-        real_cols.reshape(1), second_plane, cot_plane, feed_parts, seq_count
-    )
-    down_grad = contract(cot_plane, activated).astype(jnp.bfloat16)
-    down_grad, gate_grad, up_grad = lax.optimization_barrier((down_grad, gate_grad, up_grad))
+    normed_plane = normed_plane.reshape(-1, MODEL_WIDTH)
+    real_cols = jnp.clip((hidden_tiles - grp_here * share) * tile_width, 0, share_cols).reshape(1)
+    if grp_count == 8:
+        gate_grad, up_grad, two_part, feed_part, second_plane, context_plane, down_grad = (
+            feed_gather(
+                4, real_cols, normed_two, context, cot_plane, feed_parts[0], seq_count
+            )
+        )
+        second_plane = second_plane.reshape(-1, MODEL_WIDTH)
+    else:
+        second_plane, context_plane = exchange(
+            4,
+            [
+                (gather_plane(normed_two.shape), normed_two),
+                (gather_plane(context.shape), context),
+            ],
+        )
+        second_plane = second_plane.reshape(-1, MODEL_WIDTH)
+        activated, gate_grad, up_grad, two_part, feed_part = feed_forward(
+            real_cols, second_plane, cot_plane, feed_parts, seq_count
+        )
+        down_grad = weight_grad(activated, cot_plane, seq_count)
+    context_plane = context_plane.reshape(-1, MODEL_WIDTH)
+    down_grad, two_part = lax.optimization_barrier((down_grad, two_part))
     down_grad = lax.psum_scatter(down_grad, "seq", scatter_dimension=0, tiled=True)
-    gate_weight_grad = contract(second_plane, gate_grad).astype(jnp.bfloat16)
-    up_weight_grad = contract(second_plane, up_grad).astype(jnp.bfloat16)
-    two_part, feed_part, gate_weight_grad, up_weight_grad = lax.optimization_barrier(
-        (two_part, feed_part, gate_weight_grad, up_weight_grad)
+    norm_two_grad, gate_weight_grad, up_weight_grad = plane_sum(
+        5, two_part, gate_grad, up_grad, second_plane, seq_count
     )
     gate_weight_grad = lax.psum_scatter(gate_weight_grad, "seq", scatter_dimension=0, tiled=True)
     up_weight_grad = lax.psum_scatter(up_weight_grad, "seq", scatter_dimension=0, tiled=True)
-    norm_two_grad = plane_sum(5, two_part)
 
     out_grad = cotangent.astype(jnp.float32)
     gain_two_term = jnp.sum(norm_two_grad * hidden * inverse_two, axis=0)
@@ -936,7 +1397,6 @@
     )
     branch_grad = hidden_grad.astype(jnp.bfloat16)
     context_grad = times_transpose(branch_grad, attn_weights[:, value_end:]).astype(jnp.bfloat16)
-    context_grad, down_grad = lax.optimization_barrier((context_grad, down_grad))
     query_grad, pair_part = attend_back(
         at,
         projected,
@@ -952,17 +1412,16 @@
         pair_part = lax.dynamic_update_slice_in_dim(
             jnp.zeros((seq_count * rows_here, 2 * HD), pair_part.dtype), pair_part, first_key, 0
         )
-    pair_parts, query_share, branch_share, context_plane = exchange(
+    pair_parts, query_share, branch_share = exchange(
         6,
         [
             split_rows("seq", pair_part),
-            split_columns("grp", query_grad),
-            split_columns("grp", branch_grad),
-            (gather_plane(context.shape), context),
+            split_columns("grp", query_grad, placed=True),
+            split_columns("grp", branch_grad, placed=True),
         ],
     )
     pair_grad = jnp.sum(pair_parts.astype(jnp.float32), axis=0).astype(jnp.bfloat16)
-    pair_grad, gate_weight_grad = lax.optimization_barrier((pair_grad, gate_weight_grad))
+    pair_grad, down_grad = lax.optimization_barrier((pair_grad, down_grad))
     projected_grad = jnp.concatenate([query_grad, pair_grad], axis=1)
     norm_one_grad = times_transpose(projected_grad, attn_weights[:, :value_end])
     gain_one_term = jnp.sum(norm_one_grad * tok_float * inverse_one, axis=0)
@@ -973,39 +1432,41 @@
         * inverse_one**3
         * jnp.mean(tok_float * gains[0] * norm_one_grad, axis=-1, keepdims=True)
     )
-    normed_plane = normed_plane.reshape(-1, MODEL_WIDTH)
-    context_plane = context_plane.reshape(-1, MODEL_WIDTH)
-    query_weight_grad = contract(normed_plane, query_share.reshape(-1, share_width))
-    out_weight_grad = contract(context_plane, branch_share.reshape(-1, share_width))
+    query_weight_grad = contract(query_share.reshape(-1, share_width), normed_plane)
+    out_weight_grad = contract(branch_share.reshape(-1, share_width), context_plane)
     pair_weight_grad = contract(normed, pair_grad).astype(jnp.bfloat16)
-    shares = jnp.concatenate([query_weight_grad, out_weight_grad], axis=1).astype(jnp.bfloat16)
+    shares = jnp.concatenate([query_weight_grad, out_weight_grad], axis=0).astype(jnp.bfloat16)
     shares, down_grad, gate_weight_grad = lax.optimization_barrier(
         (shares, down_grad, gate_weight_grad)
     )
-    feed_shape = (rows_block, share_cols)
+    feed_shape = (share_cols, rows_block)
     pair_task = Exchange(
         "grp",
         (grp_count, seq_count, sub_rows, 2 * HD),
         lambda ref, index: ref.at[:, index],
         block_of,
     )
-    share_parts, pair_parts, gain_parts, down_plane, gate_plane = exchange(
-        7,
-        [
-            split_rows("seq", shares),
-            (pair_task, pair_weight_grad.reshape(seq_count, grp_count, sub_rows, 2 * HD)),
-            gather_axis("seq", jnp.stack([gain_one_term, gain_two_term])),
-            (gather_plane(feed_shape), down_grad),
-            (gather_plane(feed_shape), gate_weight_grad),
-        ],
-    )
+    work = [
+        split_columns("seq", shares),
+        (pair_task, pair_weight_grad.reshape(seq_count, grp_count, sub_rows, 2 * HD)),
+        gather_axis("seq", jnp.stack([gain_one_term, gain_two_term])),
+        (gather_plane(feed_shape), down_grad),
+        (gather_plane(feed_shape), gate_weight_grad),
+    ]
+    if grp_count == 8:
+        feed_part = feed_part.reshape(grp_count, rows_here, MODEL_WIDTH)
+        work.append((PlaneSum(rows_here, MODEL_WIDTH), feed_part))
+    share_parts, pair_parts, gain_parts, down_plane, gate_plane, *feed_out = exchange(7, work)
+    if grp_count == 8:
+        feed_out = feed_out[0]
+    else:
+        feed_out = lax.psum_scatter(feed_part, "grp", scatter_dimension=0, tiled=True)
+    block_out = (hidden + feed_out.astype(jnp.float32)).astype(jnp.bfloat16)
     gain_seq = jnp.sum(gain_parts, axis=0)
     shares = jnp.sum(share_parts.astype(jnp.float32), axis=0).astype(jnp.bfloat16)
     pair_parts = jnp.sum(pair_parts.astype(jnp.float32), axis=0).astype(jnp.bfloat16)
     pair_task = Exchange("seq", pair_parts.shape, block_of, block_of)
-    shares, up_weight_grad, feed_part = lax.optimization_barrier((shares, up_weight_grad, feed_part))
-    feed_out = lax.psum_scatter(feed_part, "grp", scatter_dimension=0, tiled=True)
-    block_out = (hidden + feed_out.astype(jnp.float32)).astype(jnp.bfloat16)
+    shares, up_weight_grad = lax.optimization_barrier((shares, up_weight_grad))
     _, pair_plane, up_plane, share_plane, gain_parts = exchange(
         8,
         [

time: 844 us -> 800 us (0.948)
  matrix products: 63.9 us -> 34 us
  Pallas kernels: 706 us -> 693 us
  local copies, waits for them, and re-layouts: 22.5 us -> 12.6 us
    pallas_call x8 -> x7, Pallas kernels: 545 us -> 494 us  [exchange(): pl.pallas_call(functools.partial(exchange_kernel, tasks, wires, len(array...]
    pallas_call x2, Pallas kernels: 90.6 us -> 128 us  [the longest x1 80.9 us: feed_gather(): pl.pallas_call(functools.partial(feed_gather_kernel, first, second), grid...]
    dot_general x6 -> x3, matrix products: 45.7 us -> 13.4 us  [contract(): lax.dot_general(left_side, right_side, (((0,), (0,)), ((), ())), preferre...]
    unnamed x90 -> x60, local copies, waits for them, and re-layouts: 14.8 us -> 5.16 us
  transfers between devices with their start and end apart: 6 -> 4, of which waited for: 0 -> 1; matrix products, arithmetic and copies ran while one was open for 10% -> 8% of each run, Pallas kernels for 72% -> 48%
where the time goes in v5:
time: 800 us; the launch traced here: 788 us
  Pallas kernels  693 us (87%)
  matrix products  34 us (4%)
  other arithmetic  30.7 us (4%)
  between operations  14.8 us (2%)
  local copies, waits for them, and re-layouts  12.6 us (2%)
    pallas_call x7, Pallas kernels, exchange(): pl.pallas_call(functools.partial(exchange_kernel, tasks, wires, len(array...  494 us
    pallas_call x1, Pallas kernels, feed_gather(): pl.pallas_call(functools.partial(feed_gather_kernel, first, second), grid...  80.9 us
    pallas_call x1, Pallas kernels, plane_sum(): pl.pallas_call(plane_sum_kernel, in_specs=[vmem, vmem, vmem, hbm], out_sp...  46.7 us
    pallas_call x1, Pallas kernels, adam(): pl.pallas_call(adam_kernel, grid_spec=pltpu.PrefetchScalarGridSpec(num_sc...  32.4 us
  transfers between devices with their start and end apart: 4, of which 1 were waited for; matrix products, arithmetic and copies ran while one was open for 8% of the time, Pallas kernels for 48%

profile of v5, /device:TPU:0, one launch (start us, length us, event | category | flops | bytes accessed | tf_op | source)
XLA Modules:
  0.0 788.3 jit_solution(2357773467838958497)
XLA Ops:
  7.3 1.2 slice.24.slots_ref
  8.6 1.9 gather_fusion
  10.5 68.3 %exchange.7 = (bf16[8,21,256,128]{3,2,1,0:T(8,128)(2,1)}, bf16[8,21,32,128]{3,2,1,0:T(8,128)(2,1)}) custom-call(bf16[21,512,128]{2,1,0:T(8,128)(2,1)} %refs_1_.3, bf16[21,512,128]{2,1,0:T(8,128)(2,1)} %refs_1_.3), custom_call_target="tpu_custom_call" | custom-call | flops 1 | bytes 1 | tf_op jit(solution)/shard_map/exchange/pallas_call | solution.py:1052
  78.8 3.2 pick.2
  82.0 63.8 %exchange.8 = (bf16[4,2,32,4352]{3,2,1,0:T(8,128)(2,1)}, bf16[8,21,256,128]{3,2,1,0:T(8,128)(2,1)}) custom-call(bf16[2,32,4352]{2,1,0:T(8,128)(2,1)} %bitcast.73, bf16[21,512,128]{2,1,0:T(8,128)(2,1)} %refs_1_.3), custom_call_target="tpu_custom_call" | custom-call | flops 1 | bytes 1 | tf_op jit(solution)/shard_map/exchange/pallas_call | solution.py:1052
  145.8 4.0 pick.3
  149.9 79.5 %exchange.9 = bf16[4,2,8,32,4352]{4,3,2,1,0:T(8,128)(2,1)} custom-call(bf16[4,2,32,4352]{3,2,1,0:T(8,128)(2,1)} %get-tuple-element.58.refs_0_), custom_call_target="tpu_custom_call" | custom-call | flops 1 | bytes 1 | tf_op jit(solution)/shard_map/exchange/pallas_call | solution.py:1052
  229.4 1.9 multiply_sine_fusion
  231.3 1.0 fusion.26
  232.7 1.3 fusion.15.x_ref.refs_3_
  234.0 10.3 %project.1.q_ref = bf16[256,2304]{1,0:T(8,128)(2,1)} custom-call(bf16[256,2048]{1,0:T(8,128)(2,1)} %fusion.15.x_ref.refs_3_, bf16[2048,4352]{1,0:T(8,128)(2,1)} %bitcast.59, f32[256,128]{1,0:T(8,128)} %get-tuple-element.133.cosine_ref, f32[256,128]{1,0:T(8,128)} %get-tuple-element.132.sine_ref), custom_call_target="tpu_custom_call" | custom-call | flops 1 | bytes 1 | tf_op jit(solution)/shard_map/project/pallas_call | solution.py:87
  244.3 1.7 slice.31.refs_0_
  246.0 74.0 %exchange.10 = (bf16[4,256,256]{2,1,0:T(8,128)(2,1)}, s32[4,2,128]{2,1,0:T(2,128)}, bf16[8,256,2048]{2,1,0:T(8,128)(2,1)}, bf16[8,256,2048]{2,1,0:T(8,128)(2,1)}) custom-call(bf16[256,256]{1,0:T(8,128)(2,1)} %slice.31.refs_0_, s32[2,128]{1,0:T(2,128)} %bitcast.56, bf16[256,2048]{1,0:T(8,128)(2,1)} %refs_2_.1, bf16[256,2048]{1,0:T(8,128)(2,1)} %fusion.15.x_ref.refs_3_), custom_call_target="tpu_custom_call" | custom-call | flops 1 | bytes 1 | tf_op jit(solution)/shard_map/exchange/pallas_call | solution.py:1052
  320.0 0.9 copy.24.key_seg_ref
  320.9 1.0 copy-done.1
  322.0 9.1 %attend.1 = (bf16[256,2048]{1,0:T(8,128)(2,1)S(1)}, f32[16,1,256]{2,1,0:T(1,128)S(1)}) custom-call(s32[1]{0:T(128)} %bitcast.at_ref, bf16[256,2304]{1,0:T(8,128)(2,1)S(1)} %copy-done, bf16[1024,256]{1,0:T(8,128)(2,1)S(1)} %bitcast.52, bf16[1024,256]{1,0:T(8,128)(2,1)S(1)} %bitcast.53, s32[1024,1]{1,0:T(8,128)S(1)} %copy.24.key_seg_ref, s32[1,256]{1,0:T(1,128)S(1)} %bitcast.57), custom_call_target="tpu_custom_call" | custom-call | flops 1 | bytes 1 | tf_op jit(solution)/shard_map/attend/pallas_call | solution.py:208
  331.1 6.5 multiply_reduce_fusion.2
  337.6 1.3 copy-done.11
  338.9 1.2 multiply_convert_fusion.own_ref
  340.1 80.9 %feed_gather.1 = (bf16[768,2048]{1,0:T(8,128)(2,1)}, bf16[768,2048]{1,0:T(8,128)(2,1)}, bf16[2048,2048]{1,0:T(8,128)(2,1)}, bf16[2048,2048]{1,0:T(8,128)(2,1)}, ...) custom-call(s32[1]{0:T(128)} %bitcast.11.real_ref, ...), custom_call_target="tpu_custom_call" | custom-call | flops 1 | bytes 1 | tf_op jit(solution)/shard_map/feed_gather/pallas_call | solution.py:453
  421.1 46.7 %plane_sum.1 = (f32[256,2048]{1,0:T(8,128)}, bf16[3072,512]{1,0:T(8,128)(2,1)}, bf16[3072,512]{1,0:T(8,128)(2,1)}) custom-call(bf16[8,256,2048]{2,1,0:T(8,128)(2,1)} %bitcast.70, bf16[768,2048]{1,0:T(8,128)(2,1)} %get-tuple-element.67.gate_ref, bf16[768,2048]{1,0:T(8,128)(2,1)} %get-tuple-element.68.up_ref, bf16[2048,2048]{1,0:T(8,128)(2,1)} %bitcast.71), custom_call_target="tpu_custom_call" | custom-call | flops 1 | bytes 1 | tf_op jit(solution)/shard_map/plane_sum/pallas_call | solution.py:1221
  468.5 1.1 scatter_custom_fusion
  470.4 1.7 pad_maximum_fusion.1
  472.3 2.3 multiply_reduce_fusion
  474.8 2.0 fusion.42
  476.8 6.3 fusion.10.grad_ref
  483.1 11.8 %attend_back.1 = (bf16[256,2048]{1,0:T(8,128)(2,1)S(1)}, bf16[1024,256]{1,0:T(8,128)(2,1)S(1)}) custom-call(s32[1]{0:T(128)} %bitcast.at_ref, bf16[256,2304]{1,0:T(8,128)(2,1)S(1)} %copy-done, bf16[1024,256]{1,0:T(8,128)(2,1)S(1)} %bitcast.54, bf16[1024,256]{1,0:T(8,128)(2,1)S(1)} %bitcast.55, bf16[256,2048]{1,0:T(8,128)(2,1)S(1)} %fusion.10.grad_ref, ...), custom_call_target="tpu_custom_call" | custom-call | flops 1 | bytes 1 | tf_op jit(solution)/shard_map/attend_back/pallas_call | solution.py:226
  494.9 1.0 copy-done.5
  495.9 0.8 copy-done.8
  496.6 46.2 %exchange.11 = (bf16[4,256,256]{2,1,0:T(8,128)(2,1)}, bf16[8,256,256]{2,1,0:T(8,128)(2,1)}, bf16[8,256,256]{2,1,0:T(8,128)(2,1)}) custom-call(bf16[1024,256]{1,0:T(8,128)(2,1)} %copy-done.8, bf16[256,2048]{1,0:T(8,128)(2,1)} %copy-done.5, bf16[256,2048]{1,0:T(8,128)(2,1)} %copy-done.23), custom_call_target="tpu_custom_call" | custom-call | flops 1 | bytes 1 | tf_op jit(solution)/shard_map/exchange/pallas_call | solution.py:1052
  542.8 1.1 reduce_sum.123
  543.9 6.1 fusion.9
  550.1 5.8 fusion.8
  555.9 1.5 pad_maximum_fusion.refs_0_
  557.4 3.4 reduce-scatter.6.cloned.1.call-done.refs_4_
  560.9 7.8 fusion.21
  569.3 1.5 convolution_convert_fusion
  570.8 104.1 %exchange.12 = (bf16[4,512,512]{2,1,0:T(8,128)(2,1)}, bf16[8,4,64,256]{3,2,1,0:T(8,128)(2,1)}, f32[4,2,2048]{2,1,0:T(2,128)}, bf16[8,768,512]{2,1,0:T(8,128)(2,1...) custom-call(bf16[512,2048]{1,0:T(8,128)(2,1)} %pad_maximum_fusion.refs_0_, bf16[4,8,64,256]{3,2,1,0:T(8,128)(2,1)} %bitcast.72, ...), custom_call_target="tpu_custom_call" | custom-call | flops 1 | bytes 1 | tf_op jit(solution)/shard_map/exchange/pallas_call | solution.py:1052
  674.9 2.2 reduce_sum.127.refs_0_
  677.1 2.9 reduce_sum.128.refs_2_
  680.0 2.5 add_convert_fusion
  682.5 0.6 reduce_sum.129.refs_3_
  683.1 58.4 %exchange.13 = (bf16[4,64,256]{2,1,0:T(8,128)(2,1)}, bf16[8,4,64,256]{3,2,1,0:T(8,128)(2,1)}, bf16[8,768,512]{2,1,0:T(8,128)(2,1)}, bf16[8,512,512]{2,1,0:T(8,128)(2,1)}, f32[8,2,2048]{2,1,0:T(2,128)}) custom-call(bf16[4,64,256]{2,1,0:T(8,128)(2,1)} %reduce_sum.127.refs_0_, bf16[768,512]{1,0:T(8,128)(2,1)} %reduce-scatter.8.cloned.1.call-done.refs_1_, ...), custom_call_target="tpu_custom_call" | custom-call | flops 1 | bytes 1 | tf_op jit(solution)/shard_map/exchange/pallas_call | solution.py:1052
  741.6 1.0 reduce_sum.131
  742.5 2.1 reduce_sum.130.pair_ref
  744.7 0.7 divide_subtract_fusion
  745.3 3.5 fusion.19
  748.9 32.4 %adam.1 = (f32[21,512,128]{2,1,0:T(8,128)}, f32[21,512,128]{2,1,0:T(8,128)}, f32[21,512,128]{2,1,0:T(8,128)}) custom-call(s32[6,21]{1,0:T(8,128)} %stack.39.at_ref, bf16[8,768,512]{2,1,0:T(8,128)(2,1)} %get-tuple-element.88.gate_ref, bf16[8,768,512]{2,1,0:T(8,128)(2,1)} %get-tuple-element.95.up_ref, bf16[8,768,512]{2,1,0:T(8,128)(2,1)} %get-tuple-element.96.down_ref, ...), custom_call_target="tpu_custom_call" | custom-call | flops 1 | bytes 1 | tf_op jit(solution)/shard_map/adam/pallas_call | solution.py:589
  (89 shorter events, 3.2 us)
Async XLA Ops:
  7.2 333.0 %all-gather.3.cloned.1.call-start = ((), (), s32[]{:S(2)}) async-start(), calls=%async_computation.6 | async-start | bytes 11796480 | tf_op jit(solution)/shard_map/all_gather | solution.py:1326
  149.8 407.6 %reduce-scatter.4.cloned.1.call-start = ((), (), s32[]{:S(2)}) async-start(), calls=%async_computation.3 | async-start | bytes 3932160 | tf_op jit(solution)/shard_map/reduce_scatter | solution.py:1382
  229.3 3.0 copy-start.15
  229.4 3.3 copy-start.27
  231.3 2.7 copy-start.19
  231.3 2.7 copy-start.21
  244.3 76.6 %copy-start = (bf16[256,2304]{1,0:T(8,128)(2,1)S(1)}, bf16[256,2304]{1,0:T(8,128)(2,1)}, u32[]{:S(2)}) copy-start(bf16[256,2304]{1,0:T(8,128)(2,1)} %project.1.q_ref) | copy-start | bytes 3538948
  244.3 76.6 %copy-start.9 = (s32[256]{0:T(256)S(1)}, s32[256]{0:T(256)}, u32[]{:S(2)}) copy-start(s32[256]{0:T(256)} %param.15) | copy-start | bytes 3076
  320.9 1.0 copy-start.1
  331.1 6.5 copy-start.7
  337.6 1.3 copy-start.11
  421.1 139.8 %reduce-scatter.6.cloned.1.call-start = ((), (), s32[]{:S(2)}) async-start(), calls=%async_computation.4 | async-start | bytes 3932160 | tf_op jit(solution)/shard_map/reduce_scatter | solution.py:1386
  467.8 0.7 copy-start.10
  467.8 2.6 copy-start.20
  467.8 214.7 %reduce-scatter.8.cloned.1.call-start = ((), (), s32[]{:S(2)}) async-start(), calls=%async_computation.5 | async-start | bytes 3932160 | tf_op jit(solution)/shard_map/reduce_scatter | solution.py:1387
  470.4 1.9 copy-start.12
  472.3 2.3 copy-start.18
  472.3 2.5 copy-start.22
  476.7 6.3 copy-start.23
  476.7 6.3 copy-start.2
  476.8 6.3 copy-start.3
  476.8 6.3 copy-start.4
  494.9 1.0 copy-start.5
  495.9 0.8 copy-start.8
  543.9 6.1 copy-start.24
  555.9 5.0 copy-start.6
  555.9 5.0 copy-start.16
  557.4 11.9 %copy-start.14 = (bf16[256,2048]{1,0:T(8,128)(2,1)S(1)}, bf16[256,2048]{1,0:T(8,128)(2,1)}, u32[]{:S(2)}) copy-start(bf16[256,2048]{1,0:T(8,128)(2,1)} %fusion.15.x_ref.refs_3_) | copy-start | bytes 3145732
  674.9 5.1 copy-start.13
  680.0 2.5 copy-start.26
  682.5 62.2 %copy-start.28 = (f32[2,2048]{1,0:T(2,128)S(1)}, f32[2,2048]{1,0:T(2,128)}, u32[]{:S(2)}) copy-start(f32[2,2048]{1,0:T(2,128)} %param.24) | copy-start | bytes 49156
  682.5 62.2 %copy-start.29 = (f32[2,2048]{1,0:T(2,128)S(1)}, f32[2,2048]{1,0:T(2,128)}, u32[]{:S(2)}) copy-start(f32[2,2048]{1,0:T(2,128)} %param.25) | copy-start | bytes 49156
  682.5 62.9 %copy-start.17 = (f32[256,2048]{1,0:T(8,128)S(1)}, f32[256,2048]{1,0:T(8,128)}, u32[]{:S(2)}) copy-start(f32[256,2048]{1,0:T(8,128)} %get-tuple-element.117) | copy-start | bytes 6291460
  742.5 6.4 copy-start.25
Sparse Core Ops, SparseCore 0:
  149.9 176.1 all-gather.2
  421.2 68.6 reduce-scatter.3
  492.2 68.6 reduce-scatter.5
  563.0 96.1 reduce-scatter.7

commit v6 on v5

--- a/solution.py
+++ b/solution.py
@@ -130,23 +130,9 @@
             total_ref[0] = highest + jnp.log(totals)
 
 
-def attend_back_kernel(
-    at_ref,
-    q_ref,
-    k_ref,
-    v_ref,
-    grad_ref,
-    total_ref,
-    key_seg_ref,
-    query_seg_ref,
-    key_cosine_ref,
-    key_sine_ref,
-    cosine_ref,
-    sine_ref,
-    query_grad_ref,
-    pair_grad_ref,
-    key_sum,
-    value_sum,
+def attend_back_head(
+    place, q_ref, k_ref, v_ref, grad_ref, total_ref, key_seg_ref, query_seg_ref, key_cosine_ref,
+    key_sine_ref, cosine_ref, sine_ref, query_grad_ref, pair_grad_ref, key_sum, value_sum,
 ):
     scale = HD ** (-0.5)
     rows = q_ref.shape[0]
@@ -159,7 +145,7 @@
 
     for block in range(SEQLEN // rows):
 
-        @pl.when(at_ref[0] == block)
+        @pl.when(place == block)
         def _():
             keys = (block + 1) * rows
             queries, grads = q_ref[...], grad_ref[...]
@@ -184,6 +170,10 @@
             key_sum[...], key_cosine_ref[...], key_sine_ref[...]
         ).astype(jnp.bfloat16)
         pair_grad_ref[:, HD:] = value_sum[...].astype(jnp.bfloat16)
+
+
+def attend_back_kernel(at_ref, *refs):
+    attend_back_head(at_ref[0], *refs)
 
 
 def attention_specs(kinds, rows):
@@ -548,69 +538,98 @@
     )(slots, *sources)
 
 
-def adam_kernel(
-    at_ref, gate_ref, up_ref, down_ref, share_ref, pair_ref, left_ref, right_ref, master_ref,
-    one_ref, two_ref, new_master_ref, new_one_ref, new_two_ref, grad,
-):
-    kind = at_ref[0, pl.program_id(0)]
-    for number, ref in enumerate((gate_ref, up_ref, down_ref, share_ref)):
-
-        @pl.when(kind == number)
+def adam_kernel(group, at_ref, *refs):
+    feeds = [refs[at * group : (at + 1) * group] for at in range(5)]
+    left_ref, right_ref, master_ref, one_ref, two_ref = refs[5 * group : 5 * group + 5]
+    new_master_ref, new_one_ref, new_two_ref, grad = refs[5 * group + 5 :]
+    low = jnp.bfloat16
+    for slot in range(group):
+        kind = at_ref[0, pl.program_id(0) * group + slot]
+        for number in range(4):
+
+            @pl.when(kind == number)
+            def _():
+                grad[slot] = feeds[number][slot][0]
+
+        @pl.when(kind == 4)
         def _():
-            grad[...] = ref[0]
-
-    @pl.when(kind == 4)
-    def _():
-        pair = pair_ref[...].reshape(grad.shape[1], grad.shape[0])
-        grad[...] = jnp.transpose(pair.astype(jnp.float32)).astype(grad.dtype)
-
-    @pl.when(kind == 5)
-    def _():
-        grad[...] = jnp.zeros_like(grad)
-
-    low = jnp.bfloat16
-    left, right = left_ref[0].astype(low), right_ref[0].astype(low)
-    turned = jnp.dot(grad[...], left, preferred_element_type=jnp.float32)
-    turned = dot_first(turned.astype(low), right)
-    new_one = BETA_ONE * one_ref[0] + (1.0 - BETA_ONE) * turned
-    new_two = BETA_TWO * two_ref[0] + (1.0 - BETA_TWO) * turned * turned
-    new_one_ref[0], new_two_ref[0] = new_one, new_two
-    scaled = new_one / (jnp.sqrt(new_two) + ADAM_EPS)
-    restored = dot_last(scaled.astype(low), right)
-    restored = jnp.dot(left, restored.astype(low), preferred_element_type=jnp.float32)
-    new_master_ref[0] = master_ref[0] * (1.0 - LEARN_RATE * WEIGHT_DECAY) - LEARN_RATE * restored
+            pair = feeds[4][slot][...].reshape(grad.shape[2], grad.shape[1])
+            grad[slot] = jnp.transpose(pair.astype(jnp.float32)).astype(grad.dtype)
+
+        @pl.when(kind == 5)
+        def _():
+            grad[slot] = jnp.zeros(grad.shape[1:], grad.dtype)
+
+    slots = range(group)
+    left = [left_ref[slot].astype(low) for slot in slots]
+    right = [right_ref[slot].astype(low) for slot in slots]
+    turned = [
+        jnp.dot(grad[slot], left[slot], preferred_element_type=jnp.float32) for slot in slots
+    ]
+    turned = [dot_first(turned[slot].astype(low), right[slot]) for slot in slots]
+    scaled = []
+    for slot in slots:
+        new_one = BETA_ONE * one_ref[slot] + (1.0 - BETA_ONE) * turned[slot]
+        new_two = BETA_TWO * two_ref[slot] + (1.0 - BETA_TWO) * turned[slot] * turned[slot]
+        new_one_ref[slot], new_two_ref[slot] = new_one, new_two
+        scaled.append((new_one / (jnp.sqrt(new_two) + ADAM_EPS)).astype(low))
+    restored = [dot_last(scaled[slot], right[slot]).astype(low) for slot in slots]
+    restored = [
+        jnp.dot(left[slot], restored[slot], preferred_element_type=jnp.float32) for slot in slots
+    ]
+    for slot in slots:
+        new_master_ref[slot] = (
+            master_ref[slot] * (1.0 - LEARN_RATE * WEIGHT_DECAY) - LEARN_RATE * restored[slot]
+        )
 
 
 def adam(at, gate, up, down, shares, pairs, left, right, master, one, two):
     slots, rows, width = master.shape
-    tile = pl.BlockSpec((1, rows, width), lambda i, at: (i, 0, 0))
+    group = 3 if slots % 3 == 0 else 1
+    tile = pl.BlockSpec((group, rows, width), lambda i, at: (i, 0, 0))
     shape = jax.ShapeDtypeStruct(master.shape, jnp.float32)
-    feed = pl.BlockSpec((1, width, rows), lambda i, at: (at[1, i], at[2, i], 0))
+
+    def feed(block, column):
+        return [
+            pl.BlockSpec(
+                (1, width, rows),
+                lambda i, at, slot=slot: (at[block, i * group + slot], at[column, i * group + slot], 0),
+            )
+            for slot in range(group)
+        ]
+
+    pair = [
+        pl.BlockSpec(
+            (*pairs.shape[:2], width), lambda i, at, slot=slot: (0, 0, at[5, i * group + slot])
+        )
+        for slot in range(group)
+    ]
     return pl.pallas_call(
-        adam_kernel,
+        functools.partial(adam_kernel, group),
         grid_spec=pltpu.PrefetchScalarGridSpec(
             num_scalar_prefetch=1,
-            grid=(slots,),
-            in_specs=[
-                feed,
-                feed,
-                feed,
-                pl.BlockSpec((1, width, rows), lambda i, at: (at[3, i], at[4, i], 0)),
-                pl.BlockSpec((*pairs.shape[:2], width), lambda i, at: (0, 0, at[5, i])),
-                pl.BlockSpec((1, rows, rows), lambda i, at: (i, 0, 0)),
-                pl.BlockSpec((1, width, width), lambda i, at: (i, 0, 0)),
+            grid=(slots // group,),
+            in_specs=feed(1, 2) * 3
+            + feed(3, 4)
+            + pair
+            + [
+                pl.BlockSpec((group, rows, rows), lambda i, at: (i, 0, 0)),
+                pl.BlockSpec((group, width, width), lambda i, at: (i, 0, 0)),
                 tile,
                 tile,
                 tile,
             ],
             out_specs=[tile] * 3,
-            scratch_shapes=[pltpu.VMEM((width, rows), jnp.bfloat16)],
+            scratch_shapes=[pltpu.VMEM((group, width, rows), jnp.bfloat16)],
         ),
         out_shape=[shape] * 3,
         compiler_params=pltpu.CompilerParams(vmem_limit_bytes=60 * 2**20),
         cost_estimate=SMALL_COST,
         name="adam",
-    )(at, gate, up, down, shares, pairs, left, right, master, one, two)
+    )(
+        at, *[gate] * group, *[up] * group, *[down] * group, *[shares] * group, *[pairs] * group,
+        left, right, master, one, two,
+    )
 
 
 MESH = pl.DeviceIdType.MESH
@@ -693,26 +712,31 @@
             there = (me + step) % self.count
             yield (there, seq) if self.axis == "grp" else (grp, there)
 
-    def start(self, source, target, sems, grp, seq):
+    def start(self, source, target, sems, grp, seq, begin=True):
         me = grp if self.axis == "grp" else seq
         self.own = pltpu.make_async_copy(
             self.source_view(source, me), self.target_view(target, me), sems[0].at[0]
         )
-        self.own.start()
         self.sent, self.due = [], []
         for step, device in enumerate(self.peers(grp, seq), 1):
             there = (me + step) % self.count
             back = (me + self.count - step) % self.count
-            copy = remote(
-                self.source_view(source, there), self.target_view(target, me), sems, step, device
+            self.sent.append(
+                remote(
+                    self.source_view(source, there), self.target_view(target, me), sems, step, device
+                )
             )
-            copy.start()
-            self.sent.append(copy)
             self.due.append(
                 remote(
                     self.source_view(source, back), self.target_view(target, back), sems, step, device
                 )
             )
+        if begin:
+            self.begin()
+
+    def begin(self):
+        for copy in [self.own] + self.sent:
+            copy.start()
 
     def forward(self):
         return iter(())
@@ -831,8 +855,7 @@
         for bits in (1, 2, 4):
             yield flip(grp, bits), seq
 
-    def start(self, source, target, sems, grp, seq, scratch):
-        self.target = target
+    def start(self, source, target, sems, grp, seq, scratch, begin=True):
         self.mine, self.core_in, self.halves, self.wholes = scratch
         core, side_x, side_y = [(flip(grp, bits), seq) for bits in (1, 2, 4)]
         half = self.rows // 2
@@ -854,6 +877,10 @@
             for at, bits in enumerate((6, 2, 4, 0))
         ]
         self.store = pltpu.make_async_copy(mine.at[3], target, sems[0].at[14])
+        if begin:
+            self.begin()
+
+    def begin(self):
         for copy in self.copies[:4] + self.loads:
             copy.start()
 
@@ -948,6 +975,259 @@
                 def _():
                     self.make(away, up).wait_send()
         self.own.wait()
+
+
+def attend_back_sum_kernel(
+    sum_task, gather_task, q_ref, k_ref, v_ref, grad_ref, total_ref, key_seg_ref, query_seg_ref,
+    key_cosine_ref, key_sine_ref, cosine_ref, sine_ref, part_hbm, down_hbm, query_grad_ref,
+    pair_grad_ref, sum_hbm, down_plane, key_sum, value_sum, mine, core_in, halves, wholes,
+    sum_send, sum_recv, gather_send, gather_recv,
+):
+    step = pl.program_id(0)
+    grp, seq = lax.axis_index("grp"), lax.axis_index("seq")
+    scratch = (mine, core_in, halves, wholes)
+    sum_task.start(part_hbm, sum_hbm, (sum_send, sum_recv), grp, seq, scratch, begin=False)
+    gather_task.start(down_hbm, down_plane, (gather_send, gather_recv), grp, seq, begin=False)
+
+    @pl.when(step == 0)
+    def _():
+        barrier = pltpu.get_barrier_semaphore()
+        for device in sum_task.peers(grp, seq):
+            pl.semaphore_signal(barrier, inc=1, device_id=device, device_id_type=MESH)
+        pl.semaphore_wait(barrier, 3)
+        sum_task.begin()
+        gather_task.begin()
+
+    @pl.when(step == 6)
+    def _():
+        sum_task.first_sums()
+
+    attend_back_head(
+        seq, q_ref, k_ref, v_ref, grad_ref, total_ref, key_seg_ref, query_seg_ref, key_cosine_ref,
+        key_sine_ref, cosine_ref, sine_ref, query_grad_ref, pair_grad_ref, key_sum, value_sum,
+    )
+
+    @pl.when(step == pl.num_programs(0) - 1)
+    def _():
+        hand_on([gather_task, sum_task])
+        gather_task.finish()
+        sum_task.finish()
+
+
+def attend_back_sum(
+    number, projected, pairs, grads, totals, key_segs, query_segs, key_tables, tables, part, down
+):
+    rows = projected.shape[0]
+    columns = NH * HD
+    low = jnp.bfloat16
+    sum_task = PlaneSum(*part.shape[1:])
+    gather_task = gather_plane(down.shape)
+    hbm = pl.BlockSpec(memory_space=pl.ANY)
+    return pl.pallas_call(
+        functools.partial(attend_back_sum_kernel, sum_task, gather_task),
+        grid=(NH,),
+        in_specs=attention_specs(
+            ["head", "keys", "values", "head", "total", "key_seg", "query_seg"]
+            + ["key_table", "key_table", "table", "table"],
+            rows,
+        )
+        + [hbm, hbm],
+        out_specs=attention_specs(["head", "pair"], rows) + [hbm, hbm],
+        out_shape=[
+            jax.ShapeDtypeStruct((rows, columns), low),
+            jax.ShapeDtypeStruct((SEQLEN, 2 * HD), low),
+            jax.ShapeDtypeStruct(sum_task.out_shape, low),
+            jax.ShapeDtypeStruct(gather_task.out_shape, low),
+        ],
+        scratch_shapes=[pltpu.VMEM((SEQLEN, HD), jnp.float32)] * 2
+        + sum_task.scratch()
+        + [pltpu.SemaphoreType.DMA((sum_task.sem_count,))] * 2
+        + [pltpu.SemaphoreType.DMA((gather_task.sem_count,))] * 2,
+        compiler_params=pltpu.CompilerParams(
+            collective_id=number, has_side_effects=True, vmem_limit_bytes=48 * 2**20
+        ),
+        cost_estimate=SMALL_COST,
+        name="attend_back_sum",
+    )(
+        projected, pairs, pairs, grads, totals, key_segs[:, None], query_segs[None, :],
+        *key_tables, *tables, part, down,
+    )
+
+
+def block_kernel(
+    first, second, pair_task, key_seg_ref, query_seg_ref, normed_ref, tokens_ref, gain_ref,
+    cosine_ref, sine_ref, cot_hbm, normed_hbm, w_ref, projected_ref, pairs_ref, context_ref,
+    total_ref, hidden_ref, second_ref, inverse_ref, cot_plane, normed_plane, own_pair, pairs,
+    first_send, first_recv, second_send, second_recv, pair_send, pair_recv,
+):
+    step = pl.program_id(0)
+    grp, seq = lax.axis_index("grp"), lax.axis_index("seq")
+    first.start(cot_hbm, cot_plane, (first_send, first_recv), grp, seq, begin=False)
+    second.start(normed_hbm, normed_plane, (second_send, second_recv), grp, seq, begin=False)
+    pair_task.start(own_pair, pairs, (pair_send, pair_recv), grp, seq, begin=False)
+    low = jnp.bfloat16
+    rows = normed_ref.shape[0]
+    wide = 2 * HD
+    couples = NH // 2
+    attend_at = 1 + couples
+    out_at = attend_at + NH
+    end = out_at + MODEL_WIDTH // wide
+
+    @pl.when(step == 0)
+    def _():
+        barrier = pltpu.get_barrier_semaphore()
+        devices = list(first.peers(grp, seq)) + list(pair_task.peers(grp, seq))
+        for device in devices:
+            pl.semaphore_signal(barrier, inc=1, device_id=device, device_id_type=MESH)
+        pl.semaphore_wait(barrier, len(devices))
+        first.begin()
+        second.begin()
+
+    @pl.when(step < attend_at)
+    def _():
+        made = jnp.dot(normed_ref[...], w_ref[...], preferred_element_type=jnp.float32)
+        cosine, sine = cosine_ref[...], sine_ref[...]
+        left = turn(made[:, :HD], cosine, sine).astype(low)
+        right = made[:, HD:]
+
+        @pl.when(step == 0)
+        def _():
+            own_pair[:, :HD] = left
+            own_pair[:, HD:] = right.astype(low)
+            pair_task.begin()
+            projected_ref[:, NH * HD :] = own_pair[...]
+
+        @pl.when(step > 0)
+        def _():
+            place = pl.multiple_of((step - 1) * wide, wide)
+            projected_ref[:, pl.ds(place, HD)] = left
+            projected_ref[:, pl.ds(pl.multiple_of(place + HD, HD), HD)] = turn(
+                right, cosine, sine
+            ).astype(low)
+
+    @pl.when(step == attend_at)
+    def _():
+        pair_task.finish()
+        for at in range(pairs.shape[0]):
+            pairs_ref[at * rows : (at + 1) * rows, :] = pairs[at]
+
+    @pl.when(step == attend_at + 2)
+    def _():
+        first.pass_on(1)
+        first.pass_on(4)
+
+    @pl.when(step == out_at)
+    def _():
+        first.pass_on(2)
+        first.pass_on(5)
+
+    @pl.when((step >= attend_at) & (step < out_at))
+    def _():
+        head = step - attend_at
+        place = pl.ds(pl.multiple_of(head * HD, HD), HD)
+        scale = HD ** (-0.5)
+        for block in range(SEQLEN // rows):
+
+            @pl.when(seq == block)
+            def _():
+                keys = (block + 1) * rows
+                scores = dot_last(pairs_ref[:keys, :HD], projected_ref[:, place]) * scale
+                scores = jnp.where(
+                    score_mask(key_seg_ref, query_seg_ref, block, rows), scores, MASKED
+                )
+                highest = jnp.max(scores, axis=0, keepdims=True)
+                exponent = jnp.exp(scores - highest)
+                totals = jnp.sum(exponent, axis=0, keepdims=True)
+                probs_low = (exponent * (1.0 / totals)).astype(low)
+                context = dot_first(probs_low, pairs_ref[:keys, HD:])
+                context_ref[:, place] = context.astype(low)
+                total_ref[head] = highest + jnp.log(totals)
+
+    @pl.when(step >= out_at)
+    def _():
+        place = pl.ds(pl.multiple_of((step - out_at) * wide, wide), wide)
+        branch = jnp.dot(context_ref[...], w_ref[...], preferred_element_type=jnp.float32)
+        hidden_ref[:, place] = tokens_ref[:, place].astype(jnp.float32) + branch
+
+    @pl.when(step == end - 1)
+    def _():
+        chunk = 32
+        gain = gain_ref[1:2, :]
+
+        def some(at, _):
+            part = pl.ds(pl.multiple_of(at * chunk, chunk), chunk)
+            hidden = hidden_ref[part, :]
+            inverse = lax.rsqrt(jnp.mean(hidden * hidden, axis=-1, keepdims=True) + NORM_EPS)
+            inverse_ref[part, :] = inverse
+            second_ref[part, :] = (hidden * inverse * gain).astype(low)
+            return 0
+
+        lax.fori_loop(0, rows // chunk, some, 0)
+        first.pass_on(6)
+        first.pass_on(3)
+        for came in (1, 4, 2, 5, 6, 3):
+            second.pass_on(came)
+        first.finish()
+        second.finish()
+
+
+def attention_block(number, normed, tokens, gains, tables, key_segs, query_segs, cotangent, weights):
+    rows, width = normed.shape
+    low, wide = jnp.bfloat16, 2 * HD
+    couples = NH // 2
+    count = SEQLEN // rows
+    first = gather_plane(cotangent.shape, placed=True)
+    second = gather_plane(normed.shape, placed=True)
+    pair_task = Exchange("seq", (count, rows, wide), whole, block_of)
+
+    def weight_block(step):
+        turned = step - NH
+        return (0, jnp.where(step == 0, couples, jnp.where(step <= couples, step - 1, jnp.maximum(turned, couples + 1))))
+
+    def full(shape):
+        return pl.BlockSpec(shape, lambda step: (0,) * len(shape))
+
+    hbm = pl.BlockSpec(memory_space=pl.ANY)
+    steps = 1 + couples + NH + width // wide
+    plane = jax.ShapeDtypeStruct((8, rows, width), low)
+    shapes = [
+        jax.ShapeDtypeStruct((rows, NH * HD + wide), low),
+        jax.ShapeDtypeStruct((SEQLEN, wide), low),
+        jax.ShapeDtypeStruct((rows, NH * HD), low),
+        jax.ShapeDtypeStruct((NH, 1, rows), jnp.float32),
+        jax.ShapeDtypeStruct((rows, width), jnp.float32),
+        jax.ShapeDtypeStruct((rows, width), low),
+        jax.ShapeDtypeStruct((rows, 1), jnp.float32),
+    ]
+    return pl.pallas_call(
+        functools.partial(block_kernel, first, second, pair_task),
+        grid=(steps,),
+        in_specs=[
+            full((SEQLEN, 1)),
+            full((1, rows)),
+            full((rows, width)),
+            full((rows, width)),
+            full((2, width)),
+            full((rows, HD)),
+            full((rows, HD)),
+            hbm,
+            hbm,
+            pl.BlockSpec((width, wide), weight_block),
+        ],
+        out_specs=[full(shape.shape) for shape in shapes] + [hbm, hbm],
+        out_shape=shapes + [plane, plane],
+        scratch_shapes=[pltpu.VMEM((rows, wide), low), pltpu.VMEM((count, rows, wide), low)]
+        + [pltpu.SemaphoreType.DMA((14,))] * 4
+        + [pltpu.SemaphoreType.DMA((pair_task.sem_count,))] * 2,
+        compiler_params=pltpu.CompilerParams(
+            collective_id=number, has_side_effects=True, vmem_limit_bytes=56 * 2**20
+        ),
+        cost_estimate=SMALL_COST,
+        name="attention_block",
+    )(
+        key_segs[:, None], query_segs[None, :], normed, tokens, gains, *tables, cotangent, normed,
+        weights,
+    )
 
 
 def half_rows(axis, height):
@@ -1312,7 +1592,9 @@
             block_of,
         )
         work.append((late_rows, weights_low))
-    tiles = [part.reshape(flat) for part in exchange(0, work)]
+    work.append(gather_axis("seq", segment_ids.reshape(-1, tile_width)))
+    *tiles, segments = exchange(0, work)
+    tiles = [part.reshape(flat) for part in tiles]
     attn_rows = pick(attn_slots, tiles, half_sub).reshape(halves, half_sub, output_end)
     if grp_count == 8 and seq_count == 4:
         work = [(LineGather(attn_rows.shape), attn_rows)]
@@ -1332,27 +1614,34 @@
     (attn_weights,) = exchange(2, [(attn_plane, attn_seq)])
     attn_weights = attn_weights.reshape(MODEL_WIDTH, output_end)
 
-    projected = project(normed, attn_weights, tables)
-    pairs, segments, cot_plane, normed_plane = exchange(
-        3,
-        [
-            gather_axis("seq", projected[:, query_cols:]),
-            gather_axis("seq", segment_ids.reshape(-1, tile_width)),
-            (gather_plane(cotangent.shape, placed=True), cotangent),
-            (gather_plane(normed.shape, placed=True), normed),
-        ],
-    )
     first_key = seq_here * rows_here - first_place
-    pairs = lax.dynamic_slice_in_dim(pairs.reshape(-1, 2 * HD), first_key, SEQLEN)
     key_segs = lax.dynamic_slice_in_dim(segments.reshape(-1), first_key, SEQLEN)
     at = (first_place // rows_here).reshape(1)
-    context, log_totals = attend(at, projected, pairs, key_segs, segment_ids)
-    branch = jnp.dot(
-        context, attn_weights[:, value_end:], preferred_element_type=jnp.float32
-    )
-    hidden = tok_float + branch
-    inverse_two = lax.rsqrt(jnp.mean(hidden * hidden, axis=-1, keepdims=True) + NORM_EPS)
-    normed_two = (hidden * inverse_two * gains[1]).astype(jnp.bfloat16)
+    if grp_count == 8 and seq_count * rows_here == SEQLEN:
+        (
+            projected, pairs, context, log_totals, hidden, normed_two, inverse_two, cot_plane,
+            normed_plane,
+        ) = attention_block(
+            3, normed, tokens, gains, tables, key_segs, segment_ids, cotangent, attn_weights
+        )
+    else:
+        projected = project(normed, attn_weights, tables)
+        pairs, cot_plane, normed_plane = exchange(
+            3,
+            [
+                gather_axis("seq", projected[:, query_cols:]),
+                (gather_plane(cotangent.shape, placed=True), cotangent),
+                (gather_plane(normed.shape, placed=True), normed),
+            ],
+        )
+        pairs = lax.dynamic_slice_in_dim(pairs.reshape(-1, 2 * HD), first_key, SEQLEN)
+        context, log_totals = attend(at, projected, pairs, key_segs, segment_ids)
+        branch = jnp.dot(
+            context, attn_weights[:, value_end:], preferred_element_type=jnp.float32
+        )
+        hidden = tok_float + branch
+        inverse_two = lax.rsqrt(jnp.mean(hidden * hidden, axis=-1, keepdims=True) + NORM_EPS)
+        normed_two = (hidden * inverse_two * gains[1]).astype(jnp.bfloat16)
 
     cot_plane = cot_plane.reshape(-1, MODEL_WIDTH)
     normed_plane = normed_plane.reshape(-1, MODEL_WIDTH)
@@ -1397,23 +1686,28 @@
     )
     branch_grad = hidden_grad.astype(jnp.bfloat16)
     context_grad = times_transpose(branch_grad, attn_weights[:, value_end:]).astype(jnp.bfloat16)
-    query_grad, pair_part = attend_back(
-        at,
-        projected,
-        pairs,
-        context_grad,
-        log_totals,
-        key_segs,
-        segment_ids,
-        key_tables,
-        tables,
-    )
+    fused = grp_count == 8 and seq_count * rows_here == SEQLEN
+    if fused:
+        feed_part = feed_part.reshape(grp_count, rows_here, MODEL_WIDTH)
+        query_grad, pair_part, feed_out, down_plane = attend_back_sum(
+            6, projected, pairs, context_grad, log_totals, key_segs, segment_ids, key_tables,
+            tables, feed_part, down_grad,
+        )
+    else:
+        query_grad, pair_part = attend_back(
+            at, projected, pairs, context_grad, log_totals, key_segs, segment_ids, key_tables, tables
+        )
+        feed_out = lax.psum_scatter(
+            feed_part.reshape(-1, MODEL_WIDTH), "grp", scatter_dimension=0, tiled=True
+        )
+        (down_plane,) = exchange(10, [(gather_plane(down_grad.shape), down_grad)])
+    block_out = (hidden + feed_out.astype(jnp.float32)).astype(jnp.bfloat16)
     if seq_count * rows_here > SEQLEN:
         pair_part = lax.dynamic_update_slice_in_dim(
             jnp.zeros((seq_count * rows_here, 2 * HD), pair_part.dtype), pair_part, first_key, 0
         )
     pair_parts, query_share, branch_share = exchange(
-        6,
+        7,
         [
             split_rows("seq", pair_part),
             split_columns("grp", query_grad, placed=True),
@@ -1421,7 +1715,7 @@
         ],
     )
     pair_grad = jnp.sum(pair_parts.astype(jnp.float32), axis=0).astype(jnp.bfloat16)
-    pair_grad, down_grad = lax.optimization_barrier((pair_grad, down_grad))
+    pair_grad, gate_weight_grad = lax.optimization_barrier((pair_grad, gate_weight_grad))
     projected_grad = jnp.concatenate([query_grad, pair_grad], axis=1)
     norm_one_grad = times_transpose(projected_grad, attn_weights[:, :value_end])
     gain_one_term = jnp.sum(norm_one_grad * tok_float * inverse_one, axis=0)
@@ -1436,9 +1730,6 @@
     out_weight_grad = contract(branch_share.reshape(-1, share_width), context_plane)
     pair_weight_grad = contract(normed, pair_grad).astype(jnp.bfloat16)
     shares = jnp.concatenate([query_weight_grad, out_weight_grad], axis=0).astype(jnp.bfloat16)
-    shares, down_grad, gate_weight_grad = lax.optimization_barrier(
-        (shares, down_grad, gate_weight_grad)
-    )
     feed_shape = (share_cols, rows_block)
     pair_task = Exchange(
         "grp",
@@ -1450,29 +1741,19 @@
         split_columns("seq", shares),
         (pair_task, pair_weight_grad.reshape(seq_count, grp_count, sub_rows, 2 * HD)),
         gather_axis("seq", jnp.stack([gain_one_term, gain_two_term])),
-        (gather_plane(feed_shape), down_grad),
         (gather_plane(feed_shape), gate_weight_grad),
+        (gather_plane(feed_shape), up_weight_grad),
     ]
-    if grp_count == 8:
-        feed_part = feed_part.reshape(grp_count, rows_here, MODEL_WIDTH)
-        work.append((PlaneSum(rows_here, MODEL_WIDTH), feed_part))
-    share_parts, pair_parts, gain_parts, down_plane, gate_plane, *feed_out = exchange(7, work)
-    if grp_count == 8:
-        feed_out = feed_out[0]
-    else:
-        feed_out = lax.psum_scatter(feed_part, "grp", scatter_dimension=0, tiled=True)
-    block_out = (hidden + feed_out.astype(jnp.float32)).astype(jnp.bfloat16)
+    share_parts, pair_parts, gain_parts, gate_plane, up_plane = exchange(8, work)
     gain_seq = jnp.sum(gain_parts, axis=0)
     shares = jnp.sum(share_parts.astype(jnp.float32), axis=0).astype(jnp.bfloat16)
     pair_parts = jnp.sum(pair_parts.astype(jnp.float32), axis=0).astype(jnp.bfloat16)
     pair_task = Exchange("seq", pair_parts.shape, block_of, block_of)
-    shares, up_weight_grad = lax.optimization_barrier((shares, up_weight_grad))
-    _, pair_plane, up_plane, share_plane, gain_parts = exchange(
-        8,
+    _, pair_plane, share_plane, gain_parts = exchange(
+        9,
         [
             (pair_task, pair_parts),
             (gather_plane(pair_parts.shape), 0),
-            (gather_plane(feed_shape), up_weight_grad),
             (gather_plane(shares.shape), shares),
             gather_axis("grp", gain_seq),
         ],

time: 800 us -> 754 us (0.943)
  Pallas kernels: 693 us -> 649 us
  waiting for transfers between devices: 3.52 us -> 16.4 us
    pallas_call x7 -> x6, Pallas kernels: 494 us -> 344 us  [exchange(): pl.pallas_call(functools.partial(exchange_kernel, tasks, wires, len(array...]
    pallas_call x4 -> x3, Pallas kernels: 63.6 us -> 169 us  [the longest x1 81.3 us: attention_block(): pl.pallas_call(functools.partial(block_kernel, first, second, pair_task),...]
    all_gather x1, waiting for transfers between devices: 0.01 us -> 8.95 us  [local(): feed_parts = [lax.all_gather(feed_rows, 'seq', axis=0, tiled=False)]]
  transfers between devices with their start and end apart: 4 -> 4, of which waited for: 1 -> 2; matrix products, arithmetic and copies ran while one was open for 8% -> 6% of each run, Pallas kernels for 48% -> 40%
where the time goes in v6:
time: 754 us; the launch traced here: 748 us
  Pallas kernels  649 us (86%)
  other arithmetic  28.6 us (4%)
  matrix products  27.7 us (4%)
  waiting for transfers between devices  16.4 us (2%)
  between operations  14.7 us (2%)
  local copies, waits for them, and re-layouts  12.2 us (2%)
    pallas_call x6, Pallas kernels, exchange(): pl.pallas_call(functools.partial(exchange_kernel, tasks, wires, len(array...  344 us
    pallas_call x1, Pallas kernels, attention_block(): pl.pallas_call(functools.partial(block_kernel, first, second, pair_task),...  81.3 us
    pallas_call x1, Pallas kernels, feed_gather(): pl.pallas_call(functools.partial(feed_gather_kernel, first, second), grid...  80.7 us
    pallas_call x1, Pallas kernels, attend_back_sum(): pl.pallas_call(functools.partial(attend_back_sum_kernel, sum_task, gather...  63.3 us
    pallas_call x1, Pallas kernels, plane_sum(): pl.pallas_call(plane_sum_kernel, in_specs=[vmem, vmem, vmem, hbm], out_sp...  47.7 us
    pallas_call x1, Pallas kernels, adam(): pl.pallas_call(functools.partial(adam_kernel, group), grid_spec=pltpu.Pre...  24.4 us
  transfers between devices with their start and end apart: 4, of which 2 were waited for; matrix products, arithmetic and copies ran while one was open for 6% of the time, Pallas kernels for 40%

profile of v6, /device:TPU:0, one launch (start us, length us, event | category | flops | bytes accessed | tf_op | source)
XLA Modules:
  0.0 748.4 jit_solution(17839423900723148591)
XLA Ops:
  7.3 1.2 slice.19.slots_ref
  8.6 1.9 gather_fusion
  10.5 69.9 %exchange.6 = (bf16[8,21,256,128]{3,2,1,0:T(8,128)(2,1)}, bf16[8,21,32,128]{3,2,1,0:T(8,128)(2,1)}, s32[4,2,128]{2,1,0:T(2,128)}) custom-call(bf16[21,512,128]{2,1,0:T(8,128)(2,1)} %refs_1_.3, bf16[21,512,128]{2,1,0:T(8,128)(2,1)} %refs_1_.3, s32[2,128]{1,0:T(2,128)} %bitcast.49), custom_call_target="tpu_custom_call" | custom-call | flops 1 | bytes 1 | tf_op jit(solution)/shard_map/exchange/pallas_call | solution.py:1332
  80.4 3.2 pick.2
  83.6 62.3 %exchange.7 = (bf16[4,2,32,4352]{3,2,1,0:T(8,128)(2,1)}, bf16[8,21,256,128]{3,2,1,0:T(8,128)(2,1)}) custom-call(bf16[2,32,4352]{2,1,0:T(8,128)(2,1)} %bitcast.65, bf16[21,512,128]{2,1,0:T(8,128)(2,1)} %refs_1_.3), custom_call_target="tpu_custom_call" | custom-call | flops 1 | bytes 1 | tf_op jit(solution)/shard_map/exchange/pallas_call | solution.py:1332
  145.8 4.0 pick.3
  150.0 79.7 %exchange.8 = bf16[4,2,8,32,4352]{4,3,2,1,0:T(8,128)(2,1)} custom-call(bf16[4,2,32,4352]{3,2,1,0:T(8,128)(2,1)} %get-tuple-element.58.refs_0_), custom_call_target="tpu_custom_call" | custom-call | flops 1 | bytes 1 | tf_op jit(solution)/shard_map/exchange/pallas_call | solution.py:1332
  229.7 1.0 copy.24.key_seg_ref
  230.7 1.9 multiply_sine_fusion
  232.7 0.8 copy-done.18
  233.8 0.9 fusion.23
  235.0 1.3 fusion.11.normed_ref.normed_hbm
  236.3 81.3 %attention_block.1 = (bf16[256,2304]{1,0:T(8,128)(2,1)}, bf16[1024,256]{1,0:T(8,128)(2,1)}, bf16[256,2048]{1,0:T(8,128)(2,1)}, f32[16,1,256]{2,1,0:T(1,128)}, f3...) custom-call(s32[1024,1]{1,0:T(8,128)} %copy.24.key_seg_ref, ...), custom_call_target="tpu_custom_call" | custom-call | flops 1 | bytes 1 | tf_op jit(solution)/shard_map/attention_block/pallas_call | solution.py:1202
  317.6 8.9 %all-gather.3.cloned.1.call-done = bf16[2048,2304]{1,0:T(8,128)(2,1)} async-done(((bf16[512,2304]{1,0:T(8,128)(2,1)}), bf16[2048,2304]{1,0:T(8,128)(2,1)}) %all-gather.3.cloned.1.call-update) | async-done | bytes 9437200 | tf_op jit(solution)/shard_map/all_gather | solution.py:1608
  326.6 80.7 %feed_gather.1 = (bf16[768,2048]{1,0:T(8,128)(2,1)}, bf16[768,2048]{1,0:T(8,128)(2,1)}, bf16[2048,2048]{1,0:T(8,128)(2,1)}, bf16[2048,2048]{1,0:T(8,128)(2,1)}, ...) custom-call(s32[1]{0:T(128)} %bitcast.9.real_ref, ...), custom_call_target="tpu_custom_call" | custom-call | flops 1 | bytes 1 | tf_op jit(solution)/shard_map/feed_gather/pallas_call | solution.py:443
  407.3 47.7 %plane_sum.1 = (f32[256,2048]{1,0:T(8,128)}, bf16[3072,512]{1,0:T(8,128)(2,1)}, bf16[3072,512]{1,0:T(8,128)(2,1)}) custom-call(bf16[8,256,2048]{2,1,0:T(8,128)(2,1)} %bitcast.62, bf16[768,2048]{1,0:T(8,128)(2,1)} %get-tuple-element.70.gate_ref, bf16[768,2048]{1,0:T(8,128)(2,1)} %get-tuple-element.71.up_ref, bf16[2048,2048]{1,0:T(8,128)(2,1)} %bitcast.63), custom_call_target="tpu_custom_call" | custom-call | flops 1 | bytes 1 | tf_op jit(solution)/shard_map/plane_sum/pallas_call | solution.py:1501
  455.1 0.6 copy-done.10
  455.7 1.1 scatter_custom_fusion
  457.0 0.6 stack.36.at_ref
  457.7 1.9 pad_maximum_fusion.1
  459.6 2.4 multiply_reduce_fusion
  462.2 2.0 fusion.40
  464.1 1.0 copy-done.22
  465.1 6.8 fusion.6.grad_ref
  472.0 1.2 copy-done.6
  473.1 63.3 %attend_back_sum.1 = (bf16[256,2048]{1,0:T(8,128)(2,1)S(1)}, bf16[1024,256]{1,0:T(8,128)(2,1)S(1)}, bf16[256,2048]{1,0:T(8,128)(2,1)S(1)}, bf16[8,768,512]{2,1,0:T(8,128)(2,1)}) custom-call(bf16[256,2304]{1,0:T(8,128)(2,1)} %get-tuple-element.60.q_ref, bf16[1024,256]{1,0:T(8,128)(2,1)S(1)} %copy-done.1, bf16[1024,256]{1,0:T(8,128)(2,1)S(1)} %copy-done.1, ...), custom_call_target="tpu_custom_call" | custom-call | flops 1 | bytes 1 | tf_op jit(solution)/shard_map/attend_back_sum/pallas_call | solution.py:1026
  536.5 1.0 copy-done.4
  537.5 0.8 copy-done.7
  538.3 26.6 %exchange.9 = (bf16[4,256,256]{2,1,0:T(8,128)(2,1)}, bf16[8,256,256]{2,1,0:T(8,128)(2,1)}, bf16[8,256,256]{2,1,0:T(8,128)(2,1)}) custom-call(bf16[1024,256]{1,0:T(8,128)(2,1)} %copy-done.7, bf16[256,2048]{1,0:T(8,128)(2,1)} %copy-done.4, bf16[256,2048]{1,0:T(8,128)(2,1)} %copy-done.22), custom_call_target="tpu_custom_call" | custom-call | flops 1 | bytes 1 | tf_op jit(solution)/shard_map/exchange/pallas_call | solution.py:1332
  564.9 1.1 reduce_sum.113
  566.1 7.9 %fusion.17 = (f32[2048]{0:T(1024)S(1)}, f32[256]{0:T(256)S(1)}, f32[256,2048]{1,0:T(8,128)}) fusion(bf16[256,2048]{1,0:T(8,128)(2,1)S(1)} %copy-done.14, f32[256]{0:T(256)S(1)} %get-tuple-element.124, f32[2048]{0:T(1024)S(1)} %bitcast.68, bf16[2048,4352]{1,0:T(8,128)(2,1)} %bitcast.54, bf16[256,256]{1,0:T(8,128)(2,1)S(1)} %reduce_sum.113, ...), kind=kOutput, calls=%fused_computation.25 | convolution fusion | flops 2421946112 | bytes 13780992 | tf_op jit(solution)/shard_map/dot_general | solution.py:36
  574.0 0.6 pad_maximum_fusion.3.refs_2_
  574.6 5.8 fusion.5
  580.4 5.7 fusion.4
  586.2 1.6 pad_maximum_fusion.refs_0_
  587.8 1.5 convolution_convert_fusion
  589.7 1.3 add_convert_fusion
  591.0 7.4 reduce-scatter.8.cloned.1.call-done.refs_4_
  598.4 73.8 %exchange.10 = (bf16[4,512,512]{2,1,0:T(8,128)(2,1)}, bf16[8,4,64,256]{3,2,1,0:T(8,128)(2,1)}, f32[4,2,2048]{2,1,0:T(2,128)}, bf16[8,768,512]{2,1,0:T(8,128)(2,1)}, bf16[8,768,512]{2,1,0:T(8,128)(2,1)}) custom-call(bf16[512,2048]{1,0:T(8,128)(2,1)} %pad_maximum_fusion.refs_0_, bf16[4,8,64,256]{3,2,1,0:T(8,128)(2,1)} %bitcast.64, ...), custom_call_target="tpu_custom_call" | custom-call | flops 1 | bytes 1 | tf_op jit(solution)/shard_map/exchange/pallas_call | solution.py:1332
  672.1 2.1 reduce_sum.117.refs_0_
  674.2 3.0 reduce_sum.118.refs_1_
  677.2 0.6 reduce_sum.119.refs_2_
  677.9 31.8 %exchange.11 = (bf16[4,64,256]{2,1,0:T(8,128)(2,1)}, bf16[8,4,64,256]{3,2,1,0:T(8,128)(2,1)}, bf16[8,512,512]{2,1,0:T(8,128)(2,1)}, f32[8,2,2048]{2,1,0:T(2,128)}) custom-call(bf16[4,64,256]{2,1,0:T(8,128)(2,1)} %reduce_sum.117.refs_0_, bf16[512,512]{1,0:T(8,128)(2,1)} %reduce_sum.118.refs_1_, f32[2,2048]{1,0:T(2,128)} %reduce_sum.119.refs_2_), custom_call_target="tpu_custom_call" | custom-call | flops 1 | bytes 1 | tf_op jit(solution)/shard_map/exchange/pallas_call | solution.py:1332
  709.7 1.0 reduce_sum.121
  710.7 2.1 reduce_sum.120.refs_12_.refs_13_.refs_14_
  712.8 0.7 divide_subtract_fusion
  713.5 3.5 fusion.13
  717.0 24.4 %adam.1 = (f32[21,512,128]{2,1,0:T(8,128)}, f32[21,512,128]{2,1,0:T(8,128)}, f32[21,512,128]{2,1,0:T(8,128)}) custom-call(s32[6,21]{1,0:T(8,128)} %stack.36.at_ref, bf16[8,768,512]{2,1,0:T(8,128)(2,1)} %get-tuple-element.89.refs_0_.refs_1_.refs_2_, bf16[8,768,512]{2,1,0:T(8,128)(2,1)} %get-tuple-element.89.refs_0_.refs_1_.refs_2_, ...), custom_call_target="tpu_custom_call" | custom-call | flops 1 | bytes 1 | tf_op jit(solution)/shard_map/adam/pallas_call | solution.py:607
  (90 shorter events, 2.1 us)
Async XLA Ops:
  7.2 319.4 %all-gather.3.cloned.1.call-start = ((), (), s32[]{:S(2)}) async-start(), calls=%async_computation.6 | async-start | bytes 11796480 | tf_op jit(solution)/shard_map/all_gather | solution.py:1608
  149.9 322.0 %reduce-scatter.4.cloned.1.call-start = ((), (), s32[]{:S(2)}) async-start(), calls=%async_computation.3 | async-start | bytes 3932160 | tf_op jit(solution)/shard_map/reduce_scatter | solution.py:1671
  150.0 79.7 %copy-start.32 = (s32[4,2,128]{2,1,0:T(2,128)S(1)}, s32[4,2,128]{2,1,0:T(2,128)}, u32[]{:S(2)}) copy-start(s32[4,2,128]{2,1,0:T(2,128)} %get-tuple-element.55) | copy-start | bytes 12292
  229.7 5.0 copy-start.13
  230.7 4.2 copy-start.25
  232.7 0.8 copy-start.18
  232.7 1.0 copy-start.19
  232.7 1.1 copy-start.20
  407.2 158.8 %reduce-scatter.6.cloned.1.call-start = ((), (), s32[]{:S(2)}) async-start(), calls=%async_computation.4 | async-start | bytes 3932160 | tf_op jit(solution)/shard_map/reduce_scatter | solution.py:1675
  455.0 0.7 copy-start.10
  455.0 2.6 copy-start.27
  455.0 143.3 %reduce-scatter.8.cloned.1.call-start = ((), (), s32[]{:S(2)}) async-start(), calls=%async_computation.5 | async-start | bytes 3932160 | tf_op jit(solution)/shard_map/reduce_scatter | solution.py:1676
  456.9 2.7 copy-start.17
  459.6 2.4 copy-start.11
  459.6 2.5 copy-start.21
  464.1 1.0 copy-start.22
  465.1 6.9 copy-start
  465.1 6.9 copy-start.1
  465.1 6.9 copy-start.2
  465.1 6.9 copy-start.3
  465.1 6.9 copy-start.8
  465.1 6.9 copy-start.9
  472.0 1.2 copy-start.6
  536.5 1.0 copy-start.4
  537.5 0.8 copy-start.7
  538.3 27.8 %copy-start.14 = (bf16[256,2048]{1,0:T(8,128)(2,1)S(1)}, bf16[256,2048]{1,0:T(8,128)(2,1)}, u32[]{:S(2)}) copy-start(bf16[256,2048]{1,0:T(8,128)(2,1)} %tokens_ref.1) | copy-start | bytes 3145732
  538.3 27.8 %copy-start.5 = (bf16[256,2048]{1,0:T(8,128)(2,1)S(1)}, bf16[256,2048]{1,0:T(8,128)(2,1)}, u32[]{:S(2)}) copy-start(bf16[256,2048]{1,0:T(8,128)(2,1)} %copy-done.4) | copy-start | bytes 3145732
  566.1 8.5 %copy-start.24 = (bf16[8,256,256]{2,1,0:T(8,128)(2,1)S(1)}, bf16[8,256,256]{2,1,0:T(8,128)(2,1)}, u32[]{:S(2)}) copy-start(bf16[8,256,256]{2,1,0:T(8,128)(2,1)} %get-tuple-element.85) | copy-start | bytes 3145732
  574.6 5.8 copy-start.23
  586.2 1.6 copy-start.15
  587.8 1.9 copy-start.12
  672.1 5.1 copy-start.29
  674.2 38.6 %copy-start.26 = (f32[2,2048]{1,0:T(2,128)S(1)}, f32[2,2048]{1,0:T(2,128)}, u32[]{:S(2)}) copy-start(f32[2,2048]{1,0:T(2,128)} %gain_ref.1) | copy-start | bytes 49156
  674.2 38.6 %copy-start.30 = (f32[2,2048]{1,0:T(2,128)S(1)}, f32[2,2048]{1,0:T(2,128)}, u32[]{:S(2)}) copy-start(f32[2,2048]{1,0:T(2,128)} %param.24) | copy-start | bytes 49156
  674.2 38.6 %copy-start.31 = (f32[2,2048]{1,0:T(2,128)S(1)}, f32[2,2048]{1,0:T(2,128)}, u32[]{:S(2)}) copy-start(f32[2,2048]{1,0:T(2,128)} %param.25) | copy-start | bytes 49156
  674.2 39.3 %copy-start.16 = (f32[256,2048]{1,0:T(8,128)S(1)}, f32[256,2048]{1,0:T(8,128)}, u32[]{:S(2)}) copy-start(f32[256,2048]{1,0:T(8,128)} %get-tuple-element.117) | copy-start | bytes 6291460
  710.7 6.4 copy-start.28
Sparse Core Ops, SparseCore 0:
  150.0 176.4 all-gather.2
  407.4 57.4 reduce-scatter.3
  467.2 60.2 reduce-scatter.5
  529.7 68.6 reduce-scatter.7

commit v7 on v6

--- a/solution.py
+++ b/solution.py
@@ -314,16 +314,19 @@
 
 
 def feed_gather_kernel(
-    first, second, real_ref, own_ref, context_ref, cot_ref, cot_all_ref, part_ref, gate_grad_ref,
-    up_grad_ref, two_ref, out_ref, second_ref, context_plane_ref, down_out, blocks, weights,
-    act_block, act, x_block, stage, load_sems, keep_sems, x_sems, out_sems, first_send,
-    first_recv, second_send, second_recv,
+    first, second, halves, real_ref, own_ref, context_ref, cot_ref, cot_all_ref, *refs
 ):
+    parts, refs = refs[:halves], refs[halves:]
+    (
+        gate_grad_ref, up_grad_ref, two_ref, out_ref, second_ref, context_plane_ref, down_out,
+        blocks, weights, act_block, act, x_block, stage, load_sems, keep_sems, x_sems, out_sems,
+        first_send, first_recv, second_send, second_recv,
+    ) = refs
     step = pl.program_id(0)
     grp, seq = lax.axis_index("grp"), lax.axis_index("seq")
     first.start(own_ref, blocks, (first_send, first_recv), grp, seq, begin=False)
     second.start(context_ref, context_plane_ref, (second_send, second_recv), grp, seq, begin=False)
-    loads = load_weights([part_ref], weights, load_sems)
+    loads = load_weights(parts, weights, load_sems)
     cols = act.shape[0]
     step_rows = act_block.shape[1]
     rows = x_block.shape[2]
@@ -429,9 +432,9 @@
             pltpu.make_async_copy(blocks.at[at], second_ref.at[at], keep_sems.at[at]).wait()
 
 
-def feed_gather(number, real_cols, normed, context, cot, part, seq_count):
+def feed_gather(number, real_cols, normed, context, cot, parts, seq_count):
     rows, width = normed.shape
-    cols = part.shape[2] // 3
+    cols = parts[0].shape[2] // 3
     low = jnp.bfloat16
     block = pl.BlockSpec((rows, width), lambda i: (i, 0))
     narrow = pl.BlockSpec((cols, rows), lambda i: (0, i))
@@ -441,9 +444,10 @@
     plane = jax.ShapeDtypeStruct((8, rows, width), low)
     model_rows = width // seq_count
     return pl.pallas_call(
-        functools.partial(feed_gather_kernel, first, second),
+        functools.partial(feed_gather_kernel, first, second, len(parts)),
         grid=(8,),
-        in_specs=[pl.BlockSpec(memory_space=pltpu.SMEM), hbm, hbm, block, hbm, hbm],
+        in_specs=[pl.BlockSpec(memory_space=pltpu.SMEM), hbm, hbm, block, hbm]
+        + [hbm] * len(parts),
         out_specs=[narrow, narrow, block, block, hbm, hbm, hbm],
         out_shape=[jax.ShapeDtypeStruct((cols, 8 * rows), low)] * 2
         + [jax.ShapeDtypeStruct((8 * rows, width), low)] * 2
@@ -455,7 +459,7 @@
             pltpu.VMEM((cols, 8 * rows), low),
             pltpu.VMEM((2, 8 * rows, model_rows), low),
             pltpu.VMEM((2, cols, model_rows), low),
-            pltpu.SemaphoreType.DMA((seq_count,)),
+            pltpu.SemaphoreType.DMA((seq_count * len(parts),)),
             pltpu.SemaphoreType.DMA((8,)),
             pltpu.SemaphoreType.DMA((2,)),
             pltpu.SemaphoreType.DMA((2,)),
@@ -466,7 +470,7 @@
         ),
         cost_estimate=SMALL_COST,
         name="feed_gather",
-    )(real_cols, normed, context, cot, cot, part)
+    )(real_cols, normed, context, cot, cot, *parts)
 
 
 def weight_grad_kernel(left_ref, x_ref, out_ref):
@@ -493,70 +497,91 @@
     )(left, x)
 
 
-def pick_kernel(share, slots_ref, *refs):
-    count = len(refs) - 2
-    sources, out_ref, sems = refs[:count], refs[count], refs[count + 1]
-    width = sources[0].shape[2]
-    start = 0
+def share_grad_kernel(query_ref, out_ref, normed_ref, context_ref, grads_ref):
+    half = query_ref.shape[1]
+    for at, (left, right) in enumerate(((query_ref, normed_ref), (out_ref, context_ref))):
+        made = dot_first(left[...], right[...])
+        grads_ref[at * half : (at + 1) * half, :] = made.astype(grads_ref.dtype)
+
+
+def share_grad(query_share, out_share, normed, context):
+    tokens_all, width = normed.shape
+    columns = query_share.shape[1]
+    step = 512
+    narrow = pl.BlockSpec((tokens_all, columns), lambda i: (0, 0))
+    block = pl.BlockSpec((tokens_all, step), lambda i: (0, i))
+    return pl.pallas_call(
+        share_grad_kernel,
+        grid=(width // step,),
+        in_specs=[narrow, narrow, block, block],
+        out_specs=pl.BlockSpec((2 * columns, step), lambda i: (0, i)),
+        out_shape=jax.ShapeDtypeStruct((2 * columns, width), jnp.bfloat16),
+        compiler_params=pltpu.CompilerParams(vmem_limit_bytes=60 * 2**20),
+        cost_estimate=SMALL_COST,
+        name="share_grad",
+    )(query_share, out_share, normed, context)
+
+
+def pick_kernel(rows, feed_ref, attn_ref, tiles_ref, feed_out, attn_out, sems):
+    grp = lax.axis_index("grp")
+    width = tiles_ref.shape[2]
     copies = []
-    for at, source in enumerate(sources):
-        rows = source.shape[1]
-        if at == 0 and share is not None:
-            rows = share
-            part = pl.ds(pl.multiple_of(lax.axis_index("grp") * rows, rows), rows)
-        else:
-            part = pl.ds(0, rows)
-        for tile in range(slots_ref.shape[0]):
-            copies.append(
-                pltpu.make_async_copy(
-                    source.at[slots_ref[tile], part],
-                    out_ref.at[pl.ds(start, rows), tile * width : (tile + 1) * width],
-                    sems.at[len(copies)],
-                )
-            )
-        start += rows
+    for at in range(feed_ref.shape[0]):
+        copies.append(
+            (tiles_ref.at[feed_ref[at]], feed_out.at[:, at * width : (at + 1) * width])
+        )
+    share = pl.ds(pl.multiple_of(grp * rows, rows), rows)
+    for at in range(attn_ref.shape[0]):
+        copies.append(
+            (tiles_ref.at[attn_ref[at], share], attn_out.at[:, at * width : (at + 1) * width])
+        )
+    copies = [
+        pltpu.make_async_copy(source, target, sems.at[at])
+        for at, (source, target) in enumerate(copies)
+    ]
     for copy in copies:
         copy.start()
     for copy in copies:
         copy.wait()
 
 
-def pick(slots, sources, share=None):
-    count, width = slots.shape[0], sources[0].shape[2]
-    rows = sum(source.shape[1] for source in sources)
-    if share is not None:
-        rows += share - sources[0].shape[1]
+def pick(tiles, feed_slots, attn_slots):
+    _, rows, width = tiles.shape
+    share = rows // lax.axis_size("grp")
+    feed, attn = feed_slots.shape[0], attn_slots.shape[0]
     return pl.pallas_call(
         functools.partial(pick_kernel, share),
-        in_specs=[pl.BlockSpec(memory_space=pltpu.SMEM)]
-        + [pl.BlockSpec(memory_space=pl.ANY)] * len(sources),
-        out_specs=pl.BlockSpec(memory_space=pltpu.VMEM),
-        out_shape=jax.ShapeDtypeStruct((rows, count * width), sources[0].dtype),
-        scratch_shapes=[pltpu.SemaphoreType.DMA((count * len(sources),))],
+        in_specs=[pl.BlockSpec(memory_space=pltpu.SMEM)] * 2 + [pl.BlockSpec(memory_space=pl.ANY)],
+        out_specs=[pl.BlockSpec(memory_space=pltpu.VMEM)] * 2,
+        out_shape=[
+            jax.ShapeDtypeStruct((rows, feed * width), tiles.dtype),
+            jax.ShapeDtypeStruct((share, attn * width), tiles.dtype),
+        ],
+        scratch_shapes=[pltpu.SemaphoreType.DMA((feed + attn,))],
         cost_estimate=SMALL_COST,
         name="pick",
-    )(slots, *sources)
+    )(feed_slots, attn_slots, tiles)
 
 
 def adam_kernel(group, at_ref, *refs):
-    feeds = [refs[at * group : (at + 1) * group] for at in range(5)]
-    left_ref, right_ref, master_ref, one_ref, two_ref = refs[5 * group : 5 * group + 5]
-    new_master_ref, new_one_ref, new_two_ref, grad = refs[5 * group + 5 :]
+    feeds = [refs[at * group : (at + 1) * group] for at in range(4)]
+    left_ref, right_ref, master_ref, one_ref, two_ref = refs[4 * group : 4 * group + 5]
+    new_master_ref, new_one_ref, new_two_ref, grad = refs[4 * group + 5 :]
     low = jnp.bfloat16
     for slot in range(group):
         kind = at_ref[0, pl.program_id(0) * group + slot]
-        for number in range(4):
+        for number in range(3):
 
             @pl.when(kind == number)
             def _():
                 grad[slot] = feeds[number][slot][0]
 
+        @pl.when(kind == 3)
+        def _():
+            pair = feeds[3][slot][...].reshape(grad.shape[2], grad.shape[1])
+            grad[slot] = jnp.transpose(pair.astype(jnp.float32)).astype(grad.dtype)
+
         @pl.when(kind == 4)
-        def _():
-            pair = feeds[4][slot][...].reshape(grad.shape[2], grad.shape[1])
-            grad[slot] = jnp.transpose(pair.astype(jnp.float32)).astype(grad.dtype)
-
-        @pl.when(kind == 5)
         def _():
             grad[slot] = jnp.zeros(grad.shape[1:], grad.dtype)
 
@@ -583,7 +608,7 @@
         )
 
 
-def adam(at, gate, up, down, shares, pairs, left, right, master, one, two):
+def adam(at, gating, down, shares, pairs, left, right, master, one, two):
     slots, rows, width = master.shape
     group = 3 if slots % 3 == 0 else 1
     tile = pl.BlockSpec((group, rows, width), lambda i, at: (i, 0, 0))
@@ -600,7 +625,7 @@
 
     pair = [
         pl.BlockSpec(
-            (*pairs.shape[:2], width), lambda i, at, slot=slot: (0, 0, at[5, i * group + slot])
+            (*pairs.shape[:2], width), lambda i, at, slot=slot: (0, 0, at[6, i * group + slot])
         )
         for slot in range(group)
     ]
@@ -609,8 +634,9 @@
         grid_spec=pltpu.PrefetchScalarGridSpec(
             num_scalar_prefetch=1,
             grid=(slots // group,),
-            in_specs=feed(1, 2) * 3
-            + feed(3, 4)
+            in_specs=feed(1, 2)
+            + feed(1, 3)
+            + feed(4, 5)
             + pair
             + [
                 pl.BlockSpec((group, rows, rows), lambda i, at: (i, 0, 0)),
@@ -627,7 +653,7 @@
         cost_estimate=SMALL_COST,
         name="adam",
     )(
-        at, *[gate] * group, *[up] * group, *[down] * group, *[shares] * group, *[pairs] * group,
+        at, *[gating] * group, *[down] * group, *[shares] * group, *[pairs] * group,
         left, right, master, one, two,
     )
 
@@ -836,8 +862,8 @@
     axis = "grp"
     sem_count = 15
 
-    def __init__(self, rows, columns):
-        self.rows, self.columns = rows, columns
+    def __init__(self, rows, columns, placed=True):
+        self.rows, self.columns, self.placed = rows, columns, placed
         self.out_shape = (rows, columns)
 
     def scratch(self):
@@ -861,8 +887,12 @@
         half = self.rows // 2
         self.low, self.high = low, high = pl.ds(0, half), pl.ds(half, half)
         mine, halves, wholes = self.mine, self.halves, self.wholes
+
+        def block(bits):
+            return source.at[PLACES[bits] if self.placed else flip(grp, bits)]
+
         self.copies = [
-            remote(source.at[PLACES[bits]], self.core_in.at[at], sems, at, core)
+            remote(block(bits), self.core_in.at[at], sems, at, core)
             for at, bits in enumerate((7, 3, 5, 1))
         ] + [
             remote(mine.at[0, low], halves.at[0], sems, 4, side_x),
@@ -873,10 +903,11 @@
             remote(mine.at[2, low], wholes.at[1, low], sems, 9, side_y),
         ]
         self.loads = [
-            pltpu.make_async_copy(source.at[PLACES[bits]], mine.at[at], sems[0].at[10 + at])
+            pltpu.make_async_copy(block(bits), mine.at[at], sems[0].at[10 + at])
             for at, bits in enumerate((6, 2, 4, 0))
         ]
-        self.store = pltpu.make_async_copy(mine.at[3], target, sems[0].at[14])
+        if target is not None:
+            self.store = pltpu.make_async_copy(mine.at[3], target, sems[0].at[14])
         if begin:
             self.begin()
 
@@ -902,11 +933,15 @@
         add_rows(mine.at[2, low], mine.at[2, low], self.halves.at[0])
         self.copies[9].start()
 
-    def finish(self):
+    def total(self):
         mine = self.mine
         for at, side, rows in ((6, 0, self.low), (7, 1, self.high), (8, 0, self.high), (9, 1, self.low)):
             self.copies[at].wait_recv()
             add_rows(mine.at[3, rows], mine.at[3, rows], self.wholes.at[side, rows])
+        return mine.at[3]
+
+    def finish(self):
+        self.total()
         self.store.start()
         for copy in self.copies:
             copy.wait_send()
@@ -1230,6 +1265,148 @@
     )
 
 
+def add_blocks(total, blocks):
+    step = min(32, total.shape[0])
+
+    def some(at, _):
+        rows = pl.ds(pl.multiple_of(at * step, step), step)
+        made = blocks[0, rows, :].astype(jnp.float32)
+        for block in range(1, blocks.shape[0]):
+            made = made + blocks[block, rows, :].astype(jnp.float32)
+        total[rows, :] = made.astype(total.dtype)
+        return 0
+
+    lax.fori_loop(0, total.shape[0] // step, some, 0)
+
+
+def tail_kernel(
+    tasks, shares_hbm, pair_hbm, gain_ref, gating_hbm, gating_plane, share_plane, pair_plane,
+    gain_plane, share_parts, share_sum, mine, core_in, halves, wholes, pair_parts, pair_sum,
+    gain_parts, gain_sum, *sems,
+):
+    gating, pair, gain_seq, gain_grp, pair_seq, pair_gather, *halves_of = tasks
+    shares, share_gathers = halves_of[:2], halves_of[2:]
+    grp, seq = lax.axis_index("grp"), lax.axis_index("seq")
+    barrier = pltpu.get_barrier_semaphore()
+    devices = list(gain_grp.peers(grp, seq)) + list(gain_seq.peers(grp, seq))
+    for device in devices:
+        pl.semaphore_signal(barrier, inc=1, device_id=device, device_id_type=MESH)
+    pl.semaphore_wait(barrier, len(devices))
+    sems = [(sems[2 * at], sems[2 * at + 1]) for at in range(len(tasks))]
+
+    def share_part(at):
+        shares[at].finish()
+        add_blocks(share_sum.at[at], share_parts.at[at])
+        share_gathers[at].start(share_sum.at[at], share_plane, sems[8 + at], grp, seq)
+
+    for at in range(2):
+        shares[at].start(shares_hbm, share_parts.at[at], sems[6 + at], grp, seq)
+    pair.start(pair_hbm, None, sems[1], grp, seq, (mine, core_in, halves, wholes))
+    gain_seq.start(gain_ref, gain_parts, sems[2], grp, seq)
+    gating.start(gating_hbm, gating_plane, sems[0], grp, seq, begin=False)
+    gating.kept.start()
+    for at in (1, 4, 7):
+        gating.out[at].start()
+    pair.first_sums()
+    for at in (2, 5):
+        gating.out[at].start()
+    gain_seq.finish()
+    gain_sum[...] = jnp.sum(gain_parts[...], axis=0)
+    gain_grp.start(gain_sum, gain_plane, sems[3], grp, seq)
+    handing = gating.forward()
+    next(handing)
+    for _ in pair.forward():
+        pass
+    share_part(0)
+    next(handing)
+    pair_seq.start(pair.total(), pair_parts, sems[4], grp, seq)
+    share_part(1)
+    next(handing)
+    pair_seq.finish()
+    add_blocks(pair_sum, pair_parts)
+    pair_gather.start(pair_sum, pair_plane, sems[5], grp, seq)
+    hand_on([share_gathers[0], share_gathers[1], pair_gather])
+    for copy in pair.copies:
+        copy.wait_send()
+    for task in (gain_grp, gating, pair_gather, *share_gathers):
+        task.finish()
+
+
+def tail_exchange(number, shares, pair, gain_terms, gating):
+    seq_count = lax.axis_size("seq")
+    low = jnp.bfloat16
+    columns, rows_all = shares.shape
+    rows = rows_all // seq_count
+    _, pair_rows, pair_columns = pair.shape
+    sub = pair_rows // seq_count
+    half = columns // 2
+
+    def share_task(at):
+        return Exchange(
+            "seq",
+            (seq_count, half, rows),
+            lambda ref, index: ref.at[
+                pl.ds(at * half, half), pl.ds(pl.multiple_of(index * rows, rows), rows)
+            ],
+            block_of,
+        )
+
+    def share_gather(at):
+        return gather_plane(
+            (half, rows),
+            target_view=lambda ref, index: ref.at[index, pl.ds(at * half, half)],
+            out_shape=(8, columns, rows),
+        )
+
+    tasks = [
+        gather_plane(gating.shape),
+        PlaneSum(pair_rows, pair_columns, placed=False),
+        gather_axis("seq", gain_terms)[0],
+        gather_axis("grp", gain_terms)[0],
+        Exchange(
+            "seq",
+            (seq_count, sub, pair_columns),
+            lambda ref, index: rows_of(ref, index, sub),
+            block_of,
+        ),
+        gather_plane((sub, pair_columns)),
+        share_task(0),
+        share_task(1),
+        share_gather(0),
+        share_gather(1),
+    ]
+    hbm = pl.BlockSpec(memory_space=pl.ANY)
+    vmem = pl.BlockSpec(memory_space=pltpu.VMEM)
+    scratch = [
+        pltpu.VMEM((2, seq_count, half, rows), low),
+        pltpu.VMEM((2, half, rows), low),
+        *tasks[1].scratch(),
+        pltpu.VMEM((seq_count, sub, pair_columns), low),
+        pltpu.VMEM((sub, pair_columns), low),
+        pltpu.VMEM((seq_count, *gain_terms.shape), jnp.float32),
+        pltpu.VMEM(gain_terms.shape, jnp.float32),
+    ]
+    for task in tasks:
+        scratch += [pltpu.SemaphoreType.DMA((task.sem_count,))] * 2
+    return pl.pallas_call(
+        functools.partial(tail_kernel, tasks),
+        in_specs=[hbm, hbm, vmem, hbm],
+        out_specs=[hbm] * 4,
+        out_shape=[
+            jax.ShapeDtypeStruct(tasks[0].out_shape, low),
+            jax.ShapeDtypeStruct((8, columns, rows), low),
+            jax.ShapeDtypeStruct((8, sub, pair_columns), low),
+            jax.ShapeDtypeStruct((8, *gain_terms.shape), jnp.float32),
+        ],
+        scratch_shapes=scratch,
+        compiler_params=pltpu.CompilerParams(
+            collective_id=number, has_side_effects=True, vmem_limit_bytes=60 * 2**20
+        ),
+        cost_estimate=SMALL_COST,
+        name="tail_exchange",
+    )(shares, pair, gain_terms, gating)
+
+
 def half_rows(axis, height):
     def half_of(view, second):
         index = (slice(None),) * axis + (pl.ds(height if second else 0, height),)
@@ -1378,7 +1555,7 @@
 
 
 def plane_sum_kernel(
-    part_ref, gate_ref, up_ref, x_ref, total_ref, gate_out, up_out, core_in, chip, half_x, half_y,
+    part_ref, gate_ref, up_ref, x_ref, total_ref, grads_out, core_in, chip, half_x, half_y,
     whole_x, whole_y, x_block, stage, send_sems, recv_sems, x_sems, out_sems,
 ):
     grp, seq = lax.axis_index("grp"), lax.axis_index("seq")
@@ -1396,12 +1573,13 @@
         return pltpu.make_async_copy(view, x_block.at[at % 2], x_sems.at[at % 2])
 
     def out_copies(at):
-        place = pl.ds(pl.multiple_of(at * cols, cols), cols)
         return [
             pltpu.make_async_copy(
-                stage.at[which, at % 2], out.at[place], out_sems.at[which, at % 2]
+                stage.at[which, at % 2],
+                grads_out.at[pl.ds(pl.multiple_of((2 * at + which) * cols, cols), cols)],
+                out_sems.at[which, at % 2],
             )
-            for which, out in enumerate((gate_out, up_out))
+            for which in range(2)
         ]
 
     x_copy(0).start()
@@ -1487,22 +1665,19 @@
     rows = rows_all // count
     if count != 8:
         total = lax.psum_scatter(part, "grp", scatter_dimension=0, tiled=True)
-        return (
-            total.astype(jnp.float32),
-            weight_grad(gate_grad, x, seq_count),
-            weight_grad(up_grad, x, seq_count),
-        )
+        both = jnp.concatenate([gate_grad, up_grad], axis=0)
+        return total.astype(jnp.float32), weight_grad(both, x, seq_count)
     low = jnp.bfloat16
     cols, tokens_all = gate_grad.shape
     width = x.shape[1] // seq_count
     vmem = pl.BlockSpec(memory_space=pltpu.VMEM)
     hbm = pl.BlockSpec(memory_space=pl.ANY)
-    grads = jax.ShapeDtypeStruct((seq_count * cols, width), low)
+    grads = jax.ShapeDtypeStruct((2 * seq_count * cols, width), low)
     return pl.pallas_call(
         plane_sum_kernel,
         in_specs=[vmem, vmem, vmem, hbm],
-        out_specs=[vmem, hbm, hbm],
-        out_shape=[jax.ShapeDtypeStruct((rows, columns), jnp.float32), grads, grads],
+        out_specs=[vmem, hbm],
+        out_shape=[jax.ShapeDtypeStruct((rows, columns), jnp.float32), grads],
         scratch_shapes=[
             pltpu.VMEM((4, rows, columns), low),
             pltpu.VMEM((3, rows, columns), low),
@@ -1582,36 +1757,32 @@
             source_view=lambda ref, index: ref.at[:, pl.ds(at * half_block, half_block)],
         )
 
-    flat = (grp_count * slots_here, -1, tile_width)
-    work = [(weight_half(0), weights_low)]
+    def attn_half(at):
+        return gather_plane(
+            (seq_count, half_sub, output_end),
+            target_view=lambda ref, index: ref.at[:, at, index],
+            out_shape=(seq_count, halves, grp_count, half_sub, output_end),
+        )
+
+    flat = (grp_count * slots_here, half_block, tile_width)
+    tiles, segments = exchange(
+        0,
+        [(weight_half(0), weights_low), gather_axis("seq", segment_ids.reshape(-1, tile_width))],
+    )
+    feed_rows, attn_rows = pick(tiles.reshape(flat), feed_slots, attn_slots)
+    feed_parts = [lax.all_gather(feed_rows, "seq", axis=0, tiled=False)]
     if halves == 2:
-        late_rows = Exchange(
-            "grp",
-            (grp_count, slots_here, half_sub, tile_width),
-            lambda ref, index: ref.at[:, pl.ds(half_block + index * half_sub, half_sub)],
-            block_of,
-        )
-        work.append((late_rows, weights_low))
-    work.append(gather_axis("seq", segment_ids.reshape(-1, tile_width)))
-    *tiles, segments = exchange(0, work)
-    tiles = [part.reshape(flat) for part in tiles]
-    attn_rows = pick(attn_slots, tiles, half_sub).reshape(halves, half_sub, output_end)
-    if grp_count == 8 and seq_count == 4:
-        work = [(LineGather(attn_rows.shape), attn_rows)]
+        tiles, attn_first = exchange(
+            1, [(weight_half(1), weights_low), gather_axis("seq", attn_rows)]
+        )
+        feed_rows, attn_rows = pick(tiles.reshape(flat), feed_slots, attn_slots)
+        feed_parts.append(lax.all_gather(feed_rows, "seq", axis=0, tiled=False))
+        attn_weights, _ = exchange(
+            2,
+            [(attn_half(0), attn_first), gather_axis("seq", attn_rows), (attn_half(1), 1, 0)],
+        )
     else:
-        work = [gather_axis("seq", attn_rows)]
-    if halves == 2:
-        work.append((weight_half(1), weights_low))
-    attn_seq, *more = exchange(1, work)
-    tiles = tiles[:1] + [part.reshape(flat) for part in more]
-    feed_rows = pick(feed_slots, tiles)
-    feed_parts = [lax.all_gather(feed_rows, "seq", axis=0, tiled=False)]
-    attn_plane = gather_plane(
-        attn_seq.shape,
-        target_view=lambda ref, index: ref.at[:, :, index],
-        out_shape=(seq_count, halves, grp_count, half_sub, output_end),
-    )
-    (attn_weights,) = exchange(2, [(attn_plane, attn_seq)])
+        _, attn_weights = exchange(2, [gather_axis("seq", attn_rows), (attn_half(0), 0)])
     attn_weights = attn_weights.reshape(MODEL_WIDTH, output_end)
 
     first_key = seq_here * rows_here - first_place
@@ -1646,10 +1817,13 @@
     cot_plane = cot_plane.reshape(-1, MODEL_WIDTH)
     normed_plane = normed_plane.reshape(-1, MODEL_WIDTH)
     real_cols = jnp.clip((hidden_tiles - grp_here * share) * tile_width, 0, share_cols).reshape(1)
+    if halves == 2:
+        some = jnp.sum(feed_parts[0][0, :8, :tile_width].astype(jnp.float32)) * 0.0
+        real_cols = real_cols + some.astype(jnp.int32)
     if grp_count == 8:
         gate_grad, up_grad, two_part, feed_part, second_plane, context_plane, down_grad = (
             feed_gather(
-                4, real_cols, normed_two, context, cot_plane, feed_parts[0], seq_count
+                4, real_cols, normed_two, context, cot_plane, feed_parts, seq_count
             )
         )
         second_plane = second_plane.reshape(-1, MODEL_WIDTH)
@@ -1669,11 +1843,10 @@
     context_plane = context_plane.reshape(-1, MODEL_WIDTH)
     down_grad, two_part = lax.optimization_barrier((down_grad, two_part))
     down_grad = lax.psum_scatter(down_grad, "seq", scatter_dimension=0, tiled=True)
-    norm_two_grad, gate_weight_grad, up_weight_grad = plane_sum(
+    norm_two_grad, gating_grads = plane_sum(
         5, two_part, gate_grad, up_grad, second_plane, seq_count
     )
-    gate_weight_grad = lax.psum_scatter(gate_weight_grad, "seq", scatter_dimension=0, tiled=True)
-    up_weight_grad = lax.psum_scatter(up_weight_grad, "seq", scatter_dimension=0, tiled=True)
+    gating_grads = lax.psum_scatter(gating_grads, "seq", scatter_dimension=0, tiled=True)
 
     out_grad = cotangent.astype(jnp.float32)
     gain_two_term = jnp.sum(norm_two_grad * hidden * inverse_two, axis=0)
@@ -1715,7 +1888,6 @@
         ],
     )
     pair_grad = jnp.sum(pair_parts.astype(jnp.float32), axis=0).astype(jnp.bfloat16)
-    pair_grad, gate_weight_grad = lax.optimization_barrier((pair_grad, gate_weight_grad))
     projected_grad = jnp.concatenate([query_grad, pair_grad], axis=1)
     norm_one_grad = times_transpose(projected_grad, attn_weights[:, :value_end])
     gain_one_term = jnp.sum(norm_one_grad * tok_float * inverse_one, axis=0)
@@ -1726,39 +1898,53 @@
         * inverse_one**3
         * jnp.mean(tok_float * gains[0] * norm_one_grad, axis=-1, keepdims=True)
     )
-    query_weight_grad = contract(query_share.reshape(-1, share_width), normed_plane)
-    out_weight_grad = contract(branch_share.reshape(-1, share_width), context_plane)
+    shares = share_grad(
+        query_share.reshape(-1, share_width),
+        branch_share.reshape(-1, share_width),
+        normed_plane,
+        context_plane,
+    )
     pair_weight_grad = contract(normed, pair_grad).astype(jnp.bfloat16)
-    shares = jnp.concatenate([query_weight_grad, out_weight_grad], axis=0).astype(jnp.bfloat16)
-    feed_shape = (share_cols, rows_block)
-    pair_task = Exchange(
-        "grp",
-        (grp_count, seq_count, sub_rows, 2 * HD),
-        lambda ref, index: ref.at[:, index],
-        block_of,
-    )
-    work = [
-        split_columns("seq", shares),
-        (pair_task, pair_weight_grad.reshape(seq_count, grp_count, sub_rows, 2 * HD)),
-        gather_axis("seq", jnp.stack([gain_one_term, gain_two_term])),
-        (gather_plane(feed_shape), gate_weight_grad),
-        (gather_plane(feed_shape), up_weight_grad),
-    ]
-    share_parts, pair_parts, gain_parts, gate_plane, up_plane = exchange(8, work)
-    gain_seq = jnp.sum(gain_parts, axis=0)
-    shares = jnp.sum(share_parts.astype(jnp.float32), axis=0).astype(jnp.bfloat16)
-    pair_parts = jnp.sum(pair_parts.astype(jnp.float32), axis=0).astype(jnp.bfloat16)
-    pair_task = Exchange("seq", pair_parts.shape, block_of, block_of)
-    _, pair_plane, share_plane, gain_parts = exchange(
-        9,
-        [
-            (pair_task, pair_parts),
-            (gather_plane(pair_parts.shape), 0),
-            (gather_plane(shares.shape), shares),
-            gather_axis("grp", gain_seq),
-        ],
-    )
-    pair_plane = jnp.sum(pair_plane.astype(jnp.float32), axis=1).astype(jnp.bfloat16)
+    gain_terms = jnp.stack([gain_one_term, gain_two_term])
+    pair_blocks = pair_weight_grad.reshape(seq_count, grp_count, sub_rows, 2 * HD)
+    if grp_count == 8:
+        pair_blocks = jnp.transpose(pair_blocks, (1, 0, 2, 3))
+        gating_plane, share_plane, pair_plane, gain_parts = tail_exchange(
+            8,
+            shares,
+            pair_blocks.reshape(grp_count, seq_count * sub_rows, 2 * HD),
+            gain_terms,
+            gating_grads,
+        )
+    else:
+        pair_task = Exchange(
+            "grp",
+            (grp_count, seq_count, sub_rows, 2 * HD),
+            lambda ref, index: ref.at[:, index],
+            block_of,
+        )
+        work = [
+            split_columns("seq", shares),
+            (pair_task, pair_blocks),
+            gather_axis("seq", gain_terms),
+            (gather_plane(gating_grads.shape), gating_grads),
+        ]
+        share_parts, pair_parts, gain_parts, gating_plane = exchange(8, work)
+        gain_seq = jnp.sum(gain_parts, axis=0)
+        shares = jnp.sum(share_parts.astype(jnp.float32), axis=0).astype(jnp.bfloat16)
+        pair_parts = jnp.sum(pair_parts.astype(jnp.float32), axis=0).astype(jnp.bfloat16)
+        pair_task = Exchange("seq", pair_parts.shape, block_of, block_of)
+        _, pair_plane, share_plane, gain_parts = exchange(
+            9,
+            [
+                (pair_task, pair_parts),
+                (gather_plane(pair_parts.shape), 0),
+                (gather_plane(shares.shape), shares),
+                gather_axis("grp", gain_seq),
+            ],
+        )
+        pair_plane = jnp.sum(pair_plane.astype(jnp.float32), axis=1).astype(jnp.bfloat16)
+
     gain_grads = jnp.sum(gain_parts, axis=0)
 
     tile_of_slot = (
@@ -1772,9 +1958,8 @@
     is_query = tiles_here < query_tiles
     is_pair = (tiles_here >= query_tiles) & (tiles_here < query_tiles + 2)
     is_feed = tiles_here >= attn_tiles
-    kind = jnp.where(is_feed, jnp.minimum(which, 2), 3)
-    kind = jnp.where(is_pair, 4, jnp.where(is_feed, kind, 3))
-    kind = jnp.where(tiles_here == tile_count, 5, kind)
+    kind = jnp.where(is_feed, jnp.where(which < 2, 0, 1), jnp.where(is_pair, 3, 2))
+    kind = jnp.where(tiles_here == tile_count, 4, kind)
     out_at = jnp.clip(tiles_here - query_tiles - 2, 0, query_tiles - 1)
     per_share = share_width // tile_width
     share_at = jnp.where(is_query, jnp.minimum(tiles_here, query_tiles - 1), out_at)
@@ -1782,6 +1967,7 @@
         [
             kind,
             column // share,
+            jnp.minimum(which, 1) * share + column % share,
             column % share,
             share_at // per_share,
             share_at % per_share + jnp.where(is_query, 0, per_share),
@@ -1790,8 +1976,7 @@
     )
     new_master, new_one, new_two = adam(
         at,
-        gate_plane,
-        up_plane,
+        gating_plane,
         down_plane,
         share_plane,
         pair_plane,

time: 754 us -> 707 us (0.938)
  waiting for transfers between devices: 16.4 us -> 0.61 us
  matrix products: 27.7 us -> 13.1 us
  other arithmetic: 28.6 us -> 16.9 us
    pallas_call x6 -> x4, Pallas kernels: 344 us -> 221 us  [exchange(): pl.pallas_call(functools.partial(exchange_kernel, tasks, wires, len(array...]
    pallas_call x1 -> x3, Pallas kernels: 80.7 us -> 188 us  [the longest x1 97.6 us: tail_exchange(): pl.pallas_call(functools.partial(tail_kernel, tasks), in_specs=[hbm, hbm,...]
    pallas_call x1, Pallas kernels: 81.3 us -> 96.9 us  [attention_block(): pl.pallas_call(functools.partial(block_kernel, first, second, pair_task),...]
    dot_general x3 -> x1, matrix products: 13 us -> 0.48 us  [contract(): lax.dot_general(left_side, right_side, (((0,), (0,)), ((), ())), preferre...]
    all_gather x1, waiting for transfers between devices: 8.95 us -> 0.02 us  [local(): feed_parts = [lax.all_gather(feed_rows, 'seq', axis=0, tiled=False)]]
  transfers between devices with their start and end apart: 4 -> 4, of which waited for: 2 -> 1; matrix products, arithmetic and copies ran while one was open for 6% -> 5% of each run, Pallas kernels for 40% -> 55%
where the time goes in v7:
time: 707 us; the launch traced here: 706 us
  Pallas kernels  647 us (92%)
  other arithmetic  16.9 us (2%)
  between operations  15 us (2%)
  matrix products  13.1 us (2%)
  local copies, waits for them, and re-layouts  12.9 us (2%)
    pallas_call x4, Pallas kernels, exchange(): pl.pallas_call(functools.partial(exchange_kernel, tasks, wires, len(array...  221 us
    pallas_call x1, Pallas kernels, tail_exchange(): pl.pallas_call(functools.partial(tail_kernel, tasks), in_specs=[hbm, hbm,...  97.6 us
    pallas_call x1, Pallas kernels, attention_block(): pl.pallas_call(functools.partial(block_kernel, first, second, pair_task),...  96.9 us
    pallas_call x1, Pallas kernels, feed_gather(): pl.pallas_call(functools.partial(feed_gather_kernel, first, second, len(p...  80 us
    pallas_call x1, Pallas kernels, attend_back_sum(): pl.pallas_call(functools.partial(attend_back_sum_kernel, sum_task, gather...  62.9 us
    pallas_call x1, Pallas kernels, plane_sum(): pl.pallas_call(plane_sum_kernel, in_specs=[vmem, vmem, vmem, hbm], out_sp...  47.9 us
    pallas_call x1, Pallas kernels, adam(): pl.pallas_call(functools.partial(adam_kernel, group), grid_spec=pltpu.Pre...  23 us
  transfers between devices with their start and end apart: 4, of which 1 were waited for; matrix products, arithmetic and copies ran while one was open for 5% of the time, Pallas kernels for 55%

profile of v7, /device:TPU:0, one launch (start us, length us, event | category | flops | bytes accessed | tf_op | source)
XLA Modules:
  0.0 705.8 jit_solution(1477138560709701754)
XLA Ops:
  7.3 1.2 slice.22.attn_ref
  8.4 0.1 broadcast_add_fusion
  8.5 0.1 add.155
  8.6 1.9 gather_fusion
  10.5 55.0 %exchange.4 = (bf16[8,21,256,128]{3,2,1,0:T(8,128)(2,1)}, s32[4,2,128]{2,1,0:T(2,128)}) custom-call(bf16[21,512,128]{2,1,0:T(8,128)(2,1)} %refs_0_.3, s32[2,128]{1,0:T(2,128)} %bitcast.45), custom_call_target="tpu_custom_call" | custom-call | flops 1 | bytes 1 | tf_op jit(solution)/shard_map/exchange/pallas_call | solution.py:1509
  65.5 3.6 pick.2
  69.1 53.1 %exchange.5 = (bf16[8,21,256,128]{3,2,1,0:T(8,128)(2,1)}, bf16[4,32,4352]{2,1,0:T(8,128)(2,1)}) custom-call(bf16[21,512,128]{2,1,0:T(8,128)(2,1)} %refs_0_.3, bf16[32,4352]{1,0:T(8,128)(2,1)} %get-tuple-element.54.refs_1_), custom_call_target="tpu_custom_call" | custom-call | flops 1 | bytes 1 | tf_op jit(solution)/shard_map/exchange/pallas_call | solution.py:1509
  122.3 3.6 pick.3
  125.9 86.5 %exchange.6 = (bf16[4,2,8,32,4352]{4,3,2,1,0:T(8,128)(2,1)}, bf16[4,32,4352]{2,1,0:T(8,128)(2,1)}) custom-call(bf16[4,32,4352]{2,1,0:T(8,128)(2,1)} %get-tuple-element.55.refs_0_, bf16[32,4352]{1,0:T(8,128)(2,1)} %get-tuple-element.57.refs_1_), custom_call_target="tpu_custom_call" | custom-call | flops 1 | bytes 1 | tf_op jit(solution)/shard_map/exchange/pallas_call | solution.py:1509
  212.5 1.0 copy.23.key_seg_ref
  213.5 1.9 multiply_sine_fusion
  215.5 0.8 fusion.21
  216.3 0.3 fusion.7
  216.6 1.3 fusion.9.normed_ref.normed_hbm
  217.9 96.9 %attention_block.1 = (bf16[256,2304]{1,0:T(8,128)(2,1)}, bf16[1024,256]{1,0:T(8,128)(2,1)}, bf16[256,2048]{1,0:T(8,128)(2,1)}, f32[16,1,256]{2,1,0:T(1,128)}, f3...) custom-call(s32[1024,1]{1,0:T(8,128)} %copy.23.key_seg_ref, ...), custom_call_target="tpu_custom_call" | custom-call | flops 1 | bytes 1 | tf_op jit(solution)/shard_map/attention_block/pallas_call | solution.py:1237
  314.9 1.3 convert_reduce_fusion
  316.9 80.0 %feed_gather.1 = (bf16[768,2048]{1,0:T(8,128)(2,1)}, bf16[768,2048]{1,0:T(8,128)(2,1)}, bf16[2048,2048]{1,0:T(8,128)(2,1)}, bf16[2048,2048]{1,0:T(8,128)(2,1)}, ...) custom-call(s32[1]{0:T(128)} %bitcast.10.real_ref, ...), custom_call_target="tpu_custom_call" | custom-call | flops 1 | bytes 1 | tf_op jit(solution)/shard_map/feed_gather/pallas_call | solution.py:446
  397.0 47.9 %plane_sum.1 = (f32[256,2048]{1,0:T(8,128)}, bf16[6144,512]{1,0:T(8,128)(2,1)}) custom-call(bf16[8,256,2048]{2,1,0:T(8,128)(2,1)} %bitcast.58, bf16[768,2048]{1,0:T(8,128)(2,1)} %get-tuple-element.71.gate_ref, bf16[768,2048]{1,0:T(8,128)(2,1)} %get-tuple-element.72.up_ref, bf16[2048,2048]{1,0:T(8,128)(2,1)} %bitcast.59), custom_call_target="tpu_custom_call" | custom-call | flops 1 | bytes 1 | tf_op jit(solution)/shard_map/plane_sum/pallas_call | solution.py:1676
  444.9 0.6 copy-done.10
  445.6 1.1 scatter_custom_fusion
  446.7 0.1 select_bitcast_fusion
  446.8 0.6 stack.40.at_ref
  447.5 0.1 fusion.34
  447.6 0.3 pad_maximum_fusion
  448.0 2.9 multiply_reduce_fusion
  451.0 0.6 copy-done.17
  451.5 2.0 fusion.36
  453.5 1.0 copy-done.21
  454.5 6.9 fusion.4.grad_ref
  461.5 1.1 copy-done.6
  462.6 62.9 %attend_back_sum.1 = (bf16[256,2048]{1,0:T(8,128)(2,1)S(1)}, bf16[1024,256]{1,0:T(8,128)(2,1)S(1)}, bf16[256,2048]{1,0:T(8,128)(2,1)S(1)}, bf16[8,768,512]{2,1,0:T(8,128)(2,1)}) custom-call(bf16[256,2304]{1,0:T(8,128)(2,1)} %get-tuple-element.60.q_ref, bf16[1024,256]{1,0:T(8,128)(2,1)S(1)} %copy-done.1, bf16[1024,256]{1,0:T(8,128)(2,1)S(1)} %copy-done.1, ...), custom_call_target="tpu_custom_call" | custom-call | flops 1 | bytes 1 | tf_op jit(solution)/shard_map/attend_back_sum/pallas_call | solution.py:1061
  525.5 1.0 copy-done.4
  526.5 0.8 copy-done.7
  527.3 26.6 %exchange.7 = (bf16[4,256,256]{2,1,0:T(8,128)(2,1)}, bf16[8,256,256]{2,1,0:T(8,128)(2,1)}, bf16[8,256,256]{2,1,0:T(8,128)(2,1)}) custom-call(bf16[1024,256]{1,0:T(8,128)(2,1)} %copy-done.7, bf16[256,2048]{1,0:T(8,128)(2,1)} %copy-done.4, bf16[256,2048]{1,0:T(8,128)(2,1)} %copy-done.21), custom_call_target="tpu_custom_call" | custom-call | flops 1 | bytes 1 | tf_op jit(solution)/shard_map/exchange/pallas_call | solution.py:1509
  553.9 10.5 %share_grad.1.shares_hbm = bf16[512,2048]{1,0:T(8,128)(2,1)} custom-call(bf16[2048,256]{1,0:T(8,128)(2,1)} %bitcast.65, bf16[2048,256]{1,0:T(8,128)(2,1)} %bitcast.66, bf16[2048,2048]{1,0:T(8,128)(2,1)} %bitcast.55, bf16[2048,2048]{1,0:T(8,128)(2,1)} %bitcast.56), custom_call_target="tpu_custom_call" | custom-call | flops 1 | bytes 1 | tf_op jit(solution)/shard_map/share_grad/pallas_call | solution.py:513
  564.4 0.1 reduce_sum.78
  564.5 0.5 convolution_convert_fusion
  565.0 1.0 copy.25
  566.1 5.7 fusion.15
  571.9 0.6 pad_maximum_fusion.2.gain_ref
  572.5 1.3 add_convert_fusion
  573.8 0.7 copy-done.16
  574.5 2.0 fusion.11
  576.5 0.5 reduce-scatter.5.cloned.1.call-done.gating_hbm
  577.0 97.6 %tail_exchange.1 = (bf16[8,1536,512]{2,1,0:T(8,128)(2,1)}, bf16[8,512,512]{2,1,0:T(8,128)(2,1)}, bf16[8,64,256]{2,1,0:T(8,128)(2,1)}, f32[8,2,2048]{2,1,0:T(2,128)}) custom-call(bf16[512,2048]{1,0:T(8,128)(2,1)} %share_grad.1.shares_hbm, bf16[8,256,256]{2,1,0:T(8,128)(2,1)} %bitcast.64, f32[2,2048]{1,0:T(2,128)} %pad_maximum_fusion.2.gain_ref, ...), custom_call_target="tpu_custom_call" | custom-call | flops 1 | bytes 1 | tf_op jit(solution)/shard_map/tail_exchange/pallas_call | solution.py:1391
  674.6 1.0 reduce_sum.82
  675.6 0.7 divide_subtract_fusion
  676.3 23.0 %adam.1 = (f32[21,512,128]{2,1,0:T(8,128)}, f32[21,512,128]{2,1,0:T(8,128)}, f32[21,512,128]{2,1,0:T(8,128)}) custom-call(s32[7,21]{1,0:T(8,128)} %stack.40.at_ref, bf16[8,1536,512]{2,1,0:T(8,128)(2,1)} %get-tuple-element.87.refs_0_.refs_1_.refs_2_, bf16[8,1536,512]{2,1,0:T(8,128)(2,1)} %get-tuple-element.87.refs_0_.refs_1_.refs_2_, ...), custom_call_target="tpu_custom_call" | custom-call | flops 1 | bytes 1 | tf_op jit(solution)/shard_map/adam/pallas_call | solution.py:632
  (80 shorter events, 0.6 us)
Async XLA Ops:
  7.2 307.7 %all-gather.5.cloned.1.call-start = ((), (), s32[]{:S(2)}) async-start(), calls=%async_computation.4 | async-start | bytes 5898240 | tf_op jit(solution)/shard_map/all_gather | solution.py:1773
  69.1 247.8 %all-gather.7.cloned.1.call-start = ((), (), s32[]{:S(2)}) async-start(), calls=%async_computation.5 | async-start | bytes 5898240 | tf_op jit(solution)/shard_map/all_gather | solution.py:1779
  125.9 86.6 %copy-start.29 = (s32[4,2,128]{2,1,0:T(2,128)S(1)}, s32[4,2,128]{2,1,0:T(2,128)}, u32[]{:S(2)}) copy-start(s32[4,2,128]{2,1,0:T(2,128)} %get-tuple-element.52) | copy-start | bytes 12292
  125.9 335.5 %reduce-scatter.3.cloned.1.call-start = ((), (), s32[]{:S(2)}) async-start(), calls=%async_computation.2 | async-start | bytes 3932160 | tf_op jit(solution)/shard_map/reduce_scatter | solution.py:1845
  212.5 3.9 copy-start.13
  213.5 3.1 copy-start.23
  215.5 2.5 copy-start.18
  396.9 180.1 %reduce-scatter.5.cloned.1.call-start = ((), (), s32[]{:S(2)}) async-start(), calls=%async_computation.3 | async-start | bytes 7864320 | tf_op jit(solution)/shard_map/reduce_scatter | solution.py:1849
  444.9 0.7 copy-start.10
  444.9 2.6 copy-start.25
  444.9 2.7 copy-start.19
  447.6 3.3 copy-start.20
  448.0 3.0 copy-start.11
  448.0 3.6 copy-start.17
  453.5 1.0 copy-start.21
  454.5 6.9 copy-start
  454.5 6.9 copy-start.1
  454.5 6.9 copy-start.2
  454.5 6.9 copy-start.3
  454.5 6.9 copy-start.8
  454.5 6.9 copy-start.9
  461.4 1.1 copy-start.6
  525.5 1.0 copy-start.4
  526.5 0.8 copy-start.7
  553.9 10.5 %copy-start.22 = (bf16[4,256,256]{2,1,0:T(8,128)(2,1)S(1)}, bf16[4,256,256]{2,1,0:T(8,128)(2,1)}, u32[]{:S(2)}) copy-start(bf16[4,256,256]{2,1,0:T(8,128)(2,1)} %get-tuple-element.81) | copy-start | bytes 1572868
  553.9 10.6 %copy-start.15 = (bf16[256,2048]{1,0:T(8,128)(2,1)S(1)}, bf16[256,2048]{1,0:T(8,128)(2,1)}, u32[]{:S(2)}) copy-start(bf16[256,2048]{1,0:T(8,128)(2,1)} %fusion.9.normed_ref.normed_hbm) | copy-start | bytes 3145732
  564.5 1.6 copy-start.5
  564.5 1.6 copy-start.14
  566.1 6.4 copy-start.12
  572.5 2.0 copy-start.16
  577.0 98.6 %copy-start.24 = (f32[2,2048]{1,0:T(2,128)S(1)}, f32[2,2048]{1,0:T(2,128)}, u32[]{:S(2)}) copy-start(f32[2,2048]{1,0:T(2,128)} %gain_ref.1) | copy-start | bytes 49156
  577.0 98.6 %copy-start.27 = (f32[2,2048]{1,0:T(2,128)S(1)}, f32[2,2048]{1,0:T(2,128)}, u32[]{:S(2)}) copy-start(f32[2,2048]{1,0:T(2,128)} %param.24) | copy-start | bytes 49156
  577.0 98.6 %copy-start.28 = (f32[2,2048]{1,0:T(2,128)S(1)}, f32[2,2048]{1,0:T(2,128)}, u32[]{:S(2)}) copy-start(f32[2,2048]{1,0:T(2,128)} %param.25) | copy-start | bytes 49156
  675.6 23.7 %copy-start.26 = (f32[2,2048]{1,0:T(2,128)}, f32[2,2048]{1,0:T(2,128)S(1)}, u32[]{:S(2)}) copy-start(f32[2,2048]{1,0:T(2,128)S(1)} %reduce_sum.82) | copy-start | bytes 49156
Sparse Core Ops, SparseCore 0:
  69.2 128.0 all-gather.4
  199.5 99.0 all-gather.6
  397.0 58.5 reduce-scatter.2
  457.7 119.1 reduce-scatter.4

commit v8 on v7

--- a/solution.py
+++ b/solution.py
@@ -1,4 +1,5 @@
 import functools
+import math
 
 import jax
 import jax.numpy as jnp
@@ -236,6 +237,10 @@
     )
 
 
+def own_columns(grp, own):
+    return pl.ds(pl.multiple_of((grp * own) % 128, math.gcd(own, 128)), own)
+
+
 def load_weights(parts, weights, sems):
     count, rows, _ = parts[0].shape
     halves = len(parts)
@@ -250,14 +255,15 @@
     ]
 
 
-def feed_block(real, x, cot, weights, act_ref, gate_grad_ref, up_grad_ref, two_ref, out_ref):
+def feed_block(own, first, x, cot, weights, act_ref, gate_grad_ref, up_grad_ref, two_ref, out_ref):
     low = jnp.bfloat16
     wide = jnp.float32
     cols = act_ref.shape[0]
     gate = jnp.dot(x, weights[:, :cols], preferred_element_type=wide)
     upper = jnp.dot(x, weights[:, cols : 2 * cols], preferred_element_type=wide)
     act_grad = jnp.dot(cot, weights[:, 2 * cols :], preferred_element_type=wide)
-    real = lax.broadcasted_iota(jnp.int32, gate.shape, 1) < real
+    column = lax.broadcasted_iota(jnp.int32, gate.shape, 1)
+    real = (column >= first) & (column < first + own)
     sigmoid = 1.0 / (1.0 + jnp.exp(-gate))
     silu = gate * sigmoid
     activated = jnp.where(real, silu * upper, 0.0).astype(low)
@@ -272,7 +278,7 @@
     out_ref[...] = dot_last(activated, weights[:, 2 * cols :]).astype(low)
 
 
-def feed_kernel(real_ref, x_ref, cot_ref, *refs):
+def feed_kernel(own, real_ref, x_ref, cot_ref, *refs):
     parts, refs = refs[:-7], refs[-7:]
     weights, sems = refs[5:]
 
@@ -284,10 +290,10 @@
         for copy in copies:
             copy.wait()
 
-    feed_block(real_ref[0], x_ref[...], cot_ref[...], weights, *refs[:5])
-
-
-def feed_forward(real_cols, x, cot, parts, seq_count):
+    feed_block(own, real_ref[0], x_ref[...], cot_ref[...], weights, *refs[:5])
+
+
+def feed_forward(own, real_cols, x, cot, parts, seq_count):
     tokens_all, width = x.shape
     _, rows, cols = parts[0].shape
     cols = cols // 3
@@ -296,7 +302,7 @@
     block = pl.BlockSpec((step, width), lambda i: (i, 0))
     narrow = pl.BlockSpec((cols, step), lambda i: (0, i))
     return pl.pallas_call(
-        feed_kernel,
+        functools.partial(feed_kernel, own),
         grid=(tokens_all // step,),
         in_specs=[pl.BlockSpec(memory_space=pltpu.SMEM), block, block]
         + [pl.BlockSpec(memory_space=pl.ANY)] * len(parts),
@@ -314,7 +320,7 @@
 
 
 def feed_gather_kernel(
-    first, second, halves, real_ref, own_ref, context_ref, cot_ref, cot_all_ref, *refs
+    own, first, second, halves, real_ref, own_ref, context_ref, cot_ref, cot_all_ref, *refs
 ):
     parts, refs = refs[:halves], refs[halves:]
     (
@@ -381,7 +387,7 @@
     keep = pltpu.make_async_copy(blocks.at[step], second_ref.at[step], keep_sems.at[step])
     keep.start()
     feed_block(
-        real_ref[0], blocks[step], cot_ref[...], weights, act_block, gate_grad_ref, up_grad_ref,
+        own, real_ref[0], blocks[step], cot_ref[...], weights, act_block, gate_grad_ref, up_grad_ref,
         two_ref, out_ref,
     )
     act[:, pl.ds(pl.multiple_of(step * step_rows, step_rows), step_rows)] = act_block[...]
@@ -391,8 +397,9 @@
         return pltpu.make_async_copy(view, x_block.at[at % 2], x_sems.at[at % 2])
 
     def out_copy(at):
-        place = pl.ds(pl.multiple_of(at * cols, cols), cols)
-        return pltpu.make_async_copy(stage.at[at % 2], down_out.at[place], out_sems.at[at % 2])
+        place = pl.ds(pl.multiple_of(at * own, own), own)
+        mine = stage.at[at % 2, own_columns(grp, own)]
+        return pltpu.make_async_copy(mine, down_out.at[place], out_sems.at[at % 2])
 
     @pl.when(step == 7)
     def _():
@@ -432,7 +439,7 @@
             pltpu.make_async_copy(blocks.at[at], second_ref.at[at], keep_sems.at[at]).wait()
 
 
-def feed_gather(number, real_cols, normed, context, cot, parts, seq_count):
+def feed_gather(number, own, real_cols, normed, context, cot, parts, seq_count):
     rows, width = normed.shape
     cols = parts[0].shape[2] // 3
     low = jnp.bfloat16
@@ -444,14 +451,14 @@
     plane = jax.ShapeDtypeStruct((8, rows, width), low)
     model_rows = width // seq_count
     return pl.pallas_call(
-        functools.partial(feed_gather_kernel, first, second, len(parts)),
+        functools.partial(feed_gather_kernel, own, first, second, len(parts)),
         grid=(8,),
         in_specs=[pl.BlockSpec(memory_space=pltpu.SMEM), hbm, hbm, block, hbm]
         + [hbm] * len(parts),
         out_specs=[narrow, narrow, block, block, hbm, hbm, hbm],
         out_shape=[jax.ShapeDtypeStruct((cols, 8 * rows), low)] * 2
         + [jax.ShapeDtypeStruct((8 * rows, width), low)] * 2
-        + [plane, plane, jax.ShapeDtypeStruct((seq_count * cols, model_rows), low)],
+        + [plane, plane, jax.ShapeDtypeStruct((seq_count * own, model_rows), low)],
         scratch_shapes=[
             pltpu.VMEM((8, rows, width), low),
             pltpu.VMEM((width, 3 * cols), low),
@@ -497,10 +504,15 @@
     )(left, x)
 
 
-def share_grad_kernel(query_ref, out_ref, normed_ref, context_ref, grads_ref):
+def share_grad_kernel(query_ref, out_ref, normed_ref, context_ref, grads_ref, turned):
     half = query_ref.shape[1]
-    for at, (left, right) in enumerate(((query_ref, normed_ref), (out_ref, context_ref))):
-        made = dot_first(left[...], right[...])
+
+    @pl.when(pl.program_id(0) == 0)
+    def _():
+        turned[0], turned[1] = jnp.transpose(query_ref[...]), jnp.transpose(out_ref[...])
+
+    for at, right in enumerate((normed_ref, context_ref)):
+        made = jnp.dot(turned[at], right[...], preferred_element_type=jnp.float32)
         grads_ref[at * half : (at + 1) * half, :] = made.astype(grads_ref.dtype)
 
 
@@ -516,6 +528,7 @@
         in_specs=[narrow, narrow, block, block],
         out_specs=pl.BlockSpec((2 * columns, step), lambda i: (0, i)),
         out_shape=jax.ShapeDtypeStruct((2 * columns, width), jnp.bfloat16),
+        scratch_shapes=[pltpu.VMEM((2, columns, tokens_all), jnp.bfloat16)],
         compiler_params=pltpu.CompilerParams(vmem_limit_bytes=60 * 2**20),
         cost_estimate=SMALL_COST,
         name="share_grad",
@@ -574,7 +587,7 @@
 
             @pl.when(kind == number)
             def _():
-                grad[slot] = feeds[number][slot][0]
+                grad[slot] = feeds[number][slot][...]
 
         @pl.when(kind == 3)
         def _():
@@ -614,18 +627,15 @@
     tile = pl.BlockSpec((group, rows, width), lambda i, at: (i, 0, 0))
     shape = jax.ShapeDtypeStruct(master.shape, jnp.float32)
 
-    def feed(block, column):
+    def feed(row):
         return [
-            pl.BlockSpec(
-                (1, width, rows),
-                lambda i, at, slot=slot: (at[block, i * group + slot], at[column, i * group + slot], 0),
-            )
+            pl.BlockSpec((width, rows), lambda i, at, slot=slot: (at[row, i * group + slot], 0))
             for slot in range(group)
         ]
 
     pair = [
         pl.BlockSpec(
-            (*pairs.shape[:2], width), lambda i, at, slot=slot: (0, 0, at[6, i * group + slot])
+            (*pairs.shape[:2], width), lambda i, at, slot=slot: (0, 0, at[4, i * group + slot])
         )
         for slot in range(group)
     ]
@@ -634,9 +644,9 @@
         grid_spec=pltpu.PrefetchScalarGridSpec(
             num_scalar_prefetch=1,
             grid=(slots // group,),
-            in_specs=feed(1, 2)
-            + feed(1, 3)
-            + feed(4, 5)
+            in_specs=feed(1)
+            + feed(2)
+            + feed(3)
             + pair
             + [
                 pl.BlockSpec((group, rows, rows), lambda i, at: (i, 0, 0)),
@@ -1279,10 +1289,57 @@
     lax.fori_loop(0, total.shape[0] // step, some, 0)
 
 
+def norm_one_back(
+    weights_hbm, query_grad_ref, pair_grad_ref, hidden_grad_ref, tokens_ref, inverse_ref, gain_ref,
+    gain_two_ref, input_grad_ref, gain_terms, w_block, norm_grad, w_sems,
+):
+    width, query_columns = tokens_ref.shape[1], query_grad_ref.shape[1]
+    rows, columns = w_block.shape[1:]
+    count = width // rows
+
+    def w_copy(at):
+        view = weights_hbm.at[pl.ds(pl.multiple_of(at * rows, rows), rows), pl.ds(0, columns)]
+        return pltpu.make_async_copy(view, w_block.at[at % 2], w_sems.at[at % 2])
+
+    w_copy(0).start()
+
+    def one(at, _):
+        w_copy(at).wait()
+
+        @pl.when(at + 1 < count)
+        def _():
+            w_copy(at + 1).start()
+
+        made = dot_last(query_grad_ref[...], w_block[at % 2, :, :query_columns])
+        made = made + dot_last(pair_grad_ref[...], w_block[at % 2, :, query_columns:])
+        norm_grad[:, pl.ds(pl.multiple_of(at * rows, rows), rows)] = made
+        return 0
+
+    lax.fori_loop(0, count, one, 0)
+    chunk = 32
+    gain = gain_ref[0:1, :]
+
+    def some(at, sums):
+        part = pl.ds(pl.multiple_of(at * chunk, chunk), chunk)
+        inverse, token = inverse_ref[part, :], tokens_ref[part, :].astype(jnp.float32)
+        made = norm_grad[part, :]
+        scaled = gain * made
+        mean = jnp.mean(token * scaled, axis=-1, keepdims=True)
+        input_grad_ref[part, :] = (
+            hidden_grad_ref[part, :] + inverse * scaled - token * (inverse * inverse * inverse * mean)
+        )
+        return sums + jnp.sum(made * token * inverse, axis=0, keepdims=True)
+
+    zeros = jnp.zeros((1, width), jnp.float32)
+    gain_terms[0:1, :] = lax.fori_loop(0, tokens_ref.shape[0] // chunk, some, zeros)
+    gain_terms[1:2, :] = gain_two_ref[...]
+
+
 def tail_kernel(
-    tasks, shares_hbm, pair_hbm, gain_ref, gating_hbm, gating_plane, share_plane, pair_plane,
-    gain_plane, share_parts, share_sum, mine, core_in, halves, wholes, pair_parts, pair_sum,
-    gain_parts, gain_sum, *sems,
+    tasks, shares_hbm, pair_hbm, gating_hbm, weights_hbm, query_grad_ref, pair_grad_ref,
+    hidden_grad_ref, tokens_ref, inverse_ref, gain_ref, gain_two_ref, gating_plane, share_plane,
+    pair_plane, gain_plane, input_grad_ref, share_parts, share_sum, mine, core_in, halves, wholes,
+    pair_parts, pair_sum, gain_terms, gain_parts, gain_sum, w_block, norm_grad, w_sems, *sems,
 ):
     gating, pair, gain_seq, gain_grp, pair_seq, pair_gather, *halves_of = tasks
     shares, share_gathers = halves_of[:2], halves_of[2:]
@@ -1299,40 +1356,55 @@
         add_blocks(share_sum.at[at], share_parts.at[at])
         share_gathers[at].start(share_sum.at[at], share_plane, sems[8 + at], grp, seq)
 
-    for at in range(2):
-        shares[at].start(shares_hbm, share_parts.at[at], sems[6 + at], grp, seq)
+    shares[0].start(shares_hbm, share_parts.at[0], sems[6], grp, seq)
     pair.start(pair_hbm, None, sems[1], grp, seq, (mine, core_in, halves, wholes))
-    gain_seq.start(gain_ref, gain_parts, sems[2], grp, seq)
     gating.start(gating_hbm, gating_plane, sems[0], grp, seq, begin=False)
     gating.kept.start()
     for at in (1, 4, 7):
         gating.out[at].start()
     pair.first_sums()
+    norm_one_back(
+        weights_hbm, query_grad_ref, pair_grad_ref, hidden_grad_ref, tokens_ref, inverse_ref,
+        gain_ref, gain_two_ref, input_grad_ref, gain_terms, w_block, norm_grad, w_sems,
+    )
+    gain_seq.start(gain_terms, gain_parts, sems[2], grp, seq)
+    for _ in pair.forward():
+        pass
     for at in (2, 5):
         gating.out[at].start()
+    handing = gating.forward()
+    next(handing)
+    pair_seq.start(pair.total(), pair_parts, sems[4], grp, seq)
+    shares[1].start(shares_hbm, share_parts.at[1], sems[7], grp, seq)
     gain_seq.finish()
     gain_sum[...] = jnp.sum(gain_parts[...], axis=0)
     gain_grp.start(gain_sum, gain_plane, sems[3], grp, seq)
-    handing = gating.forward()
-    next(handing)
-    for _ in pair.forward():
-        pass
     share_part(0)
-    next(handing)
-    pair_seq.start(pair.total(), pair_parts, sems[4], grp, seq)
-    share_part(1)
-    next(handing)
     pair_seq.finish()
     add_blocks(pair_sum, pair_parts)
     pair_gather.start(pair_sum, pair_plane, sems[5], grp, seq)
-    hand_on([share_gathers[0], share_gathers[1], pair_gather])
+    next(handing)
+    share_part(1)
+    next(handing)
+    hand_on([share_gathers[0], pair_gather, share_gathers[1]])
     for copy in pair.copies:
         copy.wait_send()
     for task in (gain_grp, gating, pair_gather, *share_gathers):
         task.finish()
 
 
-def tail_exchange(number, shares, pair, gain_terms, gating):
+def gather_gating(shape):
+    return gather_plane(
+        shape,
+        split=1,
+        target_view=lambda ref, index: ref.at[:, index],
+        out_shape=(shape[0], lax.axis_size("grp"), *shape[1:]),
+    )
+
+
+def tail_exchange(number, shares, pair, gating, weights, back):
+    gain_terms = jax.ShapeDtypeStruct((2, back[3].shape[1]), jnp.float32)
+    tokens_here = back[3].shape[0]
     seq_count = lax.axis_size("seq")
     low = jnp.bfloat16
     columns, rows_all = shares.shape
@@ -1359,7 +1431,7 @@
         )
 
     tasks = [
-        gather_plane(gating.shape),
+        gather_gating(gating.shape),
         PlaneSum(pair_rows, pair_columns, placed=False),
         gather_axis("seq", gain_terms)[0],
         gather_axis("grp", gain_terms)[0],
@@ -1383,20 +1455,25 @@
         *tasks[1].scratch(),
         pltpu.VMEM((seq_count, sub, pair_columns), low),
         pltpu.VMEM((sub, pair_columns), low),
+        pltpu.VMEM(gain_terms.shape, jnp.float32),
         pltpu.VMEM((seq_count, *gain_terms.shape), jnp.float32),
         pltpu.VMEM(gain_terms.shape, jnp.float32),
+        pltpu.VMEM((2, 2 * HD, (NH + 2) * HD), low),
+        pltpu.VMEM((tokens_here, back[3].shape[1]), jnp.float32),
+        pltpu.SemaphoreType.DMA((2,)),
     ]
     for task in tasks:
         scratch += [pltpu.SemaphoreType.DMA((task.sem_count,))] * 2
     return pl.pallas_call(
         functools.partial(tail_kernel, tasks),
-        in_specs=[hbm, hbm, vmem, hbm],
-        out_specs=[hbm] * 4,
+        in_specs=[hbm] * 4 + [vmem] * len(back),
+        out_specs=[hbm] * 4 + [vmem],
         out_shape=[
             jax.ShapeDtypeStruct(tasks[0].out_shape, low),
             jax.ShapeDtypeStruct((8, columns, rows), low),
             jax.ShapeDtypeStruct((8, sub, pair_columns), low),
             jax.ShapeDtypeStruct((8, *gain_terms.shape), jnp.float32),
+            jax.ShapeDtypeStruct((tokens_here, back[3].shape[1]), jnp.float32),
         ],
         scratch_shapes=scratch,
         compiler_params=pltpu.CompilerParams(
@@ -1404,7 +1481,7 @@
         ),
         cost_estimate=SMALL_COST,
         name="tail_exchange",
-    )(shares, pair, gain_terms, gating)
+    )(shares, pair, gating, weights, *back)
 
 
 def half_rows(axis, height):
@@ -1555,7 +1632,7 @@
 
 
 def plane_sum_kernel(
-    part_ref, gate_ref, up_ref, x_ref, total_ref, grads_out, core_in, chip, half_x, half_y,
+    own, part_ref, gate_ref, up_ref, x_ref, total_ref, grads_out, core_in, chip, half_x, half_y,
     whole_x, whole_y, x_block, stage, send_sems, recv_sems, x_sems, out_sems,
 ):
     grp, seq = lax.axis_index("grp"), lax.axis_index("seq")
@@ -1564,7 +1641,6 @@
     core_blocks = [PLACES[bits] for bits in (7, 3, 5, 1)]
     half = total_ref.shape[0] // 2
     low, high = pl.ds(0, half), pl.ds(half, half)
-    cols = gate_ref.shape[0]
     rows = x_block.shape[2]
     count = x_ref.shape[1] // rows
 
@@ -1575,8 +1651,8 @@
     def out_copies(at):
         return [
             pltpu.make_async_copy(
-                stage.at[which, at % 2],
-                grads_out.at[pl.ds(pl.multiple_of((2 * at + which) * cols, cols), cols)],
+                stage.at[which, at % 2, own_columns(grp, own)],
+                grads_out.at[pl.ds(pl.multiple_of((2 * at + which) * own, own), own)],
                 out_sems.at[which, at % 2],
             )
             for which in range(2)
@@ -1659,22 +1735,25 @@
             copy.wait()
 
 
-def plane_sum(number, part, gate_grad, up_grad, x, seq_count):
+def plane_sum(number, own, part, gate_grad, up_grad, x, seq_count):
     count = lax.axis_size("grp")
     rows_all, columns = part.shape
     rows = rows_all // count
     if count != 8:
         total = lax.psum_scatter(part, "grp", scatter_dimension=0, tiled=True)
-        both = jnp.concatenate([gate_grad, up_grad], axis=0)
+        begin = (lax.axis_index("grp") * own) % 128
+        both = jnp.concatenate(
+            [lax.dynamic_slice_in_dim(grad, begin, own) for grad in (gate_grad, up_grad)], axis=0
+        )
         return total.astype(jnp.float32), weight_grad(both, x, seq_count)
     low = jnp.bfloat16
     cols, tokens_all = gate_grad.shape
     width = x.shape[1] // seq_count
     vmem = pl.BlockSpec(memory_space=pltpu.VMEM)
     hbm = pl.BlockSpec(memory_space=pl.ANY)
-    grads = jax.ShapeDtypeStruct((2 * seq_count * cols, width), low)
+    grads = jax.ShapeDtypeStruct((2 * seq_count * own, width), low)
     return pl.pallas_call(
-        plane_sum_kernel,
+        functools.partial(plane_sum_kernel, own),
         in_specs=[vmem, vmem, vmem, hbm],
         out_specs=[vmem, hbm],
         out_shape=[jax.ShapeDtypeStruct((rows, columns), jnp.float32), grads],
@@ -1727,8 +1806,8 @@
     attn_tiles = output_end // tile_width
     query_tiles = query_cols // tile_width
     hidden_tiles = FF // tile_width
-    share = -(-hidden_tiles // grp_count)
-    share_cols = share * tile_width
+    own = FF // grp_count
+    share = max(-(-((at * own) % tile_width + own) // tile_width) for at in range(grp_count))
     share_width = MODEL_WIDTH // grp_count
     sub_rows = rows_block // grp_count
     halves = 2 if sub_rows >= 32 else 1
@@ -1737,7 +1816,7 @@
     key_tables = turn_tables(jnp.arange(SEQLEN, dtype=jnp.int32))
     tables = [lax.dynamic_slice_in_dim(table, first_place, rows_here) for table in key_tables]
 
-    hidden_ids = grp_here * share + jnp.arange(share, dtype=jnp.int32)
+    hidden_ids = grp_here * own // tile_width + jnp.arange(share, dtype=jnp.int32)
     hidden_ids = jnp.minimum(hidden_ids, hidden_tiles - 1)
     feed_ids = (
         attn_tiles
@@ -1816,14 +1895,14 @@
 
     cot_plane = cot_plane.reshape(-1, MODEL_WIDTH)
     normed_plane = normed_plane.reshape(-1, MODEL_WIDTH)
-    real_cols = jnp.clip((hidden_tiles - grp_here * share) * tile_width, 0, share_cols).reshape(1)
+    real_cols = ((grp_here * own) % tile_width).reshape(1)
     if halves == 2:
-        some = jnp.sum(feed_parts[0][0, :8, :tile_width].astype(jnp.float32)) * 0.0
+        some = jnp.max(feed_parts[0][0, :8, :tile_width].astype(jnp.float32)) * 0.0
         real_cols = real_cols + some.astype(jnp.int32)
     if grp_count == 8:
         gate_grad, up_grad, two_part, feed_part, second_plane, context_plane, down_grad = (
             feed_gather(
-                4, real_cols, normed_two, context, cot_plane, feed_parts, seq_count
+                4, own, real_cols, normed_two, context, cot_plane, feed_parts, seq_count
             )
         )
         second_plane = second_plane.reshape(-1, MODEL_WIDTH)
@@ -1837,16 +1916,18 @@
         )
         second_plane = second_plane.reshape(-1, MODEL_WIDTH)
         activated, gate_grad, up_grad, two_part, feed_part = feed_forward(
-            real_cols, second_plane, cot_plane, feed_parts, seq_count
-        )
+            own, real_cols, second_plane, cot_plane, feed_parts, seq_count
+        )
+        activated = lax.dynamic_slice_in_dim(activated, (grp_here * own) % tile_width, own)
         down_grad = weight_grad(activated, cot_plane, seq_count)
     context_plane = context_plane.reshape(-1, MODEL_WIDTH)
     down_grad, two_part = lax.optimization_barrier((down_grad, two_part))
     down_grad = lax.psum_scatter(down_grad, "seq", scatter_dimension=0, tiled=True)
     norm_two_grad, gating_grads = plane_sum(
-        5, two_part, gate_grad, up_grad, second_plane, seq_count
+        5, own, two_part, gate_grad, up_grad, second_plane, seq_count
     )
     gating_grads = lax.psum_scatter(gating_grads, "seq", scatter_dimension=0, tiled=True)
+    gating_grads = gating_grads.reshape(2, own, rows_block)
 
     out_grad = cotangent.astype(jnp.float32)
     gain_two_term = jnp.sum(norm_two_grad * hidden * inverse_two, axis=0)
@@ -1888,16 +1969,6 @@
         ],
     )
     pair_grad = jnp.sum(pair_parts.astype(jnp.float32), axis=0).astype(jnp.bfloat16)
-    projected_grad = jnp.concatenate([query_grad, pair_grad], axis=1)
-    norm_one_grad = times_transpose(projected_grad, attn_weights[:, :value_end])
-    gain_one_term = jnp.sum(norm_one_grad * tok_float * inverse_one, axis=0)
-    input_grad = (
-        hidden_grad
-        + inverse_one * gains[0] * norm_one_grad
-        - tok_float
-        * inverse_one**3
-        * jnp.mean(tok_float * gains[0] * norm_one_grad, axis=-1, keepdims=True)
-    )
     shares = share_grad(
         query_share.reshape(-1, share_width),
         branch_share.reshape(-1, share_width),
@@ -1905,18 +1976,29 @@
         context_plane,
     )
     pair_weight_grad = contract(normed, pair_grad).astype(jnp.bfloat16)
-    gain_terms = jnp.stack([gain_one_term, gain_two_term])
     pair_blocks = pair_weight_grad.reshape(seq_count, grp_count, sub_rows, 2 * HD)
     if grp_count == 8:
         pair_blocks = jnp.transpose(pair_blocks, (1, 0, 2, 3))
-        gating_plane, share_plane, pair_plane, gain_parts = tail_exchange(
+        gating_plane, share_plane, pair_plane, gain_parts, input_grad = tail_exchange(
             8,
             shares,
             pair_blocks.reshape(grp_count, seq_count * sub_rows, 2 * HD),
-            gain_terms,
             gating_grads,
+            attn_weights,
+            (query_grad, pair_grad, hidden_grad, tokens, inverse_one, gains, gain_two_term[None, :]),
         )
     else:
+        projected_grad = jnp.concatenate([query_grad, pair_grad], axis=1)
+        norm_one_grad = times_transpose(projected_grad, attn_weights[:, :value_end])
+        gain_one_term = jnp.sum(norm_one_grad * tok_float * inverse_one, axis=0)
+        input_grad = (
+            hidden_grad
+            + inverse_one * gains[0] * norm_one_grad
+            - tok_float
+            * inverse_one**3
+            * jnp.mean(tok_float * gains[0] * norm_one_grad, axis=-1, keepdims=True)
+        )
+        gain_terms = jnp.stack([gain_one_term, gain_two_term])
         pair_task = Exchange(
             "grp",
             (grp_count, seq_count, sub_rows, 2 * HD),
@@ -1927,7 +2009,7 @@
             split_columns("seq", shares),
             (pair_task, pair_blocks),
             gather_axis("seq", gain_terms),
-            (gather_plane(gating_grads.shape), gating_grads),
+            (gather_gating(gating_grads.shape), gating_grads),
         ]
         share_parts, pair_parts, gain_parts, gating_plane = exchange(8, work)
         gain_seq = jnp.sum(gain_parts, axis=0)
@@ -1966,19 +2048,19 @@
     at = jnp.stack(
         [
             kind,
-            column // share,
-            jnp.minimum(which, 1) * share + column % share,
-            column % share,
-            share_at // per_share,
-            share_at % per_share + jnp.where(is_query, 0, per_share),
+            jnp.minimum(which, 1) * hidden_tiles + column,
+            column,
+            share_at // per_share * 2 * per_share
+            + share_at % per_share
+            + jnp.where(is_query, 0, per_share),
             jnp.where(is_pair, tiles_here - query_tiles, 0),
         ]
     )
     new_master, new_one, new_two = adam(
         at,
-        gating_plane,
-        down_plane,
-        share_plane,
+        gating_plane.reshape(-1, rows_block),
+        down_plane.reshape(-1, rows_block),
+        share_plane.reshape(-1, rows_block),
         pair_plane,
         left_basis_set,
         right_basis_set,

time: 707 us -> 688 us (0.973)
  Pallas kernels: 647 us -> 633 us
    pallas_call x3, Pallas kernels: 226 us -> 214 us  [the longest x1 86.5 us: tail_exchange(): pl.pallas_call(functools.partial(tail_kernel, tasks), in_specs=[hbm] * 4...]
  transfers between devices with their start and end apart: 4 -> 4, of which waited for: 1 -> 0; matrix products, arithmetic and copies ran while one was open for 5% -> 4% of each run, Pallas kernels for 55% -> 56%
where the time goes in v8:
time: 688 us; the launch traced here: 686 us
  Pallas kernels  633 us (92%)
  other arithmetic  15.7 us (2%)
  between operations  14.9 us (2%)
  local copies, waits for them, and re-layouts  14.7 us (2%)
  matrix products  7.3 us (1%)
    pallas_call x4, Pallas kernels, exchange(): pl.pallas_call(functools.partial(exchange_kernel, tasks, wires, len(array...  221 us
    pallas_call x1, Pallas kernels, attention_block(): pl.pallas_call(functools.partial(block_kernel, first, second, pair_task),...  96.7 us
    pallas_call x1, Pallas kernels, tail_exchange(): pl.pallas_call(functools.partial(tail_kernel, tasks), in_specs=[hbm] * 4...  86.5 us
    pallas_call x1, Pallas kernels, feed_gather(): pl.pallas_call(functools.partial(feed_gather_kernel, own, first, second,...  79.9 us
    pallas_call x1, Pallas kernels, attend_back_sum(): pl.pallas_call(functools.partial(attend_back_sum_kernel, sum_task, gather...  60.8 us
    pallas_call x1, Pallas kernels, plane_sum(): pl.pallas_call(functools.partial(plane_sum_kernel, own), in_specs=[vmem,...  47.6 us
    pallas_call x1, Pallas kernels, adam(): pl.pallas_call(functools.partial(adam_kernel, group), grid_spec=pltpu.Pre...  22.2 us
  transfers between devices with their start and end apart: 4, of which 0 were waited for; matrix products, arithmetic and copies ran while one was open for 4% of the time, Pallas kernels for 56%

profile of v8, /device:TPU:0, one launch (start us, length us, event | category | flops | bytes accessed | tf_op | source)
XLA Modules:
  0.0 685.9 jit_solution(2521297611959398199)
XLA Ops:
  7.3 1.2 slice.17.attn_ref
  8.5 0.1 broadcast_add_fusion
  8.5 0.1 add.154
  8.6 1.9 gather_fusion
  10.5 55.0 %exchange.4 = (bf16[8,21,256,128]{3,2,1,0:T(8,128)(2,1)}, s32[4,2,128]{2,1,0:T(2,128)}) custom-call(bf16[21,512,128]{2,1,0:T(8,128)(2,1)} %refs_0_.3, s32[2,128]{1,0:T(2,128)} %bitcast.44), custom_call_target="tpu_custom_call" | custom-call | flops 1 | bytes 1 | tf_op jit(solution)/shard_map/exchange/pallas_call | solution.py:1586
  65.5 3.6 pick.2
  69.1 0.0 all-gather.7.cloned.1.call-start
  69.1 53.1 %exchange.5 = (bf16[8,21,256,128]{3,2,1,0:T(8,128)(2,1)}, bf16[4,32,4352]{2,1,0:T(8,128)(2,1)}) custom-call(bf16[21,512,128]{2,1,0:T(8,128)(2,1)} %refs_0_.3, bf16[32,4352]{1,0:T(8,128)(2,1)} %get-tuple-element.55.refs_1_), custom_call_target="tpu_custom_call" | custom-call | flops 1 | bytes 1 | tf_op jit(solution)/shard_map/exchange/pallas_call | solution.py:1586
  122.3 3.6 pick.3
  126.0 86.5 %exchange.6 = (bf16[4,2,8,32,4352]{4,3,2,1,0:T(8,128)(2,1)}, bf16[4,32,4352]{2,1,0:T(8,128)(2,1)}) custom-call(bf16[4,32,4352]{2,1,0:T(8,128)(2,1)} %get-tuple-element.56.refs_0_, bf16[32,4352]{1,0:T(8,128)(2,1)} %get-tuple-element.58.refs_1_), custom_call_target="tpu_custom_call" | custom-call | flops 1 | bytes 1 | tf_op jit(solution)/shard_map/exchange/pallas_call | solution.py:1586
  212.5 1.0 copy.23.key_seg_ref
  213.6 1.9 multiply_sine_fusion
  215.5 0.8 copy-done.15
  216.3 0.2 copy-done.16
  216.5 0.1 copy-done.17
  216.6 0.8 fusion.10
  217.4 0.3 fusion.5
  217.8 1.3 fusion.7.normed_ref.normed_hbm
  219.1 96.7 %attention_block.1 = (bf16[256,2304]{1,0:T(8,128)(2,1)}, bf16[1024,256]{1,0:T(8,128)(2,1)}, bf16[256,2048]{1,0:T(8,128)(2,1)}, f32[16,1,256]{2,1,0:T(1,128)}, f3...) custom-call(s32[1024,1]{1,0:T(8,128)} %copy.23.key_seg_ref, ...), custom_call_target="tpu_custom_call" | custom-call | flops 1 | bytes 1 | tf_op jit(solution)/shard_map/attention_block/pallas_call | solution.py:1247
  315.8 1.3 slice_reduce_fusion
  317.7 79.9 %feed_gather.1 = (bf16[768,2048]{1,0:T(8,128)(2,1)}, bf16[768,2048]{1,0:T(8,128)(2,1)}, bf16[2048,2048]{1,0:T(8,128)(2,1)}, bf16[2048,2048]{1,0:T(8,128)(2,1)}, ...) custom-call(s32[1]{0:T(128)} %bitcast.10.real_ref, ...), custom_call_target="tpu_custom_call" | custom-call | flops 1 | bytes 1 | tf_op jit(solution)/shard_map/feed_gather/pallas_call | solution.py:453
  397.8 47.6 %plane_sum.1 = (f32[256,2048]{1,0:T(8,128)}, bf16[5632,512]{1,0:T(8,128)(2,1)}) custom-call(bf16[8,256,2048]{2,1,0:T(8,128)(2,1)} %bitcast.66, bf16[768,2048]{1,0:T(8,128)(2,1)} %get-tuple-element.72.gate_ref, bf16[768,2048]{1,0:T(8,128)(2,1)} %get-tuple-element.73.up_ref, bf16[2048,2048]{1,0:T(8,128)(2,1)} %bitcast.67), custom_call_target="tpu_custom_call" | custom-call | flops 1 | bytes 1 | tf_op jit(solution)/shard_map/plane_sum/pallas_call | solution.py:1755
  445.4 0.8 copy.26.inverse_ref
  446.3 1.1 scatter_custom_fusion
  447.4 0.1 select_bitcast_fusion
  447.5 0.6 stack.23.at_ref
  448.1 0.1 fusion.20
  448.2 1.9 pad_maximum_fusion
  450.2 2.9 multiply_reduce_fusion
  453.1 2.0 fusion.22
  455.0 1.0 copy-done.19
  456.0 6.8 fusion.2.grad_ref
  462.9 1.1 copy-done.5
  464.0 60.8 %attend_back_sum.1 = (bf16[256,2048]{1,0:T(8,128)(2,1)S(1)}, bf16[1024,256]{1,0:T(8,128)(2,1)S(1)}, bf16[256,2048]{1,0:T(8,128)(2,1)S(1)}, bf16[8,704,512]{2,1,0:T(8,128)(2,1)}) custom-call(bf16[256,2304]{1,0:T(8,128)(2,1)} %get-tuple-element.61.q_ref, bf16[1024,256]{1,0:T(8,128)(2,1)S(1)} %copy-done.2, bf16[1024,256]{1,0:T(8,128)(2,1)S(1)} %copy-done.2, ...), custom_call_target="tpu_custom_call" | custom-call | flops 1 | bytes 1 | tf_op jit(solution)/shard_map/attend_back_sum/pallas_call | solution.py:1071
  524.9 1.0 copy-done.1
  525.8 0.8 copy-done.6
  526.6 26.5 %exchange.7 = (bf16[4,256,256]{2,1,0:T(8,128)(2,1)}, bf16[8,256,256]{2,1,0:T(8,128)(2,1)}, bf16[8,256,256]{2,1,0:T(8,128)(2,1)}) custom-call(bf16[1024,256]{1,0:T(8,128)(2,1)} %copy-done.6, bf16[256,2048]{1,0:T(8,128)(2,1)} %copy-done.1, bf16[256,2048]{1,0:T(8,128)(2,1)} %copy-done.19), custom_call_target="tpu_custom_call" | custom-call | flops 1 | bytes 1 | tf_op jit(solution)/shard_map/exchange/pallas_call | solution.py:1586
  553.1 11.0 %share_grad.1.shares_hbm = bf16[512,2048]{1,0:T(8,128)(2,1)} custom-call(bf16[2048,256]{1,0:T(8,128)(2,1)} %bitcast.74, bf16[2048,256]{1,0:T(8,128)(2,1)} %bitcast.75, bf16[2048,2048]{1,0:T(8,128)(2,1)} %bitcast.63, bf16[2048,2048]{1,0:T(8,128)(2,1)} %bitcast.64), custom_call_target="tpu_custom_call" | custom-call | flops 1 | bytes 1 | tf_op jit(solution)/shard_map/share_grad/pallas_call | solution.py:525
  564.1 0.1 reduce_sum.50.pair_grad_ref
  564.2 0.5 convolution_convert_fusion
  564.7 1.0 copy.25
  565.8 0.6 copy-done.11
  566.3 1.3 add_convert_fusion
  567.6 86.5 %tail_exchange.1 = (bf16[2,8,704,512]{3,2,1,0:T(8,128)(2,1)}, bf16[8,512,512]{2,1,0:T(8,128)(2,1)}, bf16[8,64,256]{2,1,0:T(8,128)(2,1)}, f32[8,2,2048]{2,1,0:T(2,128)}, f32[256,2048]{1,0:T(8,128)}) custom-call(bf16[512,2048]{1,0:T(8,128)(2,1)} %share_grad.1.shares_hbm, bf16[8,256,256]{2,1,0:T(8,128)(2,1)} %bitcast.71, bf16[2,704,512]{2,1,0:T(8,128)(2,1)} %bitcast.73, ...), custom_call_target="tpu_custom_call" | custom-call | flops 1 | bytes 1 | tf_op jit(solution)/shard_map/tail_exchange/pallas_call | solution.py:1467
  654.1 1.0 reduce_sum.52
  655.1 0.7 divide_subtract_fusion
  655.8 22.2 %adam.1 = (f32[21,512,128]{2,1,0:T(8,128)}, f32[21,512,128]{2,1,0:T(8,128)}, f32[21,512,128]{2,1,0:T(8,128)}) custom-call(s32[5,21]{1,0:T(8,128)} %stack.23.at_ref, bf16[11264,512]{1,0:T(8,128)(2,1)} %bitcast.47, bf16[11264,512]{1,0:T(8,128)(2,1)} %bitcast.48, bf16[11264,512]{1,0:T(8,128)(2,1)} %bitcast.49, bf16[5632,512]{1,0:T(8,128)(2,1)} %bitcast.53, ...), custom_call_target="tpu_custom_call" | custom-call | flops 1 | bytes 1 | tf_op jit(solution)/shard_map/adam/pallas_call | solution.py:642
  678.0 1.3 copy.28
  (76 shorter events, 0.5 us)
Async XLA Ops:
  7.2 308.6 %all-gather.5.cloned.1.call-start = ((), (), s32[]{:S(2)}) async-start(), calls=%async_computation.4 | async-start | bytes 5898240 | tf_op jit(solution)/shard_map/all_gather | solution.py:1852
  69.1 248.6 %all-gather.7.cloned.1.call-start = ((), (), s32[]{:S(2)}) async-start(), calls=%async_computation.5 | async-start | bytes 5898240 | tf_op jit(solution)/shard_map/all_gather | solution.py:1858
  125.9 86.6 %copy-start.29 = (s32[4,2,128]{2,1,0:T(2,128)S(1)}, s32[4,2,128]{2,1,0:T(2,128)}, u32[]{:S(2)}) copy-start(s32[4,2,128]{2,1,0:T(2,128)} %get-tuple-element.53) | copy-start | bytes 12292
  125.9 336.9 %reduce-scatter.3.cloned.1.call-start = ((), (), s32[]{:S(2)}) async-start(), calls=%async_computation.2 | async-start | bytes 3604480 | tf_op jit(solution)/shard_map/reduce_scatter | solution.py:1925
  212.5 5.0 copy-start.12
  213.6 4.2 copy-start.23
  215.5 0.8 copy-start.15
  215.5 1.0 copy-start.16
  215.5 1.1 copy-start.17
  397.7 169.9 %reduce-scatter.5.cloned.1.call-start = ((), (), s32[]{:S(2)}) async-start(), calls=%async_computation.3 | async-start | bytes 7208960 | tf_op jit(solution)/shard_map/reduce_scatter | solution.py:1929
  445.4 0.9 copy-start.9
  445.4 2.7 copy-start.25
  445.4 4.7 copy-start.10
  450.2 2.9 copy-start.14
  450.2 2.9 copy-start.18
  455.0 1.0 copy-start.19
  456.0 6.9 copy-start
  456.0 6.9 copy-start.2
  456.0 6.9 copy-start.3
  456.0 6.9 copy-start.4
  456.0 6.9 %copy-start.7 = (f32[16,1,256]{2,1,0:T(1,128)S(1)}, f32[16,1,256]{2,1,0:T(1,128)}, u32[]{:S(2)}) copy-start(f32[16,1,256]{2,1,0:T(1,128)} %get-tuple-element.76.total_ref) | copy-start | bytes 49156
  456.0 6.9 %copy-start.8 = (s32[256]{0:T(256)S(1)}, s32[256]{0:T(256)}, u32[]{:S(2)}) copy-start(s32[256]{0:T(256)} %param.15) | copy-start | bytes 3076
  462.9 1.1 copy-start.5
  524.9 1.0 copy-start.1
  525.8 0.8 copy-start.6
  553.1 11.0 %copy-start.22 = (bf16[4,256,256]{2,1,0:T(8,128)(2,1)S(1)}, bf16[4,256,256]{2,1,0:T(8,128)(2,1)}, u32[]{:S(2)}) copy-start(bf16[4,256,256]{2,1,0:T(8,128)(2,1)} %get-tuple-element.86) | copy-start | bytes 1572868
  553.1 11.1 %copy-start.13 = (bf16[256,2048]{1,0:T(8,128)(2,1)S(1)}, bf16[256,2048]{1,0:T(8,128)(2,1)}, u32[]{:S(2)}) copy-start(bf16[256,2048]{1,0:T(8,128)(2,1)} %fusion.7.normed_ref.normed_hbm) | copy-start | bytes 3145732
  564.2 1.6 copy-start.21
  564.2 2.1 copy-start.11
  567.6 87.4 %copy-start.24 = (f32[2,2048]{1,0:T(2,128)S(1)}, f32[2,2048]{1,0:T(2,128)}, u32[]{:S(2)}) copy-start(f32[2,2048]{1,0:T(2,128)} %gain_ref.3) | copy-start | bytes 49156
  567.6 87.4 %copy-start.27 = (f32[2,2048]{1,0:T(2,128)S(1)}, f32[2,2048]{1,0:T(2,128)}, u32[]{:S(2)}) copy-start(f32[2,2048]{1,0:T(2,128)} %param.24) | copy-start | bytes 49156
  567.6 87.5 %copy-start.28 = (f32[2,2048]{1,0:T(2,128)S(1)}, f32[2,2048]{1,0:T(2,128)}, u32[]{:S(2)}) copy-start(f32[2,2048]{1,0:T(2,128)} %param.25) | copy-start | bytes 49156
  655.1 22.9 %copy-start.26 = (f32[2,2048]{1,0:T(2,128)}, f32[2,2048]{1,0:T(2,128)S(1)}, u32[]{:S(2)}) copy-start(f32[2,2048]{1,0:T(2,128)S(1)} %reduce_sum.52) | copy-start | bytes 49156
  655.8 22.2 %copy-start.20 = (f32[256,2048]{1,0:T(8,128)S(1)}, f32[256,2048]{1,0:T(8,128)}, u32[]{:S(2)}) copy-start(f32[256,2048]{1,0:T(8,128)} %get-tuple-element.131) | copy-start | bytes 6291460
Sparse Core Ops, SparseCore 0:
  69.2 128.0 all-gather.4
  199.5 98.8 all-gather.6
  397.8 54.7 reduce-scatter.2
  454.8 110.5 reduce-scatter.4

commit v9 on v8

--- a/solution.py
+++ b/solution.py
@@ -181,6 +181,7 @@
     specs = {
         "at": pl.BlockSpec(memory_space=pltpu.SMEM),
         "head": pl.BlockSpec((rows, HD), lambda h: (0, h)),
+        "branch": pl.BlockSpec((rows, MODEL_WIDTH), lambda h: (0, 0)),
         "keys": pl.BlockSpec((SEQLEN, HD), lambda h: (0, 0)),
         "values": pl.BlockSpec((SEQLEN, HD), lambda h: (0, 1)),
         "pair": pl.BlockSpec((SEQLEN, 2 * HD), lambda h: (0, 0)),
@@ -1023,10 +1024,10 @@
 
 
 def attend_back_sum_kernel(
-    sum_task, gather_task, q_ref, k_ref, v_ref, grad_ref, total_ref, key_seg_ref, query_seg_ref,
-    key_cosine_ref, key_sine_ref, cosine_ref, sine_ref, part_hbm, down_hbm, query_grad_ref,
-    pair_grad_ref, sum_hbm, down_plane, key_sum, value_sum, mine, core_in, halves, wholes,
-    sum_send, sum_recv, gather_send, gather_recv,
+    sum_task, gather_task, q_ref, k_ref, v_ref, branch_ref, total_ref, key_seg_ref, query_seg_ref,
+    key_cosine_ref, key_sine_ref, cosine_ref, sine_ref, part_hbm, down_hbm, weights_hbm,
+    query_grad_ref, pair_grad_ref, sum_hbm, down_plane, key_sum, value_sum, grad_ref, w_block,
+    w_sems, mine, core_in, halves, wholes, sum_send, sum_recv, gather_send, gather_recv,
 ):
     step = pl.program_id(0)
     grp, seq = lax.axis_index("grp"), lax.axis_index("seq")
@@ -1034,8 +1035,14 @@
     sum_task.start(part_hbm, sum_hbm, (sum_send, sum_recv), grp, seq, scratch, begin=False)
     gather_task.start(down_hbm, down_plane, (gather_send, gather_recv), grp, seq, begin=False)
 
+    def w_copy(at):
+        rows = pl.ds(pl.multiple_of(at * HD, HD), HD)
+        view = weights_hbm.at[rows, pl.ds((NH + 2) * HD, MODEL_WIDTH)]
+        return pltpu.make_async_copy(view, w_block.at[at % 2], w_sems.at[at % 2])
+
     @pl.when(step == 0)
     def _():
+        w_copy(step).start()
         barrier = pltpu.get_barrier_semaphore()
         for device in sum_task.peers(grp, seq):
             pl.semaphore_signal(barrier, inc=1, device_id=device, device_id_type=MESH)
@@ -1047,6 +1054,13 @@
     def _():
         sum_task.first_sums()
 
+    w_copy(step).wait()
+
+    @pl.when(step + 1 < pl.num_programs(0))
+    def _():
+        w_copy(step + 1).start()
+
+    grad_ref[...] = dot_last(branch_ref[...], w_block[step % 2]).astype(grad_ref.dtype)
     attend_back_head(
         seq, q_ref, k_ref, v_ref, grad_ref, total_ref, key_seg_ref, query_seg_ref, key_cosine_ref,
         key_sine_ref, cosine_ref, sine_ref, query_grad_ref, pair_grad_ref, key_sum, value_sum,
@@ -1060,7 +1074,8 @@
 
 
 def attend_back_sum(
-    number, projected, pairs, grads, totals, key_segs, query_segs, key_tables, tables, part, down
+    number, projected, pairs, branch_grad, totals, key_segs, query_segs, key_tables, tables, part,
+    down, weights,
 ):
     rows = projected.shape[0]
     columns = NH * HD
@@ -1072,11 +1087,11 @@
         functools.partial(attend_back_sum_kernel, sum_task, gather_task),
         grid=(NH,),
         in_specs=attention_specs(
-            ["head", "keys", "values", "head", "total", "key_seg", "query_seg"]
+            ["head", "keys", "values", "branch", "total", "key_seg", "query_seg"]
             + ["key_table", "key_table", "table", "table"],
             rows,
         )
-        + [hbm, hbm],
+        + [hbm, hbm, hbm],
         out_specs=attention_specs(["head", "pair"], rows) + [hbm, hbm],
         out_shape=[
             jax.ShapeDtypeStruct((rows, columns), low),
@@ -1085,6 +1100,11 @@
             jax.ShapeDtypeStruct(gather_task.out_shape, low),
         ],
         scratch_shapes=[pltpu.VMEM((SEQLEN, HD), jnp.float32)] * 2
+        + [
+            pltpu.VMEM((rows, HD), low),
+            pltpu.VMEM((2, HD, MODEL_WIDTH), low),
+            pltpu.SemaphoreType.DMA((2,)),
+        ]
         + sum_task.scratch()
         + [pltpu.SemaphoreType.DMA((sum_task.sem_count,))] * 2
         + [pltpu.SemaphoreType.DMA((gather_task.sem_count,))] * 2,
@@ -1094,8 +1114,8 @@
         cost_estimate=SMALL_COST,
         name="attend_back_sum",
     )(
-        projected, pairs, pairs, grads, totals, key_segs[:, None], query_segs[None, :],
-        *key_tables, *tables, part, down,
+        projected, pairs, pairs, branch_grad, totals, key_segs[:, None], query_segs[None, :],
+        *key_tables, *tables, part, down, weights,
     )
 
 
@@ -1939,15 +1959,15 @@
         * jnp.mean(hidden * gains[1] * norm_two_grad, axis=-1, keepdims=True)
     )
     branch_grad = hidden_grad.astype(jnp.bfloat16)
-    context_grad = times_transpose(branch_grad, attn_weights[:, value_end:]).astype(jnp.bfloat16)
     fused = grp_count == 8 and seq_count * rows_here == SEQLEN
     if fused:
         feed_part = feed_part.reshape(grp_count, rows_here, MODEL_WIDTH)
         query_grad, pair_part, feed_out, down_plane = attend_back_sum(
-            6, projected, pairs, context_grad, log_totals, key_segs, segment_ids, key_tables,
-            tables, feed_part, down_grad,
+            6, projected, pairs, branch_grad, log_totals, key_segs, segment_ids, key_tables,
+            tables, feed_part, down_grad, attn_weights,
         )
     else:
+        context_grad = times_transpose(branch_grad, attn_weights[:, value_end:]).astype(jnp.bfloat16)
         query_grad, pair_part = attend_back(
             at, projected, pairs, context_grad, log_totals, key_segs, segment_ids, key_tables, tables
         )

time: 688 us -> 683 us (level)
  transfers between devices with their start and end apart: 4 -> 4, of which waited for: 0 -> 1; matrix products, arithmetic and copies ran while one was open for 4% -> 3% of each run, Pallas kernels for 56% -> 57%
where the time goes in v9:
time: 683 us; the launch traced here: 681 us
  Pallas kernels  631 us (92%)
  other arithmetic  17.3 us (3%)
  between operations  15 us (2%)
  local copies, waits for them, and re-layouts  13.5 us (2%)
    pallas_call x4, Pallas kernels, exchange(): pl.pallas_call(functools.partial(exchange_kernel, tasks, wires, len(array...  221 us
    pallas_call x1, Pallas kernels, attention_block(): pl.pallas_call(functools.partial(block_kernel, first, second, pair_task),...  96.6 us
    pallas_call x1, Pallas kernels, tail_exchange(): pl.pallas_call(functools.partial(tail_kernel, tasks), in_specs=[hbm] * 4...  83.3 us
    pallas_call x1, Pallas kernels, feed_gather(): pl.pallas_call(functools.partial(feed_gather_kernel, own, first, second,...  80 us
    pallas_call x1, Pallas kernels, attend_back_sum(): pl.pallas_call(functools.partial(attend_back_sum_kernel, sum_task, gather...  61.3 us
    pallas_call x1, Pallas kernels, plane_sum(): pl.pallas_call(functools.partial(plane_sum_kernel, own), in_specs=[vmem,...  47.6 us
    pallas_call x1, Pallas kernels, adam(): pl.pallas_call(functools.partial(adam_kernel, group), grid_spec=pltpu.Pre...  23.1 us
  transfers between devices with their start and end apart: 4, of which 1 were waited for; matrix products, arithmetic and copies ran while one was open for 3% of the time, Pallas kernels for 57%

profile of v9, /device:TPU:0, one launch (start us, length us, event | category | flops | bytes accessed | tf_op | source)
XLA Modules:
  0.0 681.3 jit_solution(17753284923283086926)
XLA Ops:
  7.3 1.2 slice.14.attn_ref
  8.5 0.1 broadcast_add_fusion
  8.5 0.1 add.154
  8.6 1.9 gather_fusion
  10.5 55.0 %exchange.4 = (bf16[8,21,256,128]{3,2,1,0:T(8,128)(2,1)}, s32[4,2,128]{2,1,0:T(2,128)}) custom-call(bf16[21,512,128]{2,1,0:T(8,128)(2,1)} %refs_0_.3, s32[2,128]{1,0:T(2,128)} %bitcast.43), custom_call_target="tpu_custom_call" | custom-call | flops 1 | bytes 1 | tf_op jit(solution)/shard_map/exchange/pallas_call | solution.py:1606
  65.5 3.6 pick.2
  69.1 0.0 all-gather.7.cloned.1.call-start
  69.1 53.1 %exchange.5 = (bf16[8,21,256,128]{3,2,1,0:T(8,128)(2,1)}, bf16[4,32,4352]{2,1,0:T(8,128)(2,1)}) custom-call(bf16[21,512,128]{2,1,0:T(8,128)(2,1)} %refs_0_.3, bf16[32,4352]{1,0:T(8,128)(2,1)} %get-tuple-element.55.refs_1_), custom_call_target="tpu_custom_call" | custom-call | flops 1 | bytes 1 | tf_op jit(solution)/shard_map/exchange/pallas_call | solution.py:1606
  122.3 3.6 pick.3
  126.0 86.5 %exchange.6 = (bf16[4,2,8,32,4352]{4,3,2,1,0:T(8,128)(2,1)}, bf16[4,32,4352]{2,1,0:T(8,128)(2,1)}) custom-call(bf16[4,32,4352]{2,1,0:T(8,128)(2,1)} %get-tuple-element.56.refs_0_, bf16[32,4352]{1,0:T(8,128)(2,1)} %get-tuple-element.58.refs_1_), custom_call_target="tpu_custom_call" | custom-call | flops 1 | bytes 1 | tf_op jit(solution)/shard_map/exchange/pallas_call | solution.py:1606
  212.5 1.0 copy.23.key_seg_ref
  213.6 1.9 multiply_sine_fusion
  215.5 0.8 copy-done.16
  216.3 0.2 copy-done.17
  216.5 0.1 copy-done.18
  216.6 0.8 fusion.5
  217.4 0.3 fusion
  217.8 1.3 fusion.2.normed_ref.normed_hbm
  219.0 96.6 %attention_block.1 = (bf16[256,2304]{1,0:T(8,128)(2,1)}, bf16[1024,256]{1,0:T(8,128)(2,1)}, bf16[256,2048]{1,0:T(8,128)(2,1)}, f32[16,1,256]{2,1,0:T(1,128)}, f3...) custom-call(s32[1024,1]{1,0:T(8,128)} %copy.23.key_seg_ref, ...), custom_call_target="tpu_custom_call" | custom-call | flops 1 | bytes 1 | tf_op jit(solution)/shard_map/attention_block/pallas_call | solution.py:1267
  315.7 1.3 slice_reduce_fusion
  317.7 80.0 %feed_gather.1 = (bf16[768,2048]{1,0:T(8,128)(2,1)}, bf16[768,2048]{1,0:T(8,128)(2,1)}, bf16[2048,2048]{1,0:T(8,128)(2,1)}, bf16[2048,2048]{1,0:T(8,128)(2,1)}, ...) custom-call(s32[1]{0:T(128)} %bitcast.10.real_ref, ...), custom_call_target="tpu_custom_call" | custom-call | flops 1 | bytes 1 | tf_op jit(solution)/shard_map/feed_gather/pallas_call | solution.py:454
  397.7 0.0 reduce-scatter.5.cloned.1.call-start
  397.7 47.6 %plane_sum.1 = (f32[256,2048]{1,0:T(8,128)}, bf16[5632,512]{1,0:T(8,128)(2,1)}) custom-call(bf16[8,256,2048]{2,1,0:T(8,128)(2,1)} %bitcast.65, bf16[768,2048]{1,0:T(8,128)(2,1)} %get-tuple-element.72.gate_ref, bf16[768,2048]{1,0:T(8,128)(2,1)} %get-tuple-element.73.up_ref, bf16[2048,2048]{1,0:T(8,128)(2,1)} %bitcast.66), custom_call_target="tpu_custom_call" | custom-call | flops 1 | bytes 1 | tf_op jit(solution)/shard_map/plane_sum/pallas_call | solution.py:1775
  445.4 0.8 copy.26.inverse_ref
  446.2 1.1 scatter_custom_fusion
  447.3 0.1 select_bitcast_fusion
  447.4 0.6 stack.23.at_ref
  448.1 0.1 fusion.15
  448.2 1.9 pad_maximum_fusion
  450.1 2.9 multiply_reduce_fusion
  453.1 3.6 fusion.17
  456.8 1.1 copy-done.5
  457.9 61.3 %attend_back_sum.1 = (bf16[256,2048]{1,0:T(8,128)(2,1)S(1)}, bf16[1024,256]{1,0:T(8,128)(2,1)S(1)}, bf16[256,2048]{1,0:T(8,128)(2,1)S(1)}, bf16[8,704,512]{2,1,0:T(8,128)(2,1)}) custom-call(bf16[256,2304]{1,0:T(8,128)(2,1)} %get-tuple-element.61.q_ref, bf16[1024,256]{1,0:T(8,128)(2,1)S(1)} %copy-done.2, bf16[1024,256]{1,0:T(8,128)(2,1)S(1)} %copy-done.2, ...), custom_call_target="tpu_custom_call" | custom-call | flops 1 | bytes 1 | tf_op jit(solution)/shard_map/attend_back_sum/pallas_call | solution.py:1086
  519.2 1.0 copy-done.1
  520.2 0.8 copy-done.6
  521.0 26.6 %exchange.7 = (bf16[4,256,256]{2,1,0:T(8,128)(2,1)}, bf16[8,256,256]{2,1,0:T(8,128)(2,1)}, bf16[8,256,256]{2,1,0:T(8,128)(2,1)}) custom-call(bf16[1024,256]{1,0:T(8,128)(2,1)} %copy-done.6, bf16[256,2048]{1,0:T(8,128)(2,1)} %copy-done.1, bf16[256,2048]{1,0:T(8,128)(2,1)} %get-tuple-element.109.branch_ref.refs_2_), custom_call_target="tpu_custom_call" | custom-call | flops 1 | bytes 1 | tf_op jit(solution)/shard_map/exchange/pallas_call | solution.py:1606
  547.6 11.1 %share_grad.1.shares_hbm = bf16[512,2048]{1,0:T(8,128)(2,1)} custom-call(bf16[2048,256]{1,0:T(8,128)(2,1)} %bitcast.73, bf16[2048,256]{1,0:T(8,128)(2,1)} %bitcast.74, bf16[2048,2048]{1,0:T(8,128)(2,1)} %bitcast.63, bf16[2048,2048]{1,0:T(8,128)(2,1)} %bitcast.64), custom_call_target="tpu_custom_call" | custom-call | flops 1 | bytes 1 | tf_op jit(solution)/shard_map/share_grad/pallas_call | solution.py:526
  558.7 0.1 reduce_sum.50.pair_grad_ref
  558.8 0.5 convolution_convert_fusion
  559.3 1.0 copy.25
  560.4 0.3 copy-done.12
  560.7 1.3 add_convert_fusion
  562.0 3.4 reduce-scatter.5.cloned.1.call-done
  565.4 83.3 %tail_exchange.1 = (bf16[2,8,704,512]{3,2,1,0:T(8,128)(2,1)}, bf16[8,512,512]{2,1,0:T(8,128)(2,1)}, bf16[8,64,256]{2,1,0:T(8,128)(2,1)}, f32[8,2,2048]{2,1,0:T(2,128)}, f32[256,2048]{1,0:T(8,128)}) custom-call(bf16[512,2048]{1,0:T(8,128)(2,1)} %share_grad.1.shares_hbm, bf16[8,256,256]{2,1,0:T(8,128)(2,1)} %bitcast.70, bf16[2,704,512]{2,1,0:T(8,128)(2,1)} %bitcast.72, ...), custom_call_target="tpu_custom_call" | custom-call | flops 1 | bytes 1 | tf_op jit(solution)/shard_map/tail_exchange/pallas_call | solution.py:1487
  648.7 1.0 reduce_sum.52
  649.7 0.7 divide_subtract_fusion
  650.3 23.1 %adam.1 = (f32[21,512,128]{2,1,0:T(8,128)}, f32[21,512,128]{2,1,0:T(8,128)}, f32[21,512,128]{2,1,0:T(8,128)}) custom-call(s32[5,21]{1,0:T(8,128)} %stack.23.at_ref, bf16[11264,512]{1,0:T(8,128)(2,1)} %bitcast.49, bf16[11264,512]{1,0:T(8,128)(2,1)} %bitcast.50, bf16[11264,512]{1,0:T(8,128)(2,1)} %bitcast.51, bf16[5632,512]{1,0:T(8,128)(2,1)} %bitcast.52, ...), custom_call_target="tpu_custom_call" | custom-call | flops 1 | bytes 1 | tf_op jit(solution)/shard_map/adam/pallas_call | solution.py:643
  673.5 1.3 copy.28
  (73 shorter events, 0.4 us)
Async XLA Ops:
  7.2 308.6 %all-gather.5.cloned.1.call-start = ((), (), s32[]{:S(2)}) async-start(), calls=%async_computation.4 | async-start | bytes 5898240 | tf_op jit(solution)/shard_map/all_gather | solution.py:1872
  69.1 248.6 %all-gather.7.cloned.1.call-start = ((), (), s32[]{:S(2)}) async-start(), calls=%async_computation.5 | async-start | bytes 5898240 | tf_op jit(solution)/shard_map/all_gather | solution.py:1878
  125.9 86.6 %copy-start.28 = (s32[4,2,128]{2,1,0:T(2,128)S(1)}, s32[4,2,128]{2,1,0:T(2,128)}, u32[]{:S(2)}) copy-start(s32[4,2,128]{2,1,0:T(2,128)} %get-tuple-element.53) | copy-start | bytes 12292
  125.9 330.8 %reduce-scatter.3.cloned.1.call-start = ((), (), s32[]{:S(2)}) async-start(), calls=%async_computation.2 | async-start | bytes 3604480 | tf_op jit(solution)/shard_map/reduce_scatter | solution.py:1945
  212.5 5.0 copy-start.13
  213.6 4.2 copy-start.22
  215.5 0.9 copy-start.16
  215.5 1.0 copy-start.17
  215.5 1.1 copy-start.18
  397.7 167.7 %reduce-scatter.5.cloned.1.call-start = ((), (), s32[]{:S(2)}) async-start(), calls=%async_computation.3 | async-start | bytes 7208960 | tf_op jit(solution)/shard_map/reduce_scatter | solution.py:1949
  445.3 0.9 copy-start.9
  445.4 2.7 copy-start.24
  445.4 4.7 copy-start.10
  450.1 2.9 copy-start.11
  450.1 2.9 copy-start.15
  453.1 3.7 copy-start
  453.1 3.7 copy-start.2
  453.1 3.7 copy-start.3
  453.1 3.7 copy-start.4
  453.1 3.7 copy-start.7
  453.1 3.7 copy-start.8
  456.8 1.1 copy-start.5
  519.2 1.0 copy-start.1
  520.2 0.8 copy-start.6
  547.6 11.1 %copy-start.21 = (bf16[4,256,256]{2,1,0:T(8,128)(2,1)S(1)}, bf16[4,256,256]{2,1,0:T(8,128)(2,1)}, u32[]{:S(2)}) copy-start(bf16[4,256,256]{2,1,0:T(8,128)(2,1)} %get-tuple-element.86) | copy-start | bytes 1572868
  547.6 11.2 %copy-start.14 = (bf16[256,2048]{1,0:T(8,128)(2,1)S(1)}, bf16[256,2048]{1,0:T(8,128)(2,1)}, u32[]{:S(2)}) copy-start(bf16[256,2048]{1,0:T(8,128)(2,1)} %fusion.2.normed_ref.normed_hbm) | copy-start | bytes 3145732
  558.8 1.6 copy-start.20
  558.8 1.9 copy-start.12
  565.4 84.3 %copy-start.23 = (f32[2,2048]{1,0:T(2,128)S(1)}, f32[2,2048]{1,0:T(2,128)}, u32[]{:S(2)}) copy-start(f32[2,2048]{1,0:T(2,128)} %gain_ref.3) | copy-start | bytes 49156
  565.4 84.3 %copy-start.26 = (f32[2,2048]{1,0:T(2,128)S(1)}, f32[2,2048]{1,0:T(2,128)}, u32[]{:S(2)}) copy-start(f32[2,2048]{1,0:T(2,128)} %param.24) | copy-start | bytes 49156
  565.4 84.3 %copy-start.27 = (f32[2,2048]{1,0:T(2,128)S(1)}, f32[2,2048]{1,0:T(2,128)}, u32[]{:S(2)}) copy-start(f32[2,2048]{1,0:T(2,128)} %param.25) | copy-start | bytes 49156
  649.7 23.8 %copy-start.25 = (f32[2,2048]{1,0:T(2,128)}, f32[2,2048]{1,0:T(2,128)S(1)}, u32[]{:S(2)}) copy-start(f32[2,2048]{1,0:T(2,128)S(1)} %reduce_sum.52) | copy-start | bytes 49156
  650.3 23.1 %copy-start.19 = (f32[256,2048]{1,0:T(8,128)S(1)}, f32[256,2048]{1,0:T(8,128)}, u32[]{:S(2)}) copy-start(f32[256,2048]{1,0:T(8,128)} %get-tuple-element.131) | copy-start | bytes 6291460
Sparse Core Ops, SparseCore 0:
  69.2 128.0 all-gather.4
  199.5 98.8 all-gather.6
  397.8 54.7 reduce-scatter.2
  454.8 110.5 reduce-scatter.4

commit v10 on v9

--- a/solution.py
+++ b/solution.py
@@ -43,19 +43,17 @@
     half_width = HD // 2
     frequency = ROPE_BASE ** (-(jnp.arange(half_width, dtype=jnp.float32) * 2.0) / HD)
     angles = places.astype(jnp.float32)[:, None] * frequency[None, :]
-    cosine, sine = jnp.cos(angles), jnp.sin(angles)
-    return (
-        jnp.concatenate([cosine, cosine], axis=1),
-        jnp.concatenate([-sine, sine], axis=1),
-    )
+    return jnp.cos(angles), jnp.sin(angles)
 
 
 def turn(rows, cosine, sine):
+    cosine = jnp.concatenate([cosine, cosine], axis=1)
+    sine = jnp.concatenate([-sine, sine], axis=1)
     return rows * cosine + pltpu.roll(rows, HD // 2, 1) * sine
 
 
 def turn_back(rows, cosine, sine):
-    return rows * cosine - pltpu.roll(rows, HD // 2, 1) * sine
+    return turn(rows, cosine, -sine)
 
 
 def dot_last(left_side, right_side):
@@ -91,8 +89,8 @@
         in_specs=[
             pl.BlockSpec((rows, width), lambda j: (0, 0)),
             pl.BlockSpec((width, 2 * HD), lambda j: (0, j)),
-            pl.BlockSpec((rows, HD), lambda j: (0, 0)),
-            pl.BlockSpec((rows, HD), lambda j: (0, 0)),
+            pl.BlockSpec((rows, HD // 2), lambda j: (0, 0)),
+            pl.BlockSpec((rows, HD // 2), lambda j: (0, 0)),
         ],
         out_specs=pl.BlockSpec((rows, 2 * HD), lambda j: (0, j)),
         out_shape=jax.ShapeDtypeStruct((rows, steps * 2 * HD), jnp.bfloat16),
@@ -188,8 +186,8 @@
         "total": pl.BlockSpec((1, 1, rows), lambda h: (h, 0, 0)),
         "key_seg": pl.BlockSpec((SEQLEN, 1), lambda h: (0, 0)),
         "query_seg": pl.BlockSpec((1, rows), lambda h: (0, 0)),
-        "key_table": pl.BlockSpec((SEQLEN, HD), lambda h: (0, 0)),
-        "table": pl.BlockSpec((rows, HD), lambda h: (0, 0)),
+        "key_table": pl.BlockSpec((SEQLEN, HD // 2), lambda h: (0, 0)),
+        "table": pl.BlockSpec((rows, HD // 2), lambda h: (0, 0)),
     }
     return [specs[kind] for kind in kinds]
 
@@ -364,6 +362,7 @@
     @pl.when(step == 3)
     def _():
         first.pass_on(5)
+        second.begin()
 
     @pl.when(step == 4)
     def _():
@@ -371,7 +370,6 @@
         first.due[9].wait_recv()
         first.pass_on(6)
         first.pass_on(3)
-        second.begin()
 
     @pl.when(step == 5)
     def _():
@@ -409,11 +407,6 @@
         second.pass_on(5)
 
         def one(at, _):
-            @pl.when(at == 2)
-            def _():
-                second.pass_on(6)
-                second.pass_on(3)
-
             x_copy(at).wait()
 
             @pl.when(at + 1 < count)
@@ -431,6 +424,8 @@
             return 0
 
         lax.fori_loop(0, count, one, 0)
+        second.pass_on(6)
+        second.pass_on(3)
         out_copy(count - 2).wait()
         out_copy(count - 1).wait()
         second.finish()
@@ -1273,8 +1268,8 @@
             full((rows, width)),
             full((rows, width)),
             full((2, width)),
-            full((rows, HD)),
-            full((rows, HD)),
+            full((rows, HD // 2)),
+            full((rows, HD // 2)),
             hbm,
             hbm,
             pl.BlockSpec((width, wide), weight_block),
@@ -2049,9 +2044,10 @@
 
     gain_grads = jnp.sum(gain_parts, axis=0)
 
+    owner_slots, _ = lax.optimization_barrier((tile_owner_slots, pair_grad))
     tile_of_slot = (
         jnp.full((grp_count * slots_here,), tile_count, jnp.int32)
-        .at[tile_owner_slots]
+        .at[owner_slots]
         .set(jnp.arange(tile_count, dtype=jnp.int32))
     )
     tiles_here = lax.dynamic_slice_in_dim(tile_of_slot, grp_here * slots_here, slots_here)

time: 683 us -> 678 us (level)
  no operation moved by 1% of the time
where the time goes in v10:
time: 678 us; the launch traced here: 677 us
  Pallas kernels  631 us (93%)
  other arithmetic  16.2 us (2%)
  between operations  14.9 us (2%)
  local copies, waits for them, and re-layouts  13.8 us (2%)
    pallas_call x4, Pallas kernels, exchange(): pl.pallas_call(functools.partial(exchange_kernel, tasks, wires, len(array...  221 us
    pallas_call x1, Pallas kernels, attention_block(): pl.pallas_call(functools.partial(block_kernel, first, second, pair_task),...  96.8 us
    pallas_call x1, Pallas kernels, tail_exchange(): pl.pallas_call(functools.partial(tail_kernel, tasks), in_specs=[hbm] * 4...  84.4 us
    pallas_call x1, Pallas kernels, feed_gather(): pl.pallas_call(functools.partial(feed_gather_kernel, own, first, second,...  77.1 us
    pallas_call x1, Pallas kernels, attend_back_sum(): pl.pallas_call(functools.partial(attend_back_sum_kernel, sum_task, gather...  62.2 us
    pallas_call x1, Pallas kernels, plane_sum(): pl.pallas_call(functools.partial(plane_sum_kernel, own), in_specs=[vmem,...  48.1 us
    pallas_call x1, Pallas kernels, adam(): pl.pallas_call(functools.partial(adam_kernel, group), grid_spec=pltpu.Pre...  23 us
  transfers between devices with their start and end apart: 4, of which 1 were waited for; matrix products, arithmetic and copies ran while one was open for 3% of the time, Pallas kernels for 57%

profile of v10, /device:TPU:0, one launch (start us, length us, event | category | flops | bytes accessed | tf_op | source)
XLA Modules:
  0.0 677.0 jit_solution(4662791617328946680)
XLA Ops:
  7.2 0.0 all-gather.5.cloned.1.call-start
  7.3 0.1 broadcast_add_fusion
  7.3 0.1 add.154
  7.4 1.2 slice.14.attn_ref
  8.6 1.9 gather_fusion
  10.5 55.0 %exchange.4 = (bf16[8,21,256,128]{3,2,1,0:T(8,128)(2,1)}, s32[4,2,128]{2,1,0:T(2,128)}) custom-call(bf16[21,512,128]{2,1,0:T(8,128)(2,1)} %refs_0_.3, s32[2,128]{1,0:T(2,128)} %bitcast.42), custom_call_target="tpu_custom_call" | custom-call | flops 1 | bytes 1 | tf_op jit(solution)/shard_map/exchange/pallas_call | solution.py:1601
  65.5 3.6 pick.2
  69.1 0.0 all-gather.7.cloned.1.call-start
  69.1 53.1 %exchange.5 = (bf16[8,21,256,128]{3,2,1,0:T(8,128)(2,1)}, bf16[4,32,4352]{2,1,0:T(8,128)(2,1)}) custom-call(bf16[21,512,128]{2,1,0:T(8,128)(2,1)} %refs_0_.3, bf16[32,4352]{1,0:T(8,128)(2,1)} %get-tuple-element.56.refs_1_), custom_call_target="tpu_custom_call" | custom-call | flops 1 | bytes 1 | tf_op jit(solution)/shard_map/exchange/pallas_call | solution.py:1601
  122.3 3.6 pick.3
  125.9 0.0 reduce-scatter.3.cloned.1.call-start
  126.0 86.5 %exchange.6 = (bf16[4,2,8,32,4352]{4,3,2,1,0:T(8,128)(2,1)}, bf16[4,32,4352]{2,1,0:T(8,128)(2,1)}) custom-call(bf16[4,32,4352]{2,1,0:T(8,128)(2,1)} %get-tuple-element.57.refs_0_, bf16[32,4352]{1,0:T(8,128)(2,1)} %get-tuple-element.59.refs_1_), custom_call_target="tpu_custom_call" | custom-call | flops 1 | bytes 1 | tf_op jit(solution)/shard_map/exchange/pallas_call | solution.py:1601
  212.5 1.0 copy.23.key_seg_ref
  213.6 1.9 multiply_sine_fusion
  215.5 0.7 constant_dynamic-slice_fusion
  216.2 0.3 fusion
  216.5 1.3 fusion.2.normed_ref.normed_hbm
  217.8 96.8 %attention_block.1 = (bf16[256,2304]{1,0:T(8,128)(2,1)}, bf16[1024,256]{1,0:T(8,128)(2,1)}, bf16[256,2048]{1,0:T(8,128)(2,1)}, f32[16,1,256]{2,1,0:T(1,128)}, f3...) custom-call(s32[1024,1]{1,0:T(8,128)} %copy.23.key_seg_ref, ...), custom_call_target="tpu_custom_call" | custom-call | flops 1 | bytes 1 | tf_op jit(solution)/shard_map/attention_block/pallas_call | solution.py:1262
  314.6 1.2 slice_reduce_fusion
  316.5 0.0 all-gather.7.cloned.1.call-done
  316.6 77.1 %feed_gather.1 = (bf16[768,2048]{1,0:T(8,128)(2,1)}, bf16[768,2048]{1,0:T(8,128)(2,1)}, bf16[2048,2048]{1,0:T(8,128)(2,1)}, bf16[2048,2048]{1,0:T(8,128)(2,1)}, ...) custom-call(s32[1]{0:T(128)} %bitcast.10.real_ref, ...), custom_call_target="tpu_custom_call" | custom-call | flops 1 | bytes 1 | tf_op jit(solution)/shard_map/feed_gather/pallas_call | solution.py:449
  393.7 0.0 reduce-scatter.5.cloned.1.call-start
  393.7 48.1 %plane_sum.1 = (f32[256,2048]{1,0:T(8,128)}, bf16[5632,512]{1,0:T(8,128)(2,1)}) custom-call(bf16[8,256,2048]{2,1,0:T(8,128)(2,1)} %bitcast.64, bf16[768,2048]{1,0:T(8,128)(2,1)} %get-tuple-element.73.gate_ref, bf16[768,2048]{1,0:T(8,128)(2,1)} %get-tuple-element.74.up_ref, bf16[2048,2048]{1,0:T(8,128)(2,1)} %bitcast.65), custom_call_target="tpu_custom_call" | custom-call | flops 1 | bytes 1 | tf_op jit(solution)/shard_map/plane_sum/pallas_call | solution.py:1770
  441.9 0.8 copy.26.inverse_ref
  442.7 0.1 copy-done.20
  442.8 0.1 fusion.12
  442.9 0.7 copy-done.10
  443.6 2.9 multiply_reduce_fusion
  446.6 3.7 fusion.14
  450.3 1.1 copy-done.5
  451.4 62.2 %attend_back_sum.1 = (bf16[256,2048]{1,0:T(8,128)(2,1)S(1)}, bf16[1024,256]{1,0:T(8,128)(2,1)S(1)}, bf16[256,2048]{1,0:T(8,128)(2,1)S(1)}, bf16[8,704,512]{2,1,0:T(8,128)(2,1)}) custom-call(bf16[256,2304]{1,0:T(8,128)(2,1)} %get-tuple-element.62.q_ref, bf16[1024,256]{1,0:T(8,128)(2,1)S(1)} %copy-done.2, bf16[1024,256]{1,0:T(8,128)(2,1)S(1)} %copy-done.2, ...), custom_call_target="tpu_custom_call" | custom-call | flops 1 | bytes 1 | tf_op jit(solution)/shard_map/attend_back_sum/pallas_call | solution.py:1081
  513.6 1.0 copy-done.1
  514.6 0.8 copy-done.6
  515.4 26.6 %exchange.7 = (bf16[4,256,256]{2,1,0:T(8,128)(2,1)}, bf16[8,256,256]{2,1,0:T(8,128)(2,1)}, bf16[8,256,256]{2,1,0:T(8,128)(2,1)}) custom-call(bf16[1024,256]{1,0:T(8,128)(2,1)} %copy-done.6, bf16[256,2048]{1,0:T(8,128)(2,1)} %copy-done.1, bf16[256,2048]{1,0:T(8,128)(2,1)} %get-tuple-element.111.branch_ref.refs_2_), custom_call_target="tpu_custom_call" | custom-call | flops 1 | bytes 1 | tf_op jit(solution)/shard_map/exchange/pallas_call | solution.py:1601
  542.0 11.0 %share_grad.1.shares_hbm = bf16[512,2048]{1,0:T(8,128)(2,1)} custom-call(bf16[2048,256]{1,0:T(8,128)(2,1)} %bitcast.72, bf16[2048,256]{1,0:T(8,128)(2,1)} %bitcast.73, bf16[2048,2048]{1,0:T(8,128)(2,1)} %bitcast.62, bf16[2048,2048]{1,0:T(8,128)(2,1)} %bitcast.63), custom_call_target="tpu_custom_call" | custom-call | flops 1 | bytes 1 | tf_op jit(solution)/shard_map/share_grad/pallas_call | solution.py:521
  553.1 0.1 reduce_sum.50.pair_grad_ref
  553.2 0.5 convolution_convert_fusion
  553.7 1.0 copy.25
  554.7 1.4 scatter_custom_fusion
  556.1 0.1 select_bitcast_fusion
  556.2 0.6 stack.23.at_ref
  556.9 2.8 add_convert_fusion
  559.7 0.3 reduce-scatter.5.cloned.1.call-done
  560.0 84.4 %tail_exchange.1 = (bf16[2,8,704,512]{3,2,1,0:T(8,128)(2,1)}, bf16[8,512,512]{2,1,0:T(8,128)(2,1)}, bf16[8,64,256]{2,1,0:T(8,128)(2,1)}, f32[8,2,2048]{2,1,0:T(2,128)}, f32[256,2048]{1,0:T(8,128)}) custom-call(bf16[512,2048]{1,0:T(8,128)(2,1)} %share_grad.1.shares_hbm, bf16[8,256,256]{2,1,0:T(8,128)(2,1)} %bitcast.69, bf16[2,704,512]{2,1,0:T(8,128)(2,1)} %bitcast.71, ...), custom_call_target="tpu_custom_call" | custom-call | flops 1 | bytes 1 | tf_op jit(solution)/shard_map/tail_exchange/pallas_call | solution.py:1482
  644.4 1.0 reduce_sum.52
  645.4 0.7 divide_subtract_fusion
  646.1 23.0 %adam.1 = (f32[21,512,128]{2,1,0:T(8,128)}, f32[21,512,128]{2,1,0:T(8,128)}, f32[21,512,128]{2,1,0:T(8,128)}) custom-call(s32[5,21]{1,0:T(8,128)} %stack.23.at_ref, bf16[11264,512]{1,0:T(8,128)(2,1)} %bitcast.48, bf16[11264,512]{1,0:T(8,128)(2,1)} %bitcast.49, bf16[11264,512]{1,0:T(8,128)(2,1)} %bitcast.50, bf16[5632,512]{1,0:T(8,128)(2,1)} %bitcast.51, ...), custom_call_target="tpu_custom_call" | custom-call | flops 1 | bytes 1 | tf_op jit(solution)/shard_map/adam/pallas_call | solution.py:638
  669.1 1.3 copy.28
  (64 shorter events, 0.3 us)
Async XLA Ops:
  7.2 307.5 %all-gather.5.cloned.1.call-start = ((), (), s32[]{:S(2)}) async-start(), calls=%async_computation.4 | async-start | bytes 5898240 | tf_op jit(solution)/shard_map/all_gather | solution.py:1867
  69.1 247.5 %all-gather.7.cloned.1.call-start = ((), (), s32[]{:S(2)}) async-start(), calls=%async_computation.5 | async-start | bytes 5898240 | tf_op jit(solution)/shard_map/all_gather | solution.py:1873
  125.9 86.6 %copy-start.24 = (s32[4,2,128]{2,1,0:T(2,128)S(1)}, s32[4,2,128]{2,1,0:T(2,128)}, u32[]{:S(2)}) copy-start(s32[4,2,128]{2,1,0:T(2,128)} %get-tuple-element.54) | copy-start | bytes 12292
  125.9 90.3 %copy-start.12 = (bf16[256,2048]{1,0:T(8,128)(2,1)S(1)}, bf16[256,2048]{1,0:T(8,128)(2,1)}, u32[]{:S(2)}) copy-start(bf16[256,2048]{1,0:T(8,128)(2,1)} %tokens_ref.3) | copy-start | bytes 3145732
  125.9 324.3 %reduce-scatter.3.cloned.1.call-start = ((), (), s32[]{:S(2)}) async-start(), calls=%async_computation.2 | async-start | bytes 3604480 | tf_op jit(solution)/shard_map/reduce_scatter | solution.py:1940
  126.0 90.5 %copy-start.18 = (f32[2,2048]{1,0:T(2,128)S(1)}, f32[2,2048]{1,0:T(2,128)}, u32[]{:S(2)}) copy-start(f32[2,2048]{1,0:T(2,128)} %gain_ref.3) | copy-start | bytes 49156
  393.7 166.4 %reduce-scatter.5.cloned.1.call-start = ((), (), s32[]{:S(2)}) async-start(), calls=%async_computation.3 | async-start | bytes 7208960 | tf_op jit(solution)/shard_map/reduce_scatter | solution.py:1944
  441.9 0.9 copy-start.20
  441.9 1.7 copy-start.10
  443.6 2.9 copy-start.11
  443.6 2.9 copy-start.14
  446.5 3.7 copy-start
  446.5 3.7 copy-start.2
  446.5 3.7 copy-start.3
  446.5 3.7 copy-start.4
  446.5 3.7 copy-start.7
  446.6 3.7 copy-start.8
  450.3 1.1 copy-start.5
  513.6 1.0 copy-start.1
  514.6 0.8 copy-start.6
  542.0 11.1 %copy-start.17 = (bf16[4,256,256]{2,1,0:T(8,128)(2,1)S(1)}, bf16[4,256,256]{2,1,0:T(8,128)(2,1)}, u32[]{:S(2)}) copy-start(bf16[4,256,256]{2,1,0:T(8,128)(2,1)} %get-tuple-element.87) | copy-start | bytes 1572868
  542.0 11.1 %copy-start.13 = (bf16[256,2048]{1,0:T(8,128)(2,1)S(1)}, bf16[256,2048]{1,0:T(8,128)(2,1)}, u32[]{:S(2)}) copy-start(bf16[256,2048]{1,0:T(8,128)(2,1)} %fusion.2.normed_ref.normed_hbm) | copy-start | bytes 3145732
  553.2 1.6 copy-start.16
  553.2 1.6 copy-start.9
  560.0 85.4 %copy-start.19 = (f32[2,2048]{1,0:T(2,128)S(1)}, f32[2,2048]{1,0:T(2,128)}, u32[]{:S(2)}) copy-start(f32[2,2048]{1,0:T(2,128)} %gain_ref.3) | copy-start | bytes 49156
  560.0 85.4 %copy-start.22 = (f32[2,2048]{1,0:T(2,128)S(1)}, f32[2,2048]{1,0:T(2,128)}, u32[]{:S(2)}) copy-start(f32[2,2048]{1,0:T(2,128)} %param.24) | copy-start | bytes 49156
  560.0 85.4 %copy-start.23 = (f32[2,2048]{1,0:T(2,128)S(1)}, f32[2,2048]{1,0:T(2,128)}, u32[]{:S(2)}) copy-start(f32[2,2048]{1,0:T(2,128)} %param.25) | copy-start | bytes 49156
  645.4 23.7 %copy-start.21 = (f32[2,2048]{1,0:T(2,128)}, f32[2,2048]{1,0:T(2,128)S(1)}, u32[]{:S(2)}) copy-start(f32[2,2048]{1,0:T(2,128)S(1)} %reduce_sum.52) | copy-start | bytes 49156
  646.1 23.0 %copy-start.15 = (f32[256,2048]{1,0:T(8,128)S(1)}, f32[256,2048]{1,0:T(8,128)}, u32[]{:S(2)}) copy-start(f32[256,2048]{1,0:T(8,128)} %get-tuple-element.130) | copy-start | bytes 6291460
Sparse Core Ops, SparseCore 0:
  69.2 128.0 all-gather.4
  199.5 98.7 all-gather.6
  393.8 53.4 reduce-scatter.2
  449.4 110.5 reduce-scatter.4

commit v11 on v10

--- a/solution.py
+++ b/solution.py
@@ -1181,6 +1181,11 @@
         first.pass_on(2)
         first.pass_on(5)
 
+    @pl.when(step == out_at + 2)
+    def _():
+        second.pass_on(1)
+        second.pass_on(4)
+
     @pl.when((step >= attend_at) & (step < out_at))
     def _():
         head = step - attend_at
@@ -1225,7 +1230,7 @@
         lax.fori_loop(0, rows // chunk, some, 0)
         first.pass_on(6)
         first.pass_on(3)
-        for came in (1, 4, 2, 5, 6, 3):
+        for came in (2, 5, 6, 3):
             second.pass_on(came)
         first.finish()
         second.finish()

time: 678 us -> 677 us (level)
  no operation moved by 1% of the time
where the time goes in v11:
time: 677 us; the launch traced here: 675 us
  Pallas kernels  629 us (93%)
  other arithmetic  16.2 us (2%)
  between operations  14.9 us (2%)
  local copies, waits for them, and re-layouts  13.8 us (2%)
    pallas_call x4, Pallas kernels, exchange(): pl.pallas_call(functools.partial(exchange_kernel, tasks, wires, len(array...  221 us
    pallas_call x1, Pallas kernels, attention_block(): pl.pallas_call(functools.partial(block_kernel, first, second, pair_task),...  94.2 us
    pallas_call x1, Pallas kernels, tail_exchange(): pl.pallas_call(functools.partial(tail_kernel, tasks), in_specs=[hbm] * 4...  84.4 us
    pallas_call x1, Pallas kernels, feed_gather(): pl.pallas_call(functools.partial(feed_gather_kernel, own, first, second,...  77.1 us
    pallas_call x1, Pallas kernels, attend_back_sum(): pl.pallas_call(functools.partial(attend_back_sum_kernel, sum_task, gather...  61.7 us
    pallas_call x1, Pallas kernels, plane_sum(): pl.pallas_call(functools.partial(plane_sum_kernel, own), in_specs=[vmem,...  49.6 us
    pallas_call x1, Pallas kernels, adam(): pl.pallas_call(functools.partial(adam_kernel, group), grid_spec=pltpu.Pre...  22.5 us
  transfers between devices with their start and end apart: 4, of which 1 were waited for; matrix products, arithmetic and copies ran while one was open for 3% of the time, Pallas kernels for 57%

profile of v11, /device:TPU:0, one launch (start us, length us, event | category | flops | bytes accessed | tf_op | source)
XLA Modules:
  0.0 675.1 jit_solution(12162264339151547559)
XLA Ops:
  7.2 0.0 all-gather.5.cloned.1.call-start
  7.3 0.1 broadcast_add_fusion
  7.3 0.1 add.154
  7.4 1.2 slice.14.attn_ref
  8.6 1.9 gather_fusion
  10.5 55.0 %exchange.4 = (bf16[8,21,256,128]{3,2,1,0:T(8,128)(2,1)}, s32[4,2,128]{2,1,0:T(2,128)}) custom-call(bf16[21,512,128]{2,1,0:T(8,128)(2,1)} %refs_0_.3, s32[2,128]{1,0:T(2,128)} %bitcast.42), custom_call_target="tpu_custom_call" | custom-call | flops 1 | bytes 1 | tf_op jit(solution)/shard_map/exchange/pallas_call | solution.py:1606
  65.5 3.6 pick.2
  69.1 0.0 all-gather.7.cloned.1.call-start
  69.1 53.1 %exchange.5 = (bf16[8,21,256,128]{3,2,1,0:T(8,128)(2,1)}, bf16[4,32,4352]{2,1,0:T(8,128)(2,1)}) custom-call(bf16[21,512,128]{2,1,0:T(8,128)(2,1)} %refs_0_.3, bf16[32,4352]{1,0:T(8,128)(2,1)} %get-tuple-element.56.refs_1_), custom_call_target="tpu_custom_call" | custom-call | flops 1 | bytes 1 | tf_op jit(solution)/shard_map/exchange/pallas_call | solution.py:1606
  122.3 3.6 pick.3
  125.9 0.0 reduce-scatter.3.cloned.1.call-start
  126.0 86.5 %exchange.6 = (bf16[4,2,8,32,4352]{4,3,2,1,0:T(8,128)(2,1)}, bf16[4,32,4352]{2,1,0:T(8,128)(2,1)}) custom-call(bf16[4,32,4352]{2,1,0:T(8,128)(2,1)} %get-tuple-element.57.refs_0_, bf16[32,4352]{1,0:T(8,128)(2,1)} %get-tuple-element.59.refs_1_), custom_call_target="tpu_custom_call" | custom-call | flops 1 | bytes 1 | tf_op jit(solution)/shard_map/exchange/pallas_call | solution.py:1606
  212.5 1.0 copy.23.key_seg_ref
  213.6 1.9 multiply_sine_fusion
  215.5 0.7 constant_dynamic-slice_fusion
  216.2 0.3 fusion
  216.5 1.3 fusion.2.normed_ref.normed_hbm
  217.8 94.2 %attention_block.1 = (bf16[256,2304]{1,0:T(8,128)(2,1)}, bf16[1024,256]{1,0:T(8,128)(2,1)}, bf16[256,2048]{1,0:T(8,128)(2,1)}, f32[16,1,256]{2,1,0:T(1,128)}, f3...) custom-call(s32[1024,1]{1,0:T(8,128)} %copy.23.key_seg_ref, ...), custom_call_target="tpu_custom_call" | custom-call | flops 1 | bytes 1 | tf_op jit(solution)/shard_map/attention_block/pallas_call | solution.py:1267
  312.0 1.2 slice_reduce_fusion
  313.9 0.0 all-gather.7.cloned.1.call-done
  314.0 77.1 %feed_gather.1 = (bf16[768,2048]{1,0:T(8,128)(2,1)}, bf16[768,2048]{1,0:T(8,128)(2,1)}, bf16[2048,2048]{1,0:T(8,128)(2,1)}, bf16[2048,2048]{1,0:T(8,128)(2,1)}, ...) custom-call(s32[1]{0:T(128)} %bitcast.10.real_ref, ...), custom_call_target="tpu_custom_call" | custom-call | flops 1 | bytes 1 | tf_op jit(solution)/shard_map/feed_gather/pallas_call | solution.py:449
  391.1 0.0 reduce-scatter.5.cloned.1.call-start
  391.1 49.6 %plane_sum.1 = (f32[256,2048]{1,0:T(8,128)}, bf16[5632,512]{1,0:T(8,128)(2,1)}) custom-call(bf16[8,256,2048]{2,1,0:T(8,128)(2,1)} %bitcast.64, bf16[768,2048]{1,0:T(8,128)(2,1)} %get-tuple-element.73.gate_ref, bf16[768,2048]{1,0:T(8,128)(2,1)} %get-tuple-element.74.up_ref, bf16[2048,2048]{1,0:T(8,128)(2,1)} %bitcast.65), custom_call_target="tpu_custom_call" | custom-call | flops 1 | bytes 1 | tf_op jit(solution)/shard_map/plane_sum/pallas_call | solution.py:1775
  440.7 0.8 copy.26.inverse_ref
  441.5 0.1 copy-done.20
  441.6 0.1 fusion.12
  441.7 0.7 copy-done.10
  442.4 2.9 multiply_reduce_fusion
  445.4 3.6 fusion.14
  449.1 1.1 copy-done.5
  450.2 61.7 %attend_back_sum.1 = (bf16[256,2048]{1,0:T(8,128)(2,1)S(1)}, bf16[1024,256]{1,0:T(8,128)(2,1)S(1)}, bf16[256,2048]{1,0:T(8,128)(2,1)S(1)}, bf16[8,704,512]{2,1,0:T(8,128)(2,1)}) custom-call(bf16[256,2304]{1,0:T(8,128)(2,1)} %get-tuple-element.62.q_ref, bf16[1024,256]{1,0:T(8,128)(2,1)S(1)} %copy-done.2, bf16[1024,256]{1,0:T(8,128)(2,1)S(1)} %copy-done.2, ...), custom_call_target="tpu_custom_call" | custom-call | flops 1 | bytes 1 | tf_op jit(solution)/shard_map/attend_back_sum/pallas_call | solution.py:1081
  511.9 1.0 copy-done.1
  512.9 0.8 copy-done.6
  513.7 26.6 %exchange.7 = (bf16[4,256,256]{2,1,0:T(8,128)(2,1)}, bf16[8,256,256]{2,1,0:T(8,128)(2,1)}, bf16[8,256,256]{2,1,0:T(8,128)(2,1)}) custom-call(bf16[1024,256]{1,0:T(8,128)(2,1)} %copy-done.6, bf16[256,2048]{1,0:T(8,128)(2,1)} %copy-done.1, bf16[256,2048]{1,0:T(8,128)(2,1)} %get-tuple-element.111.branch_ref.refs_2_), custom_call_target="tpu_custom_call" | custom-call | flops 1 | bytes 1 | tf_op jit(solution)/shard_map/exchange/pallas_call | solution.py:1606
  540.4 11.0 %share_grad.1.shares_hbm = bf16[512,2048]{1,0:T(8,128)(2,1)} custom-call(bf16[2048,256]{1,0:T(8,128)(2,1)} %bitcast.72, bf16[2048,256]{1,0:T(8,128)(2,1)} %bitcast.73, bf16[2048,2048]{1,0:T(8,128)(2,1)} %bitcast.62, bf16[2048,2048]{1,0:T(8,128)(2,1)} %bitcast.63), custom_call_target="tpu_custom_call" | custom-call | flops 1 | bytes 1 | tf_op jit(solution)/shard_map/share_grad/pallas_call | solution.py:521
  551.4 0.1 reduce_sum.50.pair_grad_ref
  551.5 0.5 convolution_convert_fusion
  552.0 1.0 copy.25
  553.0 1.4 scatter_custom_fusion
  554.4 0.1 select_bitcast_fusion
  554.5 0.6 stack.23.at_ref
  555.1 2.8 add_convert_fusion
  558.0 0.7 reduce-scatter.5.cloned.1.call-done
  558.7 84.4 %tail_exchange.1 = (bf16[2,8,704,512]{3,2,1,0:T(8,128)(2,1)}, bf16[8,512,512]{2,1,0:T(8,128)(2,1)}, bf16[8,64,256]{2,1,0:T(8,128)(2,1)}, f32[8,2,2048]{2,1,0:T(2,128)}, f32[256,2048]{1,0:T(8,128)}) custom-call(bf16[512,2048]{1,0:T(8,128)(2,1)} %share_grad.1.shares_hbm, bf16[8,256,256]{2,1,0:T(8,128)(2,1)} %bitcast.69, bf16[2,704,512]{2,1,0:T(8,128)(2,1)} %bitcast.71, ...), custom_call_target="tpu_custom_call" | custom-call | flops 1 | bytes 1 | tf_op jit(solution)/shard_map/tail_exchange/pallas_call | solution.py:1487
  643.1 1.0 reduce_sum.52
  644.1 0.7 divide_subtract_fusion
  644.7 22.5 %adam.1 = (f32[21,512,128]{2,1,0:T(8,128)}, f32[21,512,128]{2,1,0:T(8,128)}, f32[21,512,128]{2,1,0:T(8,128)}) custom-call(s32[5,21]{1,0:T(8,128)} %stack.23.at_ref, bf16[11264,512]{1,0:T(8,128)(2,1)} %bitcast.48, bf16[11264,512]{1,0:T(8,128)(2,1)} %bitcast.49, bf16[11264,512]{1,0:T(8,128)(2,1)} %bitcast.50, bf16[5632,512]{1,0:T(8,128)(2,1)} %bitcast.51, ...), custom_call_target="tpu_custom_call" | custom-call | flops 1 | bytes 1 | tf_op jit(solution)/shard_map/adam/pallas_call | solution.py:638
  667.3 1.3 copy.28
  (64 shorter events, 0.3 us)
Async XLA Ops:
  7.2 304.8 %all-gather.5.cloned.1.call-start = ((), (), s32[]{:S(2)}) async-start(), calls=%async_computation.4 | async-start | bytes 5898240 | tf_op jit(solution)/shard_map/all_gather | solution.py:1872
  69.1 244.9 %all-gather.7.cloned.1.call-start = ((), (), s32[]{:S(2)}) async-start(), calls=%async_computation.5 | async-start | bytes 5898240 | tf_op jit(solution)/shard_map/all_gather | solution.py:1878
  125.9 86.6 %copy-start.24 = (s32[4,2,128]{2,1,0:T(2,128)S(1)}, s32[4,2,128]{2,1,0:T(2,128)}, u32[]{:S(2)}) copy-start(s32[4,2,128]{2,1,0:T(2,128)} %get-tuple-element.54) | copy-start | bytes 12292
  125.9 90.3 %copy-start.12 = (bf16[256,2048]{1,0:T(8,128)(2,1)S(1)}, bf16[256,2048]{1,0:T(8,128)(2,1)}, u32[]{:S(2)}) copy-start(bf16[256,2048]{1,0:T(8,128)(2,1)} %tokens_ref.3) | copy-start | bytes 3145732
  125.9 323.1 %reduce-scatter.3.cloned.1.call-start = ((), (), s32[]{:S(2)}) async-start(), calls=%async_computation.2 | async-start | bytes 3604480 | tf_op jit(solution)/shard_map/reduce_scatter | solution.py:1945
  126.0 90.5 %copy-start.18 = (f32[2,2048]{1,0:T(2,128)S(1)}, f32[2,2048]{1,0:T(2,128)}, u32[]{:S(2)}) copy-start(f32[2,2048]{1,0:T(2,128)} %gain_ref.3) | copy-start | bytes 49156
  391.1 167.6 %reduce-scatter.5.cloned.1.call-start = ((), (), s32[]{:S(2)}) async-start(), calls=%async_computation.3 | async-start | bytes 7208960 | tf_op jit(solution)/shard_map/reduce_scatter | solution.py:1949
  440.7 0.9 copy-start.20
  440.7 1.7 copy-start.10
  442.4 2.9 copy-start.11
  442.4 2.9 copy-start.14
  445.3 3.7 copy-start
  445.4 3.7 copy-start.2
  445.4 3.7 copy-start.3
  445.4 3.7 copy-start.4
  445.4 3.7 copy-start.7
  445.4 3.7 copy-start.8
  449.1 1.1 copy-start.5
  511.9 1.0 copy-start.1
  512.9 0.8 copy-start.6
  540.3 11.0 %copy-start.17 = (bf16[4,256,256]{2,1,0:T(8,128)(2,1)S(1)}, bf16[4,256,256]{2,1,0:T(8,128)(2,1)}, u32[]{:S(2)}) copy-start(bf16[4,256,256]{2,1,0:T(8,128)(2,1)} %get-tuple-element.87) | copy-start | bytes 1572868
  540.4 11.1 %copy-start.13 = (bf16[256,2048]{1,0:T(8,128)(2,1)S(1)}, bf16[256,2048]{1,0:T(8,128)(2,1)}, u32[]{:S(2)}) copy-start(bf16[256,2048]{1,0:T(8,128)(2,1)} %fusion.2.normed_ref.normed_hbm) | copy-start | bytes 3145732
  551.5 1.6 copy-start.16
  551.5 1.5 copy-start.9
  558.7 85.4 %copy-start.19 = (f32[2,2048]{1,0:T(2,128)S(1)}, f32[2,2048]{1,0:T(2,128)}, u32[]{:S(2)}) copy-start(f32[2,2048]{1,0:T(2,128)} %gain_ref.3) | copy-start | bytes 49156
  558.7 85.4 %copy-start.22 = (f32[2,2048]{1,0:T(2,128)S(1)}, f32[2,2048]{1,0:T(2,128)}, u32[]{:S(2)}) copy-start(f32[2,2048]{1,0:T(2,128)} %param.24) | copy-start | bytes 49156
  558.7 85.4 %copy-start.23 = (f32[2,2048]{1,0:T(2,128)S(1)}, f32[2,2048]{1,0:T(2,128)}, u32[]{:S(2)}) copy-start(f32[2,2048]{1,0:T(2,128)} %param.25) | copy-start | bytes 49156
  644.1 23.2 %copy-start.21 = (f32[2,2048]{1,0:T(2,128)}, f32[2,2048]{1,0:T(2,128)S(1)}, u32[]{:S(2)}) copy-start(f32[2,2048]{1,0:T(2,128)S(1)} %reduce_sum.52) | copy-start | bytes 49156
  644.7 22.6 %copy-start.15 = (f32[256,2048]{1,0:T(8,128)S(1)}, f32[256,2048]{1,0:T(8,128)}, u32[]{:S(2)}) copy-start(f32[256,2048]{1,0:T(8,128)} %get-tuple-element.130) | copy-start | bytes 6291460
Sparse Core Ops, SparseCore 0:
  69.2 128.0 all-gather.4
  199.5 98.7 all-gather.6
  391.2 54.6 reduce-scatter.2
  448.1 110.5 reduce-scatter.4
